TPU v7x, 32 devices: a whole 2x2x4 slice. The times are simulated.
32 devices in a mesh: dp: 4 (over y, x), seq: 4 (over z), fsdp: 2 (over core).
Axes of the slice: x: 2, y: 2, z: 4, core: 2. Of those that a mesh axis runs over, the one named last changes fastest.
Arguments:
- hidden: bfloat16 [8, 2560, 768], P(('dp', 'fsdp'), 'seq'), may hold values from -6 to 6
- teacher_hidden: bfloat16 [8, 2560, 768], P(('dp', 'fsdp'), 'seq'), may hold values from -6 to 6
- segments: int32 [8, 2560], P(('dp', 'fsdp')), may hold values from 0 to 3, as said below
- latent_qkv: float32 [2304, 768], P('fsdp'), may hold values from -0.375 to 0.375
- latent_out: float32 [768, 768], P('fsdp'), may hold values from -1.25 to 1.25
- latent_up: float32 [3072, 768], P('fsdp'), may hold values from -0.21875 to 0.21875
- latent_down: float32 [768, 3072], P('fsdp'), may hold values from -0.109375 to 0.109375
- biases: float32 [4, 768], replicated, may hold values from -2.5 to 2.5
- up_bias: float32 [3072], replicated, may hold values from -2.5 to 2.5
- norm_gains: float32 [2, 768], replicated, may hold values from 0.5 to 1.5
- norm_shifts: float32 [2, 768], replicated, may hold values from -2.5 to 2.5
- teacher_qkv: bfloat16 [2304, 768], P('fsdp'), may hold values from -0.3125 to 0.3125
- teacher_out: bfloat16 [768, 768], P('fsdp'), may hold values from -1.25 to 1.25
- teacher_up: bfloat16 [3072, 768], P('fsdp'), may hold values from -0.21875 to 0.21875
- teacher_down: bfloat16 [768, 3072], P('fsdp'), may hold values from -0.109375 to 0.109375
Outputs:
- student_out: bfloat16 [8, 2560, 768], P(('dp', 'fsdp'), 'seq')
- hidden_grad: bfloat16 [8, 2560, 768], P(('dp', 'fsdp'), 'seq')
- grad_qkv: float32 [2304, 768], P('fsdp')
- grad_out: float32 [768, 768], P('fsdp')
- grad_up: float32 [3072, 768], P('fsdp')
- grad_down: float32 [768, 3072], P('fsdp')
- grad_biases: float32 [4, 768], P(None, 'fsdp')
- grad_up_bias: float32 [3072], P('fsdp')
- grad_gains: float32 [2, 768], P(None, 'fsdp')
- grad_shifts: float32 [2, 768], P(None, 'fsdp')
Inputs may be any that keep to these rules, and one draw needn't show every extreme that they name: In every group the first 1024 positions have segment 0 (the prompt). The remaining 1536 positions hold 3 continuations with segments 1 to 3 in order, each of 1 to 1024 positions, one of exactly 1024.
All inputs are finite; a program needn't handle non-finite values.
Results may differ from a plain program's by a relative error of at most 0.012.
The roundings to bfloat16 on the way count: a program that leaves them out, or rounds other values in their place, can miss the bound.
Values may be sent and summed in bfloat16 or wider, within the bound.
A program may use at most 256 MiB of HBM per device.

v0:
```python
import jax
import jax.numpy as jnp
from jax import lax
from jax.sharding import PartitionSpec as P

HEADS = 12
PROMPT = 1024
BLOCK = 512


CLIP = 2.5
EPS = 1e-05


def binarize(latent):
    row_scale = jnp.mean(jnp.abs(latent), axis=1, keepdims=True)
    return (row_scale * jnp.sign(latent)).astype(jnp.bfloat16)


def norm_rows(values, gain_row, shift_row):
    centre = jnp.mean(values, axis=-1, keepdims=True)
    shifted = values - centre
    spread = jnp.mean(shifted * shifted, axis=-1, keepdims=True)
    return shifted * lax.rsqrt(spread + EPS) * gain_row + shift_row


def clip_range(values):
    return jnp.clip(values, -CLIP, CLIP)


def gelu_exact(values):
    return jax.nn.gelu(values, approximate=False)


def project(activations, weight):
    return jnp.einsum("usd,ed->use", activations, weight, preferred_element_type=jnp.float32)


def back_project(gradients, weight):
    return jnp.einsum("use,ed->usd", gradients, weight, preferred_element_type=jnp.float32)


def weight_grad(activations, gradients):
    return jnp.einsum("usd,use->ed", activations, gradients, preferred_element_type=jnp.float32)


def split_heads(values, heads_local):
    return values.reshape(
        values.shape[0], values.shape[1], heads_local, values.shape[2] // heads_local
    )


def stack_rows(stacked):
    leading = jnp.moveaxis(stacked, 0, 1)
    return leading.reshape(
        (leading.shape[0], leading.shape[1] * leading.shape[2]) + leading.shape[3:]
    )


def stack_last(stacked):
    moved = jnp.moveaxis(stacked, 0, -2)
    return moved.reshape(moved.shape[:-2] + (moved.shape[-2] * moved.shape[-1],))


def cont_mask(segment, row_start):
    row_seg = lax.dynamic_slice_in_dim(segment, row_start, BLOCK, 1)
    allowed = (segment[:, None, :] == 0) | (segment[:, None, :] == row_seg[:, :, None])
    return allowed[:, None, :, :]


def block_scores(query_rows, key_set, allowed):
    scores = (
        jnp.einsum("uqhd,ukhd->uhqk", query_rows, key_set, preferred_element_type=jnp.float32)
        * 0.125
    )
    return jnp.where(allowed, scores, -1e30)


def block_forward(query_rows, key_set, value_set, allowed):
    scores = block_scores(query_rows, key_set, allowed)
    row_max = jnp.max(scores, axis=-1, keepdims=True)
    exponent = jnp.exp(scores - row_max)
    row_total = jnp.sum(exponent, axis=-1, keepdims=True)
    softmax_w = (exponent / row_total).astype(jnp.bfloat16)
    context = jnp.einsum(
        "uhqk,ukhd->uqhd", softmax_w, value_set, preferred_element_type=jnp.float32
    )
    return (context, row_max[..., 0] + jnp.log(row_total[..., 0]))


def attention_forward(queries, key_set, value_set, segment, heads_local):
    heads_q = split_heads(queries, heads_local)
    heads_k = split_heads(key_set, heads_local)
    heads_v = split_heads(value_set, heads_local)
    prompt_keys = heads_k[:, :PROMPT]
    prompt_vals = heads_v[:, :PROMPT]
    row_count = queries.shape[1]

    def prompt_block(row_start):
        query_rows = lax.dynamic_slice_in_dim(heads_q, row_start, BLOCK, 1)
        return block_forward(query_rows, prompt_keys, prompt_vals, True)

    def cont_block(row_start):
        query_rows = lax.dynamic_slice_in_dim(heads_q, row_start, BLOCK, 1)
        return block_forward(query_rows, heads_k, heads_v, cont_mask(segment, row_start))

    prompt_starts = jnp.arange(PROMPT // BLOCK, dtype=jnp.int32) * BLOCK
    cont_starts = PROMPT + jnp.arange((row_count - PROMPT) // BLOCK, dtype=jnp.int32) * BLOCK
    prompt_ctx, prompt_lse = lax.map(prompt_block, prompt_starts)
    cont_ctx, cont_lse = lax.map(cont_block, cont_starts)
    context = jnp.concatenate([stack_rows(prompt_ctx), stack_rows(cont_ctx)], axis=1)
    log_total = jnp.concatenate([stack_last(prompt_lse), stack_last(cont_lse)], axis=2)
    return (context.reshape(queries.shape).astype(jnp.bfloat16), log_total)


def attention_backward(queries, key_set, value_set, segment, log_total, grad_ctx, heads_local):
    heads_q = split_heads(queries, heads_local)
    heads_k = split_heads(key_set, heads_local)
    heads_v = split_heads(value_set, heads_local)
    heads_g = split_heads(grad_ctx, heads_local)
    row_count = queries.shape[1]

    def block_backward(row_start, key_rows, value_rows, allowed):
        query_rows = lax.dynamic_slice_in_dim(heads_q, row_start, BLOCK, 1)
        grad_rows = lax.dynamic_slice_in_dim(heads_g, row_start, BLOCK, 1)
        total_rows = lax.dynamic_slice_in_dim(log_total, row_start, BLOCK, 2)
        scores = block_scores(query_rows, key_rows, allowed)
        softmax_f = jnp.exp(scores - total_rows[..., None])
        grad_w = jnp.einsum(
            "uqhd,ukhd->uhqk", grad_rows, value_rows, preferred_element_type=jnp.float32
        )
        centre = jnp.sum(softmax_f * grad_w, axis=-1, keepdims=True)
        grad_s = (softmax_f * (grad_w - centre)).astype(jnp.bfloat16)
        grad_q = (
            jnp.einsum("uhqk,ukhd->uqhd", grad_s, key_rows, preferred_element_type=jnp.float32)
            * 0.125
        )
        grad_k = (
            jnp.einsum("uhqk,uqhd->ukhd", grad_s, query_rows, preferred_element_type=jnp.float32)
            * 0.125
        )
        grad_v = jnp.einsum(
            "uhqk,uqhd->ukhd",
            softmax_f.astype(jnp.bfloat16),
            grad_rows,
            preferred_element_type=jnp.float32,
        )
        return (grad_q, grad_k, grad_v)

    prompt_keys = heads_k[:, :PROMPT]
    prompt_vals = heads_v[:, :PROMPT]

    def prompt_step(running, row_start):
        grad_q, grad_k, grad_v = block_backward(row_start, prompt_keys, prompt_vals, True)
        return ((running[0] + grad_k, running[1] + grad_v), grad_q)

    def cont_step(running, row_start):
        grad_q, grad_k, grad_v = block_backward(
            row_start, heads_k, heads_v, cont_mask(segment, row_start)
        )
        return ((running[0] + grad_k, running[1] + grad_v), grad_q)

    prompt_starts = jnp.arange(PROMPT // BLOCK, dtype=jnp.int32) * BLOCK
    cont_starts = PROMPT + jnp.arange((row_count - PROMPT) // BLOCK, dtype=jnp.int32) * BLOCK
    prompt_zero = jnp.zeros(prompt_keys.shape, jnp.float32)
    full_zero = jnp.zeros(heads_k.shape, jnp.float32)
    (prompt_gk, prompt_gv), prompt_gq = lax.scan(
        prompt_step, (prompt_zero, prompt_zero), prompt_starts
    )
    (cont_gk, cont_gv), cont_gq = lax.scan(cont_step, (full_zero, full_zero), cont_starts)
    rest_zero = jnp.zeros_like(cont_gk[:, PROMPT:])
    key_grad = cont_gk + jnp.concatenate([prompt_gk, rest_zero], axis=1)
    value_grad = cont_gv + jnp.concatenate([prompt_gv, rest_zero], axis=1)
    query_grad = jnp.concatenate([stack_rows(prompt_gq), stack_rows(cont_gq)], axis=1)
    return (
        query_grad.reshape(queries.shape).astype(jnp.bfloat16),
        key_grad.reshape(queries.shape).astype(jnp.bfloat16),
        value_grad.reshape(queries.shape).astype(jnp.bfloat16),
    )


def on_device(
    hidden,
    teacher_hidden,
    segments,
    latent_qkv,
    latent_out,
    latent_up,
    latent_down,
    biases,
    up_bias,
    norm_gains,
    norm_shifts,
    teacher_qkv,
    teacher_out,
    teacher_up,
    teacher_down,
):
    full_qkv, full_out, full_up, full_down = (
        lax.all_gather(latent_qkv, "fsdp", axis=0, tiled=True),
        lax.all_gather(latent_out, "fsdp", axis=0, tiled=True),
        lax.all_gather(latent_up, "fsdp", axis=0, tiled=True),
        lax.all_gather(latent_down, "fsdp", axis=0, tiled=True),
    )
    bin_qkv = binarize(full_qkv)
    bin_out = binarize(full_out)
    bin_up = binarize(full_up)
    bin_down = binarize(full_down)
    teach_qkv, teach_out, teach_up, teach_down = (
        lax.all_gather(teacher_qkv, "fsdp", axis=0, tiled=True),
        lax.all_gather(teacher_out, "fsdp", axis=0, tiled=True),
        lax.all_gather(teacher_up, "fsdp", axis=0, tiled=True),
        lax.all_gather(teacher_down, "fsdp", axis=0, tiled=True),
    )
    heads_local = HEADS // lax.axis_size("seq")
    group_count = hidden.shape[0]
    token_count = hidden.shape[1]
    model_width = hidden.shape[2]
    stud_in = hidden.astype(jnp.float32)
    clip_in, clip_pull = jax.vjp(clip_range, stud_in)
    first_act = clip_in.astype(jnp.bfloat16)
    qkv_bias = jnp.concatenate([biases[0], jnp.zeros_like(biases[0]), biases[1]])
    stud_qkv = (project(first_act, bin_qkv) + qkv_bias).astype(jnp.bfloat16)
    teach_act = project(teacher_hidden, teach_qkv).astype(jnp.bfloat16)
    stud_heads, teach_heads = (
        lax.all_to_all(
            stud_qkv.reshape(group_count, token_count, 3, model_width),
            "seq",
            split_axis=3,
            concat_axis=1,
            tiled=True,
        ),
        lax.all_to_all(
            teach_act.reshape(group_count, token_count, 3, model_width),
            "seq",
            split_axis=3,
            concat_axis=1,
            tiled=True,
        ),
    )
    stud_ctx, stud_lse = attention_forward(
        stud_heads[:, :, 0], stud_heads[:, :, 1], stud_heads[:, :, 2], segments, heads_local
    )
    teach_ctx, unused = attention_forward(
        teach_heads[:, :, 0], teach_heads[:, :, 1], teach_heads[:, :, 2], segments, heads_local
    )
    stud_back, teach_back = (
        lax.all_to_all(stud_ctx, "seq", split_axis=1, concat_axis=2, tiled=True),
        lax.all_to_all(teach_ctx, "seq", split_axis=1, concat_axis=2, tiled=True),
    )
    attn_out = project(stud_back, bin_out) + biases[2]
    mid_norm, mid_pull = jax.vjp(norm_rows, stud_in + attn_out, norm_gains[0], norm_shifts[0])
    mid_clip, mid_clip_pull = jax.vjp(clip_range, mid_norm)
    mid_act = mid_clip.astype(jnp.bfloat16)
    pre_gelu = project(mid_act, bin_up) + up_bias
    gelu_out, gelu_pull = jax.vjp(gelu_exact, pre_gelu)
    gelu_act = gelu_out.astype(jnp.bfloat16)
    ffn_out = project(gelu_act, bin_down) + biases[3]
    final_norm, final_pull = jax.vjp(norm_rows, mid_norm + ffn_out, norm_gains[1], norm_shifts[1])
    unit_gain = jnp.ones((model_width,), jnp.float32)
    zero_shift = jnp.zeros((model_width,), jnp.float32)
    teach_res = teacher_hidden.astype(jnp.float32) + project(teach_back, teach_out)
    teach_mid = norm_rows(teach_res, unit_gain, zero_shift)
    teach_hid = gelu_exact(project(teach_mid.astype(jnp.bfloat16), teach_up)).astype(jnp.bfloat16)
    teach_final = norm_rows(teach_mid + project(teach_hid, teach_down), unit_gain, zero_shift)
    grad_final = final_norm - teach_final
    grad_sum_two, grad_gain_two, grad_shift_two = final_pull(grad_final)
    grad_ffn = grad_sum_two.astype(jnp.bfloat16)
    grad_down_w = weight_grad(gelu_act, grad_ffn)
    (grad_gelu_in,) = gelu_pull(back_project(grad_ffn, bin_down))
    grad_hidden = grad_gelu_in.astype(jnp.bfloat16)
    grad_up_w = weight_grad(mid_act, grad_hidden)
    (grad_mid_clip,) = mid_clip_pull(back_project(grad_hidden, bin_up))
    grad_res_one, grad_gain_one, grad_shift_one = mid_pull(grad_mid_clip + grad_sum_two)
    grad_attn = grad_res_one.astype(jnp.bfloat16)
    grad_out_w = weight_grad(stud_back, grad_attn)
    grad_ctx = back_project(grad_attn, bin_out).astype(jnp.bfloat16)
    heads_grad = lax.all_to_all(grad_ctx, "seq", split_axis=2, concat_axis=1, tiled=True)
    grad_query, grad_key, grad_value = attention_backward(
        stud_heads[:, :, 0],
        stud_heads[:, :, 1],
        stud_heads[:, :, 2],
        segments,
        stud_lse,
        heads_grad,
        heads_local,
    )
    token_grad = lax.all_to_all(
        jnp.stack([grad_query, grad_key, grad_value], axis=2),
        "seq",
        split_axis=1,
        concat_axis=3,
        tiled=True,
    )
    grad_qkv_act = token_grad.reshape(group_count, token_count, 3 * model_width)
    grad_qkv_w = weight_grad(first_act, grad_qkv_act)
    (grad_in_clip,) = clip_pull(back_project(grad_qkv_act, bin_qkv))
    grad_input = (grad_res_one + grad_in_clip).astype(jnp.bfloat16)
    grad_bias_rows = jnp.stack(
        [
            jnp.sum(token_grad[:, :, 0].astype(jnp.float32), axis=(0, 1)),
            jnp.sum(token_grad[:, :, 2].astype(jnp.float32), axis=(0, 1)),
            jnp.sum(grad_attn.astype(jnp.float32), axis=(0, 1)),
            jnp.sum(grad_ffn.astype(jnp.float32), axis=(0, 1)),
        ]
    )
    grad_bias_up = jnp.sum(grad_hidden.astype(jnp.float32), axis=(0, 1))
    grad_gain_rows = jnp.stack([grad_gain_one, grad_gain_two])
    grad_shift_rows = jnp.stack([grad_shift_one, grad_shift_two])
    shards = (
        lax.psum_scatter(
            grad_qkv_w.astype(jnp.bfloat16), "fsdp", scatter_dimension=0, tiled=True
        ).astype(jnp.float32),
        lax.psum_scatter(
            grad_out_w.astype(jnp.bfloat16), "fsdp", scatter_dimension=0, tiled=True
        ).astype(jnp.float32),
        lax.psum_scatter(
            grad_up_w.astype(jnp.bfloat16), "fsdp", scatter_dimension=0, tiled=True
        ).astype(jnp.float32),
        lax.psum_scatter(
            grad_down_w.astype(jnp.bfloat16), "fsdp", scatter_dimension=0, tiled=True
        ).astype(jnp.float32),
        lax.psum_scatter(
            grad_bias_rows.astype(jnp.bfloat16), "fsdp", scatter_dimension=1, tiled=True
        ).astype(jnp.float32),
        lax.psum_scatter(
            grad_bias_up.astype(jnp.bfloat16), "fsdp", scatter_dimension=0, tiled=True
        ).astype(jnp.float32),
        lax.psum_scatter(
            grad_gain_rows.astype(jnp.bfloat16), "fsdp", scatter_dimension=1, tiled=True
        ).astype(jnp.float32),
        lax.psum_scatter(
            grad_shift_rows.astype(jnp.bfloat16), "fsdp", scatter_dimension=1, tiled=True
        ).astype(jnp.float32),
    )
    totals = (
        lax.psum(shards[0].astype(jnp.bfloat16), ("dp", "seq")).astype(jnp.float32),
        lax.psum(shards[1].astype(jnp.bfloat16), ("dp", "seq")).astype(jnp.float32),
        lax.psum(shards[2].astype(jnp.bfloat16), ("dp", "seq")).astype(jnp.float32),
        lax.psum(shards[3].astype(jnp.bfloat16), ("dp", "seq")).astype(jnp.float32),
        lax.psum(shards[4].astype(jnp.bfloat16), ("dp", "seq")).astype(jnp.float32),
        lax.psum(shards[5].astype(jnp.bfloat16), ("dp", "seq")).astype(jnp.float32),
        lax.psum(shards[6].astype(jnp.bfloat16), ("dp", "seq")).astype(jnp.float32),
        lax.psum(shards[7].astype(jnp.bfloat16), ("dp", "seq")).astype(jnp.float32),
    )
    return (
        final_norm.astype(jnp.bfloat16),
        grad_input,
        totals[0],
        totals[1],
        totals[2],
        totals[3],
        totals[4],
        totals[5],
        totals[6],
        totals[7],
    )


def solution(mesh):
    placed = (
        P(("dp", "fsdp"), "seq", None),
        P(("dp", "fsdp"), "seq", None),
        P(("dp", "fsdp"), None),
        P("fsdp", None),
        P("fsdp", None),
        P("fsdp", None),
        P("fsdp", None),
        P(),
        P(),
        P(),
        P(),
        P("fsdp", None),
        P("fsdp", None),
        P("fsdp", None),
        P("fsdp", None),
    )
    return jax.shard_map(
        on_device,
        mesh=mesh,
        in_specs=placed,
        out_specs=(
            P(("dp", "fsdp"), "seq", None),
            P(("dp", "fsdp"), "seq", None),
            P("fsdp", None),
            P("fsdp", None),
            P("fsdp", None),
            P("fsdp", None),
            P(None, "fsdp"),
            P("fsdp"),
            P(None, "fsdp"),
            P(None, "fsdp"),
        ),
        check_vma=False,
    )
```

profile of v0, /device:TPU:24, one launch (start us, length us, event | category | flops | bytes accessed | tf_op | source)
XLA Modules:
  0.0 1274.6 jit_solution(16022003445447509084)
XLA Ops:
  11.9 11.6 all-gather.17.cloned.1.call-done
  23.5 6.1 convolution_convert_fusion.3
  49.0 80.5 %all-to-all-done.2 = bf16[1,640,3,768]{1,2,0,3:T(4,128)(2,1)} async-done(((bf16[1,640,3,768]{1,2,0,3:T(4,128)(2,1)}), bf16[1,640,3,768]{1,2,0,3:T(4,128)(2,1)}, u32[]{:S(2)}, u32[]{:S(2)}) %all-to-all-start.2) | async-done | bytes 2949152 | tf_op jit(solution)/shard_map/all_to_all | solution.py:233
  134.5 73.2 %while.77 = (s32[]{:T(128)}, bf16[3,1,512,3,64]{2,4,3,1,0:T(8,128)(2,1)S(1)}, s32[1,2560]{1,0:T(1,128)S(1)}, s32[3]{0:T(128)S(1)}, bf16[1,2560,3,64]{1,3,2,0:T(8...) while((s32[]{:T(128)}, ...), condition=%wide.region_23.25_spmd, body=%wide.region_20.24_spmd.sunk | while | flops 1032852480 | bytes 36701352 | solution.py:110
  138.1 13.7 %fusion.345 = (f32[3,512]{1,0:T(4,128)S(1)}, f32[3,512,2560]{2,1,0:T(8,128)}) fusion(pred[512,2560]{1,0:T(8,128)(4,1)S(1)} %compare_or_fusion.7, bf16[1,2560,3,64]{1,3,2,0:T(8,128)(2,1)} %get-tuple-element.944, bf16[1,2560,3,64]{1,3,2,0:T(8,128)(2,1)} %get-tuple-element.943, s32[]{:T(128)S(6)} %select_n.123), kind=kOutput, calls=%fused_computation.331.clone.1 | convolution fusion | flops 519047680 | bytes 18225156 | tf_op jit(solution)/shard_map/while/body/eval_jaxpr/sub | solution.py:82
  151.8 8.1 fusion.346
  163.4 12.3 fusion.345
  175.7 8.1 fusion.346
  187.4 12.3 fusion.345
  199.6 8.1 fusion.346
  209.1 25.0 %while.76 = (s32[]{:T(128)}, bf16[2,1,512,3,64]{2,4,3,1,0:T(8,128)(2,1)S(1)}, s32[2]{0:T(128)S(1)}, bf16[1,2560,3,64]{1,3,2,0:T(8,128)(2,1)}, bf16[1,1024,3,64]{...) while((s32[]{:T(128)}, ...), condition=%wide.region_19.21_spmd, body=%wide.region_16.20_spmd.sunk | while | flops 410518528 | bytes 15546551 | solution.py:109
  242.1 15.5 %reduce.68 = bf16[2560,192]{1,0:T(8,128)(2,1)} reduce(bf16[2560,1,192]{2,1,0:T(2,128)(2,1)S(1)} %bitcast.489, bf16[]{:T(256)} %broadcast.1031), dimensions={1}, to_apply=%bitcast.311.reduce_sub_computation | reduce | bytes 1966082
  289.4 7.1 all-to-all-start
  311.0 26.1 %fusion.268 = (f32[640]{0:T(1024)S(1)}, f32[1,640,768]{2,1,0:T(8,128)S(1)}) fusion(bf16[768,3072]{1,0:T(8,128)(2,1)} %all-gather.23.cloned.1.call-done, bf16[3072,768]{1,0:T(8,128)(2,1)} %all-gather.21.cloned.1.call-done, f32[1,640,768]{2,1,0:T(8,128)} %copy-done.37, f32[640]{0:T(1024)S(1)} %add_rsqrt_fusion.1, f32[640]{0:T(1024)S(1)} %broadcast_multiply_fusion.4), kind=kOutput, calls=%fused_computation.337 | convolution fusion | flops 6171033088 | bytes 13377024 | tf_op jit(solution)/shard_map/usd,ed->use/dot_general | solution.py:36
  338.4 42.9 %all-to-all-done = bf16[1,640,3,768]{1,2,0,3:T(4,128)(2,1)} async-done(((bf16[1,640,3,768]{1,2,0,3:T(4,128)(2,1)}), bf16[1,640,3,768]{1,2,0,3:T(4,128)(2,1)}, u32[]{:S(2)}, u32[]{:S(2)}) %all-to-all-start) | async-done | bytes 2949152 | tf_op jit(solution)/shard_map/all_to_all | solution.py:226
  385.2 50.5 %while.75 = (s32[]{:T(128)}, bf16[3,1,512,3,64]{2,4,3,1,0:T(8,128)(2,1)}, f32[3,1,3,512]{3,2,1,0:T(4,128)}, s32[1,2560]{1,0:T(1,128)S(1)}, s32[3]{0:T(128)S(1)},...) while((s32[]{:T(128)}, ...), condition=%wide.region_8.10_spmd, body=%wide.region_5.9_spmd.sunk | while | flops 1056441344 | bytes 59811052 | solution.py:110
  437.6 15.6 %while.74 = (s32[]{:T(128)}, bf16[2,1,512,3,64]{2,4,3,1,0:T(8,128)(2,1)}, f32[2,1,3,512]{3,2,1,0:T(4,128)S(1)}, s32[2]{0:T(128)S(1)}, bf16[1,2560,3,64]{1,3,2,0:...) while((s32[]{:T(128)}, ...), condition=%wide.region_4.6_spmd, body=%wide.region_1.5_spmd.sunk | while | flops 416807424 | bytes 25028860 | solution.py:109
  461.9 16.5 %reduce.67 = bf16[2560,192]{1,0:T(8,128)(2,1)} reduce(bf16[2560,1,192]{2,1,0:T(2,128)(2,1)} %bitcast.490, bf16[]{:T(256)} %broadcast.1031), dimensions={1}, to_apply=%bitcast.309.reduce_sub_computation | reduce | bytes 1966082
  482.6 6.7 all-to-all-start.1
  498.3 12.6 all-to-all-done.1
  527.7 26.1 %multiply_convert_fusion.4 = (bf16[640,3072]{1,0:T(8,128)(2,1)}, f32[640,3072]{1,0:T(8,128)}, f32[640,3072]{1,0:T(8,128)}) fusion(f32[3072]{0:T(1024)S(1)} %copy-done.78, f32[3072,768]{1,0:T(8,128)S(1)} %copy-done.15, f32[3072]{0:T(1024)S(1)} %broadcast_multiply_fusion, f32[1,640,768]{2,1,0:T(8,128)S(1)} %get-tuple-element.519, f32[768]{0:T(1024)S(1)} %copy-done.69, ...), kind=kOutput, calls=%fused_computation.174 | convolution fusion | flops 3159687168 | bytes 31099904 | tf_op jit(solution)/shard_map/usd,ed->use/dot_general | solution.py:36
  553.8 6.3 fusion.266
  566.9 12.6 fusion.271
  579.5 9.0 multiply_reduce_fusion.5
  593.6 8.6 convolution_convert_fusion.1
  609.7 6.7 reduce.69
  618.1 6.4 all-to-all-start.4
  624.5 8.5 convolution_convert_fusion
  633.3 12.9 %all-to-all-done.4 = bf16[4,2,61440]{2,1,0:T(2,128)(2,1)} async-done(((bf16[4,2,61440]{2,1,0:T(2,128)(2,1)}), bf16[4,2,61440]{2,1,0:T(2,128)(2,1)}, u32[]{:S(2)}, u32[]{:S(2)}) %all-to-all-start.4) | async-done | bytes 983072 | tf_op jit(solution)/shard_map/all_to_all | solution.py:278
  652.0 138.2 %while.79 = (s32[]{:T(128)}, f32[1,2560,3,64]{1,3,2,0:T(8,128)}, f32[1,2560,3,64]{1,3,2,0:T(8,128)}, bf16[3,1,512,3,64]{2,4,3,1,0:T(8,128)(2,1)}, s32[3]{0:T(128...) while((s32[]{:T(128)}, f32[1,2560,3,64]{1,3,2,0:T(8,128)}, ...), condition=%wide.region_37.39_spmd.clone, body=%wide.region_35.38_spmd.clone.sunk | while | flops 2557150208 | bytes 184567248 | solution.py:170
  655.6 9.2 fusion.367
  664.7 9.4 multiply_reduce_fusion.17
  674.1 9.5 multiply_convert_fusion.19
  701.2 9.2 fusion.367
  710.4 9.4 multiply_reduce_fusion.17
  719.8 9.5 multiply_convert_fusion.19
  747.5 9.2 fusion.367
  756.7 9.3 multiply_reduce_fusion.17
  766.0 9.5 multiply_convert_fusion.19
  791.0 31.5 %while.78 = (s32[]{:T(128)}, f32[1,1024,3,64]{1,3,2,0:T(8,128)S(1)}, f32[1,1024,3,64]{1,3,2,0:T(8,128)}, bf16[2,1,512,3,64]{2,4,3,1,0:T(8,128)(2,1)}, s32[2]{0:T...) while((s32[]{:T(128)}, ...), condition=%wide.region_34.36_spmd.clone, body=%wide.region_32.35_spmd.clone.sunk | while | flops 1026587136 | bytes 63744348 | solution.py:167
  838.9 121.2 %all_to_all.99 = bf16[1,2560,3,192]{3,2,0,1:T(4,128)(2,1)} all-to-all(bf16[1,2560,3,192]{3,2,0,1:T(4,128)(2,1)} %copy.96), channel_id=1, replica_groups=mesh['dp'=4,'seq'=4,'fsdp'=2] {'seq'}, dimensions={1} | all-to-all | bytes 5898240 | tf_op jit(solution)/shard_map/all_to_all | solution.py:288
  960.1 8.8 copy.100
  978.9 9.9 reduce-scatter.14.cloned.1.call-done
  992.9 6.9 reduce-scatter.26.cloned.1.call-done
  1000.8 10.5 reduce-scatter.24.cloned.1.call-done
  1012.3 8.2 fusion.171
  1023.1 72.0 %all-reduce.3 = (bf16[4,384]{1,0:T(4,128)(2,1)S(1)}, bf16[1536]{0:T(1024)(128)(2,1)S(1)}, bf16[2,384]{1,0:T(2,128)(2,1)S(1)}, bf16[2,384]{1,0:T(2,128)(2,1)S(1)}) all-reduce(bf16[4,384]{1,0:T(4,128)(2,1)S(1)} %copy.102, bf16[1536]{0:T(1024)(128)(2,1)S(1)} %dynamic-slice.1, ...), channel_id=1, replica_groups=mesh['dp'=4,'seq'=4,'fsdp'=2] {'dp','seq'}, use_global_device_ids=true, to_apply=%region_51.53 | all-reduce | flops 4608 | bytes 18432 | tf_op jit(solution)/shard_map/psum | solution.py:341
  1097.4 159.0 %all-reduce.7.cloned.1.call-done = (bf16[1152,768]{1,0:T(8,128)(2,1)}, bf16[384,768]{1,0:T(8,128)(2,1)}, bf16[1536,768]{1,0:T(8,128)(2,1)}, bf16[384,3072]{1,0:T(8,128)(2,1)}) async-done(((bf16[1152,768]{1,0:T(8,128)(2,1)}, bf16[384,768]{1,0:T(8,128)(2,1)}, bf16[1536,768]{1,0:T(8,128)(2,1)}, bf16[384,3072]{1,0:T(8,128)(2,1)}), (bf16[1152,768]{1,0:T(8,128)(2,1)}, bf16[384,768]{1,0:T(8,128)(2,1)}, ...) | async-done | bytes 7077904 | tf_op jit(solution)/shard_map/psum | solution.py:337
  (511 shorter events, 361.6 us)
Async XLA Ops:
  7.2 16.3 %all-gather.17.cloned.1.call-start = ((), (), s32[]{:S(2)}) async-start(), calls=%async_computation.17 | async-start | bytes 5308416 | tf_op jit(solution)/shard_map/all_gather | solution.py:210
  7.9 38.2 %all-gather.11.cloned.1.call-start = ((), (), s32[]{:S(2)}) async-start(), calls=%async_computation.14 | async-start | bytes 3538944 | tf_op jit(solution)/shard_map/all_gather | solution.py:201
  8.7 259.4 %all-gather.9.cloned.1.call-start = ((), (), s32[]{:S(2)}) async-start(), calls=%async_computation.13 | async-start | bytes 10616832 | tf_op jit(solution)/shard_map/all_gather | solution.py:200
  9.4 297.3 %all-gather.19.cloned.1.call-start = ((), (), s32[]{:S(2)}) async-start(), calls=%async_computation.18 | async-start | bytes 1769472 | tf_op jit(solution)/shard_map/all_gather | solution.py:211
  10.0 301.0 %all-gather.21.cloned.1.call-start = ((), (), s32[]{:S(2)}) async-start(), calls=%async_computation.19 | async-start | bytes 7077888 | tf_op jit(solution)/shard_map/all_gather | solution.py:212
  10.6 300.4 %all-gather.23.cloned.1.call-start = ((), (), s32[]{:S(2)}) async-start(), calls=%async_computation.20 | async-start | bytes 7077888 | tf_op jit(solution)/shard_map/all_gather | solution.py:213
  11.1 478.1 %all-gather.15.cloned.1.call-start = ((), (), s32[]{:S(2)}) async-start(), calls=%async_computation.16 | async-start | bytes 14155776 | tf_op jit(solution)/shard_map/all_gather | solution.py:203
  38.3 91.2 %all-to-all-start.2 = ((bf16[1,640,3,768]{1,2,0,3:T(4,128)(2,1)}), bf16[1,640,3,768]{1,2,0,3:T(4,128)(2,1)}, u32[]{:S(2)}, u32[]{:S(2)}) async-start(bf16[1,640,3,768]{1,2,0,3:T(4,128)(2,1)} %copy.84), calls=%async_computation.2 | async-start | bytes 7864320 | tf_op jit(solution)/shard_map/all_to_all | solution.py:233
  43.5 450.3 %all-gather.13.cloned.1.call-start = ((), (), s32[]{:S(2)}) async-start(), calls=%async_computation.15 | async-start | bytes 14155776 | tf_op jit(solution)/shard_map/all_gather | solution.py:202
  234.1 23.5 %copy-start.80 = (s32[2]{0:T(128)}, s32[2]{0:T(128)S(1)}, u32[]{:S(2)}) copy-start(s32[2]{0:T(128)S(1)} %get-tuple-element.1151) | copy-start | bytes 28
  235.8 31.7 %copy-start.55 = (f32[768]{0:T(1024)S(1)}, f32[768]{0:T(1024)}, u32[]{:S(2)}) copy-start(f32[768]{0:T(1024)} %abs_reduce_fusion.3) | copy-start | bytes 9220
  257.6 14.9 %copy-start.76 = (bf16[1,640,768]{2,1,0:T(8,128)(2,1)S(1)}, bf16[1,640,768]{2,1,0:T(8,128)(2,1)}, u32[]{:S(2)}) copy-start(bf16[1,640,768]{2,1,0:T(8,128)(2,1)} %param.30) | copy-start | bytes 2949124
  261.8 27.5 %all-to-all-start.3 = ((bf16[4,2,61440]{2,1,0:T(2,128)(2,1)}), bf16[4,2,61440]{2,1,0:T(2,128)(2,1)}, u32[]{:S(2)}, u32[]{:S(2)}) async-start(bf16[4,2,61440]{2,1,0:T(2,128)(2,1)} %reshape.1156), calls=%async_computation.3 | async-start | bytes 1966080 | tf_op jit(solution)/shard_map/all_to_all | solution.py:249
  289.4 92.0 %all-to-all-start = ((bf16[1,640,3,768]{1,2,0,3:T(4,128)(2,1)}), bf16[1,640,3,768]{1,2,0,3:T(4,128)(2,1)}, u32[]{:S(2)}, u32[]{:S(2)}) async-start(bf16[1,640,3,768]{1,2,0,3:T(4,128)(2,1)} %copy.75), calls=%async_computation | async-start | bytes 7864320 | tf_op jit(solution)/shard_map/all_to_all | solution.py:226
  337.1 47.0 %copy-start.23 = (f32[1,640,768]{2,1,0:T(8,128)}, f32[1,640,768]{2,1,0:T(8,128)S(1)}, u32[]{:S(2)}) copy-start(f32[1,640,768]{2,1,0:T(8,128)S(1)} %get-tuple-element.526) | copy-start | bytes 5898244
  337.2 47.0 %copy-start.48 = (f32[640]{0:T(1024)}, f32[640]{0:T(1024)S(1)}, u32[]{:S(2)}) copy-start(f32[640]{0:T(1024)S(1)} %broadcast_multiply_fusion.3) | copy-start | bytes 7684
  385.2 52.3 %copy-start.56 = (f32[2,1,3,512]{3,2,1,0:T(4,128)S(1)}, f32[2,1,3,512]{3,2,1,0:T(4,128)}, u32[]{:S(2)}) copy-start(f32[2,1,3,512]{3,2,1,0:T(4,128)} %custom-call.4) | copy-start | bytes 36868
  385.2 52.3 %copy-start.81 = (s32[2]{0:T(128)S(1)}, s32[2]{0:T(128)}, u32[]{:S(2)}) copy-start(s32[2]{0:T(128)} %copy-done.80) | copy-start | bytes 28
  453.1 25.3 %copy-start.3 = (bf16[1,1024,3,64]{1,3,2,0:T(8,128)(2,1)}, bf16[1,1024,3,64]{1,3,2,0:T(8,128)(2,1)S(1)}, u32[]{:S(2)}) copy-start(bf16[1,1024,3,64]{1,3,2,0:T(8,128)(2,1)S(1)} %get-tuple-element.1081) | copy-start | bytes 1179652
  453.1 25.3 %copy-start.10 = (bf16[1,2560,3,64]{1,3,2,0:T(8,128)(2,1)}, bf16[1,2560,3,64]{1,3,2,0:T(8,128)(2,1)S(1)}, u32[]{:S(2)}) copy-start(bf16[1,2560,3,64]{1,3,2,0:T(8,128)(2,1)S(1)} %get-tuple-element.1084) | copy-start | bytes 2949124
  482.6 28.3 %all-to-all-start.1 = ((bf16[4,2,61440]{2,1,0:T(2,128)(2,1)}), bf16[4,2,61440]{2,1,0:T(2,128)(2,1)}, u32[]{:S(2)}, u32[]{:S(2)}) async-start(bf16[4,2,61440]{2,1,0:T(2,128)(2,1)} %reshape.1154), calls=%async_computation.1 | async-start | bytes 1966080 | tf_op jit(solution)/shard_map/all_to_all | solution.py:248
  489.3 489.6 %reduce-scatter.16.cloned.1.call-start = ((), (), s32[]{:S(2)}) async-start(), calls=%async_computation.22 | async-start | bytes 1769472 | tf_op jit(solution)/shard_map/reduce_scatter | solution.py:314
  498.2 24.7 %copy-start.71 = (f32[768]{0:T(1024)S(1)}, f32[768]{0:T(1024)}, u32[]{:S(2)}) copy-start(f32[768]{0:T(1024)} %get-tuple-element.377) | copy-start | bytes 9220
  498.2 24.7 %copy-start.72 = (f32[768]{0:T(1024)S(1)}, f32[768]{0:T(1024)}, u32[]{:S(2)}) copy-start(f32[768]{0:T(1024)} %broadcast_multiply_fusion.7) | copy-start | bytes 9220
  522.9 30.8 %copy-start.44 = (bf16[1,640,4,192]{1,3,2,0:T(8,128)(2,1)}, bf16[1,640,4,192]{1,3,2,0:T(8,128)(2,1)S(1)}, u32[]{:S(2)}) copy-start(bf16[1,640,4,192]{1,3,2,0:T(8,128)(2,1)S(1)} %copy.82) | copy-start | bytes 2949124
  523.0 30.8 %slice-start = ((s8[9437184]{0:T(1024)(128)(4,1)}), s8[4194304]{0:T(1024)(128)(4,1)S(1)}, s32[]{:S(2)}) async-start(s8[9437184]{0:T(1024)(128)(4,1)} %bitcast.491), calls=%async_computation.29 | async-start | bytes 8388608
  527.2 26.5 %copy-start.20 = (f32[1,640,768]{2,1,0:T(8,128)}, f32[1,640,768]{2,1,0:T(8,128)S(1)}, u32[]{:S(2)}) copy-start(f32[1,640,768]{2,1,0:T(8,128)S(1)} %get-tuple-element.519) | copy-start | bytes 5898244
  527.6 26.1 %slice-start.1 = ((s8[9437184]{0:T(1024)(128)(4,1)}), s8[4194304]{0:T(1024)(128)(4,1)S(1)}, s32[]{:S(2)}) async-start(s8[9437184]{0:T(1024)(128)(4,1)} %bitcast.491), calls=%async_computation.30 | async-start | bytes 8388608
  527.6 26.1 %slice-start.2 = ((s8[9437184]{0:T(1024)(128)(4,1)}), s8[1048576]{0:T(1024)(128)(4,1)S(1)}, s32[]{:S(2)}) async-start(s8[9437184]{0:T(1024)(128)(4,1)} %bitcast.491), calls=%async_computation.31 | async-start | bytes 2097152
  527.7 26.1 %copy-start.70 = (f32[768]{0:T(1024)S(1)}, f32[768]{0:T(1024)}, u32[]{:S(2)}) copy-start(f32[768]{0:T(1024)} %get-tuple-element.374) | copy-start | bytes 9220
  593.5 385.4 %reduce-scatter.18.cloned.1.call-start = ((), (), s32[]{:S(2)}) async-start(), calls=%async_computation.23 | async-start | bytes 7077888 | tf_op jit(solution)/shard_map/reduce_scatter | solution.py:317
  605.9 18.6 %copy-start.50 = (f32[3,1,3,512]{3,2,1,0:T(4,128)S(1)}, f32[3,1,3,512]{3,2,1,0:T(4,128)}, u32[]{:S(2)}) copy-start(f32[3,1,3,512]{3,2,1,0:T(4,128)} %get-tuple-element.288) | copy-start | bytes 55300
  618.1 28.1 %all-to-all-start.4 = ((bf16[4,2,61440]{2,1,0:T(2,128)(2,1)}), bf16[4,2,61440]{2,1,0:T(2,128)(2,1)}, u32[]{:S(2)}, u32[]{:S(2)}) async-start(bf16[4,2,61440]{2,1,0:T(2,128)(2,1)} %reshape.1158), calls=%async_computation.4 | async-start | bytes 1966080 | tf_op jit(solution)/shard_map/all_to_all | solution.py:278
  624.5 354.4 %reduce-scatter.20.cloned.1.call-start = ((), (), s32[]{:S(2)}) async-start(), calls=%async_computation.24 | async-start | bytes 7077888 | tf_op jit(solution)/shard_map/reduce_scatter | solution.py:320
  633.0 18.9 %copy-start.2 = (bf16[1,2560,3,64]{1,3,2,0:T(8,128)(2,1)S(1)}, bf16[1,2560,3,64]{1,3,2,0:T(8,128)(2,1)}, u32[]{:S(2)}) copy-start(bf16[1,2560,3,64]{1,3,2,0:T(8,128)(2,1)} %copy-done.1) | copy-start | bytes 2949124
  633.1 18.9 %copy-start.28 = (s32[1,2560]{1,0:T(1,128)S(1)}, s32[1,2560]{1,0:T(1,128)}, u32[]{:S(2)}) copy-start(s32[1,2560]{1,0:T(1,128)} %copy-done.27) | copy-start | bytes 30724
  633.1 18.9 %copy-start.84 = (s32[3]{0:T(128)S(1)}, s32[3]{0:T(128)}, u32[]{:S(2)}) copy-start(s32[3]{0:T(128)} %copy-done.83) | copy-start | bytes 40
  633.1 355.7 %reduce-scatter.14.cloned.1.call-start = ((), (), s32[]{:S(2)}) async-start(), calls=%async_computation.21 | async-start | bytes 5308416 | tf_op jit(solution)/shard_map/reduce_scatter | solution.py:311
  652.0 139.1 %copy-start.4 = (bf16[1,1024,3,64]{1,3,2,0:T(8,128)(2,1)S(1)}, bf16[1,1024,3,64]{1,3,2,0:T(8,128)(2,1)}, u32[]{:S(2)}) copy-start(bf16[1,1024,3,64]{1,3,2,0:T(8,128)(2,1)} %copy-done.3) | copy-start | bytes 1179652
  652.0 139.0 %copy-start.8 = (f32[1,1024,3,64]{1,3,2,0:T(8,128)S(1)}, f32[1,1024,3,64]{1,3,2,0:T(8,128)}, u32[]{:S(2)}) copy-start(f32[1,1024,3,64]{1,3,2,0:T(8,128)} %custom-call) | copy-start | bytes 2359300
  652.0 139.0 %copy-start.82 = (s32[2]{0:T(128)S(1)}, s32[2]{0:T(128)}, u32[]{:S(2)}) copy-start(s32[2]{0:T(128)} %copy-done.80) | copy-start | bytes 28
  791.0 35.9 %copy-start.34 = (bf16[3,1,512,3,64]{2,4,3,1,0:T(8,128)(2,1)S(1)}, bf16[3,1,512,3,64]{2,4,3,1,0:T(8,128)(2,1)}, u32[]{:S(2)}) copy-start(bf16[3,1,512,3,64]{2,4,3,1,0:T(8,128)(2,1)} %get-tuple-element.1158) | copy-start | bytes 1769476
  975.4 24.4 %reduce-scatter.26.cloned.1.call-start = ((), (), s32[]{:S(2)}) async-start(), calls=%async_computation.27 | async-start | bytes 294912
  975.6 36.7 %copy-start.53 = (f32[640]{0:T(1024)S(1)}, f32[640]{0:T(1024)}, u32[]{:S(2)}) copy-start(f32[640]{0:T(1024)} %copy-done.52) | copy-start | bytes 7684
  975.6 36.7 %copy-start.60 = (f32[2304]{0:T(1024)S(1)}, f32[2304]{0:T(1024)}, u32[]{:S(2)}) copy-start(f32[2304]{0:T(1024)} %copy-done.59) | copy-start | bytes 27652
  976.5 34.8 %reduce-scatter.24.cloned.1.call-start = ((), (), s32[]{:S(2)}) async-start(), calls=%async_computation.26 | async-start | bytes 294912
  977.5 44.6 %reduce-scatter.22.cloned.1.call-start = ((), (), s32[]{:S(2)}) async-start(), calls=%async_computation.25 | async-start | bytes 294912
  978.8 277.7 %all-reduce.7.cloned.1.call-start = ((), (), s32[]{:S(2)}) async-start(), calls=%async_computation.28 | async-start | bytes 14155776 | tf_op jit(solution)/shard_map/psum | solution.py:337
  (87 other events, 408.9 us)
Sparse Core Ops, SparseCore 0:
  9.5 13.9 all-gather.16
  25.0 12.1 all-gather.10
  38.8 19.0 all-gather.8
  59.3 10.3 all-gather.18
  71.1 15.6 all-gather.20
  88.1 15.6 all-gather.22
  105.3 22.7 all-gather.14
  129.7 22.7 all-gather.12
  593.6 10.0 reduce-scatter.15
  606.4 13.8 reduce-scatter.17
  633.2 14.0 reduce-scatter.19
  975.5 13.2 reduce-scatter.13
  991.0 8.7 reduce-scatter.25
  1002.5 8.7 reduce-scatter.23
  1013.3 8.7 reduce-scatter.21
  1028.4 228.0 all-reduce.6
where the time goes:
time: 1290 us; the launch traced here: 1270 us
  matrix products  362 us (28%)
  waiting for transfers between devices  357 us (28%)
  blocking collectives  196 us (15%)
  local copies, waits for them, and re-layouts  141 us (11%)
  other arithmetic  140 us (11%)
  starting transfers between devices  32.1 us (2%)
  loops' own time  31.2 us (2%)
  between operations  16.1 us (1%)
    psum x1, waiting for transfers between devices, on_device(): lax.psum(shards[0].astype(jnp.bfloat16), ('dp', 'seq')).astype(jnp.float32)  159 us
    all_to_all x1, blocking collectives, on_device(): lax.all_to_all(jnp.stack([grad_query, grad_key, grad_value], axis=2), 'se...  121 us
    all_to_all x1, waiting for transfers between devices, on_device(): lax.all_to_all(teach_act.reshape(group_count, token_count, 3, model_width...  80.5 us
    dot_general x7, matrix products, project(): jnp.einsum('usd,ed->use', activations, weight, preferred_element_type=jnp...  75.8 us
    psum x1, blocking collectives, on_device(): lax.psum(shards[4].astype(jnp.bfloat16), ('dp', 'seq')).astype(jnp.float32)  72 us
    dot_general x10, matrix products, block_forward(): jnp.einsum('uhqk,ukhd->uqhd', softmax_w, value_set, preferred_element_typ...  49.8 us
    sub x5, matrix products, block_forward(): exponent = jnp.exp(scores - row_max)  49.7 us
    dot_general x10, matrix products, block_scores(): jnp.einsum('uqhd,ukhd->uhqk', query_rows, key_set, preferred_element_type...  44.7 us
  transfers between devices with their start and end apart: 21, of which 11 were waited for; matrix products, arithmetic and copies ran while one was open for 42% of the time, Pallas kernels for 0%

commit v1 on v0

v1 whole, which is shorter than its diff:
```python
import jax
import jax.numpy as jnp
from jax import lax
from jax.experimental import pallas as pl
from jax.experimental.pallas import tpu as pltpu
from jax.sharding import PartitionSpec as P

HEADS = 12
PROMPT = 1024
LONG = 1024
CLIP = 2.5
EPS = 1e-05
AXES = ("dp", "seq", "fsdp")
BF = jnp.bfloat16
F32 = jnp.float32
LOG2E = 1.4426950408889634
QB = 512
KC = 256
KB = 512
FC = 512
AUG = 16
VMEM_LIMIT = 56 * 2**20


def dot(left, right, left_dim, right_dim):
    return lax.dot_general(
        left, right, (((left_dim,), (right_dim,)), ((), ())), preferred_element_type=F32
    )


def xor(first, second):
    return lax.bitwise_xor(first, jnp.int32(second))


def sizes():
    return tuple(lax.axis_size(name) for name in AXES)


def permute(values, target):
    dp, seq, fsdp = sizes()
    pairs = []
    for d in range(dp):
        for s in range(seq):
            for f in range(fsdp):
                td, ts, tf = target(d, s, f)
                pairs.append(((d * seq + s) * fsdp + f, (td * seq + ts) * fsdp + tf))
    return lax.ppermute(values, AXES, pairs)


def flip(values, dp=0, seq=0, fsdp=0):
    return permute(values, lambda d, s, f: (d ^ dp, s ^ seq, f ^ fsdp))


def swap_groups(values):
    return permute(
        values, lambda d, s, f: (d, 2 * (f % 2) + s % 2, f - f % 2 + s // 2)
    )


def to_slot(values, slot):
    return flip(values, seq=slot & 1, fsdp=slot >> 1)


def bit_list(name):
    count = lax.axis_size(name)
    out, bit = [], 1
    while bit < count:
        out.append((name, bit))
        bit *= 2
    return out


def flip_bit(values, bit):
    return flip(values, **{bit[0]: bit[1]})


def side(bit):
    return lax.bitwise_and(lax.axis_index(bit[0]), bit[1]) != 0


def halve(values, bit):
    upper = side(bit).astype(jnp.int32)
    half = values.shape[0] // 2
    sent = lax.dynamic_slice_in_dim(values, (1 - upper) * half, half, 0)
    kept = lax.dynamic_slice_in_dim(values, upper * half, half, 0)
    got = flip_bit(sent, bit)
    return (kept.astype(F32) + got.astype(F32)).astype(values.dtype)


def double(values, bit):
    got = flip_bit(values, bit)
    return jnp.where(
        side(bit),
        jnp.concatenate([got, values], axis=0),
        jnp.concatenate([values, got], axis=0),
    )


def gather_rows(values):
    for bit in bit_list("fsdp"):
        values = double(values, bit)
    return values


def all_reduce(values, bits):
    for bit in bits:
        values = halve(values, bit)
    for bit in reversed(bits):
        values = double(values, bit)
    return values


def sum_small(values, bits):
    for bit in bits:
        values = values + flip_bit(values, bit)
    return values


def whole(shape):
    return pl.BlockSpec(shape, lambda *_: (0,) * len(shape))


def call(kernel, pref, args, in_specs, outs, out_specs, grid, scratch, flops, trans=0):
    moved = sum(a.size * a.dtype.itemsize for a in args)
    moved += sum(o.size * o.dtype.itemsize for o in jax.tree.leaves(outs))
    return pl.pallas_call(
        kernel,
        grid_spec=pltpu.PrefetchScalarGridSpec(
            num_scalar_prefetch=1,
            grid=grid,
            in_specs=in_specs,
            out_specs=out_specs,
            scratch_shapes=scratch,
        ),
        out_shape=outs,
        compiler_params=pltpu.CompilerParams(vmem_limit_bytes=VMEM_LIMIT),
        cost_estimate=pl.CostEstimate(flops=flops, bytes_accessed=moved, transcendentals=trans),
    )(pref, *args)


def shape_of(shape, dtype):
    return jax.ShapeDtypeStruct(shape, dtype)


def qkv_kernel(student, pref, x0, x1, x2, x3, wq, wk, wv, *rest):
    slot = pl.program_id(0)
    out = rest[-1]
    rows = wq.shape[0]
    for j, ref in enumerate((x0, x1, x2, x3)):

        @pl.when(slot == j)
        def _():
            act = ref[...]
            if student:
                act = jnp.clip(act, -CLIP, CLIP)
            for part, weight in enumerate((wq, wk, wv)):
                value = dot(weight[...], act, 1, 1)
                if student and part != 1:
                    value = value + rest[0][part // 2]
                out[part * rows : (part + 1) * rows, :] = value.astype(BF)


def qkv_project(pref, slots, weight, bias):
    tok, width = slots[0].shape
    rows = weight.shape[0] // 12
    specs = [whole((tok, width))] * 4
    specs += [
        pl.BlockSpec((rows, width), lambda j, i, o=o: (o * 4 + i[0], 0)) for o in range(3)
    ]
    args = list(slots) + [weight] * 3
    if bias is not None:
        specs.append(pl.BlockSpec((2, rows, 1), lambda j, i: (0, i[0], 0)))
        args.append(bias)
    return call(
        lambda *refs: qkv_kernel(bias is not None, *refs),
        pref,
        args,
        specs,
        shape_of((3 * rows, 4 * tok), BF),
        pl.BlockSpec((3 * rows, tok), lambda j, i: (0, lax.bitwise_xor(i[0], j))),
        (4,),
        [],
        2 * 4 * tok * width * 3 * rows,
    )


def roll_cont(values, shift):
    return jnp.concatenate(
        [values[:, :PROMPT], pltpu.roll(values[:, PROMPT:], shift, 1)], axis=1
    )


def block_list(total, rows):
    blocks = [(i, [(0, PROMPT)]) for i in range(0, PROMPT, rows)]
    blocks += [(i, [(0, PROMPT + LONG)]) for i in range(PROMPT, PROMPT + LONG, rows)]
    blocks += [
        (i, [(0, PROMPT), (PROMPT + LONG, total)]) for i in range(PROMPT + LONG, total, rows)
    ]
    return blocks


def same_segment(shape, key_axis, key_start, query_start, border):
    keys = lax.broadcasted_iota(jnp.int32, shape, key_axis) + key_start
    queries = lax.broadcasted_iota(jnp.int32, shape, 1 - key_axis) + query_start
    return (keys < border) == (queries < border)


def attention_kernel(scale, pref, q_ref, k_ref, v_ref, o0, o1, o2, o3, cf_ref, lse_ref, qs, ks, vs, cs, st):
    own, shift, border = pref[0], pref[1], pref[2]
    total = q_ref.shape[1]
    cont = total - PROMPT
    others = PROMPT + LONG
    back = lax.rem(cont - shift, cont)
    qs[...] = roll_cont(q_ref[...].astype(F32), back).astype(BF)
    ks[...] = roll_cont(k_ref[...].astype(F32), back).astype(BF)
    vs[...] = roll_cont(v_ref[...].astype(F32), back).astype(BF)
    blocks = []
    for start, parts in block_list(total, QB):
        chunks = [key for lo, hi in parts for key in range(lo, hi, KC)]
        blocks.append((start, chunks))
    top, acc, norm = {}, {}, {}

    def scores(n, i):
        start, chunks = blocks[n]
        key = chunks[i]
        value = dot(ks[:, key : key + KC], qs[:, start : start + QB], 0, 0) * scale
        if key >= others:
            mask = same_segment((KC, QB), 0, key - others, start - others, border)
            value = jnp.where(mask, value, -1e30)
        st[n % 2, i * KC : (i + 1) * KC, :] = value
        peak = jnp.max(value, axis=0, keepdims=True)
        top[n] = jnp.maximum(top[n], peak) if n in top else peak

    def weigh(n, i):
        key = blocks[n][1][i]
        prob = jnp.exp2(st[n % 2, i * KC : (i + 1) * KC, :] - top[n])
        part = jnp.sum(prob, axis=0, keepdims=True)
        value = dot(vs[:, key : key + KC], prob.astype(BF), 1, 0)
        acc[n] = acc[n] + value if n in acc else value
        norm[n] = norm[n] + part if n in norm else part

    for i in range(len(blocks[0][1])):
        scores(0, i)
    for n, (start, chunks) in enumerate(blocks):
        ahead = len(blocks[n + 1][1]) if n + 1 < len(blocks) else 0
        for i in range(max(len(chunks), ahead)):
            if i < ahead:
                scores(n + 1, i)
            if i < len(chunks):
                weigh(n, i)
        cf_ref[:, start : start + QB] = acc[n] / norm[n]
        lse_ref[:, start : start + QB] = top[n] + jnp.log2(norm[n])
    cs[...] = roll_cont(cf_ref[...], shift).astype(BF)
    tok = total // 4
    for j, out in enumerate((o0, o1, o2, o3)):
        first = pl.multiple_of(xor(own, j) * tok, 128)
        out[...] = cs[:, pl.ds(first, tok)]


def attention(pref, qkv):
    total = qkv.shape[1]
    heads = HEADS // 4
    hdim = qkv.shape[0] // (3 * heads)
    rows = qkv.shape[0] // 3
    scale = LOG2E / hdim**0.5
    return call(
        lambda *refs: attention_kernel(scale, *refs),
        pref,
        [qkv] * 3,
        [pl.BlockSpec((hdim, total), lambda h, i, o=o: (h + o * heads, 0)) for o in range(3)],
        [shape_of((rows, total // 4), BF)] * 4
        + [shape_of((rows, total), F32), shape_of((heads, 1, total), F32)],
        [pl.BlockSpec((hdim, total // 4), lambda h, i: (h, 0))] * 4
        + [
            pl.BlockSpec((hdim, total), lambda h, i: (h, 0)),
            pl.BlockSpec((None, 1, total), lambda h, i: (h, 0, 0)),
        ],
        (heads,),
        [pltpu.VMEM((hdim, total), BF)] * 4 + [pltpu.VMEM((2, PROMPT + LONG, QB), F32)],
        16 * 10**9,
        12 * 10**6,
    )


def thirds(values):
    high = values.astype(BF).astype(F32)
    middle = (values - high).astype(BF).astype(F32)
    low = values - high - middle
    row = lax.broadcasted_iota(jnp.int32, (AUG, values.shape[1]), 0)
    value = jnp.where(row == 0, high, jnp.where(row == 1, middle, jnp.where(row == 2, low, 0.0)))
    return value.astype(BF)


def attention_back_kernel(
    scale, pref, q_ref, k_ref, v_ref, g0, g1, g2, g3, cf_ref, lse_ref,
    d0, d1, d2, d3, qa, ka, va, ga, gs, dqs, dks, dvs,
):
    own, shift, border = pref[0], pref[1], pref[2]
    hdim, total = q_ref.shape
    tok = total // 4
    cont = total - PROMPT
    others = PROMPT + LONG
    back = lax.rem(cont - shift, cont)
    for j, ref in enumerate((g0, g1, g2, g3)):
        first = pl.multiple_of(xor(own, j) * tok, 128)
        gs[:, pl.ds(first, tok)] = ref[...].astype(F32)
    qa[:hdim, :] = roll_cont(q_ref[...].astype(F32), back).astype(BF)
    ka[:hdim, :] = roll_cont(k_ref[...].astype(F32), back).astype(BF)
    va[:hdim, :] = roll_cont(v_ref[...].astype(F32), back).astype(BF)
    grad = roll_cont(gs[...], back)
    ga[:hdim, :] = grad.astype(BF)
    ga[hdim:, :] = thirds(-jnp.sum(grad * cf_ref[...], axis=0, keepdims=True))
    qa[hdim:, :] = thirds(lse_ref[...] * (-1.0 / scale))
    row = lax.broadcasted_iota(jnp.int32, (AUG, total), 0)
    ones = jnp.where(row < 3, 1.0, 0.0).astype(BF)
    ka[hdim:, :] = ones
    va[hdim:, :] = ones
    seen = set()
    for start, parts in block_list(total, QB):
        queries = slice(start, start + QB)
        grad_q = None
        for lo, hi in parts:
            for key in range(lo, hi, KB):
                keys = slice(key, key + KB)
                value = dot(qa[:, queries], ka[:, keys], 0, 0) * scale
                if lo >= others:
                    mask = same_segment((QB, KB), 1, key - others, start - others, border)
                    value = jnp.where(mask, value, -1e30)
                prob = jnp.exp2(value)
                grad_p = dot(ga[:, queries], va[:, keys], 0, 0)
                grad_s = (prob * grad_p).astype(BF)
                grad_v = dot(ga[:hdim, queries], prob.astype(BF), 1, 0)
                grad_k = dot(qa[:hdim, queries], grad_s, 1, 0)
                part = dot(ka[:hdim, keys], grad_s, 1, 1)
                grad_q = part if grad_q is None else grad_q + part
                if key in seen:
                    dvs[:, keys] += grad_v
                    dks[:, keys] += grad_k
                else:
                    dvs[:, keys] = grad_v
                    dks[:, keys] = grad_k
                    seen.add(key)
        dqs[:, queries] = grad_q
    inv = 1.0 / hdim**0.5
    for part, (ref, factor) in enumerate(((dqs, inv), (dks, inv), (dvs, 1.0))):
        gs[...] = roll_cont(ref[...] * factor, shift)
        for j, out in enumerate((d0, d1, d2, d3)):
            first = pl.multiple_of(xor(own, j) * tok, 128)
            out[part] = gs[:, pl.ds(first, tok)].astype(BF)


def attention_back(pref, qkv, grads, ctx, lse):
    total = qkv.shape[1]
    heads = HEADS // 4
    hdim = qkv.shape[0] // (3 * heads)
    rows = qkv.shape[0] // 3
    scale = LOG2E / hdim**0.5
    quarter = pl.BlockSpec((hdim, total // 4), lambda h, i: (h, 0))
    return call(
        lambda *refs: attention_back_kernel(scale, *refs),
        pref,
        [qkv] * 3 + list(grads) + [ctx, lse],
        [pl.BlockSpec((hdim, total), lambda h, i, o=o: (h + o * heads, 0)) for o in range(3)]
        + [quarter] * 4
        + [
            pl.BlockSpec((hdim, total), lambda h, i: (h, 0)),
            pl.BlockSpec((None, 1, total), lambda h, i: (h, 0, 0)),
        ],
        [shape_of((3, rows, total // 4), BF)] * 4,
        [pl.BlockSpec((3, hdim, total // 4), lambda h, i: (0, h, 0))] * 4,
        (heads,),
        [pltpu.VMEM((hdim + AUG, total), BF)] * 4 + [pltpu.VMEM((hdim, total), F32)] * 4,
        30 * 10**9,
        12 * 10**6,
    )


def normalize(values):
    centre = jnp.mean(values, axis=-1, keepdims=True)
    shifted = values - centre
    spread = jnp.mean(shifted * shifted, axis=-1, keepdims=True)
    inv = lax.rsqrt(spread + EPS)
    return shifted * inv, inv


def normalize_back(grad, normed, inv):
    first = jnp.mean(grad, axis=-1, keepdims=True)
    second = jnp.mean(grad * normed, axis=-1, keepdims=True)
    return (grad - first - normed * second) * inv


def total_rows(values):
    return jnp.sum(values, axis=0, keepdims=True)


def gather_ctx(own, pieces, ctx):
    rows = pieces[0].shape[0]
    for j, ref in enumerate(pieces):
        first = pl.multiple_of(xor(own, j) * rows, 64)
        ctx[pl.ds(first, rows), :] = ref[...]


def student_kernel(
    pref, c0, c1, c2, c3, x, w_out, w_up, w_down, b_out, b_up, b_down, gain, shift,
    ctx, act_one, normed_one, inv_one, gelu, slope, result, normed_two, inv_two,
    acc, mid,
):
    step = pl.program_id(0)

    @pl.when(step == 0)
    def _():
        gather_ctx(pref[0], (c0, c1, c2, c3), ctx)
        res = x[...].astype(F32) + (dot(ctx[...], w_out[...], 0, 1) + b_out[...])
        normed, inv = normalize(res)
        normed_one[...] = normed
        inv_one[...] = inv
        middle = normed * gain[0:1] + shift[0:1]
        mid[...] = middle
        act_one[...] = jnp.clip(middle, -CLIP, CLIP).astype(BF)
        acc[...] = jnp.zeros_like(acc)

    pre = dot(act_one[...], w_up[...], 1, 1) + b_up[...]
    cdf = 0.5 * (1.0 + lax.erf(pre * 0.5**0.5))
    act = (pre * cdf).astype(BF)
    gelu[...] = act
    slope[...] = (cdf + pre * (jnp.exp(pre * pre * -0.5) * 0.3989422804014327)).astype(BF)
    acc[...] += dot(act, w_down[...], 1, 1)

    @pl.when(step == pl.num_programs(0) - 1)
    def _():
        normed, inv = normalize(mid[...] + (acc[...] + b_down[...]))
        normed_two[...] = normed
        inv_two[...] = inv
        result[...] = (normed * gain[1:2] + shift[1:2]).astype(BF)


def ffn_specs(tok, width, hidden):
    up = pl.BlockSpec((FC, width), lambda c, i: (c, 0))
    down = pl.BlockSpec((width, FC), lambda c, i: (0, c))
    wide = pl.BlockSpec((tok, FC), lambda c, i: (0, c))
    row = pl.BlockSpec((1, FC), lambda c, i: (0, c))
    return up, down, wide, row


def student_ffn(pref, pieces, x, w_out, w_up, w_down, b_out, b_up, b_down, gain, shift):
    tok, width = x.shape
    hidden = w_up.shape[0]
    up, down, wide, row = ffn_specs(tok, width, hidden)
    full, one = whole((tok, width)), whole((tok, 1))
    return call(
        student_kernel,
        pref,
        list(pieces) + [x, w_out, w_up, w_down, b_out, b_up, b_down, gain, shift],
        [whole(pieces[0].shape)] * 4
        + [full, whole(w_out.shape), up, down, whole((1, width)), row, whole((1, width))]
        + [whole((2, width))] * 2,
        [
            shape_of((width, tok), BF),
            shape_of((tok, width), BF),
            shape_of((tok, width), F32),
            shape_of((tok, 1), F32),
            shape_of((tok, hidden), BF),
            shape_of((tok, hidden), BF),
            shape_of((tok, width), BF),
            shape_of((tok, width), F32),
            shape_of((tok, 1), F32),
        ],
        [whole((width, tok)), full, full, one, wide, wide, full, full, one],
        (hidden // FC,),
        [pltpu.VMEM((tok, width), F32)] * 2,
        2 * tok * width * (2 * hidden + width),
        2 * tok * hidden,
    )


def teacher_kernel(
    pref, c0, c1, c2, c3, x, w_out, w_up, w_down, gain, shift, normed_two, inv_two,
    grad_sum, grad_ffn, vectors,
    ctx, acc, mid, act_one,
):
    step = pl.program_id(0)

    @pl.when(step == 0)
    def _():
        gather_ctx(pref[0], (c0, c1, c2, c3), ctx)
        res = x[...].astype(F32) + dot(ctx[...], w_out[...], 0, 1)
        normed, inv = normalize(res)
        mid[...] = normed
        act_one[...] = normed.astype(BF)
        acc[...] = jnp.zeros_like(acc)

    pre = dot(act_one[...], w_up[...], 1, 1)
    act = (pre * (0.5 * (1.0 + lax.erf(pre * 0.5**0.5)))).astype(BF)
    acc[...] += dot(act, w_down[...], 1, 1)

    @pl.when(step == pl.num_programs(0) - 1)
    def _():
        target, _unused = normalize(mid[...] + acc[...])
        normed = normed_two[...]
        diff = normed * gain[1:2] + shift[1:2] - target
        back = normalize_back(diff * gain[1:2], normed, inv_two[...])
        grad_sum[...] = back
        low = back.astype(BF)
        grad_ffn[...] = low
        vectors[0:1] = total_rows(diff * normed)
        vectors[1:2] = total_rows(diff)
        vectors[2:3] = total_rows(low.astype(F32))


def teacher_ffn(pref, pieces, x, w_out, w_up, w_down, gain, shift, normed_two, inv_two):
    tok, width = x.shape
    hidden = w_up.shape[0]
    up, down, wide, row = ffn_specs(tok, width, hidden)
    full, one = whole((tok, width)), whole((tok, 1))
    return call(
        teacher_kernel,
        pref,
        list(pieces) + [x, w_out, w_up, w_down, gain, shift, normed_two, inv_two],
        [whole(pieces[0].shape)] * 4
        + [full, whole(w_out.shape), up, down]
        + [whole((2, width))] * 2
        + [full, one],
        [shape_of((tok, width), F32), shape_of((tok, width), BF), shape_of((3, width), F32)],
        [full, full, whole((3, width))],
        (hidden // FC,),
        [pltpu.VMEM((width, tok), BF)]
        + [pltpu.VMEM((tok, width), F32)] * 2
        + [pltpu.VMEM((tok, width), BF)],
        2 * tok * width * (2 * hidden + width),
        tok * hidden,
    )


def back_kernel(
    pref, grad_ffn, slope, w_up, w_down, grad_sum, normed_one, inv_one, gain, shift, w_out,
    grad_hidden, grad_bias, grad_res, grad_attn, g0, g1, g2, g3, vectors,
    acc, ctx,
):
    step = pl.program_id(0)

    @pl.when(step == 0)
    def _():
        acc[...] = jnp.zeros_like(acc)

    low = (dot(grad_ffn[...], w_down[...], 1, 0) * slope[...].astype(F32)).astype(BF)
    grad_hidden[...] = low
    grad_bias[...] = total_rows(low.astype(F32))
    acc[...] += dot(low, w_up[...], 1, 0)

    @pl.when(step == pl.num_programs(0) - 1)
    def _():
        normed = normed_one[...]
        middle = normed * gain[0:1] + shift[0:1]
        grad = grad_sum[...] + jnp.where(jnp.abs(middle) < CLIP, acc[...], 0.0)
        back = normalize_back(grad * gain[0:1], normed, inv_one[...])
        grad_res[...] = back
        attn = back.astype(BF)
        grad_attn[...] = attn
        vectors[0:1] = total_rows(grad * normed)
        vectors[1:2] = total_rows(grad)
        vectors[2:3] = total_rows(attn.astype(F32))
        ctx[...] = dot(w_out[...], attn, 0, 1).astype(BF)
        rows = g0.shape[0]
        for j, ref in enumerate((g0, g1, g2, g3)):
            first = pl.multiple_of(xor(pref[0], j) * rows, 64)
            ref[...] = ctx[pl.ds(first, rows), :]


def student_back(pref, grad_ffn, slope, w_up, w_down, grad_sum, normed_one, inv_one, gain, shift, w_out):
    tok, width = grad_ffn.shape
    hidden = w_up.shape[0]
    up, down, wide, row = ffn_specs(tok, width, hidden)
    full, one = whole((tok, width)), whole((tok, 1))
    return call(
        back_kernel,
        pref,
        [grad_ffn, slope, w_up, w_down, grad_sum, normed_one, inv_one, gain, shift, w_out],
        [full, wide, up, down, full, full, one] + [whole((2, width))] * 2 + [whole(w_out.shape)],
        [
            shape_of((tok, hidden), BF),
            shape_of((1, hidden), F32),
            shape_of((tok, width), F32),
            shape_of((tok, width), BF),
        ]
        + [shape_of((width // 4, tok), BF)] * 4
        + [shape_of((3, width), F32)],
        [wide, row, full, full] + [whole((width // 4, tok))] * 4 + [whole((3, width))],
        (hidden // FC,),
        [pltpu.VMEM((tok, width), F32), pltpu.VMEM((width, tok), BF)],
        2 * tok * width * (2 * hidden + width),
    )


def weight_grad_kernel(
    pref, grad_ffn, gelu, grad_hidden, act_one, grad_attn, ctx, grad_down, grad_up, grad_out
):
    @pl.when(pl.program_id(0) == 0)
    def _():
        grad_out[...] = dot(grad_attn[...], ctx[...], 0, 1).astype(BF)

    grad_down[...] = dot(grad_ffn[...], gelu[...], 0, 0).astype(BF)
    grad_up[...] = dot(grad_hidden[...], act_one[...], 0, 0).astype(BF)


def weight_grads(pref, grad_ffn, gelu, grad_hidden, act_one, grad_attn, ctx):
    tok, width = grad_ffn.shape
    hidden = gelu.shape[1]
    up, down, wide, row = ffn_specs(tok, width, hidden)
    full = whole((tok, width))
    return call(
        weight_grad_kernel,
        pref,
        [grad_ffn, gelu, grad_hidden, act_one, grad_attn, ctx],
        [full, wide, wide, full, full, whole((width, tok))],
        [
            shape_of((width, hidden), BF),
            shape_of((hidden, width), BF),
            shape_of((width, width), BF),
        ],
        [down, up, whole((width, width))],
        (hidden // FC,),
        [],
        2 * tok * width * (2 * hidden + width),
    )


def qkv_grad_kernel(pref, d0, d1, d2, d3, x0, x1, x2, x3, out, sums, acc):
    total = None
    count = None
    for grad, x in zip((d0, d1, d2, d3), (x0, x1, x2, x3)):
        value = grad[...]
        part = dot(value, jnp.clip(x[...], -CLIP, CLIP), 1, 0)
        line = jnp.sum(value.astype(F32), axis=1, keepdims=True)
        total = part if total is None else total + part
        count = line if count is None else count + line
    out[...] = total.astype(BF)
    sums[...] = count


def qkv_grad(pref, grads, slots):
    tok, width = slots[0].shape
    rows = grads[0].shape[1]
    return call(
        qkv_grad_kernel,
        pref,
        list(grads) + list(slots),
        [pl.BlockSpec((None, rows, tok), lambda o, i: (o, 0, 0))] * 4 + [whole((tok, width))] * 4,
        [shape_of((3, rows, width), BF), shape_of((3, rows, 1), F32)],
        [
            pl.BlockSpec((None, rows, width), lambda o, i: (o, 0, 0)),
            pl.BlockSpec((None, rows, 1), lambda o, i: (o, 0, 0)),
        ],
        (3,),
        [pltpu.VMEM((8, 128), F32)],
        2 * 4 * tok * width * 3 * rows,
    )


def input_grad_kernel(pref, e0, e1, e2, e3, wq, wk, wv, grad_res, x, out, acc):
    slot = pl.program_id(0)

    @pl.when(slot == 0)
    def _():
        acc[...] = jnp.zeros_like(acc)

    for j, ref in enumerate((e0, e1, e2, e3)):

        @pl.when(slot == j)
        def _():
            part = dot(ref[0], wq[...], 0, 0)
            part = part + dot(ref[1], wk[...], 0, 0)
            acc[...] += part + dot(ref[2], wv[...], 0, 0)

    @pl.when(slot == 3)
    def _():
        size = jnp.abs(x[...].astype(F32))
        pull = jnp.where(size < CLIP, 1.0, jnp.where(size == CLIP, 0.5, 0.0))
        out[...] = (grad_res[...] + acc[...] * pull).astype(BF)


def input_grad(pref, pieces, weight, grad_res, x):
    tok, width = x.shape
    rows = pieces[0].shape[1]
    full = whole((tok, width))
    return call(
        input_grad_kernel,
        pref,
        list(pieces) + [weight] * 3 + [grad_res, x],
        [whole((3, rows, tok))] * 4
        + [
            pl.BlockSpec((rows, width), lambda j, i, o=o: (o * 4 + lax.bitwise_xor(i[0], j), 0))
            for o in range(3)
        ]
        + [full, full],
        shape_of((tok, width), BF),
        full,
        (4,),
        [pltpu.VMEM((tok, width), F32)],
        2 * 4 * tok * width * 3 * rows,
    )


def binarize(latent):
    row_scale = jnp.mean(jnp.abs(latent), axis=1, keepdims=True)
    return (row_scale * jnp.sign(latent)).astype(BF)


def segment_info(segments):
    sizes_of = [jnp.sum((segments == k).astype(jnp.int32)) for k in (1, 2, 3)]
    first, second, third = sizes_of
    shift = jnp.where(first == LONG, 0, jnp.where(second == LONG, first, first + second))
    border = jnp.where(first == LONG, second, jnp.where(second == LONG, third, first))
    return jnp.stack([shift, border])


def quarters(own):
    along = to_slot(own, 1)
    return (own, along, to_slot(own, 2), to_slot(along, 2))


def exchange(pieces):
    return (pieces[0],) + tuple(to_slot(pieces[j], j) for j in (1, 2, 3))


def on_device(
    hidden, teacher_hidden, segments, latent_qkv, latent_out, latent_up, latent_down,
    biases, up_bias, norm_gains, norm_shifts, teacher_qkv, teacher_out, teacher_up, teacher_down,
):
    seq_at, fsdp_at = lax.axis_index("seq"), lax.axis_index("fsdp")
    fsdp = lax.axis_size("fsdp")
    core = fsdp_at % 2
    own = (seq_at % 2 + 2 * core).astype(jnp.int32)
    width = hidden.shape[2]

    x = swap_groups(hidden[0])
    x_slots = quarters(x)
    bin_qkv = gather_rows(binarize(latent_qkv))
    info = segment_info(segments)
    info = jnp.where(core == seq_at // 2, info, flip(info, fsdp=1))
    pref = jnp.concatenate([own[None], info]).astype(jnp.int32)
    bin_out = gather_rows(binarize(latent_out))
    bin_up = gather_rows(binarize(latent_up))
    bin_down = gather_rows(binarize(latent_down))
    teach = swap_groups(teacher_hidden[0])
    t_slots = quarters(teach)
    t_qkv = gather_rows(teacher_qkv)
    t_out = gather_rows(teacher_out)
    t_up = gather_rows(teacher_up)
    t_down = gather_rows(teacher_down)

    bias_cols = biases[:2].reshape(2, width, 1)
    qkv = qkv_project(pref, x_slots, bin_qkv, bias_cols)
    *ctx_slots, ctx_full, lse = attention(pref, qkv)
    ctx_pieces = exchange(ctx_slots)

    t_heads = qkv_project(pref, t_slots, t_qkv, None)
    *tctx_slots, _unused, _unused_too = attention(pref, t_heads)
    tctx_pieces = exchange(tctx_slots)

    gain, shift = norm_gains, norm_shifts
    (
        ctx, act_one, normed_one, inv_one, gelu, slope, result, normed_two, inv_two,
    ) = student_ffn(
        pref, ctx_pieces, x, bin_out, bin_up, bin_down,
        biases[2:3], up_bias[None], biases[3:4], gain, shift,
    )
    student_out = swap_groups(result)
    grad_sum, grad_ffn, vec_two = teacher_ffn(
        pref, tctx_pieces, teach, t_out, t_up, t_down, gain, shift, normed_two, inv_two
    )
    grad_hidden, grad_up_bias, grad_res, grad_attn, *gctx_slots, vec_one = student_back(
        pref, grad_ffn, slope, bin_up, bin_down, grad_sum, normed_one, inv_one, gain, shift, bin_out
    )
    gctx_pieces = exchange(gctx_slots)
    grad_down, grad_up, grad_out = weight_grads(
        pref, grad_ffn, gelu, grad_hidden, act_one, grad_attn, ctx
    )
    dp_bits, seq_bits, fsdp_bits = bit_list("dp"), bit_list("seq"), bit_list("fsdp")

    def reduce_grad(value, bits):
        for bit in reversed(fsdp_bits):
            value = halve(value, bit)
        return all_reduce(value, bits).astype(F32)

    total_down = reduce_grad(grad_down, dp_bits + seq_bits)
    total_up = reduce_grad(grad_up, dp_bits[::-1] + seq_bits)
    total_out = reduce_grad(grad_out, seq_bits[:1] + dp_bits + seq_bits[1:])

    dqkv_slots = attention_back(pref, qkv, gctx_pieces, ctx_full, lse)
    dqkv_pieces = exchange(dqkv_slots)
    grad_heads, head_sums = qkv_grad(pref, dqkv_slots, x_slots)
    hidden_grad = swap_groups(input_grad(pref, dqkv_pieces, bin_qkv, grad_res, x))

    rows = width // 4
    blocks = all_reduce(grad_heads.reshape(3 * rows, width), dp_bits + seq_bits[1:] + fsdp_bits[1:])
    blocks = blocks.reshape(1, 3, rows, width)
    blocks = double(double(blocks, seq_bits[0]), fsdp_bits[0])
    whole_qkv = blocks.transpose(1, 0, 2, 3).reshape(3 * width, width)
    part = 3 * width // fsdp
    total_qkv = lax.dynamic_slice_in_dim(whole_qkv, fsdp_at * part, part, 0).astype(F32)

    placed = jnp.zeros((2, 4, rows), F32)
    placed = lax.dynamic_update_slice(
        placed, head_sums.reshape(3, 1, rows)[0::2], (0, own, 0)
    ).reshape(2, width)
    vectors = jnp.concatenate(
        [
            placed,
            vec_one[2:3],
            vec_two[2:3],
            vec_one[0:1],
            vec_two[0:1],
            vec_one[1:2],
            vec_two[1:2],
            grad_up_bias.reshape(-1, width),
        ]
    )
    vectors = sum_small(vectors, dp_bits + seq_bits + fsdp_bits)
    hid_bias = vectors[8:].reshape(-1)
    share, hid_share = width // fsdp, hid_bias.shape[0] // fsdp
    cols = lax.dynamic_slice_in_dim(vectors[:8], fsdp_at * share, share, 1)
    return (
        student_out[None],
        hidden_grad[None],
        total_qkv,
        total_out,
        total_up,
        total_down,
        cols[0:4],
        lax.dynamic_slice_in_dim(hid_bias, fsdp_at * hid_share, hid_share, 0),
        cols[4:6],
        cols[6:8],
    )


def solution(mesh):
    tokens = P(("dp", "fsdp"), "seq", None)
    rows = P("fsdp", None)
    return jax.shard_map(
        on_device,
        mesh=mesh,
        in_specs=(tokens, tokens, P(("dp", "fsdp"), None)) + (rows,) * 4 + (P(),) * 4 + (rows,) * 4,
        out_specs=(tokens, tokens)
        + (rows,) * 4
        + (P(None, "fsdp"), P("fsdp"), P(None, "fsdp"), P(None, "fsdp")),
        check_vma=False,
    )
```

time: 1290 us -> 578 us (0.45)
  matrix products: 362 us -> 0 us
  blocking collectives: 196 us -> 0 us
  Pallas kernels: 0 us -> 181 us
  waiting for transfers between devices: 357 us -> 199 us
  local copies, waits for them, and re-layouts: 141 us -> 32.2 us
  other arithmetic: 140 us -> 89.3 us
  loops' own time: 31.2 us -> 0 us
  starting transfers between devices: 32.1 us -> 59.3 us
    dot_general x55 -> x0, matrix products: 312 us -> none  [the longest x7 75.8 us: project(): jnp.einsum('usd,ed->use', activations, weight, preferred_element_type=jnp...]
    ppermute x0 -> x71, waiting for transfers between devices: none -> 199 us  [permute(): return lax.ppermute(values, AXES, pairs)]
    pallas_call x0 -> x11, Pallas kernels: none -> 181 us  [call(): pl.pallas_call(kernel, grid_spec=pltpu.PrefetchScalarGridSpec(num_scalar_...]
    psum x1 -> x0, waiting for transfers between devices: 159 us -> none  [on_device(): lax.psum(shards[0].astype(jnp.bfloat16), ('dp', 'seq')).astype(jnp.float32)]
    all_to_all x5 -> x0, waiting for transfers between devices: 152 us -> none  [the longest x1 80.5 us: on_device(): lax.all_to_all(teach_act.reshape(group_count, token_count, 3, model_width...]
    all_to_all x1 -> x0, blocking collectives: 121 us -> none  [on_device(): lax.all_to_all(jnp.stack([grad_query, grad_key, grad_value], axis=2), 'se...]
    psum x1 -> x0, blocking collectives: 72 us -> none  [on_device(): lax.psum(shards[4].astype(jnp.bfloat16), ('dp', 'seq')).astype(jnp.float32)]
    ppermute x0 -> x71, starting transfers between devices: none -> 59.3 us  [permute(): return lax.ppermute(values, AXES, pairs)]
  transfers between devices with their start and end apart: 21 -> 71, of which waited for: 11 -> 29; matrix products, arithmetic and copies ran while one was open for 42% -> 19% of each run, Pallas kernels for 0% -> 26%
where the time goes in v1:
time: 578 us; the launch traced here: 567 us
  waiting for transfers between devices  199 us (34%)
  Pallas kernels  181 us (31%)
  other arithmetic  89.3 us (15%)
  starting transfers between devices  59.3 us (10%)
  local copies, waits for them, and re-layouts  32.2 us (6%)
  between operations  6.81 us (1%)
    ppermute x71, waiting for transfers between devices, permute(): return lax.ppermute(values, AXES, pairs)  199 us
    pallas_call x11, Pallas kernels, call(): pl.pallas_call(kernel, grid_spec=pltpu.PrefetchScalarGridSpec(num_scalar_...  181 us
    ppermute x71, starting transfers between devices, permute(): return lax.ppermute(values, AXES, pairs)  59.3 us
    select_n x22, other arithmetic, double(): jnp.where(side(bit), jnp.concatenate([got, values], axis=0), jnp.concaten...  49.4 us
    unnamed x80, local copies, waits for them, and re-layouts  12.3 us
  transfers between devices with their start and end apart: 71, of which 29 were waited for; matrix products, arithmetic and copies ran while one was open for 19% of the time, Pallas kernels for 26%

profile of v1, /device:TPU:24, one launch (start us, length us, event | category | flops | bytes accessed | tf_op | source)
XLA Modules:
  0.0 566.8 jit_solution(14881226140621988850)
XLA Ops:
  18.7 4.8 collective-permute-start.13
  23.5 2.7 multiply_convert_fusion
  26.2 23.9 %collective-permute-done.1.refs_1_.x.x0 = bf16[640,768]{1,0:T(8,128)(2,1)S(1)} collective-permute-done((bf16[640,768]{1,0:T(8,128)(2,1)}, bf16[640,768]{1,0:T(8,128)(2,1)S(1)}, u32[]{:S(2)}, u32[]{:S(2)}) %collective-permute-start.1) | collective-permute-done | bytes 983072 | tf_op jit(solution)/shard_map/ppermute | solution.py:47
  52.0 8.8 %collective-permute-done.13.refs_1_.x = bf16[640,768]{1,0:T(8,128)(2,1)} collective-permute-done((bf16[640,768]{1,0:T(8,128)(2,1)}, bf16[640,768]{1,0:T(8,128)(2,1)}, u32[]{:S(2)}, u32[]{:S(2)}) %collective-permute-start.13) | collective-permute-done | bytes 983072 | tf_op jit(solution)/shard_map/ppermute | solution.py:47
  61.5 3.0 maximum_select_fusion.10.w_out
  66.6 5.0 maximum_select_fusion.4.refs_5_.refs_6_.refs_7_.wq.wk.wv
  73.6 5.1 maximum_select_fusion.5.refs_5_.refs_6_.refs_7_
  78.6 6.0 %maximum_select_fusion.w_up = bf16[3072,768]{1,0:T(8,128)(2,1)} fusion(bf16[1536,768]{1,0:T(8,128)(2,1)S(1)} %multiply_convert_fusion.1, bf16[1536,768]{1,0:T(8,128)(2,1)} %collective-permute-done.10, pred[]{:T(512)S(6)} %ne.29), kind=kLoop, calls=%fused_computation | loop fusion | flops 21233664 | bytes 9437185 | tf_op jit(solution)/shard_map/jit(_where)/select_n | solution.py:92
  84.6 6.6 %collective-permute-done.2.refs_2_.x1 = bf16[640,768]{1,0:T(8,128)(2,1)S(1)} collective-permute-done((bf16[640,768]{1,0:T(8,128)(2,1)S(1)}, bf16[640,768]{1,0:T(8,128)(2,1)S(1)}, u32[]{:S(2)}, u32[]{:S(2)}) %collective-permute-start.2) | collective-permute-done | bytes 983072 | tf_op jit(solution)/shard_map/ppermute | solution.py:47
  91.8 7.9 %maximum_select_fusion.1.w_down = bf16[768,3072]{1,0:T(8,128)(2,1)} fusion(bf16[384,3072]{1,0:T(8,128)(2,1)} %multiply_convert_fusion, bf16[384,3072]{1,0:T(8,128)(2,1)} %collective-permute-done.11, pred[]{:T(512)S(6)} %ne.29), kind=kLoop, calls=%fused_computation.1 | loop fusion | flops 21233664 | bytes 9437185 | tf_op jit(solution)/shard_map/jit(_where)/select_n | solution.py:92
  99.7 11.7 %collective-permute-done.14.refs_2_ = bf16[640,768]{1,0:T(8,128)(2,1)S(1)} collective-permute-done((bf16[640,768]{1,0:T(8,128)(2,1)}, bf16[640,768]{1,0:T(8,128)(2,1)S(1)}, u32[]{:S(2)}, u32[]{:S(2)}) %collective-permute-start.14) | collective-permute-done | bytes 983072 | tf_op jit(solution)/shard_map/ppermute | solution.py:47
  111.9 3.3 maximum_select_fusion.2.w_up
  115.3 4.1 maximum_select_fusion.3.w_down
  121.3 8.6 %shard_map.222.refs_1_.refs_2_.refs_3_ = bf16[576,2560]{1,0:T(8,128)(2,1)} custom-call(s32[3]{0:T(128)} %pad_add_fusion.1.refs_0_.pref, bf16[640,768]{1,0:T(8,128)(2,1)} %copy-done.2, bf16[640,768]{1,0:T(8,128)(2,1)} %copy-done.10, bf16[640,768]{1,0:T(8,128)(2,1)} %copy-done.11, bf16[640,768]{1,0:T(8,128)(2,1)} %copy-done.12, ...), custom_call_target="tpu_custom_call" | custom-call | flops 2264924160 | bytes 17504256 | tf_op jit(solution)/shard_map/pallas_call | solution.py:126
  129.9 21.4 %shard_map.223 = (bf16[192,640]{1,0:T(8,128)(2,1)}, bf16[192,640]{1,0:T(8,128)(2,1)}, bf16[192,640]{1,0:T(8,128)(2,1)}, bf16[192,640]{1,0:T(8,128)(2,1)}, f32[192,2560]{1,0:T(8,128)}, /*index=5*/f32[3,1,2560]{2,1,0:T(1,128)}) custom-call(s32[3]{0:T(128)} %pad_add_fusion.1.refs_0_.pref, bf16[576,2560]{1,0:T(8,128)(2,1)} %shard_map.222.refs_1_.refs_2_.refs_3_, ...), custom_call_target="tpu_custom_call" | custom-call | flops 16000000000 | bytes 11827200 | tf_op jit(solution)/shard_map/pallas_call | solution.py:126
  155.4 8.4 %shard_map.225.refs_1_.refs_2_.refs_3_ = bf16[576,2560]{1,0:T(8,128)(2,1)} custom-call(s32[3]{0:T(128)} %pad_add_fusion.1.refs_0_.pref, bf16[640,768]{1,0:T(8,128)(2,1)} %collective-permute-done.13.refs_1_.x, bf16[640,768]{1,0:T(8,128)(2,1)} %copy-done.7, bf16[640,768]{1,0:T(8,128)(2,1)} %copy-done.8, bf16[640,768]{1,0:T(8,128)(2,1)} %copy-done.9, ...), custom_call_target="tpu_custom_call" | custom-call | flops 2264924160 | bytes 17498112 | tf_op jit(solution)/shard_map/pallas_call | solution.py:126
  163.8 21.6 %shard_map.226 = (bf16[192,640]{1,0:T(8,128)(2,1)}, bf16[192,640]{1,0:T(8,128)(2,1)}, bf16[192,640]{1,0:T(8,128)(2,1)}, bf16[192,640]{1,0:T(8,128)(2,1)}, f32[192,2560]{1,0:T(8,128)}, /*index=5*/f32[3,1,2560]{2,1,0:T(1,128)}) custom-call(s32[3]{0:T(128)} %pad_add_fusion.1.refs_0_.pref, bf16[576,2560]{1,0:T(8,128)(2,1)} %shard_map.225.refs_1_.refs_2_.refs_3_, ...), custom_call_target="tpu_custom_call" | custom-call | flops 16000000000 | bytes 11827200 | tf_op jit(solution)/shard_map/pallas_call | solution.py:126
  188.4 19.6 %shard_map.224 = (bf16[768,640]{1,0:T(8,128)(2,1)}, bf16[640,768]{1,0:T(8,128)(2,1)}, f32[640,768]{1,0:T(8,128)}, f32[640,1]{1,0:T(8,128)}, bf16[640,3072]{1,0:T...) custom-call(s32[3]{0:T(128)} %pad_add_fusion.1.refs_0_.pref, ...), custom_call_target="tpu_custom_call" | custom-call | flops 6794772480 | bytes 27364352 | tf_op jit(solution)/shard_map/pallas_call | solution.py:126
  208.9 17.4 %shard_map.227 = (f32[640,768]{1,0:T(8,128)}, bf16[640,768]{1,0:T(8,128)(2,1)}, f32[3,768]{1,0:T(4,128)}) custom-call(s32[3]{0:T(128)} %pad_add_fusion.1.refs_0_.pref, bf16[192,640]{1,0:T(8,128)(2,1)} %get-tuple-element.55.c0, bf16[192,640]{1,0:T(8,128)(2,1)} %copy-done.32, bf16[192,640]{1,0:T(8,128)(2,1)} %copy-done.33, bf16[192,640]{1,0:T(8,128)(2,1)} %copy-done.34, ...), custom_call_target="tpu_custom_call" | custom-call | flops 6794772480 | bytes 17522176 | tf_op jit(solution)/shard_map/pallas_call | solution.py:126
  226.3 18.5 %shard_map.228 = (bf16[640,3072]{1,0:T(8,128)(2,1)}, f32[1,3072]{1,0:T(1,128)}, f32[640,768]{1,0:T(8,128)}, bf16[640,768]{1,0:T(8,128)(2,1)}, bf16[192,640]{1,0:...) custom-call(s32[3]{0:T(128)} %pad_add_fusion.1.refs_0_.pref, ...), custom_call_target="tpu_custom_call" | custom-call | flops 6794772480 | bytes 27364864 | tf_op jit(solution)/shard_map/pallas_call | solution.py:126
  250.4 14.2 %shard_map.232 = (bf16[768,3072]{1,0:T(8,128)(2,1)}, bf16[3072,768]{1,0:T(8,128)(2,1)}, bf16[768,768]{1,0:T(8,128)(2,1)}) custom-call(s32[3]{0:T(128)} %pad_add_fusion.1.refs_0_.pref, bf16[640,768]{1,0:T(8,128)(2,1)} %get-tuple-element.61.grad_ffn, bf16[640,3072]{1,0:T(8,128)(2,1)} %get-tuple-element.78.gelu, ...), custom_call_target="tpu_custom_call" | custom-call | flops 6794772480 | bytes 22413312 | tf_op jit(solution)/shard_map/pallas_call | solution.py:126
  268.6 33.2 %shard_map.229 = (bf16[3,192,640]{2,1,0:T(8,128)(2,1)}, bf16[3,192,640]{2,1,0:T(8,128)(2,1)}, bf16[3,192,640]{2,1,0:T(8,128)(2,1)}, bf16[3,192,640]{2,1,0:T(8,128)(2,1)}) custom-call(s32[3]{0:T(128)} %pad_add_fusion.1.refs_0_.pref, bf16[576,2560]{1,0:T(8,128)(2,1)} %shard_map.222.refs_1_.refs_2_.refs_3_, ...), custom_call_target="tpu_custom_call" | custom-call | flops 30000001024 | bytes 14776320 | tf_op jit(solution)/shard_map/pallas_call | solution.py:126
  301.7 7.8 %shard_map.231 = (bf16[3,192,768]{2,1,0:T(8,128)(2,1)}, f32[3,192,1]{2,1,0:T(8,128)}) custom-call(s32[3]{0:T(128)} %pad_add_fusion.1.refs_0_.pref, bf16[3,192,640]{2,1,0:T(8,128)(2,1)} %get-tuple-element.72.e0.d0, bf16[3,192,640]{2,1,0:T(8,128)(2,1)} %get-tuple-element.73.d1, bf16[3,192,640]{2,1,0:T(8,128)(2,1)} %get-tuple-element.74.d2, ...), custom_call_target="tpu_custom_call" | custom-call | flops 2264924160 | bytes 7768320 | tf_op jit(solution)/shard_map/pallas_call | solution.py:126
  317.5 2.9 collective-permute-done.66
  325.7 3.2 constant_dynamic-slice_fusion.10
  335.3 6.0 %collective-permute-done.40 = bf16[192,768]{1,0:T(8,128)(2,1)S(1)} collective-permute-done((bf16[192,768]{1,0:T(8,128)(2,1)S(1)}, bf16[192,768]{1,0:T(8,128)(2,1)S(1)}, u32[]{:S(2)}, u32[]{:S(2)}) %collective-permute-start.40) | collective-permute-done | bytes 294944 | tf_op jit(solution)/shard_map/ppermute | solution.py:47
  348.4 3.3 add_convert_fusion
  356.5 4.2 collective-permute-done.34
  362.5 2.9 collective-permute-start.27
  370.6 7.6 %collective-permute-done.58 = bf16[192,3072]{1,0:T(8,128)(2,1)} collective-permute-done((bf16[192,3072]{1,0:T(8,128)(2,1)S(1)}, bf16[192,3072]{1,0:T(8,128)(2,1)}, u32[]{:S(2)}, u32[]{:S(2)}) %collective-permute-start.58) | collective-permute-done | bytes 1179680 | tf_op jit(solution)/shard_map/ppermute | solution.py:47
  382.0 3.0 add_convert_fusion.1
  385.1 2.8 collective-permute-done.36
  388.8 8.9 %collective-permute-done.59 = bf16[96,3072]{1,0:T(8,128)(2,1)S(1)} collective-permute-done((bf16[96,3072]{1,0:T(8,128)(2,1)S(1)}, bf16[96,3072]{1,0:T(8,128)(2,1)S(1)}, u32[]{:S(2)}, u32[]{:S(2)}) %collective-permute-start.59) | collective-permute-done | bytes 589856 | tf_op jit(solution)/shard_map/ppermute | solution.py:47
  398.8 20.6 %collective-permute-done.49 = bf16[768,768]{1,0:T(8,128)(2,1)S(1)} collective-permute-done((bf16[768,768]{1,0:T(8,128)(2,1)S(1)}, bf16[768,768]{1,0:T(8,128)(2,1)S(1)}, u32[]{:S(2)}, u32[]{:S(2)}) %collective-permute-start.49) | collective-permute-done | bytes 1179680 | tf_op jit(solution)/shard_map/ppermute | solution.py:47
  420.7 5.4 collective-permute-done.60
  426.7 10.0 %collective-permute-done.50 = bf16[384,768]{1,0:T(8,128)(2,1)S(1)} collective-permute-done((bf16[384,768]{1,0:T(8,128)(2,1)S(1)}, bf16[384,768]{1,0:T(8,128)(2,1)S(1)}, u32[]{:S(2)}, u32[]{:S(2)}) %collective-permute-start.50) | collective-permute-done | bytes 589856 | tf_op jit(solution)/shard_map/ppermute | solution.py:47
  436.9 6.9 %collective-permute-done.61 = bf16[24,3072]{1,0:T(8,128)(2,1)S(1)} collective-permute-done((bf16[24,3072]{1,0:T(8,128)(2,1)S(1)}, bf16[24,3072]{1,0:T(8,128)(2,1)S(1)}, u32[]{:S(2)}, u32[]{:S(2)}) %collective-permute-start.61) | collective-permute-done | bytes 147488 | tf_op jit(solution)/shard_map/ppermute | solution.py:47
  444.9 7.2 %collective-permute-done.51 = bf16[192,768]{1,0:T(8,128)(2,1)S(1)} collective-permute-done((bf16[192,768]{1,0:T(8,128)(2,1)S(1)}, bf16[192,768]{1,0:T(8,128)(2,1)S(1)}, u32[]{:S(2)}, u32[]{:S(2)}) %collective-permute-start.51) | collective-permute-done | bytes 294944 | tf_op jit(solution)/shard_map/ppermute | solution.py:47
  452.5 8.2 %collective-permute-done.62 = bf16[24,3072]{1,0:T(8,128)(2,1)S(1)} collective-permute-done((bf16[24,3072]{1,0:T(8,128)(2,1)S(1)}, bf16[24,3072]{1,0:T(8,128)(2,1)S(1)}, u32[]{:S(2)}, u32[]{:S(2)}) %collective-permute-start.62) | collective-permute-done | bytes 147488 | tf_op jit(solution)/shard_map/ppermute | solution.py:47
  462.9 4.3 collective-permute-done.52
  474.7 14.5 %collective-permute-done.53 = bf16[96,768]{1,0:T(8,128)(2,1)S(1)} collective-permute-done((bf16[96,768]{1,0:T(8,128)(2,1)S(1)}, bf16[96,768]{1,0:T(8,128)(2,1)S(1)}, u32[]{:S(2)}, u32[]{:S(2)}) %collective-permute-start.53) | collective-permute-done | bytes 147488 | tf_op jit(solution)/shard_map/ppermute | solution.py:47
  492.2 9.8 %shard_map.230 = bf16[640,768]{1,0:T(8,128)(2,1)} custom-call(s32[3]{0:T(128)} %pad_add_fusion.1.refs_0_.pref, bf16[3,192,640]{2,1,0:T(8,128)(2,1)} %get-tuple-element.72.e0.d0, bf16[3,192,640]{2,1,0:T(8,128)(2,1)} %copy-done.14, bf16[3,192,640]{2,1,0:T(8,128)(2,1)} %copy-done.15, bf16[3,192,640]{2,1,0:T(8,128)(2,1)} %copy-done.16, ...), custom_call_target="tpu_custom_call" | custom-call | flops 2264924160 | bytes 17498112 | tf_op jit(solution)/shard_map/pallas_call | solution.py:126
  517.2 6.0 %collective-permute-done.47 = bf16[192,768]{1,0:T(8,128)(2,1)} collective-permute-done((bf16[192,768]{1,0:T(8,128)(2,1)}, bf16[192,768]{1,0:T(8,128)(2,1)}, u32[]{:S(2)}, u32[]{:S(2)}) %collective-permute-start.47) | collective-permute-done | bytes 294944 | tf_op jit(solution)/shard_map/ppermute | solution.py:47
  525.5 4.4 collective-permute-done.30
  536.9 10.9 %collective-permute-done.65 = bf16[192,3072]{1,0:T(8,128)(2,1)} collective-permute-done((bf16[192,3072]{1,0:T(8,128)(2,1)S(1)}, bf16[192,3072]{1,0:T(8,128)(2,1)}, u32[]{:S(2)}, u32[]{:S(2)}) %collective-permute-start.65) | collective-permute-done | bytes 1179680 | tf_op jit(solution)/shard_map/ppermute | solution.py:47
  547.8 4.6 fusion.1
  552.4 7.1 %collective-permute-done.56 = bf16[768,768]{1,0:T(8,128)(2,1)S(1)} collective-permute-done((bf16[768,768]{1,0:T(8,128)(2,1)S(1)}, bf16[768,768]{1,0:T(8,128)(2,1)S(1)}, u32[]{:S(2)}, u32[]{:S(2)}) %collective-permute-start.56) | collective-permute-done | bytes 1179680 | tf_op jit(solution)/shard_map/ppermute | solution.py:47
  559.5 2.7 fusion
  (291 shorter events, 129.1 us)
Async XLA Ops:
  7.5 10.6 %collective-permute-start = (s32[2]{0:T(128)S(1)}, s32[2]{0:T(128)S(1)}, u32[]{:S(2)}, u32[]{:S(2)}) collective-permute-start(s32[2]{0:T(128)S(1)} %pad_add_fusion), channel_id=1, source_target_pairs={{0,1},{1,0},{2,3},{3,2},{4,5},{5,4},{6,7},{7,6},{8,9},{9,8},{10,11... | collective-permute-start | bytes 32 | tf_op jit(solution)/shard_map/ppermute | solution.py:47
  12.2 53.9 %collective-permute-start.5 = (bf16[1152,768]{1,0:T(8,128)(2,1)}, bf16[1152,768]{1,0:T(8,128)(2,1)}, u32[]{:S(2)}, u32[]{:S(2)}) collective-permute-start(bf16[1152,768]{1,0:T(8,128)(2,1)} %multiply_convert_fusion.2), channel_id=1, source_target_pairs={{0,1},{1,0},{2,3},{3,2},{4,5},{5,4},{6,7},{7,6},{8,9},{9,8},{10,11... | collective-permute-start | bytes 5308424 | tf_op jit(solution)/shard_map/ppermute | solution.py:47
  12.7 37.5 %collective-permute-start.1 = (bf16[640,768]{1,0:T(8,128)(2,1)}, bf16[640,768]{1,0:T(8,128)(2,1)S(1)}, u32[]{:S(2)}, u32[]{:S(2)}) collective-permute-start(bf16[640,768]{1,0:T(8,128)(2,1)} %bitcast.26), channel_id=1, source_target_pairs={{0,0},{1,4},{2,2},{3,6},{4,1},{5,5},{6,3},{7,7},{8,8},{9,12},{10,1... | collective-permute-start | bytes 2949128 | tf_op jit(solution)/shard_map/ppermute | solution.py:47
  18.1 53.5 %collective-permute-start.10 = (bf16[1536,768]{1,0:T(8,128)(2,1)S(1)}, bf16[1536,768]{1,0:T(8,128)(2,1)}, u32[]{:S(2)}, u32[]{:S(2)}) collective-permute-start(bf16[1536,768]{1,0:T(8,128)(2,1)S(1)} %multiply_convert_fusion.1), channel_id=1, source_target_pairs={{0,1},{1,0},{2,3},{3,2},{4,5},{5,4},{6,7},{7,6},{8,9},{9,8},{10,11... | collective-permute-start | bytes 7077896 | tf_op jit(solution)/shard_map/ppermute | solution.py:47
  18.2 48.4 %collective-permute-start.17 = (bf16[1152,768]{1,0:T(8,128)(2,1)}, bf16[1152,768]{1,0:T(8,128)(2,1)}, u32[]{:S(2)}, u32[]{:S(2)}) collective-permute-start(bf16[1152,768]{1,0:T(8,128)(2,1)} %param.26), channel_id=1, source_target_pairs={{0,1},{1,0},{2,3},{3,2},{4,5},{5,4},{6,7},{7,6},{8,9},{9,8},{10,11... | collective-permute-start | bytes 5308424 | tf_op jit(solution)/shard_map/ppermute | solution.py:47
  18.7 42.1 %collective-permute-start.13 = (bf16[640,768]{1,0:T(8,128)(2,1)}, bf16[640,768]{1,0:T(8,128)(2,1)}, u32[]{:S(2)}, u32[]{:S(2)}) collective-permute-start(bf16[640,768]{1,0:T(8,128)(2,1)} %bitcast.7), channel_id=1, source_target_pairs={{0,0},{1,4},{2,2},{3,6},{4,1},{5,5},{6,3},{7,7},{8,8},{9,12},{10,1... | collective-permute-start | bytes 2949128 | tf_op jit(solution)/shard_map/ppermute | solution.py:47
  50.2 41.1 %collective-permute-start.11 = (bf16[384,3072]{1,0:T(8,128)(2,1)}, bf16[384,3072]{1,0:T(8,128)(2,1)}, u32[]{:S(2)}, u32[]{:S(2)}) collective-permute-start(bf16[384,3072]{1,0:T(8,128)(2,1)} %multiply_convert_fusion), channel_id=1, source_target_pairs={{0,1},{1,0},{2,3},{3,2},{4,5},{5,4},{6,7},{7,6},{8,9},{9,8},{10,11... | collective-permute-start | bytes 7077896 | tf_op jit(solution)/shard_map/ppermute | solution.py:47
  60.8 50.6 %collective-permute-start.22 = (bf16[1536,768]{1,0:T(8,128)(2,1)}, bf16[1536,768]{1,0:T(8,128)(2,1)S(1)}, u32[]{:S(2)}, u32[]{:S(2)}) collective-permute-start(bf16[1536,768]{1,0:T(8,128)(2,1)} %param.28), channel_id=1, source_target_pairs={{0,1},{1,0},{2,3},{3,2},{4,5},{5,4},{6,7},{7,6},{8,9},{9,8},{10,11... | collective-permute-start | bytes 7077896 | tf_op jit(solution)/shard_map/ppermute | solution.py:47
  66.1 49.2 %collective-permute-start.23 = (bf16[384,3072]{1,0:T(8,128)(2,1)S(1)}, bf16[384,3072]{1,0:T(8,128)(2,1)S(1)}, u32[]{:S(2)}, u32[]{:S(2)}) collective-permute-start(bf16[384,3072]{1,0:T(8,128)(2,1)S(1)} %copy-done.5), channel_id=1, source_target_pairs={{0,1},{1,0},{2,3},{3,2},{4,5},{5,4},{6,7},{7,6},{8,9},{9,8},{10,11... | collective-permute-start | bytes 7077896 | tf_op jit(solution)/shard_map/ppermute | solution.py:47
  66.6 24.6 %collective-permute-start.2 = (bf16[640,768]{1,0:T(8,128)(2,1)S(1)}, bf16[640,768]{1,0:T(8,128)(2,1)S(1)}, u32[]{:S(2)}, u32[]{:S(2)}) collective-permute-start(bf16[640,768]{1,0:T(8,128)(2,1)S(1)} %collective-permute-done.1.refs_1_.x.x0), channel_id=1, source_target_pairs={{0,2},{1,3},{2,0},{3,1},{4,6},{5,7},{6,4},{7,5},{8,10},{9,11},{10,... | collective-permute-start | bytes 2949128 | tf_op jit(solution)/shard_map/ppermute | solution.py:47
  71.6 39.8 %collective-permute-start.14 = (bf16[640,768]{1,0:T(8,128)(2,1)}, bf16[640,768]{1,0:T(8,128)(2,1)S(1)}, u32[]{:S(2)}, u32[]{:S(2)}) collective-permute-start(bf16[640,768]{1,0:T(8,128)(2,1)} %collective-permute-done.13.refs_1_.x), channel_id=1, source_target_pairs={{0,2},{1,3},{2,0},{3,1},{4,6},{5,7},{6,4},{7,5},{8,10},{9,11},{10,... | collective-permute-start | bytes 2949128 | tf_op jit(solution)/shard_map/ppermute | solution.py:47
  91.2 28.1 %collective-permute-start.3 = (bf16[640,768]{1,0:T(8,128)(2,1)S(1)}, bf16[640,768]{1,0:T(8,128)(2,1)S(1)}, u32[]{:S(2)}, u32[]{:S(2)}) collective-permute-start(bf16[640,768]{1,0:T(8,128)(2,1)S(1)} %collective-permute-done.1.refs_1_.x.x0), channel_id=1, source_target_pairs={{0,1},{1,0},{2,3},{3,2},{4,5},{5,4},{6,7},{7,6},{8,9},{9,8},{10,11... | collective-permute-start | bytes 2949128 | tf_op jit(solution)/shard_map/ppermute | solution.py:47
  91.3 28.1 %collective-permute-start.4 = (bf16[640,768]{1,0:T(8,128)(2,1)S(1)}, bf16[640,768]{1,0:T(8,128)(2,1)S(1)}, u32[]{:S(2)}, u32[]{:S(2)}) collective-permute-start(bf16[640,768]{1,0:T(8,128)(2,1)S(1)} %collective-permute-done.2.refs_2_.x1), channel_id=1, source_target_pairs={{0,1},{1,0},{2,3},{3,2},{4,5},{5,4},{6,7},{7,6},{8,9},{9,8},{10,11... | collective-permute-start | bytes 2949128 | tf_op jit(solution)/shard_map/ppermute | solution.py:47
  111.4 42.1 %collective-permute-start.15 = (bf16[640,768]{1,0:T(8,128)(2,1)}, bf16[640,768]{1,0:T(8,128)(2,1)S(1)}, u32[]{:S(2)}, u32[]{:S(2)}) collective-permute-start(bf16[640,768]{1,0:T(8,128)(2,1)} %collective-permute-done.13.refs_1_.x), channel_id=1, source_target_pairs={{0,1},{1,0},{2,3},{3,2},{4,5},{5,4},{6,7},{7,6},{8,9},{9,8},{10,11... | collective-permute-start | bytes 2949128 | tf_op jit(solution)/shard_map/ppermute | solution.py:47
  111.4 42.1 %collective-permute-start.16 = (bf16[640,768]{1,0:T(8,128)(2,1)S(1)}, bf16[640,768]{1,0:T(8,128)(2,1)S(1)}, u32[]{:S(2)}, u32[]{:S(2)}) collective-permute-start(bf16[640,768]{1,0:T(8,128)(2,1)S(1)} %collective-permute-done.14.refs_2_), channel_id=1, source_target_pairs={{0,1},{1,0},{2,3},{3,2},{4,5},{5,4},{6,7},{7,6},{8,9},{9,8},{10,11... | collective-permute-start | bytes 2949128 | tf_op jit(solution)/shard_map/ppermute | solution.py:47
  151.3 34.5 %collective-permute-start.6 = (bf16[192,640]{1,0:T(8,128)(2,1)}, bf16[192,640]{1,0:T(8,128)(2,1)S(1)}, u32[]{:S(2)}, u32[]{:S(2)}) collective-permute-start(bf16[192,640]{1,0:T(8,128)(2,1)} %get-tuple-element.51), channel_id=1, source_target_pairs={{0,2},{1,3},{2,0},{3,1},{4,6},{5,7},{6,4},{7,5},{8,10},{9,11},{10,... | collective-permute-start | bytes 737288 | tf_op jit(solution)/shard_map/ppermute | solution.py:47
  151.6 36.1 %collective-permute-start.7 = (bf16[192,640]{1,0:T(8,128)(2,1)}, bf16[192,640]{1,0:T(8,128)(2,1)S(1)}, u32[]{:S(2)}, u32[]{:S(2)}) collective-permute-start(bf16[192,640]{1,0:T(8,128)(2,1)} %get-tuple-element.52), channel_id=1, source_target_pairs={{0,1},{1,0},{2,3},{3,2},{4,5},{5,4},{6,7},{7,6},{8,9},{9,8},{10,11... | collective-permute-start | bytes 737288 | tf_op jit(solution)/shard_map/ppermute | solution.py:47
  151.6 36.1 %collective-permute-start.8 = (bf16[192,640]{1,0:T(8,128)(2,1)}, bf16[192,640]{1,0:T(8,128)(2,1)S(1)}, u32[]{:S(2)}, u32[]{:S(2)}) collective-permute-start(bf16[192,640]{1,0:T(8,128)(2,1)} %get-tuple-element.53), channel_id=1, source_target_pairs={{0,3},{1,2},{2,1},{3,0},{4,7},{5,6},{6,5},{7,4},{8,11},{9,10},{10,... | collective-permute-start | bytes 737288 | tf_op jit(solution)/shard_map/ppermute | solution.py:47
  185.4 22.6 %collective-permute-start.18 = (bf16[192,640]{1,0:T(8,128)(2,1)}, bf16[192,640]{1,0:T(8,128)(2,1)S(1)}, u32[]{:S(2)}, u32[]{:S(2)}) collective-permute-start(bf16[192,640]{1,0:T(8,128)(2,1)} %get-tuple-element.56), channel_id=1, source_target_pairs={{0,2},{1,3},{2,0},{3,1},{4,6},{5,7},{6,4},{7,5},{8,10},{9,11},{10,... | collective-permute-start | bytes 737288 | tf_op jit(solution)/shard_map/ppermute | solution.py:47
  185.7 22.3 %collective-permute-start.19 = (bf16[192,640]{1,0:T(8,128)(2,1)}, bf16[192,640]{1,0:T(8,128)(2,1)S(1)}, u32[]{:S(2)}, u32[]{:S(2)}) collective-permute-start(bf16[192,640]{1,0:T(8,128)(2,1)} %get-tuple-element.57), channel_id=1, source_target_pairs={{0,1},{1,0},{2,3},{3,2},{4,5},{5,4},{6,7},{7,6},{8,9},{9,8},{10,11... | collective-permute-start | bytes 737288 | tf_op jit(solution)/shard_map/ppermute | solution.py:47
  185.8 22.3 %collective-permute-start.20 = (bf16[192,640]{1,0:T(8,128)(2,1)}, bf16[192,640]{1,0:T(8,128)(2,1)S(1)}, u32[]{:S(2)}, u32[]{:S(2)}) collective-permute-start(bf16[192,640]{1,0:T(8,128)(2,1)} %get-tuple-element.58), channel_id=1, source_target_pairs={{0,3},{1,2},{2,1},{3,0},{4,7},{5,6},{6,5},{7,4},{8,11},{9,10},{10,... | collective-permute-start | bytes 737288 | tf_op jit(solution)/shard_map/ppermute | solution.py:47
  244.8 23.7 %collective-permute-start.24 = (bf16[192,640]{1,0:T(8,128)(2,1)}, bf16[192,640]{1,0:T(8,128)(2,1)}, u32[]{:S(2)}, u32[]{:S(2)}) collective-permute-start(bf16[192,640]{1,0:T(8,128)(2,1)} %get-tuple-element.67), channel_id=1, source_target_pairs={{0,2},{1,3},{2,0},{3,1},{4,6},{5,7},{6,4},{7,5},{8,10},{9,11},{10,... | collective-permute-start | bytes 737288 | tf_op jit(solution)/shard_map/ppermute | solution.py:47
  245.1 23.4 %collective-permute-start.25 = (bf16[192,640]{1,0:T(8,128)(2,1)}, bf16[192,640]{1,0:T(8,128)(2,1)}, u32[]{:S(2)}, u32[]{:S(2)}) collective-permute-start(bf16[192,640]{1,0:T(8,128)(2,1)} %get-tuple-element.68), channel_id=1, source_target_pairs={{0,1},{1,0},{2,3},{3,2},{4,5},{5,4},{6,7},{7,6},{8,9},{9,8},{10,11... | collective-permute-start | bytes 737288 | tf_op jit(solution)/shard_map/ppermute | solution.py:47
  245.2 23.4 %collective-permute-start.26 = (bf16[192,640]{1,0:T(8,128)(2,1)}, bf16[192,640]{1,0:T(8,128)(2,1)}, u32[]{:S(2)}, u32[]{:S(2)}) collective-permute-start(bf16[192,640]{1,0:T(8,128)(2,1)} %get-tuple-element.69), channel_id=1, source_target_pairs={{0,3},{1,2},{2,1},{3,0},{4,7},{5,6},{6,5},{7,4},{8,11},{9,10},{10,... | collective-permute-start | bytes 737288 | tf_op jit(solution)/shard_map/ppermute | solution.py:47
  266.5 81.8 %collective-permute-start.57 = (bf16[384,3072]{1,0:T(8,128)(2,1)S(1)}, bf16[384,3072]{1,0:T(8,128)(2,1)}, u32[]{:S(2)}, u32[]{:S(2)}) collective-permute-start(bf16[384,3072]{1,0:T(8,128)(2,1)S(1)} %constant_dynamic-slice_fusion.5), channel_id=1, source_target_pairs={{0,1},{1,0},{2,3},{3,2},{4,5},{5,4},{6,7},{7,6},{8,9},{9,8},{10,11... | collective-permute-start | bytes 7077896 | tf_op jit(solution)/shard_map/ppermute | solution.py:47
  267.5 62.8 %collective-permute-start.39 = (bf16[384,768]{1,0:T(8,128)(2,1)}, bf16[384,768]{1,0:T(8,128)(2,1)}, u32[]{:S(2)}, u32[]{:S(2)}) collective-permute-start(bf16[384,768]{1,0:T(8,128)(2,1)} %constant_dynamic-slice_fusion.15), channel_id=1, source_target_pairs={{0,1},{1,0},{2,3},{3,2},{4,5},{5,4},{6,7},{7,6},{8,9},{9,8},{10,11... | collective-permute-start | bytes 1769480 | tf_op jit(solution)/shard_map/ppermute | solution.py:47
  323.8 10.7 %collective-permute-start.31 = (bf16[288,768]{1,0:T(8,128)(2,1)S(1)}, bf16[288,768]{1,0:T(8,128)(2,1)S(1)}, u32[]{:S(2)}, u32[]{:S(2)}) collective-permute-start(bf16[288,768]{1,0:T(8,128)(2,1)S(1)} %constant_dynamic-slice_fusion.18), channel_id=1, source_target_pairs={{0,8},{1,9},{2,10},{3,11},{4,12},{5,13},{6,14},{7,15},{8,0},{9,1},... | collective-permute-start | bytes 1327112 | tf_op jit(solution)/shard_map/ppermute | solution.py:47
  328.9 52.6 %collective-permute-start.48 = (bf16[1536,768]{1,0:T(8,128)(2,1)}, bf16[1536,768]{1,0:T(8,128)(2,1)}, u32[]{:S(2)}, u32[]{:S(2)}) collective-permute-start(bf16[1536,768]{1,0:T(8,128)(2,1)} %constant_dynamic-slice_fusion.10), channel_id=1, source_target_pairs={{0,1},{1,0},{2,3},{3,2},{4,5},{5,4},{6,7},{7,6},{8,9},{9,8},{10,11... | collective-permute-start | bytes 7077896 | tf_op jit(solution)/shard_map/ppermute | solution.py:47
  330.2 32.4 %collective-permute-start.69 = (f32[12,768]{1,0:T(8,128)}, f32[12,768]{1,0:T(8,128)}, u32[]{:S(2)}, u32[]{:S(2)}) collective-permute-start(f32[12,768]{1,0:T(8,128)} %add.202), channel_id=1, source_target_pairs={{0,4},{1,5},{2,6},{3,7},{4,0},{5,1},{6,2},{7,3},{8,12},{9,13},{10,... | collective-permute-start | bytes 110600 | tf_op jit(solution)/shard_map/ppermute | solution.py:47
  351.7 26.5 %collective-permute-start.58 = (bf16[192,3072]{1,0:T(8,128)(2,1)S(1)}, bf16[192,3072]{1,0:T(8,128)(2,1)}, u32[]{:S(2)}, u32[]{:S(2)}) collective-permute-start(bf16[192,3072]{1,0:T(8,128)(2,1)S(1)} %constant_dynamic-slice_fusion.4), channel_id=1, source_target_pairs={{0,8},{1,9},{2,10},{3,11},{4,12},{5,13},{6,14},{7,15},{8,0},{9,1},... | collective-permute-start | bytes 3538952 | tf_op jit(solution)/shard_map/ppermute | solution.py:47
  362.5 106.2 %collective-permute-start.27 = (bf16[3,192,640]{2,1,0:T(8,128)(2,1)}, bf16[3,192,640]{2,1,0:T(8,128)(2,1)S(1)}, u32[]{:S(2)}, u32[]{:S(2)}) collective-permute-start(bf16[3,192,640]{2,1,0:T(8,128)(2,1)} %get-tuple-element.73.d1), channel_id=1, source_target_pairs={{0,2},{1,3},{2,0},{3,1},{4,6},{5,7},{6,4},{7,5},{8,10},{9,11},{10,... | collective-permute-start | bytes 2211848 | tf_op jit(solution)/shard_map/ppermute | solution.py:47
  367.9 123.0 %collective-permute-start.28 = (bf16[3,192,640]{2,1,0:T(8,128)(2,1)}, bf16[3,192,640]{2,1,0:T(8,128)(2,1)S(1)}, u32[]{:S(2)}, u32[]{:S(2)}) collective-permute-start(bf16[3,192,640]{2,1,0:T(8,128)(2,1)} %get-tuple-element.74.d2), channel_id=1, source_target_pairs={{0,1},{1,0},{2,3},{3,2},{4,5},{5,4},{6,7},{7,6},{8,9},{9,8},{10,11... | collective-permute-start | bytes 2211848 | tf_op jit(solution)/shard_map/ppermute | solution.py:47
  368.8 122.6 %collective-permute-start.29 = (bf16[3,192,640]{2,1,0:T(8,128)(2,1)}, bf16[3,192,640]{2,1,0:T(8,128)(2,1)S(1)}, u32[]{:S(2)}, u32[]{:S(2)}) collective-permute-start(bf16[3,192,640]{2,1,0:T(8,128)(2,1)} %get-tuple-element.75.d3), channel_id=1, source_target_pairs={{0,3},{1,2},{2,1},{3,0},{4,7},{5,6},{6,5},{7,4},{8,11},{9,10},{10,... | collective-permute-start | bytes 2211848 | tf_op jit(solution)/shard_map/ppermute | solution.py:47
  381.5 16.3 %collective-permute-start.59 = (bf16[96,3072]{1,0:T(8,128)(2,1)S(1)}, bf16[96,3072]{1,0:T(8,128)(2,1)S(1)}, u32[]{:S(2)}, u32[]{:S(2)}) collective-permute-start(bf16[96,3072]{1,0:T(8,128)(2,1)S(1)} %constant_dynamic-slice_fusion.3), channel_id=1, source_target_pairs={{0,16},{1,17},{2,18},{3,19},{4,20},{5,21},{6,22},{7,23},{8,24},{9,... | collective-permute-start | bytes 1769480 | tf_op jit(solution)/shard_map/ppermute | solution.py:47
  387.9 31.5 %collective-permute-start.49 = (bf16[768,768]{1,0:T(8,128)(2,1)S(1)}, bf16[768,768]{1,0:T(8,128)(2,1)S(1)}, u32[]{:S(2)}, u32[]{:S(2)}) collective-permute-start(bf16[768,768]{1,0:T(8,128)(2,1)S(1)} %constant_dynamic-slice_fusion.9), channel_id=1, source_target_pairs={{0,16},{1,17},{2,18},{3,19},{4,20},{5,21},{6,22},{7,23},{8,24},{9,... | collective-permute-start | bytes 3538952 | tf_op jit(solution)/shard_map/ppermute | solution.py:47
  397.8 62.9 %collective-permute-start.37 = (bf16[1,3,192,768]{3,2,0,1:T(8,128)(2,1)S(1)}, bf16[1,3,192,768]{3,2,0,1:T(8,128)(2,1)S(1)}, u32[]{:S(2)}, u32[]{:S(2)}) collective-permute-start(bf16[1,3,192,768]{3,2,0,1:T(8,128)(2,1)S(1)} %bitcast.22), channel_id=1, source_target_pairs={{0,2},{1,3},{2,0},{3,1},{4,6},{5,7},{6,4},{7,5},{8,10},{9,11},{10,... | collective-permute-start | bytes 2654216 | tf_op jit(solution)/shard_map/ppermute | solution.py:47
  426.1 10.6 %collective-permute-start.50 = (bf16[384,768]{1,0:T(8,128)(2,1)S(1)}, bf16[384,768]{1,0:T(8,128)(2,1)S(1)}, u32[]{:S(2)}, u32[]{:S(2)}) collective-permute-start(bf16[384,768]{1,0:T(8,128)(2,1)S(1)} %constant_dynamic-slice_fusion.8), channel_id=1, source_target_pairs={{0,8},{1,9},{2,10},{3,11},{4,12},{5,13},{6,14},{7,15},{8,0},{9,1},... | collective-permute-start | bytes 1769480 | tf_op jit(solution)/shard_map/ppermute | solution.py:47
  468.8 63.8 %collective-permute-start.38 = (bf16[2,3,192,768]{3,2,0,1:T(8,128)(2,1)S(1)}, bf16[2,3,192,768]{3,2,0,1:T(8,128)(2,1)}, u32[]{:S(2)}, u32[]{:S(2)}) collective-permute-start(bf16[2,3,192,768]{3,2,0,1:T(8,128)(2,1)S(1)} %maximum_select_fusion.9), channel_id=1, source_target_pairs={{0,1},{1,0},{2,3},{3,2},{4,5},{5,4},{6,7},{7,6},{8,9},{9,8},{10,11... | collective-permute-start | bytes 5308424 | tf_op jit(solution)/shard_map/ppermute | solution.py:47
  469.1 20.1 %collective-permute-start.53 = (bf16[96,768]{1,0:T(8,128)(2,1)S(1)}, bf16[96,768]{1,0:T(8,128)(2,1)S(1)}, u32[]{:S(2)}, u32[]{:S(2)}) collective-permute-start(bf16[96,768]{1,0:T(8,128)(2,1)S(1)} %add_convert_fusion.13), channel_id=1, source_target_pairs={{0,4},{1,5},{2,6},{3,7},{4,0},{5,1},{6,2},{7,3},{8,12},{9,13},{10,... | collective-permute-start | bytes 442376 | tf_op jit(solution)/shard_map/ppermute | solution.py:47
  472.8 41.2 %collective-permute-start.12 = (bf16[640,768]{1,0:T(8,128)(2,1)}, bf16[640,768]{1,0:T(8,128)(2,1)}, u32[]{:S(2)}, u32[]{:S(2)}) collective-permute-start(bf16[640,768]{1,0:T(8,128)(2,1)} %get-tuple-element.54), channel_id=1, source_target_pairs={{0,0},{1,4},{2,2},{3,6},{4,1},{5,5},{6,3},{7,7},{8,8},{9,12},{10,1... | collective-permute-start | bytes 2949128 | tf_op jit(solution)/shard_map/ppermute | solution.py:47
  489.2 20.8 %collective-permute-start.64 = (bf16[96,3072]{1,0:T(8,128)(2,1)S(1)}, bf16[96,3072]{1,0:T(8,128)(2,1)S(1)}, u32[]{:S(2)}, u32[]{:S(2)}) collective-permute-start(bf16[96,3072]{1,0:T(8,128)(2,1)S(1)} %maximum_select_fusion.17), channel_id=1, source_target_pairs={{0,16},{1,17},{2,18},{3,19},{4,20},{5,21},{6,22},{7,23},{8,24},{9,... | collective-permute-start | bytes 1769480 | tf_op jit(solution)/shard_map/ppermute | solution.py:47
  490.9 11.2 %collective-permute-start.46 = (bf16[96,768]{1,0:T(8,128)(2,1)S(1)}, bf16[96,768]{1,0:T(8,128)(2,1)S(1)}, u32[]{:S(2)}, u32[]{:S(2)}) collective-permute-start(bf16[96,768]{1,0:T(8,128)(2,1)S(1)} %maximum_select_fusion.23), channel_id=1, source_target_pairs={{0,8},{1,9},{2,10},{3,11},{4,12},{5,13},{6,14},{7,15},{8,0},{9,1},... | collective-permute-start | bytes 442376 | tf_op jit(solution)/shard_map/ppermute | solution.py:47
  491.4 15.3 %collective-permute-start.54 = (bf16[192,768]{1,0:T(8,128)(2,1)S(1)}, bf16[192,768]{1,0:T(8,128)(2,1)}, u32[]{:S(2)}, u32[]{:S(2)}) collective-permute-start(bf16[192,768]{1,0:T(8,128)(2,1)S(1)} %maximum_select_fusion.20), channel_id=1, source_target_pairs={{0,2},{1,3},{2,0},{3,1},{4,6},{5,7},{6,4},{7,5},{8,10},{9,11},{10,... | collective-permute-start | bytes 884744 | tf_op jit(solution)/shard_map/ppermute | solution.py:47
  502.7 27.2 %collective-permute-start.30 = (bf16[640,768]{1,0:T(8,128)(2,1)}, bf16[640,768]{1,0:T(8,128)(2,1)}, u32[]{:S(2)}, u32[]{:S(2)}) collective-permute-start(bf16[640,768]{1,0:T(8,128)(2,1)} %shard_map.230), channel_id=1, source_target_pairs={{0,0},{1,4},{2,2},{3,6},{4,1},{5,5},{6,3},{7,7},{8,8},{9,12},{10,1... | collective-permute-start | bytes 2949128 | tf_op jit(solution)/shard_map/ppermute | solution.py:47
  506.7 16.5 %collective-permute-start.47 = (bf16[192,768]{1,0:T(8,128)(2,1)}, bf16[192,768]{1,0:T(8,128)(2,1)}, u32[]{:S(2)}, u32[]{:S(2)}) collective-permute-start(bf16[192,768]{1,0:T(8,128)(2,1)} %maximum_select_fusion.19), channel_id=1, source_target_pairs={{0,2},{1,3},{2,0},{3,1},{4,6},{5,7},{6,4},{7,5},{8,10},{9,11},{10,... | collective-permute-start | bytes 884744 | tf_op jit(solution)/shard_map/ppermute | solution.py:47
  510.8 19.1 %collective-permute-start.55 = (bf16[384,768]{1,0:T(8,128)(2,1)}, bf16[384,768]{1,0:T(8,128)(2,1)}, u32[]{:S(2)}, u32[]{:S(2)}) collective-permute-start(bf16[384,768]{1,0:T(8,128)(2,1)} %maximum_select_fusion.16), channel_id=1, source_target_pairs={{0,8},{1,9},{2,10},{3,11},{4,12},{5,13},{6,14},{7,15},{8,0},{9,1},... | collective-permute-start | bytes 1769480 | tf_op jit(solution)/shard_map/ppermute | solution.py:47
  514.0 33.9 %collective-permute-start.65 = (bf16[192,3072]{1,0:T(8,128)(2,1)S(1)}, bf16[192,3072]{1,0:T(8,128)(2,1)}, u32[]{:S(2)}, u32[]{:S(2)}) collective-permute-start(bf16[192,3072]{1,0:T(8,128)(2,1)S(1)} %maximum_select_fusion.13), channel_id=1, source_target_pairs={{0,8},{1,9},{2,10},{3,11},{4,12},{5,13},{6,14},{7,15},{8,0},{9,1},... | collective-permute-start | bytes 3538952 | tf_op jit(solution)/shard_map/ppermute | solution.py:47
  531.8 27.7 %collective-permute-start.56 = (bf16[768,768]{1,0:T(8,128)(2,1)S(1)}, bf16[768,768]{1,0:T(8,128)(2,1)S(1)}, u32[]{:S(2)}, u32[]{:S(2)}) collective-permute-start(bf16[768,768]{1,0:T(8,128)(2,1)S(1)} %maximum_select_fusion.12), channel_id=1, source_target_pairs={{0,16},{1,17},{2,18},{3,19},{4,20},{5,21},{6,22},{7,23},{8,24},{9,... | collective-permute-start | bytes 3538952 | tf_op jit(solution)/shard_map/ppermute | solution.py:47
  (62 other events, 516.7 us)

commit v2 on v1

--- a/solution.py
+++ b/solution.py
@@ -596,16 +596,20 @@
 ):
     @pl.when(pl.program_id(0) == 0)
     def _():
-        grad_out[...] = dot(grad_attn[...], ctx[...], 0, 1).astype(BF)
-
-    grad_down[...] = dot(grad_ffn[...], gelu[...], 0, 0).astype(BF)
-    grad_up[...] = dot(grad_hidden[...], act_one[...], 0, 0).astype(BF)
+        value = dot(grad_attn[...], ctx[...], 0, 1).astype(BF)
+        grad_out[...] = value.reshape(grad_out.shape)
+
+    value = dot(grad_ffn[...], gelu[...], 0, 0).astype(BF)
+    grad_down[...] = value.reshape(grad_down.shape)
+    value = dot(grad_hidden[...], act_one[...], 0, 0).astype(BF)
+    grad_up[...] = value.reshape(grad_up.shape)
 
 
 def weight_grads(pref, grad_ffn, gelu, grad_hidden, act_one, grad_attn, ctx):
     tok, width = grad_ffn.shape
     hidden = gelu.shape[1]
-    up, down, wide, row = ffn_specs(tok, width, hidden)
+    count, half = hidden // width, width // 2
+    wide = pl.BlockSpec((tok, width), lambda c, i: (0, c))
     full = whole((tok, width))
     return call(
         weight_grad_kernel,
@@ -613,28 +617,40 @@
         [grad_ffn, gelu, grad_hidden, act_one, grad_attn, ctx],
         [full, wide, wide, full, full, whole((width, tok))],
         [
-            shape_of((width, hidden), BF),
-            shape_of((hidden, width), BF),
-            shape_of((width, width), BF),
+            shape_of((2, count, half, width), BF),
+            shape_of((2 * count, half, width), BF),
+            shape_of((2, half, width), BF),
         ],
-        [down, up, whole((width, width))],
-        (hidden // FC,),
+        [
+            pl.BlockSpec((2, 1, half, width), lambda c, i: (0, c, 0, 0)),
+            pl.BlockSpec((2, half, width), lambda c, i: (c, 0, 0)),
+            whole((2, half, width)),
+        ],
+        (count,),
         [],
         2 * tok * width * (2 * hidden + width),
     )
 
 
-def qkv_grad_kernel(pref, d0, d1, d2, d3, x0, x1, x2, x3, out, sums, acc):
+def qkv_grad_kernel(pref, d0, d1, d2, d3, x0, x1, x2, x3, out, sums):
+    own = pref[0]
     total = None
     count = None
+    ones = jnp.ones((8, d0.shape[1]), BF)
     for grad, x in zip((d0, d1, d2, d3), (x0, x1, x2, x3)):
         value = grad[...]
         part = dot(value, jnp.clip(x[...], -CLIP, CLIP), 1, 0)
-        line = jnp.sum(value.astype(F32), axis=1, keepdims=True)
+        line = dot(ones, value, 1, 1)
         total = part if total is None else total + part
         count = line if count is None else count + line
     out[...] = total.astype(BF)
-    sums[...] = count
+    sums[...] = jnp.zeros_like(sums)
+    rows = out.shape[0]
+    for j in range(4):
+
+        @pl.when(own == j)
+        def _():
+            sums[:, j * rows : (j + 1) * rows] = count
 
 
 def qkv_grad(pref, grads, slots):
@@ -645,13 +661,13 @@
         pref,
         list(grads) + list(slots),
         [pl.BlockSpec((None, rows, tok), lambda o, i: (o, 0, 0))] * 4 + [whole((tok, width))] * 4,
-        [shape_of((3, rows, width), BF), shape_of((3, rows, 1), F32)],
+        [shape_of((3, rows, width), BF), shape_of((3, 8, width), F32)],
         [
             pl.BlockSpec((None, rows, width), lambda o, i: (o, 0, 0)),
-            pl.BlockSpec((None, rows, 1), lambda o, i: (o, 0, 0)),
+            pl.BlockSpec((None, 8, width), lambda o, i: (o, 0, 0)),
         ],
         (3,),
-        [pltpu.VMEM((8, 128), F32)],
+        [],
         2 * 4 * tok * width * 3 * rows,
     )
 
@@ -700,6 +716,280 @@
     )
 
 
+def place(bit):
+    name, mask = bit
+    at = lax.axis_index(name)
+    upper = lax.rem(lax.div(at, jnp.int32(mask)), jnp.int32(2))
+    return upper, {name: at + mask * (1 - 2 * upper)}
+
+
+def greet(bits):
+    barrier = pltpu.get_barrier_semaphore()
+    for bit in bits:
+        pl.semaphore_signal(
+            barrier, inc=1, device_id=place(bit)[1], device_id_type=pl.DeviceIdType.MESH
+        )
+    pl.semaphore_wait(barrier, len(bits))
+
+
+class Copies:
+    def __init__(self, send, recv, local):
+        self.send, self.recv, self.local_sem = send, recv, local
+        self.sent, self.kept = [], 0
+
+    def remote(self, source, target, device):
+        n = len(self.sent)
+        copy = pltpu.make_async_remote_copy(
+            src_ref=source,
+            dst_ref=target,
+            send_sem=self.send.at[n],
+            recv_sem=self.recv.at[n],
+            device_id=device,
+            device_id_type=pl.DeviceIdType.MESH,
+        )
+        copy.start()
+        self.sent.append(copy)
+        return copy
+
+    def local(self, source, target):
+        copy = pltpu.make_async_copy(source, target, self.local_sem.at[self.kept])
+        self.kept += 1
+        copy.start()
+        return copy
+
+    def finish(self):
+        for copy in self.sent:
+            copy.wait_send()
+
+
+def window(ref, region):
+    row, rows, col, cols = region
+    return ref.at[pl.ds(row, rows), pl.ds(col, cols)]
+
+
+def add_window(target, left, right, region, start):
+    row, rows, col, cols = region
+    step = 48 if rows % 48 == 0 else 16
+
+    def body(i, carry):
+        there = pl.ds(pl.multiple_of(row + i * step, 16), step)
+        here = pl.ds(pl.multiple_of(start + i * step, 16), step)
+        value = left[there, pl.ds(col, cols)].astype(F32) + right[here, :cols].astype(F32)
+        target[there, pl.ds(col, cols)] = value.astype(target.dtype)
+        return carry
+
+    lax.fori_loop(0, rows // step, body, 0)
+
+
+def scatter_sum(copies, work, far, full, bits):
+    rows, cols = work.shape
+    region, used, parts = (0, rows, 0, cols), 0, []
+    for n, bit in enumerate(bits):
+        upper, device = place(bit)
+        row, rows, col, cols = region
+        if (rows // 2) % 16 == 0:
+            rows //= 2
+            kept = (pl.multiple_of(row + upper * rows, 16), rows, col, cols)
+            sent = (pl.multiple_of(row + (1 - upper) * rows, 16), rows, col, cols)
+        else:
+            cols //= 2
+            kept = (row, rows, pl.multiple_of(col + upper * cols, 128), cols)
+            sent = (row, rows, pl.multiple_of(col + (1 - upper) * cols, 128), cols)
+        slot = far.at[pl.ds(used, rows), pl.ds(0, cols)]
+        copy = copies.remote(window(work, sent), slot, device)
+        yield
+        copy.wait_recv()
+        add_window(full if n == len(bits) - 1 else work, work, far, kept, used)
+        used += rows
+        region = kept
+        parts.append((bit, kept))
+    return parts
+
+
+def sum_flow(copies, own, other, work, near, far, full, result, core, bits):
+    copy = copies.remote(other, near, place(core)[1])
+    load = copies.local(own, work)
+    yield
+    copy.wait_recv()
+    load.wait()
+    add_window(work, work, near, (0, work.shape[0], 0, work.shape[1]), 0)
+    parts = yield from scatter_sum(copies, work, far, full, bits)
+    for bit, kept in reversed(parts):
+        copy = copies.remote(window(full, kept), window(full, kept), place(bit)[1])
+        yield
+        copy.wait_recv()
+    store = copies.local(full, result)
+    yield
+    store.wait()
+
+
+def vector_flow(copies, sums, far, bits):
+    for n, bit in enumerate(bits):
+        yield
+        copy = copies.remote(sums.at[n], far.at[n], place(bit)[1])
+        yield
+        copy.wait_recv()
+        sums[n + 1] = sums[n] + far[n]
+
+
+def run_flows(flows, step):
+    events = []
+    for delay, flow in flows:
+        next(flow)
+        events.append([delay, len(events), flow])
+    while events:
+        events.sort(key=lambda e: e[:2])
+        event = events[0]
+        try:
+            next(event[2])
+            event[0] += step
+        except StopIteration:
+            events.pop(0)
+
+
+def rotate(items, count):
+    count %= len(items)
+    return items[count:] + items[:count]
+
+
+def sum_kernel(
+    dp, seq, core, down, up, out, two, one, bias, heads, down_sum, up_sum, out_sum, totals,
+    work, near, far, full, sums, sums_far, send, recv, local,
+):
+    greet(dp + seq + [core])
+    copies = Copies(send, recv, local)
+    side_of = place(core)[0]
+    count, half, width = down.shape[1:]
+    pieces = [(up.at[side_of, p], up.at[1 - side_of, p], up_sum.at[p]) for p in range(count)]
+    pieces += [
+        (
+            down.at[side_of, p],
+            down.at[1 - side_of, p],
+            down_sum.at[:, pl.ds(p * width, width)],
+        )
+        for p in range(count)
+    ]
+    pieces.append((out.at[side_of], out.at[1 - side_of], out_sum))
+    first = dp + seq[:1]
+    flows = []
+    for n, (own, other, result) in enumerate(pieces):
+        bits = rotate(first, n) + seq[1:]
+        flow = sum_flow(
+            copies, own, other, work.at[n], near.at[n], far.at[n], full.at[n], result, core, bits
+        )
+        flows.append((n // len(first), flow))
+    sums[0] = jnp.zeros(sums.shape[1:], F32)
+    sums[0, 0:1] = heads[0, 0:1]
+    sums[0, 1:2] = heads[2, 0:1]
+    sums[0, 2:3] = one[2:3]
+    sums[0, 3:4] = two[2:3]
+    sums[0, 4:5] = one[0:1]
+    sums[0, 5:6] = two[0:1]
+    sums[0, 6:7] = one[1:2]
+    sums[0, 7:8] = two[1:2]
+    for p in range(count):
+        sums[0, 8 + p : 9 + p] = bias[:, p * width : (p + 1) * width]
+    flows.append((0.5, vector_flow(copies, sums, sums_far, [core] + dp + seq)))
+    run_flows(flows, 1.5)
+    totals[...] = sums[sums.shape[0] - 1]
+    copies.finish()
+
+
+def remote_call(kernel, args, in_specs, outs, out_specs, scratch, copies, local, number):
+    sems = pltpu.SemaphoreType.DMA
+    return pl.pallas_call(
+        kernel,
+        in_specs=in_specs,
+        out_specs=out_specs,
+        out_shape=outs,
+        scratch_shapes=scratch + [sems((copies,)), sems((copies,)), sems((local,))],
+        compiler_params=pltpu.CompilerParams(
+            vmem_limit_bytes=VMEM_LIMIT, collective_id=number, has_side_effects=True
+        ),
+        cost_estimate=pl.CostEstimate(flops=5 * 10**10, bytes_accessed=10**8, transcendentals=0),
+    )(*args)
+
+
+ANY = pl.BlockSpec(memory_space=pl.ANY)
+IN_VMEM = pl.BlockSpec(memory_space=pltpu.VMEM)
+
+
+def sum_grads(dp, seq, core, down, up, out, two, one, bias, heads):
+    sides, count, half, width = down.shape
+    pieces, steps = 2 * count + 1, len(dp) + len(seq)
+    lines = 16
+    return remote_call(
+        lambda *refs: sum_kernel(dp, seq, core, *refs),
+        [down, up, out, two, one, bias, heads],
+        [ANY] * 3 + [IN_VMEM] * 4,
+        [
+            shape_of((half, count * width), BF),
+            shape_of((count, half, width), BF),
+            shape_of((half, width), BF),
+            shape_of((lines, width), F32),
+        ],
+        [ANY] * 3 + [IN_VMEM],
+        [pltpu.VMEM((pieces, half, width), BF)] * 4
+        + [pltpu.VMEM((steps + 2, lines, width), F32), pltpu.VMEM((steps + 1, lines, width), F32)],
+        pieces * (1 + 2 * steps) + steps + 1,
+        2 * pieces,
+        1,
+    )
+
+
+def head_sum_kernel(dp, seq, core, heads, result, work, far, full, send, recv, local):
+    greet(dp + seq + [core])
+    copies = Copies(send, recv, local)
+    side_of, partner = place(core)
+    along = place(seq[0])[0]
+    rows = dp + seq[1:]
+
+    def flow(n):
+        if n == 1:
+            copy = copies.remote(heads.at[2 - 2 * side_of], work.at[n], partner)
+            yield
+            copy.wait_recv()
+        else:
+            load = copies.local(heads.at[n // 2 + side_of], work.at[n])
+            yield
+            load.wait()
+        bits = (rotate(dp, n) if n < 2 else dp) + seq[1:]
+        mine = full.at[2 * n + along]
+        parts = yield from scatter_sum(copies, work.at[n], far.at[n], mine, bits)
+        steps = [(bit, kept, False) for bit, kept in reversed(parts)]
+        cut = len(steps) if n == 2 else 1
+        held = steps[cut][1] if n < 2 else (0, mine.shape[0], 0, mine.shape[1])
+        steps = steps[:cut] + [(seq[0], held, False)] + [(b, k, True) for b, k, _ in steps[cut:]]
+        for bit, (row, size, col, cols), both in steps:
+            first, count = (2 * n, 2) if both else (2 * n + along, 1)
+            part = full.at[pl.ds(first, count), pl.ds(row, size), pl.ds(col, cols)]
+            copy = copies.remote(part, part, place(bit)[1])
+            yield
+            copy.wait_recv()
+        store = copies.local(full.at[pl.ds(2 * n, 2)], result.at[pl.ds(2 * n, 2)])
+        yield
+        store.wait()
+
+    run_flows([(0, flow(0)), (0, flow(2)), (0, flow(1))], 1.0)
+    copies.finish()
+
+
+def head_sums_of(dp, seq, core, heads):
+    _, rows, width = heads.shape
+    steps = len(dp) + len(seq) - 1
+    return remote_call(
+        lambda *refs: head_sum_kernel(dp, seq, core, *refs),
+        [heads],
+        [ANY],
+        shape_of((6, rows, width), BF),
+        ANY,
+        [pltpu.VMEM((3, rows, width), BF)] * 2 + [pltpu.VMEM((6, rows, width), BF)],
+        3 * (2 * steps + 1) + 1,
+        5,
+        2,
+    )
+
+
 def binarize(latent):
     row_scale = jnp.mean(jnp.abs(latent), axis=1, keepdims=True)
     return (row_scale * jnp.sign(latent)).astype(BF)
@@ -776,56 +1066,74 @@
         pref, grad_ffn, gelu, grad_hidden, act_one, grad_attn, ctx
     )
     dp_bits, seq_bits, fsdp_bits = bit_list("dp"), bit_list("seq"), bit_list("fsdp")
-
-    def reduce_grad(value, bits):
-        for bit in reversed(fsdp_bits):
-            value = halve(value, bit)
-        return all_reduce(value, bits).astype(F32)
-
-    total_down = reduce_grad(grad_down, dp_bits + seq_bits)
-    total_up = reduce_grad(grad_up, dp_bits[::-1] + seq_bits)
-    total_out = reduce_grad(grad_out, seq_bits[:1] + dp_bits + seq_bits[1:])
-
     dqkv_slots = attention_back(pref, qkv, gctx_pieces, ctx_full, lse)
     dqkv_pieces = exchange(dqkv_slots)
     grad_heads, head_sums = qkv_grad(pref, dqkv_slots, x_slots)
-    hidden_grad = swap_groups(input_grad(pref, dqkv_pieces, bin_qkv, grad_res, x))
-
-    rows = width // 4
-    blocks = all_reduce(grad_heads.reshape(3 * rows, width), dp_bits + seq_bits[1:] + fsdp_bits[1:])
-    blocks = blocks.reshape(1, 3, rows, width)
-    blocks = double(double(blocks, seq_bits[0]), fsdp_bits[0])
-    whole_qkv = blocks.transpose(1, 0, 2, 3).reshape(3 * width, width)
-    part = 3 * width // fsdp
-    total_qkv = lax.dynamic_slice_in_dim(whole_qkv, fsdp_at * part, part, 0).astype(F32)
-
-    placed = jnp.zeros((2, 4, rows), F32)
-    placed = lax.dynamic_update_slice(
-        placed, head_sums.reshape(3, 1, rows)[0::2], (0, own, 0)
-    ).reshape(2, width)
-    vectors = jnp.concatenate(
-        [
-            placed,
-            vec_one[2:3],
-            vec_two[2:3],
-            vec_one[0:1],
-            vec_two[0:1],
-            vec_one[1:2],
-            vec_two[1:2],
-            grad_up_bias.reshape(-1, width),
-        ]
-    )
-    vectors = sum_small(vectors, dp_bits + seq_bits + fsdp_bits)
-    hid_bias = vectors[8:].reshape(-1)
+    rows, hidden_units = width // 4, up_bias.shape[0]
+    _, count, half, _ = grad_down.shape
+
+    if fsdp == 2:
+        total_down, total_up, total_out, vectors = sum_grads(
+            dp_bits,
+            seq_bits,
+            fsdp_bits[0],
+            grad_down,
+            grad_up.reshape(grad_down.shape),
+            grad_out,
+            vec_two,
+            vec_one,
+            grad_up_bias,
+            head_sums,
+        )
+        total_up = total_up.reshape(-1, width)
+        hidden_grad = swap_groups(input_grad(pref, dqkv_pieces, bin_qkv, grad_res, x))
+        total_qkv = head_sums_of(dp_bits, seq_bits, fsdp_bits[0], grad_heads).reshape(-1, width)
+    else:
+        hidden_grad = swap_groups(input_grad(pref, dqkv_pieces, bin_qkv, grad_res, x))
+
+        def reduce_grad(value, bits):
+            for bit in reversed(fsdp_bits):
+                value = halve(value, bit)
+            return all_reduce(value, bits)
+
+        grad_down = grad_down.transpose(0, 2, 1, 3).reshape(width, hidden_units)
+        total_down = reduce_grad(grad_down, dp_bits + seq_bits)
+        total_up = reduce_grad(grad_up.reshape(hidden_units, width), dp_bits[::-1] + seq_bits)
+        total_out = reduce_grad(
+            grad_out.reshape(width, width), seq_bits[:1] + dp_bits + seq_bits[1:]
+        )
+        blocks = all_reduce(
+            grad_heads.reshape(3 * rows, width), dp_bits + seq_bits[1:] + fsdp_bits[1:]
+        )
+        blocks = blocks.reshape(1, 3, rows, width)
+        blocks = double(double(blocks, seq_bits[0]), fsdp_bits[0])
+        whole_qkv = blocks.transpose(1, 0, 2, 3).reshape(3 * width, width)
+        part = 3 * width // fsdp
+        total_qkv = lax.dynamic_slice_in_dim(whole_qkv, fsdp_at * part, part, 0)
+        vectors = jnp.concatenate(
+            [
+                head_sums[0, :1],
+                head_sums[2, :1],
+                vec_one[2:3],
+                vec_two[2:3],
+                vec_one[0:1],
+                vec_two[0:1],
+                vec_one[1:2],
+                vec_two[1:2],
+                grad_up_bias.reshape(-1, width),
+            ]
+        )
+        vectors = sum_small(vectors, dp_bits + seq_bits + fsdp_bits)
+    hid_bias = vectors[8 : 8 + hidden_units // width].reshape(-1)
     share, hid_share = width // fsdp, hid_bias.shape[0] // fsdp
     cols = lax.dynamic_slice_in_dim(vectors[:8], fsdp_at * share, share, 1)
     return (
         student_out[None],
         hidden_grad[None],
-        total_qkv,
-        total_out,
-        total_up,
-        total_down,
+        total_qkv.astype(F32),
+        total_out.astype(F32),
+        total_up.astype(F32),
+        total_down.astype(F32),
         cols[0:4],
         lax.dynamic_slice_in_dim(hid_bias, fsdp_at * hid_share, hid_share, 0),
         cols[4:6],

time: 578 us -> 511 us (0.88)
  the two profiles are of different devices: /device:TPU:24 before, /device:TPU:1 now
where the time goes in v2:
time: 511 us; the launch traced here: 504 us
  Pallas kernels  327 us (64%)
  waiting for transfers between devices  63.6 us (12%)
  other arithmetic  58.3 us (11%)
  starting transfers between devices  34.9 us (7%)
  local copies, waits for them, and re-layouts  13.6 us (3%)
  between operations  6.63 us (1%)
    pallas_call x11, Pallas kernels, call(): pl.pallas_call(kernel, grid_spec=pltpu.PrefetchScalarGridSpec(num_scalar_...  181 us
    pallas_call x2, Pallas kernels, remote_call(): pl.pallas_call(kernel, in_specs=in_specs, out_specs=out_specs, out_shape=...  147 us
    ppermute x31, waiting for transfers between devices, permute(): return lax.ppermute(values, AXES, pairs)  63.6 us
    select_n x8, other arithmetic, double(): jnp.where(side(bit), jnp.concatenate([got, values], axis=0), jnp.concaten...  37.1 us
    ppermute x31, starting transfers between devices, permute(): return lax.ppermute(values, AXES, pairs)  34.9 us
  transfers between devices with their start and end apart: 31, of which 5 were waited for; matrix products, arithmetic and copies ran while one was open for 12% of the time, Pallas kernels for 58%

profile of v2, /device:TPU:1, one launch (start us, length us, event | category | flops | bytes accessed | tf_op | source)
XLA Modules:
  0.0 504.3 jit_solution(8103333757071471534)
XLA Ops:
  0.7 1.6 fusion.2
  7.5 2.5 abs_reduce_fusion.2
  10.0 2.2 multiply_convert_fusion.2
  12.7 5.6 %collective-permute-start.1 = (bf16[640,768]{1,0:T(8,128)(2,1)}, bf16[640,768]{1,0:T(8,128)(2,1)S(1)}, u32[]{:S(2)}, u32[]{:S(2)}) collective-permute-start(bf16[640,768]{1,0:T(8,128)(2,1)} %bitcast.22), channel_id=1, source_target_pairs={{0,0},{1,4},{2,2},{3,6},{4,1},{5,5},{6,3},{7,7},{8,8},{9,12},{10,1... | collective-permute-start | bytes 2949128 | tf_op jit(solution)/shard_map/ppermute | solution.py:47
  19.9 1.3 multiply_convert_fusion.1
  22.3 2.2 collective-permute-start.13
  24.5 2.8 multiply_convert_fusion
  27.3 24.1 %collective-permute-done.1.refs_1_.x.x0 = bf16[640,768]{1,0:T(8,128)(2,1)S(1)} collective-permute-done((bf16[640,768]{1,0:T(8,128)(2,1)}, bf16[640,768]{1,0:T(8,128)(2,1)S(1)}, u32[]{:S(2)}, u32[]{:S(2)}) %collective-permute-start.1) | collective-permute-done | bytes 983072 | tf_op jit(solution)/shard_map/ppermute | solution.py:47
  51.4 1.2 copy.25.refs_8_
  53.2 8.8 %collective-permute-done.13.refs_1_.x = bf16[640,768]{1,0:T(8,128)(2,1)} collective-permute-done((bf16[640,768]{1,0:T(8,128)(2,1)}, bf16[640,768]{1,0:T(8,128)(2,1)}, u32[]{:S(2)}, u32[]{:S(2)}) %collective-permute-start.13) | collective-permute-done | bytes 983072 | tf_op jit(solution)/shard_map/ppermute | solution.py:47
  62.7 3.0 maximum_select_fusion.6.w_out
  65.6 3.0 maximum_select_fusion.7.w_out
  69.6 5.1 %maximum_select_fusion.4.refs_5_.refs_6_.refs_7_.wq.wk.wv = bf16[2304,768]{1,0:T(8,128)(2,1)} fusion(bf16[1152,768]{1,0:T(8,128)(2,1)} %multiply_convert_fusion.2, bf16[1152,768]{1,0:T(8,128)(2,1)} %collective-permute-done.5, pred[]{:T(512)S(6)} %ne.29), kind=kLoop, calls=%fused_computation.8 | loop fusion | flops 15925248 | bytes 7077889 | tf_op jit(solution)/shard_map/jit(_where)/select_n | solution.py:92
  74.7 1.0 collective-permute-start.14
  75.7 4.8 maximum_select_fusion.5.refs_5_.refs_6_.refs_7_
  80.5 6.0 %maximum_select_fusion.w_up = bf16[3072,768]{1,0:T(8,128)(2,1)} fusion(bf16[1536,768]{1,0:T(8,128)(2,1)S(1)} %multiply_convert_fusion.1, bf16[1536,768]{1,0:T(8,128)(2,1)} %collective-permute-done.10, pred[]{:T(512)S(6)} %ne.29), kind=kLoop, calls=%fused_computation | loop fusion | flops 21233664 | bytes 9437185 | tf_op jit(solution)/shard_map/jit(_where)/select_n | solution.py:92
  86.5 5.9 %collective-permute-done.2.refs_2_.x1 = bf16[640,768]{1,0:T(8,128)(2,1)S(1)} collective-permute-done((bf16[640,768]{1,0:T(8,128)(2,1)S(1)}, bf16[640,768]{1,0:T(8,128)(2,1)S(1)}, u32[]{:S(2)}, u32[]{:S(2)}) %collective-permute-start.2) | collective-permute-done | bytes 983072 | tf_op jit(solution)/shard_map/ppermute | solution.py:47
  92.4 1.5 collective-permute-start.3
  94.0 7.7 %maximum_select_fusion.1.w_down = bf16[768,3072]{1,0:T(8,128)(2,1)} fusion(bf16[384,3072]{1,0:T(8,128)(2,1)} %multiply_convert_fusion, bf16[384,3072]{1,0:T(8,128)(2,1)} %collective-permute-done.11, pred[]{:T(512)S(6)} %ne.29), kind=kLoop, calls=%fused_computation.1 | loop fusion | flops 21233664 | bytes 9437185 | tf_op jit(solution)/shard_map/jit(_where)/select_n | solution.py:92
  101.7 11.8 %collective-permute-done.14.refs_2_ = bf16[640,768]{1,0:T(8,128)(2,1)S(1)} collective-permute-done((bf16[640,768]{1,0:T(8,128)(2,1)}, bf16[640,768]{1,0:T(8,128)(2,1)S(1)}, u32[]{:S(2)}, u32[]{:S(2)}) %collective-permute-start.14) | collective-permute-done | bytes 983072 | tf_op jit(solution)/shard_map/ppermute | solution.py:47
  114.5 3.3 maximum_select_fusion.2.w_up
  117.8 4.2 maximum_select_fusion.3.w_down
  123.0 8.7 %shard_map.222.refs_1_.refs_2_.refs_3_ = bf16[576,2560]{1,0:T(8,128)(2,1)} custom-call(s32[3]{0:T(128)} %pad_add_fusion.1.refs_0_.pref, bf16[640,768]{1,0:T(8,128)(2,1)} %copy-done.2, bf16[640,768]{1,0:T(8,128)(2,1)} %copy-done.12, bf16[640,768]{1,0:T(8,128)(2,1)} %copy-done.13, bf16[640,768]{1,0:T(8,128)(2,1)} %collective-permute-done.4.refs_4_.x3, ...), custom_call_target="tpu_custom_call" | custom-call | flops 2264924160 | bytes 17504256 | tf_op jit(solution)/shard_map/pallas_call | solution.py:126
  131.6 21.3 %shard_map.223 = (bf16[192,640]{1,0:T(8,128)(2,1)}, bf16[192,640]{1,0:T(8,128)(2,1)}, bf16[192,640]{1,0:T(8,128)(2,1)}, bf16[192,640]{1,0:T(8,128)(2,1)}, f32[192,2560]{1,0:T(8,128)}, /*index=5*/f32[3,1,2560]{2,1,0:T(1,128)}) custom-call(s32[3]{0:T(128)} %pad_add_fusion.1.refs_0_.pref, bf16[576,2560]{1,0:T(8,128)(2,1)} %shard_map.222.refs_1_.refs_2_.refs_3_, ...), custom_call_target="tpu_custom_call" | custom-call | flops 16000000000 | bytes 11827200 | tf_op jit(solution)/shard_map/pallas_call | solution.py:126
  156.0 1.0 copy-done.11
  156.9 8.4 %shard_map.225.refs_1_.refs_2_.refs_3_ = bf16[576,2560]{1,0:T(8,128)(2,1)} custom-call(s32[3]{0:T(128)} %pad_add_fusion.1.refs_0_.pref, bf16[640,768]{1,0:T(8,128)(2,1)} %collective-permute-done.13.refs_1_.x, bf16[640,768]{1,0:T(8,128)(2,1)} %copy-done.9, bf16[640,768]{1,0:T(8,128)(2,1)} %copy-done.10, bf16[640,768]{1,0:T(8,128)(2,1)} %copy-done.11, ...), custom_call_target="tpu_custom_call" | custom-call | flops 2264924160 | bytes 17498112 | tf_op jit(solution)/shard_map/pallas_call | solution.py:126
  165.4 21.4 %shard_map.226 = (bf16[192,640]{1,0:T(8,128)(2,1)}, bf16[192,640]{1,0:T(8,128)(2,1)}, bf16[192,640]{1,0:T(8,128)(2,1)}, bf16[192,640]{1,0:T(8,128)(2,1)}, f32[192,2560]{1,0:T(8,128)}, /*index=5*/f32[3,1,2560]{2,1,0:T(1,128)}) custom-call(s32[3]{0:T(128)} %pad_add_fusion.1.refs_0_.pref, bf16[576,2560]{1,0:T(8,128)(2,1)} %shard_map.225.refs_1_.refs_2_.refs_3_, ...), custom_call_target="tpu_custom_call" | custom-call | flops 16000000000 | bytes 11827200 | tf_op jit(solution)/shard_map/pallas_call | solution.py:126
  188.1 1.0 collective-permute-start.20
  189.9 19.7 %shard_map.224 = (bf16[768,640]{1,0:T(8,128)(2,1)}, bf16[640,768]{1,0:T(8,128)(2,1)}, f32[640,768]{1,0:T(8,128)}, f32[640,1]{1,0:T(8,128)}, bf16[640,3072]{1,0:T...) custom-call(s32[3]{0:T(128)} %pad_add_fusion.1.refs_0_.pref, ...), custom_call_target="tpu_custom_call" | custom-call | flops 6794772480 | bytes 27364352 | tf_op jit(solution)/shard_map/pallas_call | solution.py:126
  210.5 17.3 %shard_map.227 = (f32[640,768]{1,0:T(8,128)}, bf16[640,768]{1,0:T(8,128)(2,1)}, f32[3,768]{1,0:T(4,128)}) custom-call(s32[3]{0:T(128)} %pad_add_fusion.1.refs_0_.pref, bf16[192,640]{1,0:T(8,128)(2,1)} %get-tuple-element.59.c0, bf16[192,640]{1,0:T(8,128)(2,1)} %copy-done.26, bf16[192,640]{1,0:T(8,128)(2,1)} %copy-done.27, bf16[192,640]{1,0:T(8,128)(2,1)} %copy-done.28, ...), custom_call_target="tpu_custom_call" | custom-call | flops 6794772480 | bytes 17522176 | tf_op jit(solution)/shard_map/pallas_call | solution.py:126
  227.8 18.3 %shard_map.228 = (bf16[640,3072]{1,0:T(8,128)(2,1)}, f32[1,3072]{1,0:T(1,128)}, f32[640,768]{1,0:T(8,128)}, bf16[640,768]{1,0:T(8,128)(2,1)}, bf16[192,640]{1,0:...) custom-call(s32[3]{0:T(128)} %pad_add_fusion.1.refs_0_.pref, ...), custom_call_target="tpu_custom_call" | custom-call | flops 6794772480 | bytes 27364864 | tf_op jit(solution)/shard_map/pallas_call | solution.py:126
  248.3 4.3 collective-permute-start.12
  252.6 15.1 %shard_map.233 = (bf16[2,4,384,768]{3,2,1,0:T(8,128)(2,1)}, bf16[8,384,768]{2,1,0:T(8,128)(2,1)}, bf16[2,384,768]{2,1,0:T(8,128)(2,1)}) custom-call(s32[3]{0:T(128)} %pad_add_fusion.1.refs_0_.pref, bf16[640,768]{1,0:T(8,128)(2,1)} %get-tuple-element.65.grad_ffn, bf16[640,3072]{1,0:T(8,128)(2,1)} %get-tuple-element.82.gelu, ...), custom_call_target="tpu_custom_call" | custom-call | flops 6794772480 | bytes 22413312 | tf_op jit(solution)/shard_map/pallas_call | solution.py:126
  268.6 32.9 %shard_map.229 = (bf16[3,192,640]{2,1,0:T(8,128)(2,1)}, bf16[3,192,640]{2,1,0:T(8,128)(2,1)}, bf16[3,192,640]{2,1,0:T(8,128)(2,1)}, bf16[3,192,640]{2,1,0:T(8,128)(2,1)}) custom-call(s32[3]{0:T(128)} %pad_add_fusion.1.refs_0_.pref, bf16[576,2560]{1,0:T(8,128)(2,1)} %shard_map.222.refs_1_.refs_2_.refs_3_, ...), custom_call_target="tpu_custom_call" | custom-call | flops 30000001024 | bytes 14776320 | tf_op jit(solution)/shard_map/pallas_call | solution.py:126
  301.5 1.5 collective-permute-start.27
  303.0 4.3 collective-permute-start.28
  307.3 1.0 collective-permute-start.29
  308.3 8.2 %shard_map.231 = (bf16[3,192,768]{2,1,0:T(8,128)(2,1)}, f32[3,8,768]{2,1,0:T(8,128)}) custom-call(s32[3]{0:T(128)} %pad_add_fusion.1.refs_0_.pref, bf16[3,192,640]{2,1,0:T(8,128)(2,1)} %get-tuple-element.76.e0.d0, bf16[3,192,640]{2,1,0:T(8,128)(2,1)} %get-tuple-element.77.d1, bf16[3,192,640]{2,1,0:T(8,128)(2,1)} %get-tuple-element.78.d2, ...), custom_call_target="tpu_custom_call" | custom-call | flops 2264924160 | bytes 7839744 | tf_op jit(solution)/shard_map/pallas_call | solution.py:126
  316.5 39.6 %shard_map.232 = bf16[6,192,768]{2,1,0:T(8,128)(2,1)} custom-call(bf16[3,192,768]{2,1,0:T(8,128)(2,1)} %get-tuple-element.81.refs_0_), custom_call_target="tpu_custom_call" | custom-call | flops 49999998976 | bytes 100000000 | tf_op jit(solution)/shard_map/pallas_call | solution.py:900
  356.1 106.9 %shard_map.234 = (bf16[384,3072]{1,0:T(8,128)(2,1)}, bf16[4,384,768]{2,1,0:T(8,128)(2,1)}, bf16[384,768]{1,0:T(8,128)(2,1)}, f32[16,768]{1,0:T(8,128)}) custom-call(bf16[2,4,384,768]{3,2,1,0:T(8,128)(2,1)} %get-tuple-element.87.refs_0_, bf16[2,4,384,768]{3,2,1,0:T(8,128)(2,1)} %bitcast.24, bf16[2,384,768]{2,1,0:T(8,128)(2,1)} %get-tuple-element.89.refs_2_, ...), custom_call_target="tpu_custom_call" | custom-call | flops 49999998976 | bytes 100000000 | tf_op jit(solution)/shard_map/pallas_call | solution.py:900
  464.4 9.4 %shard_map.230 = bf16[640,768]{1,0:T(8,128)(2,1)} custom-call(s32[3]{0:T(128)} %pad_add_fusion.1.refs_0_.pref, bf16[3,192,640]{2,1,0:T(8,128)(2,1)} %get-tuple-element.76.e0.d0, bf16[3,192,640]{2,1,0:T(8,128)(2,1)} %copy-done.14, bf16[3,192,640]{2,1,0:T(8,128)(2,1)} %copy-done.15, bf16[3,192,640]{2,1,0:T(8,128)(2,1)} %copy-done.16, ...), custom_call_target="tpu_custom_call" | custom-call | flops 2264924160 | bytes 17498112 | tf_op jit(solution)/shard_map/pallas_call | solution.py:126
  473.8 3.2 collective-permute-start.30
  477.1 2.7 bitcast_convert_fusion
  479.8 2.8 convert_element_type.51
  482.6 1.1 convert_element_type.48
  485.6 2.2 bitcast_convert_fusion.1
  487.8 13.1 %collective-permute-done.30 = bf16[640,768]{1,0:T(8,128)(2,1)S(1)} collective-permute-done((bf16[640,768]{1,0:T(8,128)(2,1)}, bf16[640,768]{1,0:T(8,128)(2,1)S(1)}, u32[]{:S(2)}, u32[]{:S(2)}) %collective-permute-start.30) | collective-permute-done | bytes 983072 | tf_op jit(solution)/shard_map/ppermute | solution.py:47
  500.8 2.2 copy.28
  (140 shorter events, 20.6 us)
Async XLA Ops:
  0.6 9.4 %copy-start = (f32[1152,768]{1,0:T(8,128)S(1)}, f32[1152,768]{1,0:T(8,128)}, u32[]{:S(2)}) copy-start(f32[1152,768]{1,0:T(8,128)} %param.18) | copy-start | bytes 10616836
  7.5 14.2 %collective-permute-start = (s32[2]{0:T(128)S(1)}, s32[2]{0:T(128)S(1)}, u32[]{:S(2)}, u32[]{:S(2)}) collective-permute-start(s32[2]{0:T(128)S(1)} %pad_add_fusion), channel_id=1, source_target_pairs={{0,1},{1,0},{2,3},{3,2},{4,5},{5,4},{6,7},{7,6},{8,9},{9,8},{10,11... | collective-permute-start | bytes 32 | tf_op jit(solution)/shard_map/ppermute | solution.py:47
  7.5 12.0 %slice-start = ((s8[4718592]{0:T(1024)(128)(4,1)}), s8[4194304]{0:T(1024)(128)(4,1)S(1)}, s32[]{:S(2)}) async-start(s8[4718592]{0:T(1024)(128)(4,1)} %bitcast.17), calls=%async_computation | async-start | bytes 8388608
  10.0 8.3 %copy-start.1 = (f32[384,768]{1,0:T(8,128)S(1)}, f32[384,768]{1,0:T(8,128)}, u32[]{:S(2)}) copy-start(f32[384,768]{1,0:T(8,128)} %param.19) | copy-start | bytes 3538948
  10.0 8.9 %copy-start.17 = (bf16[384,768]{1,0:T(8,128)(2,1)S(1)}, bf16[384,768]{1,0:T(8,128)(2,1)}, u32[]{:S(2)}) copy-start(bf16[384,768]{1,0:T(8,128)(2,1)} %param.27) | copy-start | bytes 1769476
  10.0 9.4 %slice-start.1 = ((s8[4718592]{0:T(1024)(128)(4,1)}), s8[524288]{0:T(1024)(128)(4,1)S(1)}, s32[]{:S(2)}) async-start(s8[4718592]{0:T(1024)(128)(4,1)} %bitcast.17), calls=%async_computation.1 | async-start | bytes 1048576
  12.2 56.4 %collective-permute-start.5 = (bf16[1152,768]{1,0:T(8,128)(2,1)}, bf16[1152,768]{1,0:T(8,128)(2,1)}, u32[]{:S(2)}, u32[]{:S(2)}) collective-permute-start(bf16[1152,768]{1,0:T(8,128)(2,1)} %multiply_convert_fusion.2), channel_id=1, source_target_pairs={{0,1},{1,0},{2,3},{3,2},{4,5},{5,4},{6,7},{7,6},{8,9},{9,8},{10,11... | collective-permute-start | bytes 5308424 | tf_op jit(solution)/shard_map/ppermute | solution.py:47
  12.7 38.6 %collective-permute-start.1 = (bf16[640,768]{1,0:T(8,128)(2,1)}, bf16[640,768]{1,0:T(8,128)(2,1)S(1)}, u32[]{:S(2)}, u32[]{:S(2)}) collective-permute-start(bf16[640,768]{1,0:T(8,128)(2,1)} %bitcast.22), channel_id=1, source_target_pairs={{0,0},{1,4},{2,2},{3,6},{4,1},{5,5},{6,3},{7,7},{8,8},{9,12},{10,1... | collective-permute-start | bytes 2949128 | tf_op jit(solution)/shard_map/ppermute | solution.py:47
  18.3 2.9 slice-start.2
  18.9 3.0 collective-permute-start.9
  19.0 3.3 collective-permute-start.21
  21.7 53.0 %collective-permute-start.10 = (bf16[1536,768]{1,0:T(8,128)(2,1)S(1)}, bf16[1536,768]{1,0:T(8,128)(2,1)}, u32[]{:S(2)}, u32[]{:S(2)}) collective-permute-start(bf16[1536,768]{1,0:T(8,128)(2,1)S(1)} %multiply_convert_fusion.1), channel_id=1, source_target_pairs={{0,1},{1,0},{2,3},{3,2},{4,5},{5,4},{6,7},{7,6},{8,9},{9,8},{10,11... | collective-permute-start | bytes 7077896 | tf_op jit(solution)/shard_map/ppermute | solution.py:47
  21.8 5.5 %copy-start.18 = (bf16[384,768]{1,0:T(8,128)(2,1)}, bf16[384,768]{1,0:T(8,128)(2,1)S(1)}, u32[]{:S(2)}) copy-start(bf16[384,768]{1,0:T(8,128)(2,1)S(1)} %collective-permute-done.9) | copy-start | bytes 1769476
  21.8 47.3 %collective-permute-start.17 = (bf16[1152,768]{1,0:T(8,128)(2,1)}, bf16[1152,768]{1,0:T(8,128)(2,1)}, u32[]{:S(2)}, u32[]{:S(2)}) collective-permute-start(bf16[1152,768]{1,0:T(8,128)(2,1)} %param.26), channel_id=1, source_target_pairs={{0,1},{1,0},{2,3},{3,2},{4,5},{5,4},{6,7},{7,6},{8,9},{9,8},{10,11... | collective-permute-start | bytes 5308424 | tf_op jit(solution)/shard_map/ppermute | solution.py:47
  22.3 5.0 copy-start.19
  22.3 29.1 %copy-start.22 = (f32[4,768]{1,0:T(4,128)S(1)}, f32[4,768]{1,0:T(4,128)}, u32[]{:S(2)}) copy-start(f32[4,768]{1,0:T(4,128)} %param.22) | copy-start | bytes 36868
  22.3 39.7 %collective-permute-start.13 = (bf16[640,768]{1,0:T(8,128)(2,1)}, bf16[640,768]{1,0:T(8,128)(2,1)}, u32[]{:S(2)}, u32[]{:S(2)}) collective-permute-start(bf16[640,768]{1,0:T(8,128)(2,1)} %bitcast.7), channel_id=1, source_target_pairs={{0,0},{1,4},{2,2},{3,6},{4,1},{5,5},{6,3},{7,7},{8,8},{9,12},{10,1... | collective-permute-start | bytes 2949128 | tf_op jit(solution)/shard_map/ppermute | solution.py:47
  51.3 41.0 %copy-start.2 = (bf16[640,768]{1,0:T(8,128)(2,1)}, bf16[640,768]{1,0:T(8,128)(2,1)S(1)}, u32[]{:S(2)}) copy-start(bf16[640,768]{1,0:T(8,128)(2,1)S(1)} %collective-permute-done.1.refs_1_.x.x0) | copy-start | bytes 2949124
  51.4 42.5 %collective-permute-start.11 = (bf16[384,3072]{1,0:T(8,128)(2,1)}, bf16[384,3072]{1,0:T(8,128)(2,1)}, u32[]{:S(2)}, u32[]{:S(2)}) collective-permute-start(bf16[384,3072]{1,0:T(8,128)(2,1)} %multiply_convert_fusion), channel_id=1, source_target_pairs={{0,1},{1,0},{2,3},{3,2},{4,5},{5,4},{6,7},{7,6},{8,9},{9,8},{10,11... | collective-permute-start | bytes 7077896 | tf_op jit(solution)/shard_map/ppermute | solution.py:47
  52.6 16.0 %copy-start.7 = (bf16[384,3072]{1,0:T(8,128)(2,1)S(1)}, bf16[384,3072]{1,0:T(8,128)(2,1)}, u32[]{:S(2)}) copy-start(bf16[384,3072]{1,0:T(8,128)(2,1)} %param.29) | copy-start | bytes 7077892
  62.0 52.4 %collective-permute-start.22 = (bf16[1536,768]{1,0:T(8,128)(2,1)}, bf16[1536,768]{1,0:T(8,128)(2,1)S(1)}, u32[]{:S(2)}, u32[]{:S(2)}) collective-permute-start(bf16[1536,768]{1,0:T(8,128)(2,1)} %param.28), channel_id=1, source_target_pairs={{0,1},{1,0},{2,3},{3,2},{4,5},{5,4},{6,7},{7,6},{8,9},{9,8},{10,11... | collective-permute-start | bytes 7077896 | tf_op jit(solution)/shard_map/ppermute | solution.py:47
  68.6 49.2 %collective-permute-start.23 = (bf16[384,3072]{1,0:T(8,128)(2,1)S(1)}, bf16[384,3072]{1,0:T(8,128)(2,1)S(1)}, u32[]{:S(2)}, u32[]{:S(2)}) collective-permute-start(bf16[384,3072]{1,0:T(8,128)(2,1)S(1)} %copy-done.7), channel_id=1, source_target_pairs={{0,1},{1,0},{2,3},{3,2},{4,5},{5,4},{6,7},{7,6},{8,9},{9,8},{10,11... | collective-permute-start | bytes 7077896 | tf_op jit(solution)/shard_map/ppermute | solution.py:47
  69.2 23.2 %collective-permute-start.2 = (bf16[640,768]{1,0:T(8,128)(2,1)S(1)}, bf16[640,768]{1,0:T(8,128)(2,1)S(1)}, u32[]{:S(2)}, u32[]{:S(2)}) collective-permute-start(bf16[640,768]{1,0:T(8,128)(2,1)S(1)} %collective-permute-done.1.refs_1_.x.x0), channel_id=1, source_target_pairs={{0,2},{1,3},{2,0},{3,1},{4,6},{5,7},{6,4},{7,5},{8,10},{9,11},{10,... | collective-permute-start | bytes 2949128 | tf_op jit(solution)/shard_map/ppermute | solution.py:47
  74.7 38.8 %collective-permute-start.14 = (bf16[640,768]{1,0:T(8,128)(2,1)}, bf16[640,768]{1,0:T(8,128)(2,1)S(1)}, u32[]{:S(2)}, u32[]{:S(2)}) collective-permute-start(bf16[640,768]{1,0:T(8,128)(2,1)} %collective-permute-done.13.refs_1_.x), channel_id=1, source_target_pairs={{0,2},{1,3},{2,0},{3,1},{4,6},{5,7},{6,4},{7,5},{8,10},{9,11},{10,... | collective-permute-start | bytes 2949128 | tf_op jit(solution)/shard_map/ppermute | solution.py:47
  86.5 28.0 %copy-start.6 = (bf16[1536,768]{1,0:T(8,128)(2,1)S(1)}, bf16[1536,768]{1,0:T(8,128)(2,1)}, u32[]{:S(2)}) copy-start(bf16[1536,768]{1,0:T(8,128)(2,1)} %param.28) | copy-start | bytes 7077892
  92.4 9.3 %copy-start.12 = (bf16[640,768]{1,0:T(8,128)(2,1)}, bf16[640,768]{1,0:T(8,128)(2,1)S(1)}, u32[]{:S(2)}) copy-start(bf16[640,768]{1,0:T(8,128)(2,1)S(1)} %collective-permute-done.2.refs_2_.x1) | copy-start | bytes 2949124
  92.4 29.6 %collective-permute-start.3 = (bf16[640,768]{1,0:T(8,128)(2,1)S(1)}, bf16[640,768]{1,0:T(8,128)(2,1)S(1)}, u32[]{:S(2)}, u32[]{:S(2)}) collective-permute-start(bf16[640,768]{1,0:T(8,128)(2,1)S(1)} %collective-permute-done.1.refs_1_.x.x0), channel_id=1, source_target_pairs={{0,1},{1,0},{2,3},{3,2},{4,5},{5,4},{6,7},{7,6},{8,9},{9,8},{10,11... | collective-permute-start | bytes 2949128 | tf_op jit(solution)/shard_map/ppermute | solution.py:47
  93.9 28.1 %collective-permute-start.4 = (bf16[640,768]{1,0:T(8,128)(2,1)S(1)}, bf16[640,768]{1,0:T(8,128)(2,1)}, u32[]{:S(2)}, u32[]{:S(2)}) collective-permute-start(bf16[640,768]{1,0:T(8,128)(2,1)S(1)} %collective-permute-done.2.refs_2_.x1), channel_id=1, source_target_pairs={{0,1},{1,0},{2,3},{3,2},{4,5},{5,4},{6,7},{7,6},{8,9},{9,8},{10,11... | collective-permute-start | bytes 2949128 | tf_op jit(solution)/shard_map/ppermute | solution.py:47
  113.5 4.4 copy-start.9
  113.5 41.5 %collective-permute-start.15 = (bf16[640,768]{1,0:T(8,128)(2,1)}, bf16[640,768]{1,0:T(8,128)(2,1)S(1)}, u32[]{:S(2)}, u32[]{:S(2)}) collective-permute-start(bf16[640,768]{1,0:T(8,128)(2,1)} %collective-permute-done.13.refs_1_.x), channel_id=1, source_target_pairs={{0,1},{1,0},{2,3},{3,2},{4,5},{5,4},{6,7},{7,6},{8,9},{9,8},{10,11... | collective-permute-start | bytes 2949128 | tf_op jit(solution)/shard_map/ppermute | solution.py:47
  114.4 40.6 %collective-permute-start.16 = (bf16[640,768]{1,0:T(8,128)(2,1)S(1)}, bf16[640,768]{1,0:T(8,128)(2,1)S(1)}, u32[]{:S(2)}, u32[]{:S(2)}) collective-permute-start(bf16[640,768]{1,0:T(8,128)(2,1)S(1)} %collective-permute-done.14.refs_2_), channel_id=1, source_target_pairs={{0,1},{1,0},{2,3},{3,2},{4,5},{5,4},{6,7},{7,6},{8,9},{9,8},{10,11... | collective-permute-start | bytes 2949128 | tf_op jit(solution)/shard_map/ppermute | solution.py:47
  152.9 35.1 %collective-permute-start.6 = (bf16[192,640]{1,0:T(8,128)(2,1)}, bf16[192,640]{1,0:T(8,128)(2,1)S(1)}, u32[]{:S(2)}, u32[]{:S(2)}) collective-permute-start(bf16[192,640]{1,0:T(8,128)(2,1)} %get-tuple-element.55), channel_id=1, source_target_pairs={{0,2},{1,3},{2,0},{3,1},{4,6},{5,7},{6,4},{7,5},{8,10},{9,11},{10,... | collective-permute-start | bytes 737288 | tf_op jit(solution)/shard_map/ppermute | solution.py:47
  153.3 35.8 %collective-permute-start.7 = (bf16[192,640]{1,0:T(8,128)(2,1)}, bf16[192,640]{1,0:T(8,128)(2,1)S(1)}, u32[]{:S(2)}, u32[]{:S(2)}) collective-permute-start(bf16[192,640]{1,0:T(8,128)(2,1)} %get-tuple-element.56), channel_id=1, source_target_pairs={{0,1},{1,0},{2,3},{3,2},{4,5},{5,4},{6,7},{7,6},{8,9},{9,8},{10,11... | collective-permute-start | bytes 737288 | tf_op jit(solution)/shard_map/ppermute | solution.py:47
  154.1 35.1 %collective-permute-start.8 = (bf16[192,640]{1,0:T(8,128)(2,1)}, bf16[192,640]{1,0:T(8,128)(2,1)S(1)}, u32[]{:S(2)}, u32[]{:S(2)}) collective-permute-start(bf16[192,640]{1,0:T(8,128)(2,1)} %get-tuple-element.57), channel_id=1, source_target_pairs={{0,3},{1,2},{2,1},{3,0},{4,7},{5,6},{6,5},{7,4},{8,11},{9,10},{10,... | collective-permute-start | bytes 737288 | tf_op jit(solution)/shard_map/ppermute | solution.py:47
  186.8 22.8 %collective-permute-start.18 = (bf16[192,640]{1,0:T(8,128)(2,1)}, bf16[192,640]{1,0:T(8,128)(2,1)S(1)}, u32[]{:S(2)}, u32[]{:S(2)}) collective-permute-start(bf16[192,640]{1,0:T(8,128)(2,1)} %get-tuple-element.60), channel_id=1, source_target_pairs={{0,2},{1,3},{2,0},{3,1},{4,6},{5,7},{6,4},{7,5},{8,10},{9,11},{10,... | collective-permute-start | bytes 737288 | tf_op jit(solution)/shard_map/ppermute | solution.py:47
  187.3 22.3 %collective-permute-start.19 = (bf16[192,640]{1,0:T(8,128)(2,1)}, bf16[192,640]{1,0:T(8,128)(2,1)S(1)}, u32[]{:S(2)}, u32[]{:S(2)}) collective-permute-start(bf16[192,640]{1,0:T(8,128)(2,1)} %get-tuple-element.61), channel_id=1, source_target_pairs={{0,1},{1,0},{2,3},{3,2},{4,5},{5,4},{6,7},{7,6},{8,9},{9,8},{10,11... | collective-permute-start | bytes 737288 | tf_op jit(solution)/shard_map/ppermute | solution.py:47
  188.1 21.6 %collective-permute-start.20 = (bf16[192,640]{1,0:T(8,128)(2,1)}, bf16[192,640]{1,0:T(8,128)(2,1)S(1)}, u32[]{:S(2)}, u32[]{:S(2)}) collective-permute-start(bf16[192,640]{1,0:T(8,128)(2,1)} %get-tuple-element.62), channel_id=1, source_target_pairs={{0,3},{1,2},{2,1},{3,0},{4,7},{5,6},{6,5},{7,4},{8,11},{9,10},{10,... | collective-permute-start | bytes 737288 | tf_op jit(solution)/shard_map/ppermute | solution.py:47
  246.2 21.5 %collective-permute-start.24 = (bf16[192,640]{1,0:T(8,128)(2,1)}, bf16[192,640]{1,0:T(8,128)(2,1)S(1)}, u32[]{:S(2)}, u32[]{:S(2)}) collective-permute-start(bf16[192,640]{1,0:T(8,128)(2,1)} %get-tuple-element.71), channel_id=1, source_target_pairs={{0,2},{1,3},{2,0},{3,1},{4,6},{5,7},{6,4},{7,5},{8,10},{9,11},{10,... | collective-permute-start | bytes 737288 | tf_op jit(solution)/shard_map/ppermute | solution.py:47
  246.6 21.1 %collective-permute-start.25 = (bf16[192,640]{1,0:T(8,128)(2,1)}, bf16[192,640]{1,0:T(8,128)(2,1)S(1)}, u32[]{:S(2)}, u32[]{:S(2)}) collective-permute-start(bf16[192,640]{1,0:T(8,128)(2,1)} %get-tuple-element.72), channel_id=1, source_target_pairs={{0,1},{1,0},{2,3},{3,2},{4,5},{5,4},{6,7},{7,6},{8,9},{9,8},{10,11... | collective-permute-start | bytes 737288 | tf_op jit(solution)/shard_map/ppermute | solution.py:47
  247.3 20.4 %collective-permute-start.26 = (bf16[192,640]{1,0:T(8,128)(2,1)}, bf16[192,640]{1,0:T(8,128)(2,1)S(1)}, u32[]{:S(2)}, u32[]{:S(2)}) collective-permute-start(bf16[192,640]{1,0:T(8,128)(2,1)} %get-tuple-element.73), channel_id=1, source_target_pairs={{0,3},{1,2},{2,1},{3,0},{4,7},{5,6},{6,5},{7,4},{8,11},{9,10},{10,... | collective-permute-start | bytes 737288 | tf_op jit(solution)/shard_map/ppermute | solution.py:47
  248.3 239.5 %collective-permute-start.12 = (bf16[640,768]{1,0:T(8,128)(2,1)}, bf16[640,768]{1,0:T(8,128)(2,1)}, u32[]{:S(2)}, u32[]{:S(2)}) collective-permute-start(bf16[640,768]{1,0:T(8,128)(2,1)} %get-tuple-element.58), channel_id=1, source_target_pairs={{0,0},{1,4},{2,2},{3,6},{4,1},{5,5},{6,3},{7,7},{8,8},{9,12},{10,1... | collective-permute-start | bytes 2949128 | tf_op jit(solution)/shard_map/ppermute | solution.py:47
  301.5 161.6 %collective-permute-start.27 = (bf16[3,192,640]{2,1,0:T(8,128)(2,1)}, bf16[3,192,640]{2,1,0:T(8,128)(2,1)S(1)}, u32[]{:S(2)}, u32[]{:S(2)}) collective-permute-start(bf16[3,192,640]{2,1,0:T(8,128)(2,1)} %get-tuple-element.77.d1), channel_id=1, source_target_pairs={{0,2},{1,3},{2,0},{3,1},{4,6},{5,7},{6,4},{7,5},{8,10},{9,11},{10,... | collective-permute-start | bytes 2211848 | tf_op jit(solution)/shard_map/ppermute | solution.py:47
  303.0 160.1 %collective-permute-start.28 = (bf16[3,192,640]{2,1,0:T(8,128)(2,1)}, bf16[3,192,640]{2,1,0:T(8,128)(2,1)S(1)}, u32[]{:S(2)}, u32[]{:S(2)}) collective-permute-start(bf16[3,192,640]{2,1,0:T(8,128)(2,1)} %get-tuple-element.78.d2), channel_id=1, source_target_pairs={{0,1},{1,0},{2,3},{3,2},{4,5},{5,4},{6,7},{7,6},{8,9},{9,8},{10,11... | collective-permute-start | bytes 2211848 | tf_op jit(solution)/shard_map/ppermute | solution.py:47
  307.3 155.8 %collective-permute-start.29 = (bf16[3,192,640]{2,1,0:T(8,128)(2,1)}, bf16[3,192,640]{2,1,0:T(8,128)(2,1)S(1)}, u32[]{:S(2)}, u32[]{:S(2)}) collective-permute-start(bf16[3,192,640]{2,1,0:T(8,128)(2,1)} %get-tuple-element.79.d3), channel_id=1, source_target_pairs={{0,3},{1,2},{2,1},{3,0},{4,7},{5,6},{6,5},{7,4},{8,11},{9,10},{10,... | collective-permute-start | bytes 2211848 | tf_op jit(solution)/shard_map/ppermute | solution.py:47
  464.4 12.6 %copy-start.4 = (bf16[4,384,768]{2,1,0:T(8,128)(2,1)S(1)}, bf16[4,384,768]{2,1,0:T(8,128)(2,1)}, u32[]{:S(2)}) copy-start(bf16[4,384,768]{2,1,0:T(8,128)(2,1)} %get-tuple-element.95) | copy-start | bytes 7077892
  473.8 27.0 %collective-permute-start.30 = (bf16[640,768]{1,0:T(8,128)(2,1)}, bf16[640,768]{1,0:T(8,128)(2,1)S(1)}, u32[]{:S(2)}, u32[]{:S(2)}) collective-permute-start(bf16[640,768]{1,0:T(8,128)(2,1)} %shard_map.230), channel_id=1, source_target_pairs={{0,0},{1,4},{2,2},{3,6},{4,1},{5,5},{6,3},{7,7},{8,8},{9,12},{10,1... | collective-permute-start | bytes 2949128 | tf_op jit(solution)/shard_map/ppermute | solution.py:47
  479.8 2.8 copy-start.20
  479.8 5.8 %copy-start.8 = (bf16[6,192,768]{2,1,0:T(8,128)(2,1)S(1)}, bf16[6,192,768]{2,1,0:T(8,128)(2,1)}, u32[]{:S(2)}) copy-start(bf16[6,192,768]{2,1,0:T(8,128)(2,1)} %shard_map.232) | copy-start | bytes 5308420
  (19 other events, 23.4 us)

commit v3 on v2

--- a/solution.py
+++ b/solution.py
@@ -735,11 +735,12 @@
 class Copies:
     def __init__(self, send, recv, local):
         self.send, self.recv, self.local_sem = send, recv, local
-        self.sent, self.kept = [], 0
-
-    def remote(self, source, target, device):
-        n = len(self.sent)
-        copy = pltpu.make_async_remote_copy(
+        self.sent, self.planned, self.kept = [], 0, 0
+
+    def plan(self, source, target, device):
+        n = self.planned
+        self.planned += 1
+        return pltpu.make_async_remote_copy(
             src_ref=source,
             dst_ref=target,
             send_sem=self.send.at[n],
@@ -747,13 +748,19 @@
             device_id=device,
             device_id_type=pl.DeviceIdType.MESH,
         )
+
+    def remote(self, source, target, device):
+        copy = self.plan(source, target, device)
         copy.start()
         self.sent.append(copy)
         return copy
 
+    def plan_local(self, source, target):
+        self.kept += 1
+        return pltpu.make_async_copy(source, target, self.local_sem.at[self.kept - 1])
+
     def local(self, source, target):
-        copy = pltpu.make_async_copy(source, target, self.local_sem.at[self.kept])
-        self.kept += 1
+        copy = self.plan_local(source, target)
         copy.start()
         return copy
 
@@ -990,6 +997,204 @@
     )
 
 
+def binarize_rows(source, target):
+    rows, cols = target.shape
+    step = 96 if cols < 2048 else 32
+
+    def body(i, carry):
+        at = pl.ds(pl.multiple_of(i * step, 16), step)
+        value = source[at, :]
+        scale = jnp.sum(jnp.abs(value), axis=1, keepdims=True) * (1.0 / cols)
+        signed = jnp.where(value > 0, scale, jnp.where(value < 0, -scale, 0.0))
+        target[at, :] = signed.astype(BF)
+        return carry
+
+    lax.fori_loop(0, rows // step, body, 0)
+
+
+def entry_kernel(
+    seq, core, hidden, teach, l_qkv, l_out, l_up, l_down, t_qkv, t_out, t_up, t_down, bias,
+    o_qkv, x0, x1, x2, x3, o_teach, b_qkv, b_out, b_up, b_down, e_qkv, e_out, e_up, e_down,
+    xs, held, w_qkv, w_out, w_up, w_down, f_qkv, f_out, f_up, f_down,
+    s_qkv, s_out, s_up, s_down, proj, send, recv, local,
+):
+    tok, width = hidden.shape
+    parts, size = 4, tok // 4
+    along, next_chip = place(seq[0])
+    side_of, sibling = place(core)
+    half = lax.div(lax.axis_index("seq"), jnp.int32(2))
+    stays = half == side_of
+    moves = half != side_of
+    partner = {"seq": 2 * side_of + along, "fsdp": half}
+    mesh = pl.DeviceIdType.MESH
+
+    barrier = pltpu.get_barrier_semaphore()
+    for device in (next_chip, sibling):
+        pl.semaphore_signal(barrier, inc=1, device_id=device, device_id_type=mesh)
+
+    @pl.when(moves)
+    def _():
+        pl.semaphore_signal(barrier, inc=1, device_id=partner, device_id_type=mesh)
+        pl.semaphore_wait(barrier, 3)
+
+    @pl.when(stays)
+    def _():
+        pl.semaphore_wait(barrier, 2)
+
+    copies = Copies(send, recv, local)
+    cuts = [pl.ds(c * size, size) for c in range(parts)]
+    swap = [copies.plan(hidden.at[cut], xs.at[0, cut], partner) for cut in cuts]
+    load = [copies.plan_local(hidden.at[cut], xs.at[0, cut]) for cut in cuts]
+    over = [copies.plan(xs.at[0, cut], xs.at[1, cut], next_chip) for cut in cuts]
+    beside = [copies.plan(xs.at[0, cut], xs.at[2, cut], sibling) for cut in cuts]
+    relay = [copies.plan(xs.at[1, cut], xs.at[3, cut], sibling) for cut in cuts]
+    t_swap = copies.plan(teach, held, partner)
+    t_load = copies.plan_local(teach, held)
+
+    @pl.when(moves)
+    def _():
+        for copy in swap:
+            copy.start()
+
+    @pl.when(stays)
+    def _():
+        for copy in load:
+            copy.start()
+        t_load.start()
+
+    latent = [
+        (copies.local(source, target), target)
+        for source, target in ((l_qkv, f_qkv), (l_out, f_out), (l_up, f_up), (l_down, f_down))
+    ]
+    staged = [
+        (copies.local(source, target), target, result)
+        for source, target, result in (
+            (t_qkv, s_qkv, e_qkv),
+            (t_out, s_out, e_out),
+            (t_up, s_up, e_up),
+            (t_down, s_down, e_down),
+        )
+    ]
+
+    @pl.when(stays)
+    def _():
+        for c in range(parts):
+            load[c].wait()
+            over[c].start()
+            beside[c].start()
+
+    rows_qkv = l_qkv.shape[0]
+    mine = w_qkv.at[pl.ds(pl.multiple_of(side_of * rows_qkv, 16), rows_qkv)]
+    latent[0][0].wait()
+    binarize_rows(f_qkv, mine)
+    qkv_copy = copies.remote(mine, mine, sibling)
+    stores, arrivals = [], []
+    for (copy, source), target, result in zip(
+        latent[1:], (w_out, w_up, w_down), (b_out, b_up, b_down)
+    ):
+        copy.wait()
+        binarize_rows(source, target)
+        arrivals.append(copies.remote(target, result.at[side_of], sibling))
+        stores.append(copies.local(target, result.at[side_of]))
+    for source, (_, _, result) in zip((t_qkv, t_out, t_up, t_down), staged):
+        arrivals.append(copies.remote(source, result.at[side_of], sibling))
+    for copy, target, result in staged:
+        copy.wait()
+        stores.append(copies.local(target, result.at[side_of]))
+
+    @pl.when(moves)
+    def _():
+        for c in range(parts):
+            swap[c].wait_recv()
+            over[c].start()
+            beside[c].start()
+        t_swap.start()
+
+    qkv_copy.wait_recv()
+    stores.append(copies.local(w_qkv, b_qkv))
+    rows = width // 4
+    own = along + 2 * side_of
+
+    def project(slot):
+        act = jnp.clip(xs[slot], -CLIP, CLIP)
+        first = (1 - along if slot % 2 else along) + 2 * (1 - side_of if slot // 2 else side_of)
+        there = pl.ds(pl.multiple_of(first * tok, 128), tok)
+        for part in range(3):
+            at = pl.multiple_of(part * width + own * rows, 16)
+            value = dot(w_qkv[pl.ds(at, rows), :], act, 1, 1)
+            if part != 1:
+                value = value + bias[part // 2, pl.ds(pl.multiple_of(own * rows, 8), rows), :]
+            proj[part * rows : (part + 1) * rows, there] = value.astype(BF)
+        stores.append(copies.local(proj.at[:, there], o_qkv.at[:, there]))
+        stores.append(copies.local(xs.at[slot], (x0, x1, x2, x3)[slot]))
+
+    project(0)
+    for copy in beside:
+        copy.wait_recv()
+    project(2)
+    for c in range(parts):
+        over[c].wait_recv()
+        relay[c].start()
+    project(1)
+    for copy in relay:
+        copy.wait_recv()
+    project(3)
+
+    @pl.when(moves)
+    def _():
+        t_swap.wait_recv()
+
+    @pl.when(stays)
+    def _():
+        t_load.wait()
+
+    stores.append(copies.local(held, o_teach))
+    for copy in arrivals:
+        copy.wait_recv()
+    for copy in stores:
+        copy.wait()
+
+    @pl.when(moves)
+    def _():
+        for copy in swap + [t_swap]:
+            copy.wait_send()
+
+    for copy in over + beside + relay:
+        copy.wait_send()
+    copies.finish()
+
+
+def entry(seq, core, hidden, teach, latents, teachers, bias):
+    tok, width = hidden.shape
+    halves = [w.shape for w in latents]
+    sides = [shape_of((2,) + shape, BF) for shape in halves]
+    own = [pltpu.VMEM(shape, BF) for shape in halves]
+    sides[0] = shape_of((2 * halves[0][0], halves[0][1]), BF)
+    sides_t = [shape_of((2,) + shape, BF) for shape in halves]
+    outs = remote_call(
+        lambda *refs: entry_kernel(seq, core, *refs),
+        [hidden, teach] + list(latents) + list(teachers) + [bias],
+        [ANY] * 10 + [IN_VMEM],
+        [shape_of((3 * width // 4, 4 * tok), BF)]
+        + [shape_of((tok, width), BF)] * 5
+        + sides
+        + sides_t,
+        [ANY] * 14,
+        [pltpu.VMEM((4, tok, width), BF), pltpu.VMEM((tok, width), BF)]
+        + [pltpu.VMEM(sides[0].shape, BF)]
+        + own[1:]
+        + [pltpu.VMEM(shape, F32) for shape in halves]
+        + own
+        + [pltpu.VMEM((3 * width // 4, 4 * tok), BF)],
+        25,
+        30,
+        3,
+    )
+    qkv, x0, x1, x2, x3, teach = outs[:6]
+    weights = [w.reshape((-1, w.shape[-1])) for w in outs[6:]]
+    return qkv, (x0, x1, x2, x3), teach, weights[:4], weights[4:]
+
+
 def binarize(latent):
     row_scale = jnp.mean(jnp.abs(latent), axis=1, keepdims=True)
     return (row_scale * jnp.sign(latent)).astype(BF)
@@ -1022,24 +1227,29 @@
     own = (seq_at % 2 + 2 * core).astype(jnp.int32)
     width = hidden.shape[2]
 
-    x = swap_groups(hidden[0])
-    x_slots = quarters(x)
-    bin_qkv = gather_rows(binarize(latent_qkv))
     info = segment_info(segments)
     info = jnp.where(core == seq_at // 2, info, flip(info, fsdp=1))
     pref = jnp.concatenate([own[None], info]).astype(jnp.int32)
-    bin_out = gather_rows(binarize(latent_out))
-    bin_up = gather_rows(binarize(latent_up))
-    bin_down = gather_rows(binarize(latent_down))
-    teach = swap_groups(teacher_hidden[0])
+    bias_cols = biases[:2].reshape(2, width, 1)
+    latents = (latent_qkv, latent_out, latent_up, latent_down)
+    teachers = (teacher_qkv, teacher_out, teacher_up, teacher_down)
+    if fsdp == 2:
+        qkv, x_slots, teach, bins, t_weights = entry(
+            bit_list("seq"), bit_list("fsdp")[0], hidden[0], teacher_hidden[0],
+            latents, teachers, bias_cols,
+        )
+        x = x_slots[0]
+    else:
+        x = swap_groups(hidden[0])
+        x_slots = quarters(x)
+        bins = [gather_rows(binarize(w)) for w in latents]
+        teach = swap_groups(teacher_hidden[0])
+        t_weights = [gather_rows(w) for w in teachers]
+        qkv = qkv_project(pref, x_slots, bins[0], bias_cols)
+    bin_qkv, bin_out, bin_up, bin_down = bins
+    t_qkv, t_out, t_up, t_down = t_weights
     t_slots = quarters(teach)
-    t_qkv = gather_rows(teacher_qkv)
-    t_out = gather_rows(teacher_out)
-    t_up = gather_rows(teacher_up)
-    t_down = gather_rows(teacher_down)
-
-    bias_cols = biases[:2].reshape(2, width, 1)
-    qkv = qkv_project(pref, x_slots, bin_qkv, bias_cols)
+
     *ctx_slots, ctx_full, lse = attention(pref, qkv)
     ctx_pieces = exchange(ctx_slots)
 

time: 511 us -> 479 us (0.937)
  the two profiles are of different devices: /device:TPU:1 before, /device:TPU:24 now
where the time goes in v3:
time: 479 us; the launch traced here: 470 us
  Pallas kernels  376 us (78%)
  waiting for transfers between devices  51.1 us (11%)
  starting transfers between devices  14.4 us (3%)
  local copies, waits for them, and re-layouts  12.5 us (3%)
  other arithmetic  10.1 us (2%)
  between operations  6.4 us (1%)
    pallas_call x3, Pallas kernels, remote_call(): pl.pallas_call(kernel, in_specs=in_specs, out_specs=out_specs, out_shape=...  203 us
    pallas_call x10, Pallas kernels, call(): pl.pallas_call(kernel, grid_spec=pltpu.PrefetchScalarGridSpec(num_scalar_...  173 us
    ppermute x18, waiting for transfers between devices, permute(): return lax.ppermute(values, AXES, pairs)  51.1 us
    ppermute x18, starting transfers between devices, permute(): return lax.ppermute(values, AXES, pairs)  14.4 us
  transfers between devices with their start and end apart: 18, of which 7 were waited for; matrix products, arithmetic and copies ran while one was open for 3% of the time, Pallas kernels for 52%

profile of v3, /device:TPU:24, one launch (start us, length us, event | category | flops | bytes accessed | tf_op | source)
XLA Modules:
  0.0 470.2 jit_solution(12409325885618725927)
XLA Ops:
  0.6 0.7 slice_bitcast_fusion
  1.4 1.2 copy.25.refs_10_
  2.5 50.9 %shard_map.222 = (bf16[576,2560]{1,0:T(8,128)(2,1)}, bf16[640,768]{1,0:T(8,128)(2,1)}, bf16[640,768]{1,0:T(8,128)(2,1)}, bf16[640,768]{1,0:T(8,128)(2,1)}, bf16[...) custom-call(bf16[640,768]{1,0:T(8,128)(2,1)} %bitcast.28, ...), custom_call_target="tpu_custom_call" | custom-call | flops 49999998976 | bytes 100000000 | tf_op jit(solution)/shard_map/pallas_call | solution.py:907
  53.6 0.7 fusion.2
  59.6 0.5 collective-permute-start
  60.1 0.8 collective-permute-done
  61.0 0.6 pad_add_fusion.1.refs_0_.pref
  61.6 14.7 %collective-permute-done.5.refs_2_ = bf16[640,768]{1,0:T(8,128)(2,1)S(1)} collective-permute-done((bf16[640,768]{1,0:T(8,128)(2,1)}, bf16[640,768]{1,0:T(8,128)(2,1)S(1)}, u32[]{:S(2)}, u32[]{:S(2)}) %collective-permute-start.5) | collective-permute-done | bytes 983072 | tf_op jit(solution)/shard_map/ppermute | solution.py:47
  76.3 21.5 %shard_map.223 = (bf16[192,640]{1,0:T(8,128)(2,1)}, bf16[192,640]{1,0:T(8,128)(2,1)}, bf16[192,640]{1,0:T(8,128)(2,1)}, bf16[192,640]{1,0:T(8,128)(2,1)}, f32[192,2560]{1,0:T(8,128)}, /*index=5*/f32[3,1,2560]{2,1,0:T(1,128)}) custom-call(s32[3]{0:T(128)} %pad_add_fusion.1.refs_0_.pref, bf16[576,2560]{1,0:T(8,128)(2,1)} %get-tuple-element.68.refs_1_.refs_2_.refs_3_, ...), custom_call_target="tpu_custom_call" | custom-call | flops 16000000000 | bytes 11827200 | tf_op jit(solution)/shard_map/pallas_call | solution.py:126
  98.4 1.6 collective-permute-start.3
  100.0 0.6 fusion.4
  100.6 6.3 %collective-permute-done.1.c1 = bf16[192,640]{1,0:T(8,128)(2,1)S(1)} collective-permute-done((bf16[192,640]{1,0:T(8,128)(2,1)}, bf16[192,640]{1,0:T(8,128)(2,1)S(1)}, u32[]{:S(2)}, u32[]{:S(2)}) %collective-permute-start.1) | collective-permute-done | bytes 245792 | tf_op jit(solution)/shard_map/ppermute | solution.py:47
  106.9 4.3 collective-permute-done.3.c3
  111.2 0.7 copy-done.23
  111.9 19.5 %shard_map.224 = (bf16[768,640]{1,0:T(8,128)(2,1)}, bf16[640,768]{1,0:T(8,128)(2,1)}, f32[640,768]{1,0:T(8,128)}, f32[640,1]{1,0:T(8,128)}, bf16[640,3072]{1,0:T...) custom-call(s32[3]{0:T(128)} %pad_add_fusion.1.refs_0_.pref, ...), custom_call_target="tpu_custom_call" | custom-call | flops 6794772480 | bytes 27364352 | tf_op jit(solution)/shard_map/pallas_call | solution.py:126
  131.4 1.9 collective-permute-start.4
  133.4 0.9 copy-done.6
  134.7 8.9 %shard_map.225.refs_1_.refs_2_.refs_3_ = bf16[576,2560]{1,0:T(8,128)(2,1)} custom-call(s32[3]{0:T(128)} %pad_add_fusion.1.refs_0_.pref, bf16[640,768]{1,0:T(8,128)(2,1)} %get-tuple-element.78.refs_1_.x, bf16[640,768]{1,0:T(8,128)(2,1)} %copy-done.5, bf16[640,768]{1,0:T(8,128)(2,1)} %copy-done.6, bf16[640,768]{1,0:T(8,128)(2,1)} %copy-done.7, ...), custom_call_target="tpu_custom_call" | custom-call | flops 2264924160 | bytes 17498112 | tf_op jit(solution)/shard_map/pallas_call | solution.py:126
  143.6 21.0 %shard_map.226 = (bf16[192,640]{1,0:T(8,128)(2,1)}, bf16[192,640]{1,0:T(8,128)(2,1)}, bf16[192,640]{1,0:T(8,128)(2,1)}, bf16[192,640]{1,0:T(8,128)(2,1)}, f32[192,2560]{1,0:T(8,128)}, /*index=5*/f32[3,1,2560]{2,1,0:T(1,128)}) custom-call(s32[3]{0:T(128)} %pad_add_fusion.1.refs_0_.pref, bf16[576,2560]{1,0:T(8,128)(2,1)} %shard_map.225.refs_1_.refs_2_.refs_3_, ...), custom_call_target="tpu_custom_call" | custom-call | flops 16000000000 | bytes 11827200 | tf_op jit(solution)/shard_map/pallas_call | solution.py:126
  164.8 1.7 collective-permute-start.8
  166.6 6.1 %collective-permute-done.10.c3 = bf16[192,640]{1,0:T(8,128)(2,1)S(1)} collective-permute-done((bf16[192,640]{1,0:T(8,128)(2,1)}, bf16[192,640]{1,0:T(8,128)(2,1)S(1)}, u32[]{:S(2)}, u32[]{:S(2)}) %collective-permute-start.10) | collective-permute-done | bytes 245792 | tf_op jit(solution)/shard_map/ppermute | solution.py:47
  172.7 5.7 %collective-permute-done.8.c1 = bf16[192,640]{1,0:T(8,128)(2,1)S(1)} collective-permute-done((bf16[192,640]{1,0:T(8,128)(2,1)}, bf16[192,640]{1,0:T(8,128)(2,1)S(1)}, u32[]{:S(2)}, u32[]{:S(2)}) %collective-permute-start.8) | collective-permute-done | bytes 245792 | tf_op jit(solution)/shard_map/ppermute | solution.py:47
  178.4 0.7 copy-done.16
  179.2 17.4 %shard_map.227 = (f32[640,768]{1,0:T(8,128)}, bf16[640,768]{1,0:T(8,128)(2,1)}, f32[3,768]{1,0:T(4,128)}) custom-call(s32[3]{0:T(128)} %pad_add_fusion.1.refs_0_.pref, bf16[192,640]{1,0:T(8,128)(2,1)} %get-tuple-element.80.c0, bf16[192,640]{1,0:T(8,128)(2,1)} %copy-done.16, bf16[192,640]{1,0:T(8,128)(2,1)} %copy-done.17, bf16[192,640]{1,0:T(8,128)(2,1)} %copy-done.15, ...), custom_call_target="tpu_custom_call" | custom-call | flops 6794772480 | bytes 17522176 | tf_op jit(solution)/shard_map/pallas_call | solution.py:126
  196.6 18.4 %shard_map.228 = (bf16[640,3072]{1,0:T(8,128)(2,1)}, f32[1,3072]{1,0:T(1,128)}, f32[640,768]{1,0:T(8,128)}, bf16[640,768]{1,0:T(8,128)(2,1)}, bf16[192,640]{1,0:...) custom-call(s32[3]{0:T(128)} %pad_add_fusion.1.refs_0_.pref, ...), custom_call_target="tpu_custom_call" | custom-call | flops 6794772480 | bytes 27364864 | tf_op jit(solution)/shard_map/pallas_call | solution.py:126
  214.9 0.7 collective-permute-start.11
  215.6 1.5 collective-permute-start.13
  217.1 14.9 %shard_map.233 = (bf16[2,4,384,768]{3,2,1,0:T(8,128)(2,1)}, bf16[8,384,768]{2,1,0:T(8,128)(2,1)}, bf16[2,384,768]{2,1,0:T(8,128)(2,1)}) custom-call(s32[3]{0:T(128)} %pad_add_fusion.1.refs_0_.pref, bf16[640,768]{1,0:T(8,128)(2,1)} %get-tuple-element.89.grad_ffn, bf16[640,3072]{1,0:T(8,128)(2,1)} %get-tuple-element.110.gelu, ...), custom_call_target="tpu_custom_call" | custom-call | flops 6794772480 | bytes 22413312 | tf_op jit(solution)/shard_map/pallas_call | solution.py:126
  232.1 0.6 copy-done.18
  232.9 33.1 %shard_map.229 = (bf16[3,192,640]{2,1,0:T(8,128)(2,1)}, bf16[3,192,640]{2,1,0:T(8,128)(2,1)}, bf16[3,192,640]{2,1,0:T(8,128)(2,1)}, bf16[3,192,640]{2,1,0:T(8,128)(2,1)}) custom-call(s32[3]{0:T(128)} %pad_add_fusion.1.refs_0_.pref, bf16[576,2560]{1,0:T(8,128)(2,1)} %get-tuple-element.68.refs_1_.refs_2_.refs_3_, ...), custom_call_target="tpu_custom_call" | custom-call | flops 30000001024 | bytes 14776320 | tf_op jit(solution)/shard_map/pallas_call | solution.py:126
  266.0 0.7 collective-permute-start.14
  266.6 1.5 collective-permute-start.16
  268.2 8.3 %shard_map.231 = (bf16[3,192,768]{2,1,0:T(8,128)(2,1)}, f32[3,8,768]{2,1,0:T(8,128)}) custom-call(s32[3]{0:T(128)} %pad_add_fusion.1.refs_0_.pref, bf16[3,192,640]{2,1,0:T(8,128)(2,1)} %get-tuple-element.100.e0.d0, bf16[3,192,640]{2,1,0:T(8,128)(2,1)} %get-tuple-element.101.d1, bf16[3,192,640]{2,1,0:T(8,128)(2,1)} %get-tuple-element.102.d2, ...), custom_call_target="tpu_custom_call" | custom-call | flops 2264924160 | bytes 7839744 | tf_op jit(solution)/shard_map/pallas_call | solution.py:126
  276.4 51.8 %shard_map.232 = bf16[6,192,768]{2,1,0:T(8,128)(2,1)} custom-call(bf16[3,192,768]{2,1,0:T(8,128)(2,1)} %get-tuple-element.109.refs_0_), custom_call_target="tpu_custom_call" | custom-call | flops 49999998976 | bytes 100000000 | tf_op jit(solution)/shard_map/pallas_call | solution.py:907
  328.3 100.3 %shard_map.234 = (bf16[384,3072]{1,0:T(8,128)(2,1)}, bf16[4,384,768]{2,1,0:T(8,128)(2,1)}, bf16[384,768]{1,0:T(8,128)(2,1)}, f32[16,768]{1,0:T(8,128)}) custom-call(bf16[2,4,384,768]{3,2,1,0:T(8,128)(2,1)} %get-tuple-element.115.refs_0_, bf16[2,4,384,768]{3,2,1,0:T(8,128)(2,1)} %bitcast.37, bf16[2,384,768]{2,1,0:T(8,128)(2,1)} %get-tuple-element.117.refs_2_, ...), custom_call_target="tpu_custom_call" | custom-call | flops 49999998976 | bytes 100000000 | tf_op jit(solution)/shard_map/pallas_call | solution.py:907
  428.7 0.8 copy-done.8
  430.0 9.6 %shard_map.230 = bf16[640,768]{1,0:T(8,128)(2,1)} custom-call(s32[3]{0:T(128)} %pad_add_fusion.1.refs_0_.pref, bf16[3,192,640]{2,1,0:T(8,128)(2,1)} %get-tuple-element.100.e0.d0, bf16[3,192,640]{2,1,0:T(8,128)(2,1)} %copy-done.8, bf16[3,192,640]{2,1,0:T(8,128)(2,1)} %copy-done.9, bf16[3,192,640]{2,1,0:T(8,128)(2,1)} %copy-done.10, ...), custom_call_target="tpu_custom_call" | custom-call | flops 2264924160 | bytes 17498112 | tf_op jit(solution)/shard_map/pallas_call | solution.py:126
  439.6 3.3 collective-permute-start.17
  442.9 2.7 bitcast_convert_fusion
  445.7 2.8 convert_element_type.35
  448.4 1.1 convert_element_type.32
  449.5 0.7 dynamic_slice.7
  450.2 0.6 constant_dynamic-slice_fusion
  450.8 0.7 fusion.3
  451.5 2.2 bitcast_convert_fusion.1
  453.7 13.1 %collective-permute-done.17 = bf16[640,768]{1,0:T(8,128)(2,1)} collective-permute-done((bf16[640,768]{1,0:T(8,128)(2,1)}, bf16[640,768]{1,0:T(8,128)(2,1)}, u32[]{:S(2)}, u32[]{:S(2)}) %collective-permute-start.17) | collective-permute-done | bytes 983072 | tf_op jit(solution)/shard_map/ppermute | solution.py:47
  466.7 0.9 copy.28
  467.7 2.2 copy.29
  (68 shorter events, 2.4 us)
Async XLA Ops:
  2.5 51.1 %copy-start.14 = (s32[1,2560]{1,0:T(1,128)S(1)}, s32[1,2560]{1,0:T(1,128)}, u32[]{:S(2)}) copy-start(s32[1,2560]{1,0:T(1,128)} %param.17) | copy-start | bytes 30724
  53.5 22.8 %collective-permute-start.5 = (bf16[640,768]{1,0:T(8,128)(2,1)}, bf16[640,768]{1,0:T(8,128)(2,1)S(1)}, u32[]{:S(2)}, u32[]{:S(2)}) collective-permute-start(bf16[640,768]{1,0:T(8,128)(2,1)} %get-tuple-element.78.refs_1_.x), channel_id=1, source_target_pairs={{0,2},{1,3},{2,0},{3,1},{4,6},{5,7},{6,4},{7,5},{8,10},{9,11},{10,... | collective-permute-start | bytes 2949128 | tf_op jit(solution)/shard_map/ppermute | solution.py:47
  53.5 79.8 %collective-permute-start.6 = (bf16[640,768]{1,0:T(8,128)(2,1)}, bf16[640,768]{1,0:T(8,128)(2,1)S(1)}, u32[]{:S(2)}, u32[]{:S(2)}) collective-permute-start(bf16[640,768]{1,0:T(8,128)(2,1)} %get-tuple-element.78.refs_1_.x), channel_id=1, source_target_pairs={{0,1},{1,0},{2,3},{3,2},{4,5},{5,4},{6,7},{7,6},{8,9},{9,8},{10,11... | collective-permute-start | bytes 2949128 | tf_op jit(solution)/shard_map/ppermute | solution.py:47
  59.6 1.3 collective-permute-start
  76.3 21.5 %copy-start.5 = (bf16[640,768]{1,0:T(8,128)(2,1)}, bf16[640,768]{1,0:T(8,128)(2,1)S(1)}, u32[]{:S(2)}) copy-start(bf16[640,768]{1,0:T(8,128)(2,1)S(1)} %collective-permute-done.5.refs_2_) | copy-start | bytes 2949124
  76.3 57.0 %collective-permute-start.7 = (bf16[640,768]{1,0:T(8,128)(2,1)S(1)}, bf16[640,768]{1,0:T(8,128)(2,1)S(1)}, u32[]{:S(2)}, u32[]{:S(2)}) collective-permute-start(bf16[640,768]{1,0:T(8,128)(2,1)S(1)} %collective-permute-done.5.refs_2_), channel_id=1, source_target_pairs={{0,1},{1,0},{2,3},{3,2},{4,5},{5,4},{6,7},{7,6},{8,9},{9,8},{10,11... | collective-permute-start | bytes 2949128 | tf_op jit(solution)/shard_map/ppermute | solution.py:47
  76.3 23.7 %copy-start.13 = (f32[4,768]{1,0:T(4,128)S(1)}, f32[4,768]{1,0:T(4,128)}, u32[]{:S(2)}) copy-start(f32[4,768]{1,0:T(4,128)} %param.22) | copy-start | bytes 36868
  97.8 9.1 %collective-permute-start.1 = (bf16[192,640]{1,0:T(8,128)(2,1)}, bf16[192,640]{1,0:T(8,128)(2,1)S(1)}, u32[]{:S(2)}, u32[]{:S(2)}) collective-permute-start(bf16[192,640]{1,0:T(8,128)(2,1)} %get-tuple-element.70), channel_id=1, source_target_pairs={{0,2},{1,3},{2,0},{3,1},{4,6},{5,7},{6,4},{7,5},{8,10},{9,11},{10,... | collective-permute-start | bytes 737288 | tf_op jit(solution)/shard_map/ppermute | solution.py:47
  98.1 8.8 %collective-permute-start.2 = (bf16[192,640]{1,0:T(8,128)(2,1)}, bf16[192,640]{1,0:T(8,128)(2,1)S(1)}, u32[]{:S(2)}, u32[]{:S(2)}) collective-permute-start(bf16[192,640]{1,0:T(8,128)(2,1)} %get-tuple-element.71), channel_id=1, source_target_pairs={{0,1},{1,0},{2,3},{3,2},{4,5},{5,4},{6,7},{7,6},{8,9},{9,8},{10,11... | collective-permute-start | bytes 737288 | tf_op jit(solution)/shard_map/ppermute | solution.py:47
  98.4 12.8 %collective-permute-start.3 = (bf16[192,640]{1,0:T(8,128)(2,1)}, bf16[192,640]{1,0:T(8,128)(2,1)S(1)}, u32[]{:S(2)}, u32[]{:S(2)}) collective-permute-start(bf16[192,640]{1,0:T(8,128)(2,1)} %get-tuple-element.72), channel_id=1, source_target_pairs={{0,3},{1,2},{2,1},{3,0},{4,7},{5,6},{6,5},{7,4},{8,11},{9,10},{10,... | collective-permute-start | bytes 737288 | tf_op jit(solution)/shard_map/ppermute | solution.py:47
  106.9 4.3 copy-start.20
  106.9 4.3 copy-start.22
  111.2 0.7 copy-start.23
  131.4 35.2 %collective-permute-start.4 = (bf16[640,768]{1,0:T(8,128)(2,1)}, bf16[640,768]{1,0:T(8,128)(2,1)S(1)}, u32[]{:S(2)}, u32[]{:S(2)}) collective-permute-start(bf16[640,768]{1,0:T(8,128)(2,1)} %get-tuple-element.77), channel_id=1, source_target_pairs={{0,0},{1,4},{2,2},{3,6},{4,1},{5,5},{6,3},{7,7},{8,8},{9,12},{10,1... | collective-permute-start | bytes 2949128 | tf_op jit(solution)/shard_map/ppermute | solution.py:47
  133.3 1.0 copy-start.6
  133.4 1.3 copy-start.7
  164.6 8.1 %collective-permute-start.10 = (bf16[192,640]{1,0:T(8,128)(2,1)}, bf16[192,640]{1,0:T(8,128)(2,1)S(1)}, u32[]{:S(2)}, u32[]{:S(2)}) collective-permute-start(bf16[192,640]{1,0:T(8,128)(2,1)} %get-tuple-element.83), channel_id=1, source_target_pairs={{0,3},{1,2},{2,1},{3,0},{4,7},{5,6},{6,5},{7,4},{8,11},{9,10},{10,... | collective-permute-start | bytes 737288 | tf_op jit(solution)/shard_map/ppermute | solution.py:47
  164.8 13.6 %collective-permute-start.8 = (bf16[192,640]{1,0:T(8,128)(2,1)}, bf16[192,640]{1,0:T(8,128)(2,1)S(1)}, u32[]{:S(2)}, u32[]{:S(2)}) collective-permute-start(bf16[192,640]{1,0:T(8,128)(2,1)} %get-tuple-element.81), channel_id=1, source_target_pairs={{0,2},{1,3},{2,0},{3,1},{4,6},{5,7},{6,4},{7,5},{8,10},{9,11},{10,... | collective-permute-start | bytes 737288 | tf_op jit(solution)/shard_map/ppermute | solution.py:47
  166.6 11.9 %collective-permute-start.9 = (bf16[192,640]{1,0:T(8,128)(2,1)}, bf16[192,640]{1,0:T(8,128)(2,1)S(1)}, u32[]{:S(2)}, u32[]{:S(2)}) collective-permute-start(bf16[192,640]{1,0:T(8,128)(2,1)} %get-tuple-element.82), channel_id=1, source_target_pairs={{0,1},{1,0},{2,3},{3,2},{4,5},{5,4},{6,7},{7,6},{8,9},{9,8},{10,11... | collective-permute-start | bytes 737288 | tf_op jit(solution)/shard_map/ppermute | solution.py:47
  166.6 30.0 %copy-start.3 = (bf16[640,768]{1,0:T(8,128)(2,1)}, bf16[640,768]{1,0:T(8,128)(2,1)S(1)}, u32[]{:S(2)}) copy-start(bf16[640,768]{1,0:T(8,128)(2,1)S(1)} %collective-permute-done.4) | copy-start | bytes 2949124
  172.7 5.7 %copy-start.15 = (bf16[192,640]{1,0:T(8,128)(2,1)}, bf16[192,640]{1,0:T(8,128)(2,1)S(1)}, u32[]{:S(2)}) copy-start(bf16[192,640]{1,0:T(8,128)(2,1)S(1)} %collective-permute-done.10.c3) | copy-start | bytes 737284
  178.4 0.7 copy-start.16
  178.4 0.8 copy-start.17
  214.9 17.1 %collective-permute-start.11 = (bf16[192,640]{1,0:T(8,128)(2,1)}, bf16[192,640]{1,0:T(8,128)(2,1)S(1)}, u32[]{:S(2)}, u32[]{:S(2)}) collective-permute-start(bf16[192,640]{1,0:T(8,128)(2,1)} %get-tuple-element.95), channel_id=1, source_target_pairs={{0,2},{1,3},{2,0},{3,1},{4,6},{5,7},{6,4},{7,5},{8,10},{9,11},{10,... | collective-permute-start | bytes 737288 | tf_op jit(solution)/shard_map/ppermute | solution.py:47
  215.6 16.4 %collective-permute-start.12 = (bf16[192,640]{1,0:T(8,128)(2,1)}, bf16[192,640]{1,0:T(8,128)(2,1)S(1)}, u32[]{:S(2)}, u32[]{:S(2)}) collective-permute-start(bf16[192,640]{1,0:T(8,128)(2,1)} %get-tuple-element.96), channel_id=1, source_target_pairs={{0,1},{1,0},{2,3},{3,2},{4,5},{5,4},{6,7},{7,6},{8,9},{9,8},{10,11... | collective-permute-start | bytes 737288 | tf_op jit(solution)/shard_map/ppermute | solution.py:47
  215.6 16.4 %collective-permute-start.13 = (bf16[192,640]{1,0:T(8,128)(2,1)}, bf16[192,640]{1,0:T(8,128)(2,1)S(1)}, u32[]{:S(2)}, u32[]{:S(2)}) collective-permute-start(bf16[192,640]{1,0:T(8,128)(2,1)} %get-tuple-element.97), channel_id=1, source_target_pairs={{0,3},{1,2},{2,1},{3,0},{4,7},{5,6},{6,5},{7,4},{8,11},{9,10},{10,... | collective-permute-start | bytes 737288 | tf_op jit(solution)/shard_map/ppermute | solution.py:47
  232.0 0.7 copy-start.18
  232.0 0.8 copy-start.19
  232.0 0.8 copy-start.21
  266.0 162.6 %collective-permute-start.14 = (bf16[3,192,640]{2,1,0:T(8,128)(2,1)}, bf16[3,192,640]{2,1,0:T(8,128)(2,1)S(1)}, u32[]{:S(2)}, u32[]{:S(2)}) collective-permute-start(bf16[3,192,640]{2,1,0:T(8,128)(2,1)} %get-tuple-element.101.d1), channel_id=1, source_target_pairs={{0,2},{1,3},{2,0},{3,1},{4,6},{5,7},{6,4},{7,5},{8,10},{9,11},{10,... | collective-permute-start | bytes 2211848 | tf_op jit(solution)/shard_map/ppermute | solution.py:47
  266.6 162.0 %collective-permute-start.15 = (bf16[3,192,640]{2,1,0:T(8,128)(2,1)}, bf16[3,192,640]{2,1,0:T(8,128)(2,1)S(1)}, u32[]{:S(2)}, u32[]{:S(2)}) collective-permute-start(bf16[3,192,640]{2,1,0:T(8,128)(2,1)} %get-tuple-element.102.d2), channel_id=1, source_target_pairs={{0,1},{1,0},{2,3},{3,2},{4,5},{5,4},{6,7},{7,6},{8,9},{9,8},{10,11... | collective-permute-start | bytes 2211848 | tf_op jit(solution)/shard_map/ppermute | solution.py:47
  266.6 162.0 %collective-permute-start.16 = (bf16[3,192,640]{2,1,0:T(8,128)(2,1)}, bf16[3,192,640]{2,1,0:T(8,128)(2,1)S(1)}, u32[]{:S(2)}, u32[]{:S(2)}) collective-permute-start(bf16[3,192,640]{2,1,0:T(8,128)(2,1)} %get-tuple-element.103.d3), channel_id=1, source_target_pairs={{0,3},{1,2},{2,1},{3,0},{4,7},{5,6},{6,5},{7,4},{8,11},{9,10},{10,... | collective-permute-start | bytes 2211848 | tf_op jit(solution)/shard_map/ppermute | solution.py:47
  428.6 0.9 copy-start.8
  428.6 1.1 copy-start.9
  428.7 1.3 copy-start.10
  430.0 12.9 %copy-start.1 = (bf16[4,384,768]{2,1,0:T(8,128)(2,1)S(1)}, bf16[4,384,768]{2,1,0:T(8,128)(2,1)}, u32[]{:S(2)}) copy-start(bf16[4,384,768]{2,1,0:T(8,128)(2,1)} %get-tuple-element.123) | copy-start | bytes 7077892
  439.6 27.2 %collective-permute-start.17 = (bf16[640,768]{1,0:T(8,128)(2,1)}, bf16[640,768]{1,0:T(8,128)(2,1)}, u32[]{:S(2)}, u32[]{:S(2)}) collective-permute-start(bf16[640,768]{1,0:T(8,128)(2,1)} %shard_map.230), channel_id=1, source_target_pairs={{0,0},{1,4},{2,2},{3,6},{4,1},{5,5},{6,3},{7,7},{8,8},{9,12},{10,1... | collective-permute-start | bytes 2949128 | tf_op jit(solution)/shard_map/ppermute | solution.py:47
  442.9 2.7 copy-start.12
  442.9 2.7 copy-start
  445.7 2.8 copy-start.11
  445.7 5.8 %copy-start.2 = (bf16[6,192,768]{2,1,0:T(8,128)(2,1)S(1)}, bf16[6,192,768]{2,1,0:T(8,128)(2,1)}, u32[]{:S(2)}) copy-start(bf16[6,192,768]{2,1,0:T(8,128)(2,1)} %shard_map.232) | copy-start | bytes 5308420
  449.5 17.2 %copy-start.4 = (bf16[640,768]{1,0:T(8,128)(2,1)S(1)}, bf16[640,768]{1,0:T(8,128)(2,1)}, u32[]{:S(2)}) copy-start(bf16[640,768]{1,0:T(8,128)(2,1)} %copy-done.3) | copy-start | bytes 2949124

commit v4 on v3

--- a/solution.py
+++ b/solution.py
@@ -1013,10 +1013,10 @@
 
 
 def entry_kernel(
-    seq, core, hidden, teach, l_qkv, l_out, l_up, l_down, t_qkv, t_out, t_up, t_down, bias,
-    o_qkv, x0, x1, x2, x3, o_teach, b_qkv, b_out, b_up, b_down, e_qkv, e_out, e_up, e_down,
+    seq, core, hidden, teach, segments, l_qkv, l_out, l_up, l_down, t_qkv, t_out, t_up, t_down, bias,
+    o_pref, o_qkv, x0, x1, x2, x3, o_teach, b_qkv, b_out, b_up, b_down, e_qkv, e_out, e_up, e_down,
     xs, held, w_qkv, w_out, w_up, w_down, f_qkv, f_out, f_up, f_down,
-    s_qkv, s_out, s_up, s_down, proj, send, recv, local,
+    s_qkv, s_out, s_up, s_down, proj, others, send, recv, local,
 ):
     tok, width = hidden.shape
     parts, size = 4, tok // 4
@@ -1050,6 +1050,7 @@
     relay = [copies.plan(xs.at[1, cut], xs.at[3, cut], sibling) for cut in cuts]
     t_swap = copies.plan(teach, held, partner)
     t_load = copies.plan_local(teach, held)
+    seg_copy = copies.remote(segments, others, sibling)
 
     @pl.when(moves)
     def _():
@@ -1128,6 +1129,16 @@
         stores.append(copies.local(proj.at[:, there], o_qkv.at[:, there]))
         stores.append(copies.local(xs.at[slot], (x0, x1, x2, x3)[slot]))
 
+    seg_copy.wait_recv()
+    counts = [jnp.sum(jnp.where(segments[...] == k, 1.0, 0.0)) for k in (1, 2, 3)]
+    theirs = [jnp.sum(jnp.where(others[...] == k, 1.0, 0.0)) for k in (1, 2, 3)]
+    first, second, third = [
+        jnp.where(stays, a, b).astype(jnp.int32) for a, b in zip(counts, theirs)
+    ]
+    o_pref[0] = own
+    o_pref[1] = jnp.where(first == LONG, 0, jnp.where(second == LONG, first, first + second))
+    o_pref[2] = jnp.where(first == LONG, second, jnp.where(second == LONG, third, first))
+
     project(0)
     for copy in beside:
         copy.wait_recv()
@@ -1164,7 +1175,7 @@
     copies.finish()
 
 
-def entry(seq, core, hidden, teach, latents, teachers, bias):
+def entry(seq, core, hidden, teach, segments, latents, teachers, bias):
     tok, width = hidden.shape
     halves = [w.shape for w in latents]
     sides = [shape_of((2,) + shape, BF) for shape in halves]
@@ -1173,26 +1184,26 @@
     sides_t = [shape_of((2,) + shape, BF) for shape in halves]
     outs = remote_call(
         lambda *refs: entry_kernel(seq, core, *refs),
-        [hidden, teach] + list(latents) + list(teachers) + [bias],
-        [ANY] * 10 + [IN_VMEM],
-        [shape_of((3 * width // 4, 4 * tok), BF)]
+        [hidden, teach, segments] + list(latents) + list(teachers) + [bias],
+        [ANY] * 2 + [IN_VMEM] + [ANY] * 8 + [IN_VMEM],
+        [shape_of((3,), jnp.int32), shape_of((3 * width // 4, 4 * tok), BF)]
         + [shape_of((tok, width), BF)] * 5
         + sides
         + sides_t,
-        [ANY] * 14,
+        [pl.BlockSpec(memory_space=pltpu.SMEM)] + [ANY] * 14,
         [pltpu.VMEM((4, tok, width), BF), pltpu.VMEM((tok, width), BF)]
         + [pltpu.VMEM(sides[0].shape, BF)]
         + own[1:]
         + [pltpu.VMEM(shape, F32) for shape in halves]
         + own
-        + [pltpu.VMEM((3 * width // 4, 4 * tok), BF)],
-        25,
+        + [pltpu.VMEM((3 * width // 4, 4 * tok), BF), pltpu.VMEM(segments.shape, jnp.int32)],
+        26,
         30,
         3,
     )
-    qkv, x0, x1, x2, x3, teach = outs[:6]
-    weights = [w.reshape((-1, w.shape[-1])) for w in outs[6:]]
-    return qkv, (x0, x1, x2, x3), teach, weights[:4], weights[4:]
+    pref, qkv, x0, x1, x2, x3, teach = outs[:7]
+    weights = [w.reshape((-1, w.shape[-1])) for w in outs[7:]]
+    return pref, qkv, (x0, x1, x2, x3), teach, weights[:4], weights[4:]
 
 
 def binarize(latent):
@@ -1227,19 +1238,19 @@
     own = (seq_at % 2 + 2 * core).astype(jnp.int32)
     width = hidden.shape[2]
 
-    info = segment_info(segments)
-    info = jnp.where(core == seq_at // 2, info, flip(info, fsdp=1))
-    pref = jnp.concatenate([own[None], info]).astype(jnp.int32)
     bias_cols = biases[:2].reshape(2, width, 1)
     latents = (latent_qkv, latent_out, latent_up, latent_down)
     teachers = (teacher_qkv, teacher_out, teacher_up, teacher_down)
     if fsdp == 2:
-        qkv, x_slots, teach, bins, t_weights = entry(
-            bit_list("seq"), bit_list("fsdp")[0], hidden[0], teacher_hidden[0],
+        pref, qkv, x_slots, teach, bins, t_weights = entry(
+            bit_list("seq"), bit_list("fsdp")[0], hidden[0], teacher_hidden[0], segments,
             latents, teachers, bias_cols,
         )
         x = x_slots[0]
     else:
+        info = segment_info(segments)
+        info = jnp.where(core == seq_at // 2, info, flip(info, fsdp=1))
+        pref = jnp.concatenate([own[None], info]).astype(jnp.int32)
         x = swap_groups(hidden[0])
         x_slots = quarters(x)
         bins = [gather_rows(binarize(w)) for w in latents]
@@ -1248,13 +1259,15 @@
         qkv = qkv_project(pref, x_slots, bins[0], bias_cols)
     bin_qkv, bin_out, bin_up, bin_down = bins
     t_qkv, t_out, t_up, t_down = t_weights
-    t_slots = quarters(teach)
-
+    t_along, t_beside = to_slot(teach, 1), to_slot(teach, 2)
     *ctx_slots, ctx_full, lse = attention(pref, qkv)
+    t_along, ctx_slots = lax.optimization_barrier((t_along, ctx_slots))
+    t_slots = (teach, t_along, t_beside, to_slot(t_along, 2))
     ctx_pieces = exchange(ctx_slots)
 
     t_heads = qkv_project(pref, t_slots, t_qkv, None)
     *tctx_slots, _unused, _unused_too = attention(pref, t_heads)
+    tctx_slots, ctx_pieces = lax.optimization_barrier((tctx_slots, ctx_pieces))
     tctx_pieces = exchange(tctx_slots)
 
     gain, shift = norm_gains, norm_shifts

time: 479 us -> 441 us (0.921)
  waiting for transfers between devices: 51.1 us -> 14.9 us
  starting transfers between devices: 14.4 us -> 19.8 us
  between operations: 6.4 us -> 1.28 us
    ppermute x18 -> x17, waiting for transfers between devices: 51.1 us -> 14.9 us  [permute(): return lax.ppermute(values, AXES, pairs)]
    ppermute x18 -> x17, starting transfers between devices: 14.4 us -> 19.8 us  [permute(): return lax.ppermute(values, AXES, pairs)]
  transfers between devices with their start and end apart: 18 -> 17, of which waited for: 7 -> 2; matrix products, arithmetic and copies ran while one was open for 3% -> 3% of each run, Pallas kernels for 52% -> 75%
where the time goes in v4:
time: 441 us; the launch traced here: 434 us
  Pallas kernels  377 us (85%)
  starting transfers between devices  19.8 us (4%)
  waiting for transfers between devices  14.9 us (3%)
  local copies, waits for them, and re-layouts  11.9 us (3%)
  other arithmetic  8.72 us (2%)
    pallas_call x3, Pallas kernels, remote_call(): pl.pallas_call(kernel, in_specs=in_specs, out_specs=out_specs, out_shape=...  205 us
    pallas_call x10, Pallas kernels, call(): pl.pallas_call(kernel, grid_spec=pltpu.PrefetchScalarGridSpec(num_scalar_...  172 us
    ppermute x17, starting transfers between devices, permute(): return lax.ppermute(values, AXES, pairs)  19.8 us
    ppermute x17, waiting for transfers between devices, permute(): return lax.ppermute(values, AXES, pairs)  14.9 us
  transfers between devices with their start and end apart: 17, of which 2 were waited for; matrix products, arithmetic and copies ran while one was open for 3% of the time, Pallas kernels for 75%

profile of v4, /device:TPU:24, one launch (start us, length us, event | category | flops | bytes accessed | tf_op | source)
XLA Modules:
  0.0 433.8 jit_solution(3165421358250702537)
XLA Ops:
  0.6 0.7 slice_bitcast_fusion
  1.4 1.2 copy.25.refs_11_
  2.5 51.4 %shard_map.222 = (s32[3]{0:T(128)}, bf16[576,2560]{1,0:T(8,128)(2,1)}, bf16[640,768]{1,0:T(8,128)(2,1)}, bf16[640,768]{1,0:T(8,128)(2,1)}, bf16[640,768]{1,0:T(8...) custom-call(bf16[640,768]{1,0:T(8,128)(2,1)} %bitcast.25, ...), custom_call_target="tpu_custom_call" | custom-call | flops 49999998976 | bytes 100000000 | tf_op jit(solution)/shard_map/pallas_call | solution.py:907
  54.2 21.3 %shard_map.223 = (bf16[192,640]{1,0:T(8,128)(2,1)}, bf16[192,640]{1,0:T(8,128)(2,1)}, bf16[192,640]{1,0:T(8,128)(2,1)}, bf16[192,640]{1,0:T(8,128)(2,1)}, f32[192,2560]{1,0:T(8,128)}, /*index=5*/f32[3,1,2560]{2,1,0:T(1,128)}) custom-call(s32[3]{0:T(128)} %get-tuple-element.82.refs_0_.pref, bf16[576,2560]{1,0:T(8,128)(2,1)} %get-tuple-element.84.refs_1_.refs_2_.refs_3_, ...), custom_call_target="tpu_custom_call" | custom-call | flops 16000000000 | bytes 11827200 | tf_op jit(solution)/shard_map/pallas_call | solution.py:126
  75.5 1.4 collective-permute-done.refs_2_
  76.8 0.6 fusion.1
  77.5 1.2 collective-permute-start.3
  78.7 0.9 collective-permute-start.5
  79.7 0.9 copy-done.4
  80.6 0.3 copy-done.5
  80.9 8.4 %shard_map.224.refs_1_.refs_2_.refs_3_ = bf16[576,2560]{1,0:T(8,128)(2,1)} custom-call(s32[3]{0:T(128)} %get-tuple-element.82.refs_0_.pref, bf16[640,768]{1,0:T(8,128)(2,1)} %get-tuple-element.83.refs_1_.x, bf16[640,768]{1,0:T(8,128)(2,1)} %copy-done.3, bf16[640,768]{1,0:T(8,128)(2,1)} %copy-done.4, bf16[640,768]{1,0:T(8,128)(2,1)} %copy-done.5, ...), custom_call_target="tpu_custom_call" | custom-call | flops 2264924160 | bytes 17498112 | tf_op jit(solution)/shard_map/pallas_call | solution.py:126
  89.3 21.5 %shard_map.225 = (bf16[192,640]{1,0:T(8,128)(2,1)}, bf16[192,640]{1,0:T(8,128)(2,1)}, bf16[192,640]{1,0:T(8,128)(2,1)}, bf16[192,640]{1,0:T(8,128)(2,1)}, f32[192,2560]{1,0:T(8,128)}, /*index=5*/f32[3,1,2560]{2,1,0:T(1,128)}) custom-call(s32[3]{0:T(128)} %get-tuple-element.82.refs_0_.pref, bf16[576,2560]{1,0:T(8,128)(2,1)} %shard_map.224.refs_1_.refs_2_.refs_3_, ...), custom_call_target="tpu_custom_call" | custom-call | flops 16000000000 | bytes 11827200 | tf_op jit(solution)/shard_map/pallas_call | solution.py:126
  110.9 1.3 collective-permute-start.7
  112.2 0.9 collective-permute-start.9
  113.1 19.5 %shard_map.226 = (bf16[768,640]{1,0:T(8,128)(2,1)}, bf16[640,768]{1,0:T(8,128)(2,1)}, f32[640,768]{1,0:T(8,128)}, f32[640,1]{1,0:T(8,128)}, bf16[640,3072]{1,0:T...) custom-call(s32[3]{0:T(128)} %get-tuple-element.82.refs_0_.pref, ...), custom_call_target="tpu_custom_call" | custom-call | flops 6794772480 | bytes 27364352 | tf_op jit(solution)/shard_map/pallas_call | solution.py:126
  132.6 2.9 collective-permute-start.6
  135.6 0.7 copy-done.15
  136.3 0.1 copy-done.17
  136.4 17.4 %shard_map.227 = (f32[640,768]{1,0:T(8,128)}, bf16[640,768]{1,0:T(8,128)(2,1)}, f32[3,768]{1,0:T(4,128)}) custom-call(s32[3]{0:T(128)} %get-tuple-element.82.refs_0_.pref, bf16[192,640]{1,0:T(8,128)(2,1)} %get-tuple-element.108.c0, bf16[192,640]{1,0:T(8,128)(2,1)} %copy-done.15, bf16[192,640]{1,0:T(8,128)(2,1)} %copy-done.16, bf16[192,640]{1,0:T(8,128)(2,1)} %copy-done.17, ...), custom_call_target="tpu_custom_call" | custom-call | flops 6794772480 | bytes 17522176 | tf_op jit(solution)/shard_map/pallas_call | solution.py:126
  153.8 18.3 %shard_map.228 = (bf16[640,3072]{1,0:T(8,128)(2,1)}, f32[1,3072]{1,0:T(1,128)}, f32[640,768]{1,0:T(8,128)}, bf16[640,768]{1,0:T(8,128)(2,1)}, bf16[192,640]{1,0:...) custom-call(s32[3]{0:T(128)} %get-tuple-element.82.refs_0_.pref, ...), custom_call_target="tpu_custom_call" | custom-call | flops 6794772480 | bytes 27364864 | tf_op jit(solution)/shard_map/pallas_call | solution.py:126
  172.1 0.5 collective-permute-start.10
  172.6 6.5 %collective-permute-start.11 = (bf16[192,640]{1,0:T(8,128)(2,1)}, bf16[192,640]{1,0:T(8,128)(2,1)S(1)}, u32[]{:S(2)}, u32[]{:S(2)}) collective-permute-start(bf16[192,640]{1,0:T(8,128)(2,1)} %get-tuple-element.124), channel_id=1, source_target_pairs={{0,1},{1,0},{2,3},{3,2},{4,5},{5,4},{6,7},{7,6},{8,9},{9,8},{10,11... | collective-permute-start | bytes 737288 | tf_op jit(solution)/shard_map/ppermute | solution.py:47
  179.1 0.4 collective-permute-start.12
  179.5 14.9 %shard_map.233 = (bf16[2,4,384,768]{3,2,1,0:T(8,128)(2,1)}, bf16[8,384,768]{2,1,0:T(8,128)(2,1)}, bf16[2,384,768]{2,1,0:T(8,128)(2,1)}) custom-call(s32[3]{0:T(128)} %get-tuple-element.82.refs_0_.pref, bf16[640,768]{1,0:T(8,128)(2,1)} %get-tuple-element.117.grad_ffn, bf16[640,3072]{1,0:T(8,128)(2,1)} %get-tuple-element.138.gelu, ...), custom_call_target="tpu_custom_call" | custom-call | flops 6794772480 | bytes 22413312 | tf_op jit(solution)/shard_map/pallas_call | solution.py:126
  194.4 0.6 copy-done.18
  195.1 0.1 copy-done.19
  195.2 33.1 %shard_map.229 = (bf16[3,192,640]{2,1,0:T(8,128)(2,1)}, bf16[3,192,640]{2,1,0:T(8,128)(2,1)}, bf16[3,192,640]{2,1,0:T(8,128)(2,1)}, bf16[3,192,640]{2,1,0:T(8,128)(2,1)}) custom-call(s32[3]{0:T(128)} %get-tuple-element.82.refs_0_.pref, bf16[576,2560]{1,0:T(8,128)(2,1)} %get-tuple-element.84.refs_1_.refs_2_.refs_3_, ...), custom_call_target="tpu_custom_call" | custom-call | flops 30000001024 | bytes 14776320 | tf_op jit(solution)/shard_map/pallas_call | solution.py:126
  228.3 1.3 collective-permute-start.13
  229.6 0.2 collective-permute-start.14
  229.8 0.7 collective-permute-start.15
  230.5 8.3 %shard_map.231 = (bf16[3,192,768]{2,1,0:T(8,128)(2,1)}, f32[3,8,768]{2,1,0:T(8,128)}) custom-call(s32[3]{0:T(128)} %get-tuple-element.82.refs_0_.pref, bf16[3,192,640]{2,1,0:T(8,128)(2,1)} %get-tuple-element.128.e0.d0, bf16[3,192,640]{2,1,0:T(8,128)(2,1)} %get-tuple-element.129.d1, bf16[3,192,640]{2,1,0:T(8,128)(2,1)} %get-tuple-element.130.d2, ...), custom_call_target="tpu_custom_call" | custom-call | flops 2264924160 | bytes 7839744 | tf_op jit(solution)/shard_map/pallas_call | solution.py:126
  238.8 52.6 %shard_map.232 = bf16[6,192,768]{2,1,0:T(8,128)(2,1)} custom-call(bf16[3,192,768]{2,1,0:T(8,128)(2,1)} %get-tuple-element.137.refs_0_), custom_call_target="tpu_custom_call" | custom-call | flops 49999998976 | bytes 100000000 | tf_op jit(solution)/shard_map/pallas_call | solution.py:907
  291.4 101.0 %shard_map.234 = (bf16[384,3072]{1,0:T(8,128)(2,1)}, bf16[4,384,768]{2,1,0:T(8,128)(2,1)}, bf16[384,768]{1,0:T(8,128)(2,1)}, f32[16,768]{1,0:T(8,128)}) custom-call(bf16[2,4,384,768]{3,2,1,0:T(8,128)(2,1)} %get-tuple-element.143.refs_0_, bf16[2,4,384,768]{3,2,1,0:T(8,128)(2,1)} %bitcast.34, bf16[2,384,768]{2,1,0:T(8,128)(2,1)} %get-tuple-element.145.refs_2_, ...), custom_call_target="tpu_custom_call" | custom-call | flops 49999998976 | bytes 100000000 | tf_op jit(solution)/shard_map/pallas_call | solution.py:907
  392.5 0.8 copy-done.6
  393.3 0.2 copy-done.7
  393.5 0.2 copy-done.8
  393.8 9.6 %shard_map.230 = bf16[640,768]{1,0:T(8,128)(2,1)} custom-call(s32[3]{0:T(128)} %get-tuple-element.82.refs_0_.pref, bf16[3,192,640]{2,1,0:T(8,128)(2,1)} %get-tuple-element.128.e0.d0, bf16[3,192,640]{2,1,0:T(8,128)(2,1)} %copy-done.6, bf16[3,192,640]{2,1,0:T(8,128)(2,1)} %copy-done.7, bf16[3,192,640]{2,1,0:T(8,128)(2,1)} %copy-done.8, ...), custom_call_target="tpu_custom_call" | custom-call | flops 2264924160 | bytes 17498112 | tf_op jit(solution)/shard_map/pallas_call | solution.py:126
  403.4 2.8 collective-permute-start.16
  406.2 2.7 bitcast_convert_fusion
  408.9 2.8 convert_element_type.23
  411.7 1.1 convert_element_type.20
  412.8 0.7 dynamic_slice.7
  413.5 0.6 constant_dynamic-slice_fusion
  414.1 0.7 fusion
  414.7 2.2 bitcast_convert_fusion.1
  416.9 13.5 %collective-permute-done.16 = bf16[640,768]{1,0:T(8,128)(2,1)S(1)} collective-permute-done((bf16[640,768]{1,0:T(8,128)(2,1)}, bf16[640,768]{1,0:T(8,128)(2,1)S(1)}, u32[]{:S(2)}, u32[]{:S(2)}) %collective-permute-start.16) | collective-permute-done | bytes 983072 | tf_op jit(solution)/shard_map/ppermute | solution.py:47
  430.4 2.2 copy.28
  432.6 0.9 copy.29
  (56 shorter events, 0.4 us)
Async XLA Ops:
  54.0 22.8 %collective-permute-start = (bf16[640,768]{1,0:T(8,128)(2,1)}, bf16[640,768]{1,0:T(8,128)(2,1)S(1)}, u32[]{:S(2)}, u32[]{:S(2)}) collective-permute-start(bf16[640,768]{1,0:T(8,128)(2,1)} %get-tuple-element.83.refs_1_.x), channel_id=1, source_target_pairs={{0,2},{1,3},{2,0},{3,1},{4,6},{5,7},{6,4},{7,5},{8,10},{9,11},{10,... | collective-permute-start | bytes 2949128 | tf_op jit(solution)/shard_map/ppermute | solution.py:47
  54.1 25.6 %collective-permute-start.1 = (bf16[640,768]{1,0:T(8,128)(2,1)}, bf16[640,768]{1,0:T(8,128)(2,1)S(1)}, u32[]{:S(2)}, u32[]{:S(2)}) collective-permute-start(bf16[640,768]{1,0:T(8,128)(2,1)} %get-tuple-element.83.refs_1_.x), channel_id=1, source_target_pairs={{0,1},{1,0},{2,3},{3,2},{4,5},{5,4},{6,7},{7,6},{8,9},{9,8},{10,11... | collective-permute-start | bytes 2949128 | tf_op jit(solution)/shard_map/ppermute | solution.py:47
  54.2 22.7 %copy-start.11 = (f32[4,768]{1,0:T(4,128)S(1)}, f32[4,768]{1,0:T(4,128)}, u32[]{:S(2)}) copy-start(f32[4,768]{1,0:T(4,128)} %param.22) | copy-start | bytes 36868
  76.8 2.8 copy-start.3
  76.8 2.8 collective-permute-start.2
  77.5 33.3 %collective-permute-start.3 = (bf16[192,640]{1,0:T(8,128)(2,1)}, bf16[192,640]{1,0:T(8,128)(2,1)S(1)}, u32[]{:S(2)}, u32[]{:S(2)}) collective-permute-start(bf16[192,640]{1,0:T(8,128)(2,1)} %get-tuple-element.96), channel_id=1, source_target_pairs={{0,2},{1,3},{2,0},{3,1},{4,6},{5,7},{6,4},{7,5},{8,10},{9,11},{10,... | collective-permute-start | bytes 737288 | tf_op jit(solution)/shard_map/ppermute | solution.py:47
  78.7 32.1 %collective-permute-start.4 = (bf16[192,640]{1,0:T(8,128)(2,1)}, bf16[192,640]{1,0:T(8,128)(2,1)S(1)}, u32[]{:S(2)}, u32[]{:S(2)}) collective-permute-start(bf16[192,640]{1,0:T(8,128)(2,1)} %get-tuple-element.97), channel_id=1, source_target_pairs={{0,1},{1,0},{2,3},{3,2},{4,5},{5,4},{6,7},{7,6},{8,9},{9,8},{10,11... | collective-permute-start | bytes 737288 | tf_op jit(solution)/shard_map/ppermute | solution.py:47
  78.7 32.2 %collective-permute-start.5 = (bf16[192,640]{1,0:T(8,128)(2,1)}, bf16[192,640]{1,0:T(8,128)(2,1)S(1)}, u32[]{:S(2)}, u32[]{:S(2)}) collective-permute-start(bf16[192,640]{1,0:T(8,128)(2,1)} %get-tuple-element.98), channel_id=1, source_target_pairs={{0,3},{1,2},{2,1},{3,0},{4,7},{5,6},{6,5},{7,4},{8,11},{9,10},{10,... | collective-permute-start | bytes 737288 | tf_op jit(solution)/shard_map/ppermute | solution.py:47
  79.6 0.9 copy-start.4
  79.6 1.3 copy-start.5
  110.8 2.3 copy-start.12
  110.9 2.2 copy-start.13
  110.9 2.2 copy-start.14
  110.9 24.7 %collective-permute-start.7 = (bf16[192,640]{1,0:T(8,128)(2,1)}, bf16[192,640]{1,0:T(8,128)(2,1)S(1)}, u32[]{:S(2)}, u32[]{:S(2)}) collective-permute-start(bf16[192,640]{1,0:T(8,128)(2,1)} %get-tuple-element.109), channel_id=1, source_target_pairs={{0,2},{1,3},{2,0},{3,1},{4,6},{5,7},{6,4},{7,5},{8,10},{9,11},{10,... | collective-permute-start | bytes 737288 | tf_op jit(solution)/shard_map/ppermute | solution.py:47
  112.2 23.4 %collective-permute-start.8 = (bf16[192,640]{1,0:T(8,128)(2,1)}, bf16[192,640]{1,0:T(8,128)(2,1)S(1)}, u32[]{:S(2)}, u32[]{:S(2)}) collective-permute-start(bf16[192,640]{1,0:T(8,128)(2,1)} %get-tuple-element.110), channel_id=1, source_target_pairs={{0,1},{1,0},{2,3},{3,2},{4,5},{5,4},{6,7},{7,6},{8,9},{9,8},{10,11... | collective-permute-start | bytes 737288 | tf_op jit(solution)/shard_map/ppermute | solution.py:47
  112.2 23.4 %collective-permute-start.9 = (bf16[192,640]{1,0:T(8,128)(2,1)}, bf16[192,640]{1,0:T(8,128)(2,1)S(1)}, u32[]{:S(2)}, u32[]{:S(2)}) collective-permute-start(bf16[192,640]{1,0:T(8,128)(2,1)} %get-tuple-element.111), channel_id=1, source_target_pairs={{0,3},{1,2},{2,1},{3,0},{4,7},{5,6},{6,5},{7,4},{8,11},{9,10},{10,... | collective-permute-start | bytes 737288 | tf_op jit(solution)/shard_map/ppermute | solution.py:47
  132.6 284.3 %collective-permute-start.6 = (bf16[640,768]{1,0:T(8,128)(2,1)}, bf16[640,768]{1,0:T(8,128)(2,1)}, u32[]{:S(2)}, u32[]{:S(2)}) collective-permute-start(bf16[640,768]{1,0:T(8,128)(2,1)} %get-tuple-element.107), channel_id=1, source_target_pairs={{0,0},{1,4},{2,2},{3,6},{4,1},{5,5},{6,3},{7,7},{8,8},{9,12},{10,1... | collective-permute-start | bytes 2949128 | tf_op jit(solution)/shard_map/ppermute | solution.py:47
  135.6 0.7 copy-start.15
  135.6 0.8 copy-start.16
  135.6 0.8 copy-start.17
  172.1 22.2 %collective-permute-start.10 = (bf16[192,640]{1,0:T(8,128)(2,1)}, bf16[192,640]{1,0:T(8,128)(2,1)S(1)}, u32[]{:S(2)}, u32[]{:S(2)}) collective-permute-start(bf16[192,640]{1,0:T(8,128)(2,1)} %get-tuple-element.123), channel_id=1, source_target_pairs={{0,2},{1,3},{2,0},{3,1},{4,6},{5,7},{6,4},{7,5},{8,10},{9,11},{10,... | collective-permute-start | bytes 737288 | tf_op jit(solution)/shard_map/ppermute | solution.py:47
  172.6 21.8 %collective-permute-start.11 = (bf16[192,640]{1,0:T(8,128)(2,1)}, bf16[192,640]{1,0:T(8,128)(2,1)S(1)}, u32[]{:S(2)}, u32[]{:S(2)}) collective-permute-start(bf16[192,640]{1,0:T(8,128)(2,1)} %get-tuple-element.124), channel_id=1, source_target_pairs={{0,1},{1,0},{2,3},{3,2},{4,5},{5,4},{6,7},{7,6},{8,9},{9,8},{10,11... | collective-permute-start | bytes 737288 | tf_op jit(solution)/shard_map/ppermute | solution.py:47
  179.1 15.3 %collective-permute-start.12 = (bf16[192,640]{1,0:T(8,128)(2,1)}, bf16[192,640]{1,0:T(8,128)(2,1)S(1)}, u32[]{:S(2)}, u32[]{:S(2)}) collective-permute-start(bf16[192,640]{1,0:T(8,128)(2,1)} %get-tuple-element.125), channel_id=1, source_target_pairs={{0,3},{1,2},{2,1},{3,0},{4,7},{5,6},{6,5},{7,4},{8,11},{9,10},{10,... | collective-permute-start | bytes 737288 | tf_op jit(solution)/shard_map/ppermute | solution.py:47
  194.4 0.7 copy-start.18
  194.4 0.8 copy-start.19
  194.4 0.8 copy-start.20
  228.3 164.1 %collective-permute-start.13 = (bf16[3,192,640]{2,1,0:T(8,128)(2,1)}, bf16[3,192,640]{2,1,0:T(8,128)(2,1)S(1)}, u32[]{:S(2)}, u32[]{:S(2)}) collective-permute-start(bf16[3,192,640]{2,1,0:T(8,128)(2,1)} %get-tuple-element.129.d1), channel_id=1, source_target_pairs={{0,2},{1,3},{2,0},{3,1},{4,6},{5,7},{6,4},{7,5},{8,10},{9,11},{10,... | collective-permute-start | bytes 2211848 | tf_op jit(solution)/shard_map/ppermute | solution.py:47
  229.6 162.8 %collective-permute-start.14 = (bf16[3,192,640]{2,1,0:T(8,128)(2,1)}, bf16[3,192,640]{2,1,0:T(8,128)(2,1)S(1)}, u32[]{:S(2)}, u32[]{:S(2)}) collective-permute-start(bf16[3,192,640]{2,1,0:T(8,128)(2,1)} %get-tuple-element.130.d2), channel_id=1, source_target_pairs={{0,1},{1,0},{2,3},{3,2},{4,5},{5,4},{6,7},{7,6},{8,9},{9,8},{10,11... | collective-permute-start | bytes 2211848 | tf_op jit(solution)/shard_map/ppermute | solution.py:47
  229.8 162.6 %collective-permute-start.15 = (bf16[3,192,640]{2,1,0:T(8,128)(2,1)}, bf16[3,192,640]{2,1,0:T(8,128)(2,1)S(1)}, u32[]{:S(2)}, u32[]{:S(2)}) collective-permute-start(bf16[3,192,640]{2,1,0:T(8,128)(2,1)} %get-tuple-element.131.d3), channel_id=1, source_target_pairs={{0,3},{1,2},{2,1},{3,0},{4,7},{5,6},{6,5},{7,4},{8,11},{9,10},{10,... | collective-permute-start | bytes 2211848 | tf_op jit(solution)/shard_map/ppermute | solution.py:47
  392.4 0.9 copy-start.6
  392.4 1.1 copy-start.7
  392.4 1.3 copy-start.8
  393.8 12.4 %copy-start.1 = (bf16[4,384,768]{2,1,0:T(8,128)(2,1)S(1)}, bf16[4,384,768]{2,1,0:T(8,128)(2,1)}, u32[]{:S(2)}) copy-start(bf16[4,384,768]{2,1,0:T(8,128)(2,1)} %get-tuple-element.151) | copy-start | bytes 7077892
  403.4 27.0 %collective-permute-start.16 = (bf16[640,768]{1,0:T(8,128)(2,1)}, bf16[640,768]{1,0:T(8,128)(2,1)S(1)}, u32[]{:S(2)}, u32[]{:S(2)}) collective-permute-start(bf16[640,768]{1,0:T(8,128)(2,1)} %shard_map.230), channel_id=1, source_target_pairs={{0,0},{1,4},{2,2},{3,6},{4,1},{5,5},{6,3},{7,7},{8,8},{9,12},{10,1... | collective-permute-start | bytes 2949128 | tf_op jit(solution)/shard_map/ppermute | solution.py:47
  406.2 2.7 copy-start.10
  406.2 2.7 copy-start
  408.9 2.8 copy-start.9
  408.9 5.8 %copy-start.2 = (bf16[6,192,768]{2,1,0:T(8,128)(2,1)S(1)}, bf16[6,192,768]{2,1,0:T(8,128)(2,1)}, u32[]{:S(2)}) copy-start(bf16[6,192,768]{2,1,0:T(8,128)(2,1)} %shard_map.232) | copy-start | bytes 5308420

commit v5 on v4

--- a/solution.py
+++ b/solution.py
@@ -205,7 +205,11 @@
     return (keys < border) == (queries < border)
 
 
-def attention_kernel(scale, pref, q_ref, k_ref, v_ref, o0, o1, o2, o3, cf_ref, lse_ref, qs, ks, vs, cs, st):
+def attention_kernel(scale, kept, pref, q_ref, k_ref, v_ref, o0, o1, o2, o3, cf_ref, lse_ref, *rest):
+    if kept:
+        qs, ks, vs, cs, st = rest
+    else:
+        cs, st, qs, ks, vs = rest
     own, shift, border = pref[0], pref[1], pref[2]
     total = q_ref.shape[1]
     cont = total - PROMPT
@@ -257,26 +261,29 @@
         out[...] = cs[:, pl.ds(first, tok)]
 
 
-def attention(pref, qkv):
+def attention(pref, qkv, kept):
     total = qkv.shape[1]
     heads = HEADS // 4
     hdim = qkv.shape[0] // (3 * heads)
     rows = qkv.shape[0] // 3
     scale = LOG2E / hdim**0.5
     return call(
-        lambda *refs: attention_kernel(scale, *refs),
+        lambda *refs: attention_kernel(scale, kept, *refs),
         pref,
         [qkv] * 3,
         [pl.BlockSpec((hdim, total), lambda h, i, o=o: (h + o * heads, 0)) for o in range(3)],
         [shape_of((rows, total // 4), BF)] * 4
-        + [shape_of((rows, total), F32), shape_of((heads, 1, total), F32)],
+        + [shape_of((rows, total), F32), shape_of((heads, 1, total), F32)]
+        + [shape_of((rows, total), BF)] * (3 if kept else 0),
         [pl.BlockSpec((hdim, total // 4), lambda h, i: (h, 0))] * 4
         + [
             pl.BlockSpec((hdim, total), lambda h, i: (h, 0)),
             pl.BlockSpec((None, 1, total), lambda h, i: (h, 0, 0)),
-        ],
+        ]
+        + [pl.BlockSpec((hdim, total), lambda h, i: (h, 0))] * (3 if kept else 0),
         (heads,),
-        [pltpu.VMEM((hdim, total), BF)] * 4 + [pltpu.VMEM((2, PROMPT + LONG, QB), F32)],
+        [pltpu.VMEM((hdim, total), BF), pltpu.VMEM((2, PROMPT + LONG, QB), F32)]
+        + [pltpu.VMEM((hdim, total), BF)] * (0 if kept else 3),
         16 * 10**9,
         12 * 10**6,
     )
@@ -723,15 +730,6 @@
     return upper, {name: at + mask * (1 - 2 * upper)}
 
 
-def greet(bits):
-    barrier = pltpu.get_barrier_semaphore()
-    for bit in bits:
-        pl.semaphore_signal(
-            barrier, inc=1, device_id=place(bit)[1], device_id_type=pl.DeviceIdType.MESH
-        )
-    pl.semaphore_wait(barrier, len(bits))
-
-
 class Copies:
     def __init__(self, send, recv, local):
         self.send, self.recv, self.local_sem = send, recv, local
@@ -839,67 +837,9 @@
         sums[n + 1] = sums[n] + far[n]
 
 
-def run_flows(flows, step):
-    events = []
-    for delay, flow in flows:
-        next(flow)
-        events.append([delay, len(events), flow])
-    while events:
-        events.sort(key=lambda e: e[:2])
-        event = events[0]
-        try:
-            next(event[2])
-            event[0] += step
-        except StopIteration:
-            events.pop(0)
-
-
 def rotate(items, count):
     count %= len(items)
     return items[count:] + items[:count]
-
-
-def sum_kernel(
-    dp, seq, core, down, up, out, two, one, bias, heads, down_sum, up_sum, out_sum, totals,
-    work, near, far, full, sums, sums_far, send, recv, local,
-):
-    greet(dp + seq + [core])
-    copies = Copies(send, recv, local)
-    side_of = place(core)[0]
-    count, half, width = down.shape[1:]
-    pieces = [(up.at[side_of, p], up.at[1 - side_of, p], up_sum.at[p]) for p in range(count)]
-    pieces += [
-        (
-            down.at[side_of, p],
-            down.at[1 - side_of, p],
-            down_sum.at[:, pl.ds(p * width, width)],
-        )
-        for p in range(count)
-    ]
-    pieces.append((out.at[side_of], out.at[1 - side_of], out_sum))
-    first = dp + seq[:1]
-    flows = []
-    for n, (own, other, result) in enumerate(pieces):
-        bits = rotate(first, n) + seq[1:]
-        flow = sum_flow(
-            copies, own, other, work.at[n], near.at[n], far.at[n], full.at[n], result, core, bits
-        )
-        flows.append((n // len(first), flow))
-    sums[0] = jnp.zeros(sums.shape[1:], F32)
-    sums[0, 0:1] = heads[0, 0:1]
-    sums[0, 1:2] = heads[2, 0:1]
-    sums[0, 2:3] = one[2:3]
-    sums[0, 3:4] = two[2:3]
-    sums[0, 4:5] = one[0:1]
-    sums[0, 5:6] = two[0:1]
-    sums[0, 6:7] = one[1:2]
-    sums[0, 7:8] = two[1:2]
-    for p in range(count):
-        sums[0, 8 + p : 9 + p] = bias[:, p * width : (p + 1) * width]
-    flows.append((0.5, vector_flow(copies, sums, sums_far, [core] + dp + seq)))
-    run_flows(flows, 1.5)
-    totals[...] = sums[sums.shape[0] - 1]
-    copies.finish()
 
 
 def remote_call(kernel, args, in_specs, outs, out_specs, scratch, copies, local, number):
@@ -919,82 +859,6 @@
 
 ANY = pl.BlockSpec(memory_space=pl.ANY)
 IN_VMEM = pl.BlockSpec(memory_space=pltpu.VMEM)
-
-
-def sum_grads(dp, seq, core, down, up, out, two, one, bias, heads):
-    sides, count, half, width = down.shape
-    pieces, steps = 2 * count + 1, len(dp) + len(seq)
-    lines = 16
-    return remote_call(
-        lambda *refs: sum_kernel(dp, seq, core, *refs),
-        [down, up, out, two, one, bias, heads],
-        [ANY] * 3 + [IN_VMEM] * 4,
-        [
-            shape_of((half, count * width), BF),
-            shape_of((count, half, width), BF),
-            shape_of((half, width), BF),
-            shape_of((lines, width), F32),
-        ],
-        [ANY] * 3 + [IN_VMEM],
-        [pltpu.VMEM((pieces, half, width), BF)] * 4
-        + [pltpu.VMEM((steps + 2, lines, width), F32), pltpu.VMEM((steps + 1, lines, width), F32)],
-        pieces * (1 + 2 * steps) + steps + 1,
-        2 * pieces,
-        1,
-    )
-
-
-def head_sum_kernel(dp, seq, core, heads, result, work, far, full, send, recv, local):
-    greet(dp + seq + [core])
-    copies = Copies(send, recv, local)
-    side_of, partner = place(core)
-    along = place(seq[0])[0]
-    rows = dp + seq[1:]
-
-    def flow(n):
-        if n == 1:
-            copy = copies.remote(heads.at[2 - 2 * side_of], work.at[n], partner)
-            yield
-            copy.wait_recv()
-        else:
-            load = copies.local(heads.at[n // 2 + side_of], work.at[n])
-            yield
-            load.wait()
-        bits = (rotate(dp, n) if n < 2 else dp) + seq[1:]
-        mine = full.at[2 * n + along]
-        parts = yield from scatter_sum(copies, work.at[n], far.at[n], mine, bits)
-        steps = [(bit, kept, False) for bit, kept in reversed(parts)]
-        cut = len(steps) if n == 2 else 1
-        held = steps[cut][1] if n < 2 else (0, mine.shape[0], 0, mine.shape[1])
-        steps = steps[:cut] + [(seq[0], held, False)] + [(b, k, True) for b, k, _ in steps[cut:]]
-        for bit, (row, size, col, cols), both in steps:
-            first, count = (2 * n, 2) if both else (2 * n + along, 1)
-            part = full.at[pl.ds(first, count), pl.ds(row, size), pl.ds(col, cols)]
-            copy = copies.remote(part, part, place(bit)[1])
-            yield
-            copy.wait_recv()
-        store = copies.local(full.at[pl.ds(2 * n, 2)], result.at[pl.ds(2 * n, 2)])
-        yield
-        store.wait()
-
-    run_flows([(0, flow(0)), (0, flow(2)), (0, flow(1))], 1.0)
-    copies.finish()
-
-
-def head_sums_of(dp, seq, core, heads):
-    _, rows, width = heads.shape
-    steps = len(dp) + len(seq) - 1
-    return remote_call(
-        lambda *refs: head_sum_kernel(dp, seq, core, *refs),
-        [heads],
-        [ANY],
-        shape_of((6, rows, width), BF),
-        ANY,
-        [pltpu.VMEM((3, rows, width), BF)] * 2 + [pltpu.VMEM((6, rows, width), BF)],
-        3 * (2 * steps + 1) + 1,
-        5,
-        2,
-    )
 
 
 def binarize_rows(source, target):
@@ -1206,6 +1070,331 @@
     return pref, qkv, (x0, x1, x2, x3), teach, weights[:4], weights[4:]
 
 
+class Pump:
+    def __init__(self, step):
+        self.step, self.events = step, []
+
+    def add(self, time, flow):
+        gap = next(flow)
+        self.events.append([time + (gap or 0), len(self.events), flow])
+
+    def run(self, time=1e9):
+        while self.events:
+            event = min(self.events, key=lambda e: e[:2])
+            if event[0] > time:
+                return
+            try:
+                gap = next(event[2])
+                event[0] += self.step if gap is None else gap
+            except StopIteration:
+                self.events.remove(event)
+
+
+def head_flow(copies, n, gh, work, far, full, result, seq, core, dp):
+    side_of, partner = place(core)
+    along = place(seq[0])[0]
+    if n == 1:
+        copy = copies.remote(gh.at[2 - 2 * side_of], work, partner)
+        yield
+        copy.wait_recv()
+    else:
+        load = copies.local(gh.at[n // 2 + side_of], work)
+        yield
+        load.wait()
+    bits = (rotate(dp, n) if n < 2 else dp) + seq[1:]
+    mine = full.at[2 * n + along]
+    parts = yield from scatter_sum(copies, work, far, mine, bits)
+    steps = [(bit, kept, False) for bit, kept in reversed(parts)]
+    cut = len(steps) if n == 2 else 1
+    held = steps[cut][1] if n < 2 else (0, mine.shape[0], 0, mine.shape[1])
+    steps = steps[:cut] + [(seq[0], held, False)] + [(b, k, True) for b, k, _ in steps[cut:]]
+    for bit, (row, size, col, cols), both in steps:
+        first, count = (2 * n, 2) if both else (2 * n + along, 1)
+        part = full.at[pl.ds(first, count), pl.ds(row, size), pl.ds(col, cols)]
+        copy = copies.remote(part, part, place(bit)[1])
+        yield
+        copy.wait_recv()
+    store = copies.local(full.at[pl.ds(2 * n, 2)], result.at[pl.ds(2 * n, 2)])
+    yield
+    store.wait()
+
+
+def tail_kernel(
+    dp, seq, core, scale, pref, down, up, out, two, one, bias,
+    q_in, k_in, v_in, g0, g1, g2, g3, cf_in, lse, x0, x1, x2, x3, w_in, res_in,
+    down_sum, up_sum, out_sum, totals, qkv_sum, hidden_out,
+    work, near, far, full, sums, sums_far, gh, h_work, h_far, h_full,
+    qs, ks, vs, gp, cf, xs, weight, res, qa, ka, va, ga, gs, dqs, dks, dvs, dn, er, acc, hid,
+    send, recv, local,
+):
+    shift, border = pref[1], pref[2]
+    heads_all, total = qs.shape
+    hdim = qa.shape[0] - AUG
+    heads = heads_all // hdim
+    tok = total // 4
+    width = xs.shape[2]
+    cont, others = total - PROMPT, PROMPT + LONG
+    back = lax.rem(cont - shift, cont)
+    along, next_chip = place(seq[0])
+    side_of, sibling = place(core)
+    across = {**next_chip, **sibling}
+    half = lax.div(lax.axis_index("seq"), jnp.int32(2))
+    stays, moves = half == side_of, half != side_of
+    partner = {"seq": 2 * side_of + along, "fsdp": half}
+    own = along + 2 * side_of
+
+    def place_of(slot):
+        return (1 - along if slot % 2 else along) + 2 * (1 - side_of if slot // 2 else side_of)
+
+    copies = Copies(send, recv, local)
+    first_loads = [
+        copies.local(source, target)
+        for source, target in (
+            (g0, gp.at[0]), (g1, gp.at[1]), (g2, gp.at[2]), (g3, gp.at[3]),
+            (q_in, qs), (k_in, ks), (v_in, vs), (cf_in, cf),
+        )
+    ]
+
+    mesh = pl.DeviceIdType.MESH
+    barrier = pltpu.get_barrier_semaphore()
+    friends = [place(bit)[1] for bit in dp + seq] + [sibling, across]
+    for device in friends:
+        pl.semaphore_signal(barrier, inc=1, device_id=device, device_id_type=mesh)
+
+    @pl.when(moves)
+    def _():
+        pl.semaphore_signal(barrier, inc=1, device_id=partner, device_id_type=mesh)
+        pl.semaphore_wait(barrier, len(friends) + 1)
+
+    @pl.when(stays)
+    def _():
+        pl.semaphore_wait(barrier, len(friends))
+
+    pump = Pump(6.5)
+    count, rows_half = down.shape[1:3]
+    ups = [(up.at[side_of, p], up.at[1 - side_of, p], up_sum.at[p]) for p in range(count)]
+    downs = [
+        (
+            down.at[side_of, p],
+            down.at[1 - side_of, p],
+            down_sum.at[:, pl.ds(p * width, width)],
+        )
+        for p in range(count)
+    ]
+    queue = [(dp + seq, p, k) for k, p in enumerate(ups)]
+    queue += [(dp[::-1] + seq, p, k) for k, p in enumerate(downs)]
+    queue.append((seq[:1] + dp + seq[1:], (out.at[side_of], out.at[1 - side_of], out_sum), 1))
+    queue.sort(key=lambda item: item[2])
+    for n, (bits, (mine, theirs, result), k) in enumerate(queue):
+        flow = sum_flow(
+            copies, mine, theirs, work.at[n], near.at[n], far.at[n], full.at[n], result, core, bits
+        )
+        pump.add(2.0 + 5 * k, flow)
+
+    late_loads = [
+        copies.local(source, target)
+        for source, target in (
+            (x0, xs.at[0]), (x1, xs.at[1]), (x2, xs.at[2]), (x3, xs.at[3]),
+            (w_in, weight), (res_in, res),
+        )
+    ]
+    for copy in first_loads:
+        copy.wait()
+
+    row = lax.broadcasted_iota(jnp.int32, (AUG, total), 0)
+    ones = jnp.where(row < 3, 1.0, 0.0).astype(BF)
+    ka[hdim:, :] = ones
+    va[hdim:, :] = ones
+    clock = 1.0
+    pieces = {1: [], 2: [], 3: []}
+    devices = {1: next_chip, 2: sibling, 3: across}
+    for h in range(heads):
+        lines = slice(h * hdim, (h + 1) * hdim)
+        for j in range(4):
+            gs[:, pl.ds(pl.multiple_of(place_of(j) * tok, 128), tok)] = gp[j, lines, :].astype(F32)
+        qa[:hdim, :] = qs[lines, :]
+        ka[:hdim, :] = ks[lines, :]
+        va[:hdim, :] = vs[lines, :]
+        grad = roll_cont(gs[...], back)
+        ga[:hdim, :] = grad.astype(BF)
+        ga[hdim:, :] = thirds(-jnp.sum(grad * cf[lines, :], axis=0, keepdims=True))
+        qa[hdim:, :] = thirds(lse[h] * (-1.0 / scale))
+        seen = set()
+        for start, parts in block_list(total, QB):
+            queries = slice(start, start + QB)
+            grad_q = None
+            for lo, hi in parts:
+                for key in range(lo, hi, KB):
+                    keys = slice(key, key + KB)
+                    value = dot(qa[:, queries], ka[:, keys], 0, 0) * scale
+                    if lo >= others:
+                        mask = same_segment((QB, KB), 1, key - others, start - others, border)
+                        value = jnp.where(mask, value, -1e30)
+                    prob = jnp.exp2(value)
+                    grad_p = dot(ga[:, queries], va[:, keys], 0, 0)
+                    grad_s = (prob * grad_p).astype(BF)
+                    grad_v = dot(ga[:hdim, queries], prob.astype(BF), 1, 0)
+                    grad_k = dot(qa[:hdim, queries], grad_s, 1, 0)
+                    part = dot(ka[:hdim, keys], grad_s, 1, 1)
+                    grad_q = part if grad_q is None else grad_q + part
+                    if key in seen:
+                        dvs[:, keys] += grad_v
+                        dks[:, keys] += grad_k
+                    else:
+                        dvs[:, keys] = grad_v
+                        dks[:, keys] = grad_k
+                        seen.add(key)
+                    clock += 0.65
+            dqs[:, queries] = grad_q
+            pump.run(clock)
+        inv = 1.0 / hdim**0.5
+        for part, (ref, factor) in enumerate(((dqs, inv), (dks, inv), (dvs, 1.0))):
+            gs[...] = roll_cont(ref[...] * factor, shift)
+            for j in range(4):
+                there = pl.ds(pl.multiple_of(place_of(j) * tok, 128), tok)
+                dn[j, part, lines, :] = gs[:, there].astype(BF)
+        for j in (1, 3, 2):
+            at = pl.ds(h * hdim, hdim)
+            copy = copies.remote(dn.at[j, :, at, :], er.at[j - 1, :, at, :], devices[j])
+            pieces[j].append(copy)
+        clock += 1.5
+        pump.run(clock)
+
+    for copy in late_loads:
+        copy.wait()
+    rows = width // 4
+    one_rows = jnp.ones((8, tok), BF)
+    counts = []
+    for o in range(3):
+        value, line = None, None
+        for j in range(4):
+            part = dot(dn[j, o], jnp.clip(xs[j], -CLIP, CLIP), 1, 0)
+            ends = dot(one_rows, dn[j, o], 1, 1)
+            value = part if value is None else value + part
+            line = ends if line is None else line + ends
+        gh[o] = value.astype(BF)
+        counts.append(line)
+        clock += 2.7
+        pump.run(clock)
+    sums[0] = jnp.zeros(sums.shape[1:], F32)
+    for j in range(4):
+
+        @pl.when(own == j)
+        def _():
+            sums[0, 0:1, j * rows : (j + 1) * rows] = counts[0][0:1]
+            sums[0, 1:2, j * rows : (j + 1) * rows] = counts[2][0:1]
+
+    sums[0, 2:3] = one[2:3]
+    sums[0, 3:4] = two[2:3]
+    sums[0, 4:5] = one[0:1]
+    sums[0, 5:6] = two[0:1]
+    sums[0, 6:7] = one[1:2]
+    sums[0, 7:8] = two[1:2]
+    for p in range(count):
+        sums[0, 8 + p : 9 + p] = bias[:, p * width : (p + 1) * width]
+
+    swap = copies.plan(hid, hidden_out, partner)
+    keep = copies.plan_local(hid, hidden_out)
+
+    def hidden_flow():
+        yield 0.0
+        for gap, j in ((2.0, 0), (5.0, 2), (3.0, 1), (0.0, 3)):
+            for copy in pieces.get(j, []):
+                copy.wait_recv()
+            part = None
+            for o in range(3):
+                at = pl.multiple_of(o * width + place_of(j) * rows, 16)
+                source = dn[0, o] if j == 0 else er[j - 1, o]
+                piece = dot(source, weight[pl.ds(at, rows), :], 0, 0)
+                part = piece if part is None else part + piece
+            if j == 0:
+                acc[...] = part
+            elif j != 3:
+                acc[...] += part
+            else:
+                size = jnp.abs(xs[0].astype(F32))
+                pull = jnp.where(size < CLIP, 1.0, jnp.where(size == CLIP, 0.5, 0.0))
+                hid[...] = (res[...] + (acc[...] + part) * pull).astype(BF)
+            yield gap
+
+        @pl.when(moves)
+        def _():
+            swap.start()
+
+        @pl.when(stays)
+        def _():
+            keep.start()
+
+        yield 30.0
+
+        @pl.when(moves)
+        def _():
+            swap.wait_recv()
+            swap.wait_send()
+
+        @pl.when(stays)
+        def _():
+            keep.wait()
+
+    pump.add(clock, hidden_flow())
+    for n in (0, 2, 1):
+        flow = head_flow(
+            copies, n, gh, h_work.at[n], h_far.at[n], h_full, qkv_sum, seq, core, dp
+        )
+        pump.add(clock + 1, flow)
+    pump.add(clock + 1, vector_flow(copies, sums, sums_far, [core] + dp + seq))
+    pump.run()
+    totals[...] = sums[sums.shape[0] - 1]
+    copies.finish()
+
+
+def tail(
+    dp, seq, core, pref, down, up, out, two, one, bias, rolled, grads, cf, lse, slots, weight, res
+):
+    sides, count, half, width = down.shape
+    pieces, steps, lines = 2 * count + 1, len(dp) + len(seq), 16
+    rows, total = rolled[0].shape
+    tok = total // 4
+    heads = HEADS // 4
+    hdim = rows // heads
+    scale = LOG2E / hdim**0.5
+    smem = pl.BlockSpec(memory_space=pltpu.SMEM)
+    return remote_call(
+        lambda *refs: tail_kernel(dp, seq, core, scale, *refs),
+        [pref, down, up, out, two, one, bias]
+        + list(rolled)
+        + list(grads)
+        + [cf, lse]
+        + list(slots)
+        + [weight, res],
+        [smem] + [ANY] * 3 + [IN_VMEM] * 3 + [ANY] * 8 + [IN_VMEM] + [ANY] * 6,
+        [
+            shape_of((half, count * width), BF),
+            shape_of((count, half, width), BF),
+            shape_of((half, width), BF),
+            shape_of((lines, width), F32),
+            shape_of((6, rows, width), BF),
+            shape_of((tok, width), BF),
+        ],
+        [ANY] * 3 + [IN_VMEM] + [ANY] * 2,
+        [pltpu.VMEM((pieces, half, width), BF)] * 4
+        + [pltpu.VMEM((steps + 2, lines, width), F32), pltpu.VMEM((steps + 1, lines, width), F32)]
+        + [pltpu.VMEM((3, rows, width), BF)] * 3
+        + [pltpu.VMEM((6, rows, width), BF)]
+        + [pltpu.VMEM((rows, total), BF)] * 3
+        + [pltpu.VMEM((4, rows, tok), BF), pltpu.VMEM((rows, total), F32)]
+        + [pltpu.VMEM((4, tok, width), BF), pltpu.VMEM(weight.shape, BF)]
+        + [pltpu.VMEM((tok, width), F32)]
+        + [pltpu.VMEM((hdim + AUG, total), BF)] * 4
+        + [pltpu.VMEM((hdim, total), F32)] * 4
+        + [pltpu.VMEM((4, 3, rows, tok), BF), pltpu.VMEM((3, 3, rows, tok), BF)]
+        + [pltpu.VMEM((tok, width), F32), pltpu.VMEM((tok, width), BF)],
+        pieces * (1 + 2 * steps) + steps + 1 + 3 * heads + 1 + 3 * (2 * steps - 1) + 1,
+        2 * pieces + 14 + 1 + 5,
+        4,
+    )
+
+
 def binarize(latent):
     row_scale = jnp.mean(jnp.abs(latent), axis=1, keepdims=True)
     return (row_scale * jnp.sign(latent)).astype(BF)
@@ -1260,13 +1449,13 @@
     bin_qkv, bin_out, bin_up, bin_down = bins
     t_qkv, t_out, t_up, t_down = t_weights
     t_along, t_beside = to_slot(teach, 1), to_slot(teach, 2)
-    *ctx_slots, ctx_full, lse = attention(pref, qkv)
+    *ctx_slots, ctx_full, lse, q_roll, k_roll, v_roll = attention(pref, qkv, True)
     t_along, ctx_slots = lax.optimization_barrier((t_along, ctx_slots))
     t_slots = (teach, t_along, t_beside, to_slot(t_along, 2))
     ctx_pieces = exchange(ctx_slots)
 
     t_heads = qkv_project(pref, t_slots, t_qkv, None)
-    *tctx_slots, _unused, _unused_too = attention(pref, t_heads)
+    *tctx_slots, _unused, _unused_too = attention(pref, t_heads, False)
     tctx_slots, ctx_pieces = lax.optimization_barrier((tctx_slots, ctx_pieces))
     tctx_pieces = exchange(tctx_slots)
 
@@ -1289,29 +1478,20 @@
         pref, grad_ffn, gelu, grad_hidden, act_one, grad_attn, ctx
     )
     dp_bits, seq_bits, fsdp_bits = bit_list("dp"), bit_list("seq"), bit_list("fsdp")
-    dqkv_slots = attention_back(pref, qkv, gctx_pieces, ctx_full, lse)
-    dqkv_pieces = exchange(dqkv_slots)
-    grad_heads, head_sums = qkv_grad(pref, dqkv_slots, x_slots)
     rows, hidden_units = width // 4, up_bias.shape[0]
-    _, count, half, _ = grad_down.shape
 
     if fsdp == 2:
-        total_down, total_up, total_out, vectors = sum_grads(
-            dp_bits,
-            seq_bits,
-            fsdp_bits[0],
-            grad_down,
-            grad_up.reshape(grad_down.shape),
-            grad_out,
-            vec_two,
-            vec_one,
-            grad_up_bias,
-            head_sums,
+        total_down, total_up, total_out, vectors, total_qkv, hidden_grad = tail(
+            dp_bits, seq_bits, fsdp_bits[0], pref,
+            grad_down, grad_up.reshape(grad_down.shape), grad_out, vec_two, vec_one, grad_up_bias,
+            (q_roll, k_roll, v_roll), gctx_pieces, ctx_full, lse, x_slots, bin_qkv, grad_res,
         )
         total_up = total_up.reshape(-1, width)
-        hidden_grad = swap_groups(input_grad(pref, dqkv_pieces, bin_qkv, grad_res, x))
-        total_qkv = head_sums_of(dp_bits, seq_bits, fsdp_bits[0], grad_heads).reshape(-1, width)
+        total_qkv = total_qkv.reshape(-1, width)
     else:
+        dqkv_slots = attention_back(pref, qkv, gctx_pieces, ctx_full, lse)
+        dqkv_pieces = exchange(dqkv_slots)
+        grad_heads, head_sums = qkv_grad(pref, dqkv_slots, x_slots)
         hidden_grad = swap_groups(input_grad(pref, dqkv_pieces, bin_qkv, grad_res, x))
 
         def reduce_grad(value, bits):

time: 441 us -> 376 us (0.85)
  Pallas kernels: 377 us -> 336 us
  waiting for transfers between devices: 14.9 us -> 0.97 us
  starting transfers between devices: 19.8 us -> 10 us
    pallas_call x10 -> x7, Pallas kernels: 172 us -> 122 us  [call(): pl.pallas_call(kernel, grid_spec=pltpu.PrefetchScalarGridSpec(num_scalar_...]
    ppermute x17 -> x13, waiting for transfers between devices: 14.9 us -> 0.97 us  [permute(): return lax.ppermute(values, AXES, pairs)]
    ppermute x17 -> x13, starting transfers between devices: 19.8 us -> 10 us  [permute(): return lax.ppermute(values, AXES, pairs)]
    pallas_call x3 -> x2, Pallas kernels: 205 us -> 214 us  [remote_call(): pl.pallas_call(kernel, in_specs=in_specs, out_specs=out_specs, out_shape=...]
  transfers between devices with their start and end apart: 17 -> 13, of which waited for: 2 -> 1; matrix products, arithmetic and copies ran while one was open for 3% -> 4% of each run, Pallas kernels for 75% -> 77%
where the time goes in v5:
time: 376 us; the launch traced here: 368 us
  Pallas kernels  336 us (89%)
  other arithmetic  10.4 us (3%)
  starting transfers between devices  10 us (3%)
  local copies, waits for them, and re-layouts  9.31 us (2%)
    pallas_call x2, Pallas kernels, remote_call(): pl.pallas_call(kernel, in_specs=in_specs, out_specs=out_specs, out_shape=...  214 us
    pallas_call x7, Pallas kernels, call(): pl.pallas_call(kernel, grid_spec=pltpu.PrefetchScalarGridSpec(num_scalar_...  122 us
    ppermute x13, starting transfers between devices, permute(): return lax.ppermute(values, AXES, pairs)  10 us
  transfers between devices with their start and end apart: 13, of which 1 were waited for; matrix products, arithmetic and copies ran while one was open for 4% of the time, Pallas kernels for 77%

profile of v5, /device:TPU:24, one launch (start us, length us, event | category | flops | bytes accessed | tf_op | source)
XLA Modules:
  0.0 368.2 jit_solution(6358728785968564210)
XLA Ops:
  0.6 0.7 slice_bitcast_fusion
  1.4 1.2 copy.25.refs_11_
  2.5 51.5 %shard_map.222 = (s32[3]{0:T(128)}, bf16[576,2560]{1,0:T(8,128)(2,1)}, bf16[640,768]{1,0:T(8,128)(2,1)}, bf16[640,768]{1,0:T(8,128)(2,1)}, bf16[640,768]{1,0:T(8...) custom-call(bf16[640,768]{1,0:T(8,128)(2,1)} %bitcast.26, ...), custom_call_target="tpu_custom_call" | custom-call | flops 49999998976 | bytes 100000000 | tf_op jit(solution)/shard_map/pallas_call | solution.py:847
  54.0 0.1 collective-permute-start
  54.1 0.1 collective-permute-start.1
  54.2 0.0 copy-start.8
  54.2 21.7 %shard_map.223 = (bf16[192,640]{1,0:T(8,128)(2,1)}, bf16[192,640]{1,0:T(8,128)(2,1)}, bf16[192,640]{1,0:T(8,128)(2,1)}, bf16[192,640]{1,0:T(8,128)(2,1)}, f32[19...) custom-call(s32[3]{0:T(128)} %get-tuple-element.81.refs_0_.pref, ...), custom_call_target="tpu_custom_call" | custom-call | flops 16000000000 | bytes 14776320 | tf_op jit(solution)/shard_map/pallas_call | solution.py:126
  75.9 0.9 collective-permute-done.refs_2_
  76.8 0.6 fusion.1
  77.5 1.6 collective-permute-start.3
  79.1 0.5 collective-permute-start.5
  79.6 0.0 collective-permute-done.2.refs_4_
  79.6 0.0 copy-start.4
  79.7 0.9 copy-done.3
  80.6 0.3 copy-done.4
  80.9 8.4 %shard_map.224.refs_1_.refs_2_.refs_3_ = bf16[576,2560]{1,0:T(8,128)(2,1)} custom-call(s32[3]{0:T(128)} %get-tuple-element.81.refs_0_.pref, bf16[640,768]{1,0:T(8,128)(2,1)} %get-tuple-element.82.refs_1_.x, bf16[640,768]{1,0:T(8,128)(2,1)} %copy-done.2, bf16[640,768]{1,0:T(8,128)(2,1)} %copy-done.3, bf16[640,768]{1,0:T(8,128)(2,1)} %copy-done.4, ...), custom_call_target="tpu_custom_call" | custom-call | flops 2264924160 | bytes 17498112 | tf_op jit(solution)/shard_map/pallas_call | solution.py:126
  89.3 21.2 %shard_map.225 = (bf16[192,640]{1,0:T(8,128)(2,1)}, bf16[192,640]{1,0:T(8,128)(2,1)}, bf16[192,640]{1,0:T(8,128)(2,1)}, bf16[192,640]{1,0:T(8,128)(2,1)}, f32[192,2560]{1,0:T(8,128)}, /*index=5*/f32[3,1,2560]{2,1,0:T(1,128)}) custom-call(s32[3]{0:T(128)} %get-tuple-element.81.refs_0_.pref, bf16[576,2560]{1,0:T(8,128)(2,1)} %shard_map.224.refs_1_.refs_2_.refs_3_, ...), custom_call_target="tpu_custom_call" | custom-call | flops 16000000000 | bytes 11827200 | tf_op jit(solution)/shard_map/pallas_call | solution.py:126
  110.5 0.0 collective-permute-done.4.c2
  110.6 0.0 collective-permute-done.5.c3
  110.6 1.7 collective-permute-start.7
  112.3 0.5 collective-permute-start.9
  112.8 19.5 %shard_map.226 = (bf16[768,640]{1,0:T(8,128)(2,1)}, bf16[640,768]{1,0:T(8,128)(2,1)}, f32[640,768]{1,0:T(8,128)}, f32[640,1]{1,0:T(8,128)}, bf16[640,3072]{1,0:T...) custom-call(s32[3]{0:T(128)} %get-tuple-element.81.refs_0_.pref, ...), custom_call_target="tpu_custom_call" | custom-call | flops 6794772480 | bytes 27364352 | tf_op jit(solution)/shard_map/pallas_call | solution.py:126
  132.3 3.3 collective-permute-start.6
  135.7 0.0 collective-permute-done.8.c2
  135.7 0.7 copy-done.15
  136.4 0.1 copy-done.16
  136.5 0.1 copy-done.17
  136.6 17.6 %shard_map.227 = (f32[640,768]{1,0:T(8,128)}, bf16[640,768]{1,0:T(8,128)(2,1)}, f32[3,768]{1,0:T(4,128)}) custom-call(s32[3]{0:T(128)} %get-tuple-element.81.refs_0_.pref, bf16[192,640]{1,0:T(8,128)(2,1)} %get-tuple-element.107.c0, bf16[192,640]{1,0:T(8,128)(2,1)} %copy-done.15, bf16[192,640]{1,0:T(8,128)(2,1)} %copy-done.16, bf16[192,640]{1,0:T(8,128)(2,1)} %copy-done.17, ...), custom_call_target="tpu_custom_call" | custom-call | flops 6794772480 | bytes 17522176 | tf_op jit(solution)/shard_map/pallas_call | solution.py:126
  154.2 18.4 %shard_map.228 = (bf16[640,3072]{1,0:T(8,128)(2,1)}, f32[1,3072]{1,0:T(1,128)}, f32[640,768]{1,0:T(8,128)}, bf16[640,768]{1,0:T(8,128)(2,1)}, bf16[192,640]{1,0:...) custom-call(s32[3]{0:T(128)} %get-tuple-element.81.refs_0_.pref, ...), custom_call_target="tpu_custom_call" | custom-call | flops 6794772480 | bytes 27364864 | tf_op jit(solution)/shard_map/pallas_call | solution.py:126
  172.5 0.5 collective-permute-start.10
  173.0 1.7 collective-permute-start.12
  174.8 14.9 %shard_map.229 = (bf16[2,4,384,768]{3,2,1,0:T(8,128)(2,1)}, bf16[8,384,768]{2,1,0:T(8,128)(2,1)}, bf16[2,384,768]{2,1,0:T(8,128)(2,1)}) custom-call(s32[3]{0:T(128)} %get-tuple-element.81.refs_0_.pref, bf16[640,768]{1,0:T(8,128)(2,1)} %get-tuple-element.116.grad_ffn, bf16[640,3072]{1,0:T(8,128)(2,1)} %get-tuple-element.117.gelu, ...), custom_call_target="tpu_custom_call" | custom-call | flops 6794772480 | bytes 22413312 | tf_op jit(solution)/shard_map/pallas_call | solution.py:126
  189.6 0.0 collective-permute-done.10.refs_11_
  189.6 0.0 copy-start.12
  189.6 0.0 collective-permute-done.11.refs_12_
  189.7 0.6 copy-done.12
  190.3 0.1 copy-done.13
  190.4 0.1 copy-done.14
  190.5 162.9 %shard_map.230 = (bf16[384,3072]{1,0:T(8,128)(2,1)}, bf16[4,384,768]{2,1,0:T(8,128)(2,1)}, bf16[384,768]{1,0:T(8,128)(2,1)}, f32[16,768]{1,0:T(8,128)}, bf16[6,1...) custom-call(s32[3]{0:T(128)} %get-tuple-element.81.refs_0_.pref, bf16[2,4,384,768]{3,2,1,0:T(8,128)(2,1)} %get-tuple-element.126.refs_1_, ...), custom_call_target="tpu_custom_call" | custom-call | flops 49999998976 | bytes 100000000 | tf_op jit(solution)/shard_map/pallas_call | solution.py:847
  353.4 4.4 %bitcast_convert_fusion = f32[1536,768]{1,0:T(8,128)} fusion(bf16[4,384,768]{2,1,0:T(8,128)(2,1)} %get-tuple-element.149), kind=kLoop, calls=%fused_computation | loop fusion | flops 1179648 | bytes 7077888 | tf_op jit(solution)/shard_map/convert_element_type | solution.py:1538
  357.8 2.8 convert_element_type.23
  360.6 1.1 convert_element_type.20
  361.7 0.7 dynamic_slice.7
  362.3 0.6 constant_dynamic-slice_fusion
  362.9 0.7 fusion
  363.6 2.2 bitcast_convert_fusion.1
  365.8 0.9 copy.28
  366.7 0.9 copy.29
  (38 shorter events, 0.1 us)
Async XLA Ops:
  54.0 22.8 %collective-permute-start = (bf16[640,768]{1,0:T(8,128)(2,1)}, bf16[640,768]{1,0:T(8,128)(2,1)S(1)}, u32[]{:S(2)}, u32[]{:S(2)}) collective-permute-start(bf16[640,768]{1,0:T(8,128)(2,1)} %get-tuple-element.82.refs_1_.x), channel_id=1, source_target_pairs={{0,2},{1,3},{2,0},{3,1},{4,6},{5,7},{6,4},{7,5},{8,10},{9,11},{10,... | collective-permute-start | bytes 2949128 | tf_op jit(solution)/shard_map/ppermute | solution.py:47
  54.1 25.5 %collective-permute-start.1 = (bf16[640,768]{1,0:T(8,128)(2,1)}, bf16[640,768]{1,0:T(8,128)(2,1)S(1)}, u32[]{:S(2)}, u32[]{:S(2)}) collective-permute-start(bf16[640,768]{1,0:T(8,128)(2,1)} %get-tuple-element.82.refs_1_.x), channel_id=1, source_target_pairs={{0,1},{1,0},{2,3},{3,2},{4,5},{5,4},{6,7},{7,6},{8,9},{9,8},{10,11... | collective-permute-start | bytes 2949128 | tf_op jit(solution)/shard_map/ppermute | solution.py:47
  54.2 22.6 %copy-start.8 = (f32[4,768]{1,0:T(4,128)S(1)}, f32[4,768]{1,0:T(4,128)}, u32[]{:S(2)}) copy-start(f32[4,768]{1,0:T(4,128)} %param.22) | copy-start | bytes 36868
  76.8 2.8 copy-start.2
  76.8 2.8 collective-permute-start.2
  77.5 33.0 %collective-permute-start.3 = (bf16[192,640]{1,0:T(8,128)(2,1)}, bf16[192,640]{1,0:T(8,128)(2,1)S(1)}, u32[]{:S(2)}, u32[]{:S(2)}) collective-permute-start(bf16[192,640]{1,0:T(8,128)(2,1)} %get-tuple-element.95), channel_id=1, source_target_pairs={{0,2},{1,3},{2,0},{3,1},{4,6},{5,7},{6,4},{7,5},{8,10},{9,11},{10,... | collective-permute-start | bytes 737288 | tf_op jit(solution)/shard_map/ppermute | solution.py:47
  79.1 31.4 %collective-permute-start.4 = (bf16[192,640]{1,0:T(8,128)(2,1)}, bf16[192,640]{1,0:T(8,128)(2,1)S(1)}, u32[]{:S(2)}, u32[]{:S(2)}) collective-permute-start(bf16[192,640]{1,0:T(8,128)(2,1)} %get-tuple-element.96), channel_id=1, source_target_pairs={{0,1},{1,0},{2,3},{3,2},{4,5},{5,4},{6,7},{7,6},{8,9},{9,8},{10,11... | collective-permute-start | bytes 737288 | tf_op jit(solution)/shard_map/ppermute | solution.py:47
  79.1 31.4 %collective-permute-start.5 = (bf16[192,640]{1,0:T(8,128)(2,1)}, bf16[192,640]{1,0:T(8,128)(2,1)S(1)}, u32[]{:S(2)}, u32[]{:S(2)}) collective-permute-start(bf16[192,640]{1,0:T(8,128)(2,1)} %get-tuple-element.97), channel_id=1, source_target_pairs={{0,3},{1,2},{2,1},{3,0},{4,7},{5,6},{6,5},{7,4},{8,11},{9,10},{10,... | collective-permute-start | bytes 737288 | tf_op jit(solution)/shard_map/ppermute | solution.py:47
  79.6 0.9 copy-start.3
  79.6 1.3 copy-start.4
  110.5 2.3 copy-start.9
  110.5 2.2 copy-start.10
  110.6 2.2 copy-start.11
  110.6 25.1 %collective-permute-start.7 = (bf16[192,640]{1,0:T(8,128)(2,1)}, bf16[192,640]{1,0:T(8,128)(2,1)S(1)}, u32[]{:S(2)}, u32[]{:S(2)}) collective-permute-start(bf16[192,640]{1,0:T(8,128)(2,1)} %get-tuple-element.108), channel_id=1, source_target_pairs={{0,2},{1,3},{2,0},{3,1},{4,6},{5,7},{6,4},{7,5},{8,10},{9,11},{10,... | collective-permute-start | bytes 737288 | tf_op jit(solution)/shard_map/ppermute | solution.py:47
  112.3 23.4 %collective-permute-start.8 = (bf16[192,640]{1,0:T(8,128)(2,1)}, bf16[192,640]{1,0:T(8,128)(2,1)S(1)}, u32[]{:S(2)}, u32[]{:S(2)}) collective-permute-start(bf16[192,640]{1,0:T(8,128)(2,1)} %get-tuple-element.109), channel_id=1, source_target_pairs={{0,1},{1,0},{2,3},{3,2},{4,5},{5,4},{6,7},{7,6},{8,9},{9,8},{10,11... | collective-permute-start | bytes 737288 | tf_op jit(solution)/shard_map/ppermute | solution.py:47
  112.3 23.4 %collective-permute-start.9 = (bf16[192,640]{1,0:T(8,128)(2,1)}, bf16[192,640]{1,0:T(8,128)(2,1)S(1)}, u32[]{:S(2)}, u32[]{:S(2)}) collective-permute-start(bf16[192,640]{1,0:T(8,128)(2,1)} %get-tuple-element.110), channel_id=1, source_target_pairs={{0,3},{1,2},{2,1},{3,0},{4,7},{5,6},{6,5},{7,4},{8,11},{9,10},{10,... | collective-permute-start | bytes 737288 | tf_op jit(solution)/shard_map/ppermute | solution.py:47
  132.3 233.5 %collective-permute-start.6 = (bf16[640,768]{1,0:T(8,128)(2,1)}, bf16[640,768]{1,0:T(8,128)(2,1)S(1)}, u32[]{:S(2)}, u32[]{:S(2)}) collective-permute-start(bf16[640,768]{1,0:T(8,128)(2,1)} %get-tuple-element.106), channel_id=1, source_target_pairs={{0,0},{1,4},{2,2},{3,6},{4,1},{5,5},{6,3},{7,7},{8,8},{9,12},{10,1... | collective-permute-start | bytes 2949128 | tf_op jit(solution)/shard_map/ppermute | solution.py:47
  135.7 0.7 copy-start.15
  135.7 0.8 copy-start.16
  135.7 0.8 copy-start.17
  172.5 17.1 %collective-permute-start.10 = (bf16[192,640]{1,0:T(8,128)(2,1)}, bf16[192,640]{1,0:T(8,128)(2,1)S(1)}, u32[]{:S(2)}, u32[]{:S(2)}) collective-permute-start(bf16[192,640]{1,0:T(8,128)(2,1)} %get-tuple-element.136), channel_id=1, source_target_pairs={{0,2},{1,3},{2,0},{3,1},{4,6},{5,7},{6,4},{7,5},{8,10},{9,11},{10,... | collective-permute-start | bytes 737288 | tf_op jit(solution)/shard_map/ppermute | solution.py:47
  173.0 16.6 %collective-permute-start.11 = (bf16[192,640]{1,0:T(8,128)(2,1)}, bf16[192,640]{1,0:T(8,128)(2,1)S(1)}, u32[]{:S(2)}, u32[]{:S(2)}) collective-permute-start(bf16[192,640]{1,0:T(8,128)(2,1)} %get-tuple-element.137), channel_id=1, source_target_pairs={{0,1},{1,0},{2,3},{3,2},{4,5},{5,4},{6,7},{7,6},{8,9},{9,8},{10,11... | collective-permute-start | bytes 737288 | tf_op jit(solution)/shard_map/ppermute | solution.py:47
  173.0 16.6 %collective-permute-start.12 = (bf16[192,640]{1,0:T(8,128)(2,1)}, bf16[192,640]{1,0:T(8,128)(2,1)S(1)}, u32[]{:S(2)}, u32[]{:S(2)}) collective-permute-start(bf16[192,640]{1,0:T(8,128)(2,1)} %get-tuple-element.138), channel_id=1, source_target_pairs={{0,3},{1,2},{2,1},{3,0},{4,7},{5,6},{6,5},{7,4},{8,11},{9,10},{10,... | collective-permute-start | bytes 737288 | tf_op jit(solution)/shard_map/ppermute | solution.py:47
  189.6 0.7 copy-start.12
  189.6 0.8 copy-start.13
  189.7 0.8 copy-start.14
  353.4 4.4 %copy-start.7 = (f32[16,768]{1,0:T(8,128)S(1)}, f32[16,768]{1,0:T(8,128)}, u32[]{:S(2)}) copy-start(f32[16,768]{1,0:T(8,128)} %get-tuple-element.151) | copy-start | bytes 147460
  353.4 4.4 %copy-start = (bf16[384,3072]{1,0:T(8,128)(2,1)S(1)}, bf16[384,3072]{1,0:T(8,128)(2,1)}, u32[]{:S(2)}) copy-start(bf16[384,3072]{1,0:T(8,128)(2,1)} %get-tuple-element.150) | copy-start | bytes 7077892
  357.8 2.8 copy-start.6
  357.8 5.8 %copy-start.1 = (bf16[6,192,768]{2,1,0:T(8,128)(2,1)S(1)}, bf16[6,192,768]{2,1,0:T(8,128)(2,1)}, u32[]{:S(2)}) copy-start(bf16[6,192,768]{2,1,0:T(8,128)(2,1)} %get-tuple-element.147) | copy-start | bytes 5308420
  363.6 3.1 copy-start.5

commit v6 on v5

--- a/solution.py
+++ b/solution.py
@@ -17,9 +17,28 @@
 QB = 512
 KC = 256
 KB = 512
-FC = 512
+FC = 1024
 AUG = 16
 VMEM_LIMIT = 56 * 2**20
+ORDERS = ((0, 1, 2), (1, 0, 2), (0, 2, 1), (1, 2, 0), (2, 0, 1), (2, 1, 0))
+PIECE_PLAN = (
+    (2, 20.0, 95.4, 86.9),
+    (0, 170.2, 97.1, 111.4),
+    (1, 20.8, 80.9, 96.5),
+    (3, 19.5, 100.8, 153.8),
+    (1, 294.8, 80.8, 122.2),
+    (0, 19.9, 101.0, 166.8),
+    (4, 10.7, 73.5, 199.5),
+    (1, 169.6, 90.3, 133.2),
+    (3, 33.7, 57.9, 88.5),
+)
+HEAD_PLAN = (
+    (0, 1, 24.6, 50.5, 104.3),
+    (1, 1, 29.3, 52.8, 136.5),
+    (0, 3, 312.0, 93.4, 93.4),
+)
+HIDDEN_PLAN = (0.0, (203.8, 62.6, 390.1, 383.5))
+VECTOR_PLAN = (7.8, 182.0)
 
 
 def dot(left, right, left_dim, right_dim):
@@ -779,8 +798,7 @@
     def body(i, carry):
         there = pl.ds(pl.multiple_of(row + i * step, 16), step)
         here = pl.ds(pl.multiple_of(start + i * step, 16), step)
-        value = left[there, pl.ds(col, cols)].astype(F32) + right[here, :cols].astype(F32)
-        target[there, pl.ds(col, cols)] = value.astype(target.dtype)
+        target[there, pl.ds(col, cols)] = left[there, pl.ds(col, cols)] + right[here, :cols]
         return carry
 
     lax.fori_loop(0, rows // step, body, 0)
@@ -835,11 +853,6 @@
         yield
         copy.wait_recv()
         sums[n + 1] = sums[n] + far[n]
-
-
-def rotate(items, count):
-    count %= len(items)
-    return items[count:] + items[:count]
 
 
 def remote_call(kernel, args, in_specs, outs, out_specs, scratch, copies, local, number):
@@ -1071,12 +1084,13 @@
 
 
 class Pump:
-    def __init__(self, step):
-        self.step, self.events = step, []
-
-    def add(self, time, flow):
+    def __init__(self):
+        self.events, self.added = [], 0
+
+    def add(self, time, flow, first, then, turn):
         gap = next(flow)
-        self.events.append([time + (gap or 0), len(self.events), flow])
+        self.events.append([time + (gap or 0.0), self.added, flow, 0, (first, then, turn)])
+        self.added += 1
 
     def run(self, time=1e9):
         while self.events:
@@ -1085,9 +1099,14 @@
                 return
             try:
                 gap = next(event[2])
-                event[0] += self.step if gap is None else gap
             except StopIteration:
                 self.events.remove(event)
+                continue
+            event[3] += 1
+            first, then, turn = event[4]
+            if gap is None:
+                gap = first if event[3] <= turn else then
+            event[0] += gap
 
 
 def head_flow(copies, n, gh, work, far, full, result, seq, core, dp):
@@ -1101,12 +1120,13 @@
         load = copies.local(gh.at[n // 2 + side_of], work)
         yield
         load.wait()
-    bits = (rotate(dp, n) if n < 2 else dp) + seq[1:]
+    turned, cut = HEAD_PLAN[n][:2]
+    bits = (dp[::-1] if turned else dp) + seq[1:]
     mine = full.at[2 * n + along]
     parts = yield from scatter_sum(copies, work, far, mine, bits)
     steps = [(bit, kept, False) for bit, kept in reversed(parts)]
-    cut = len(steps) if n == 2 else 1
-    held = steps[cut][1] if n < 2 else (0, mine.shape[0], 0, mine.shape[1])
+    cut = min(cut, len(steps))
+    held = steps[cut][1] if cut < len(steps) else (0, mine.shape[0], 0, mine.shape[1])
     steps = steps[:cut] + [(seq[0], held, False)] + [(b, k, True) for b, k, _ in steps[cut:]]
     for bit, (row, size, col, cols), both in steps:
         first, count = (2 * n, 2) if both else (2 * n + along, 1)
@@ -1170,7 +1190,7 @@
     def _():
         pl.semaphore_wait(barrier, len(friends))
 
-    pump = Pump(6.5)
+    pump = Pump()
     count, rows_half = down.shape[1:3]
     ups = [(up.at[side_of, p], up.at[1 - side_of, p], up_sum.at[p]) for p in range(count)]
     downs = [
@@ -1181,15 +1201,16 @@
         )
         for p in range(count)
     ]
-    queue = [(dp + seq, p, k) for k, p in enumerate(ups)]
-    queue += [(dp[::-1] + seq, p, k) for k, p in enumerate(downs)]
-    queue.append((seq[:1] + dp + seq[1:], (out.at[side_of], out.at[1 - side_of], out_sum), 1))
-    queue.sort(key=lambda item: item[2])
-    for n, (bits, (mine, theirs, result), k) in enumerate(queue):
+    queue = ups + downs + [(out.at[side_of], out.at[1 - side_of], out_sum)]
+    near_bits = dp + seq[:1]
+    orders = [tuple(near_bits[i] for i in order) for order in ORDERS]
+    for n, (mine, theirs, result) in enumerate(queue):
+        order, time, first, then = PIECE_PLAN[n % len(PIECE_PLAN)]
+        bits = list(orders[order]) + seq[1:]
         flow = sum_flow(
             copies, mine, theirs, work.at[n], near.at[n], far.at[n], full.at[n], result, core, bits
         )
-        pump.add(2.0 + 5 * k, flow)
+        pump.add(time, flow, first, then, 1 + len(bits))
 
     late_loads = [
         copies.local(source, target)
@@ -1298,7 +1319,8 @@
 
     def hidden_flow():
         yield 0.0
-        for gap, j in ((2.0, 0), (5.0, 2), (3.0, 1), (0.0, 3)):
+        gaps = HIDDEN_PLAN[1]
+        for gap, j in zip(gaps, (0, 2, 1, 3)):
             for copy in pieces.get(j, []):
                 copy.wait_recv()
             part = None
@@ -1315,7 +1337,8 @@
                 size = jnp.abs(xs[0].astype(F32))
                 pull = jnp.where(size < CLIP, 1.0, jnp.where(size == CLIP, 0.5, 0.0))
                 hid[...] = (res[...] + (acc[...] + part) * pull).astype(BF)
-            yield gap
+            if j != 3:
+                yield gap
 
         @pl.when(moves)
         def _():
@@ -1325,7 +1348,7 @@
         def _():
             keep.start()
 
-        yield 30.0
+        yield gaps[3]
 
         @pl.when(moves)
         def _():
@@ -1336,13 +1359,15 @@
         def _():
             keep.wait()
 
-    pump.add(clock, hidden_flow())
+    pump.add(clock + HIDDEN_PLAN[0], hidden_flow(), 0.0, 0.0, 0)
     for n in (0, 2, 1):
         flow = head_flow(
             copies, n, gh, h_work.at[n], h_far.at[n], h_full, qkv_sum, seq, core, dp
         )
-        pump.add(clock + 1, flow)
-    pump.add(clock + 1, vector_flow(copies, sums, sums_far, [core] + dp + seq))
+        time, first, then = HEAD_PLAN[n][2:]
+        pump.add(clock + time, flow, first, then, 4)
+    time, gap = VECTOR_PLAN
+    pump.add(clock + time, vector_flow(copies, sums, sums_far, [core] + dp + seq), gap, gap, 0)
     pump.run()
     totals[...] = sums[sums.shape[0] - 1]
     copies.finish()

time: 376 us -> 359 us (0.955)
  the two profiles are of different devices: /device:TPU:24 before, /device:TPU:0 now
where the time goes in v6:
time: 359 us; the launch traced here: 354 us
  Pallas kernels  319 us (89%)
  starting transfers between devices  14 us (4%)
  other arithmetic  10.4 us (3%)
  local copies, waits for them, and re-layouts  9.38 us (3%)
    pallas_call x2, Pallas kernels, remote_call(): pl.pallas_call(kernel, in_specs=in_specs, out_specs=out_specs, out_shape=...  199 us
    pallas_call x7, Pallas kernels, call(): pl.pallas_call(kernel, grid_spec=pltpu.PrefetchScalarGridSpec(num_scalar_...  120 us
    ppermute x13, starting transfers between devices, permute(): return lax.ppermute(values, AXES, pairs)  14 us
  transfers between devices with their start and end apart: 13, of which 0 were waited for; matrix products, arithmetic and copies ran while one was open for 4% of the time, Pallas kernels for 76%

profile of v6, /device:TPU:0, one launch (start us, length us, event | category | flops | bytes accessed | tf_op | source)
XLA Modules:
  0.0 354.4 jit_solution(11832157443464102431)
XLA Ops:
  0.6 0.7 slice_bitcast_fusion
  1.4 1.2 copy.25.refs_11_
  2.5 51.4 %shard_map.222 = (s32[3]{0:T(128)}, bf16[576,2560]{1,0:T(8,128)(2,1)}, bf16[640,768]{1,0:T(8,128)(2,1)}, bf16[640,768]{1,0:T(8,128)(2,1)}, bf16[640,768]{1,0:T(8...) custom-call(bf16[640,768]{1,0:T(8,128)(2,1)} %bitcast.26, ...), custom_call_target="tpu_custom_call" | custom-call | flops 49999998976 | bytes 100000000 | tf_op jit(solution)/shard_map/pallas_call | solution.py:860
  54.0 0.1 collective-permute-start
  54.1 3.7 %collective-permute-start.1 = (bf16[640,768]{1,0:T(8,128)(2,1)}, bf16[640,768]{1,0:T(8,128)(2,1)S(1)}, u32[]{:S(2)}, u32[]{:S(2)}) collective-permute-start(bf16[640,768]{1,0:T(8,128)(2,1)} %get-tuple-element.82.refs_1_.x), channel_id=1, source_target_pairs={{0,1},{1,0},{2,3},{3,2},{4,5},{5,4},{6,7},{7,6},{8,9},{9,8},{10,11... | collective-permute-start | bytes 2949128 | tf_op jit(solution)/shard_map/ppermute | solution.py:66
  57.7 22.2 %shard_map.223 = (bf16[192,640]{1,0:T(8,128)(2,1)}, bf16[192,640]{1,0:T(8,128)(2,1)}, bf16[192,640]{1,0:T(8,128)(2,1)}, bf16[192,640]{1,0:T(8,128)(2,1)}, f32[19...) custom-call(s32[3]{0:T(128)} %get-tuple-element.81.refs_0_.pref, ...), custom_call_target="tpu_custom_call" | custom-call | flops 16000000000 | bytes 14776320 | tf_op jit(solution)/shard_map/pallas_call | solution.py:145
  79.9 0.0 collective-permute-done.refs_2_
  79.9 0.0 copy-start.2
  79.9 0.1 collective-permute-start.2
  80.0 0.7 fusion.1
  80.7 1.7 collective-permute-start.3
  82.4 0.1 collective-permute-start.4
  82.5 0.4 collective-permute-start.5
  82.8 0.0 collective-permute-done.1.refs_3_
  82.9 0.0 collective-permute-done.2.refs_4_
  82.9 0.0 copy-start.4
  82.9 0.9 copy-done.3
  83.8 0.3 copy-done.4
  84.1 8.4 %shard_map.224.refs_1_.refs_2_.refs_3_ = bf16[576,2560]{1,0:T(8,128)(2,1)} custom-call(s32[3]{0:T(128)} %get-tuple-element.81.refs_0_.pref, bf16[640,768]{1,0:T(8,128)(2,1)} %get-tuple-element.82.refs_1_.x, bf16[640,768]{1,0:T(8,128)(2,1)} %copy-done.2, bf16[640,768]{1,0:T(8,128)(2,1)} %copy-done.3, bf16[640,768]{1,0:T(8,128)(2,1)} %copy-done.4, ...), custom_call_target="tpu_custom_call" | custom-call | flops 2264924160 | bytes 17498112 | tf_op jit(solution)/shard_map/pallas_call | solution.py:145
  92.5 21.2 %shard_map.225 = (bf16[192,640]{1,0:T(8,128)(2,1)}, bf16[192,640]{1,0:T(8,128)(2,1)}, bf16[192,640]{1,0:T(8,128)(2,1)}, bf16[192,640]{1,0:T(8,128)(2,1)}, f32[192,2560]{1,0:T(8,128)}, /*index=5*/f32[3,1,2560]{2,1,0:T(1,128)}) custom-call(s32[3]{0:T(128)} %get-tuple-element.81.refs_0_.pref, bf16[576,2560]{1,0:T(8,128)(2,1)} %shard_map.224.refs_1_.refs_2_.refs_3_, ...), custom_call_target="tpu_custom_call" | custom-call | flops 16000000000 | bytes 11827200 | tf_op jit(solution)/shard_map/pallas_call | solution.py:145
  113.7 0.0 collective-permute-done.4.c2
  113.7 1.7 collective-permute-start.7
  115.5 0.5 collective-permute-start.9
  116.0 18.5 %shard_map.226 = (bf16[768,640]{1,0:T(8,128)(2,1)}, bf16[640,768]{1,0:T(8,128)(2,1)}, f32[640,768]{1,0:T(8,128)}, f32[640,1]{1,0:T(8,128)}, bf16[640,3072]{1,0:T...) custom-call(s32[3]{0:T(128)} %get-tuple-element.81.refs_0_.pref, ...), custom_call_target="tpu_custom_call" | custom-call | flops 6794772480 | bytes 27364352 | tf_op jit(solution)/shard_map/pallas_call | solution.py:145
  134.5 1.9 collective-permute-start.6
  136.4 0.7 copy-done.15
  137.1 0.1 copy-done.16
  137.2 0.1 copy-done.17
  137.2 16.7 %shard_map.227 = (f32[640,768]{1,0:T(8,128)}, bf16[640,768]{1,0:T(8,128)(2,1)}, f32[3,768]{1,0:T(4,128)}) custom-call(s32[3]{0:T(128)} %get-tuple-element.81.refs_0_.pref, bf16[192,640]{1,0:T(8,128)(2,1)} %get-tuple-element.107.c0, bf16[192,640]{1,0:T(8,128)(2,1)} %copy-done.15, bf16[192,640]{1,0:T(8,128)(2,1)} %copy-done.16, bf16[192,640]{1,0:T(8,128)(2,1)} %copy-done.17, ...), custom_call_target="tpu_custom_call" | custom-call | flops 6794772480 | bytes 17522176 | tf_op jit(solution)/shard_map/pallas_call | solution.py:145
  154.0 17.6 %shard_map.228 = (bf16[640,3072]{1,0:T(8,128)(2,1)}, f32[1,3072]{1,0:T(1,128)}, f32[640,768]{1,0:T(8,128)}, bf16[640,768]{1,0:T(8,128)(2,1)}, bf16[192,640]{1,0:...) custom-call(s32[3]{0:T(128)} %get-tuple-element.81.refs_0_.pref, ...), custom_call_target="tpu_custom_call" | custom-call | flops 6794772480 | bytes 27364864 | tf_op jit(solution)/shard_map/pallas_call | solution.py:145
  171.6 1.7 collective-permute-start.10
  173.4 1.0 collective-permute-start.11
  174.4 1.3 collective-permute-start.12
  175.6 15.3 %shard_map.229 = (bf16[2,4,384,768]{3,2,1,0:T(8,128)(2,1)}, bf16[8,384,768]{2,1,0:T(8,128)(2,1)}, bf16[2,384,768]{2,1,0:T(8,128)(2,1)}) custom-call(s32[3]{0:T(128)} %get-tuple-element.81.refs_0_.pref, bf16[640,768]{1,0:T(8,128)(2,1)} %get-tuple-element.116.grad_ffn, bf16[640,3072]{1,0:T(8,128)(2,1)} %get-tuple-element.117.gelu, ...), custom_call_target="tpu_custom_call" | custom-call | flops 6794772480 | bytes 22413312 | tf_op jit(solution)/shard_map/pallas_call | solution.py:145
  190.9 0.0 copy-start.12
  191.0 0.6 copy-done.12
  191.6 0.1 copy-done.13
  191.7 0.1 copy-done.14
  191.8 148.0 %shard_map.230 = (bf16[384,3072]{1,0:T(8,128)(2,1)}, bf16[4,384,768]{2,1,0:T(8,128)(2,1)}, bf16[384,768]{1,0:T(8,128)(2,1)}, f32[16,768]{1,0:T(8,128)}, bf16[6,1...) custom-call(s32[3]{0:T(128)} %get-tuple-element.81.refs_0_.pref, bf16[2,4,384,768]{3,2,1,0:T(8,128)(2,1)} %get-tuple-element.126.refs_1_, ...), custom_call_target="tpu_custom_call" | custom-call | flops 49999998976 | bytes 100000000 | tf_op jit(solution)/shard_map/pallas_call | solution.py:860
  339.8 4.4 %bitcast_convert_fusion = f32[1536,768]{1,0:T(8,128)} fusion(bf16[4,384,768]{2,1,0:T(8,128)(2,1)} %get-tuple-element.149), kind=kLoop, calls=%fused_computation | loop fusion | flops 1179648 | bytes 7077888 | tf_op jit(solution)/shard_map/convert_element_type | solution.py:1563
  344.2 2.8 convert_element_type.23
  347.0 1.1 convert_element_type.20
  348.1 0.7 dynamic_slice.7
  348.8 0.6 constant_dynamic-slice_fusion
  349.4 0.7 fusion
  350.0 2.2 bitcast_convert_fusion.1
  352.2 0.9 copy.28
  353.2 0.9 copy.29
  (38 shorter events, 0.1 us)
Async XLA Ops:
  54.0 25.9 %collective-permute-start = (bf16[640,768]{1,0:T(8,128)(2,1)}, bf16[640,768]{1,0:T(8,128)(2,1)S(1)}, u32[]{:S(2)}, u32[]{:S(2)}) collective-permute-start(bf16[640,768]{1,0:T(8,128)(2,1)} %get-tuple-element.82.refs_1_.x), channel_id=1, source_target_pairs={{0,2},{1,3},{2,0},{3,1},{4,6},{5,7},{6,4},{7,5},{8,10},{9,11},{10,... | collective-permute-start | bytes 2949128 | tf_op jit(solution)/shard_map/ppermute | solution.py:66
  54.1 28.8 %collective-permute-start.1 = (bf16[640,768]{1,0:T(8,128)(2,1)}, bf16[640,768]{1,0:T(8,128)(2,1)S(1)}, u32[]{:S(2)}, u32[]{:S(2)}) collective-permute-start(bf16[640,768]{1,0:T(8,128)(2,1)} %get-tuple-element.82.refs_1_.x), channel_id=1, source_target_pairs={{0,1},{1,0},{2,3},{3,2},{4,5},{5,4},{6,7},{7,6},{8,9},{9,8},{10,11... | collective-permute-start | bytes 2949128 | tf_op jit(solution)/shard_map/ppermute | solution.py:66
  57.7 22.3 %copy-start.8 = (f32[4,768]{1,0:T(4,128)S(1)}, f32[4,768]{1,0:T(4,128)}, u32[]{:S(2)}) copy-start(f32[4,768]{1,0:T(4,128)} %param.22) | copy-start | bytes 36868
  79.9 3.0 copy-start.2
  79.9 2.9 collective-permute-start.2
  80.7 33.0 %collective-permute-start.3 = (bf16[192,640]{1,0:T(8,128)(2,1)}, bf16[192,640]{1,0:T(8,128)(2,1)S(1)}, u32[]{:S(2)}, u32[]{:S(2)}) collective-permute-start(bf16[192,640]{1,0:T(8,128)(2,1)} %get-tuple-element.95), channel_id=1, source_target_pairs={{0,2},{1,3},{2,0},{3,1},{4,6},{5,7},{6,4},{7,5},{8,10},{9,11},{10,... | collective-permute-start | bytes 737288 | tf_op jit(solution)/shard_map/ppermute | solution.py:66
  82.4 31.3 %collective-permute-start.4 = (bf16[192,640]{1,0:T(8,128)(2,1)}, bf16[192,640]{1,0:T(8,128)(2,1)S(1)}, u32[]{:S(2)}, u32[]{:S(2)}) collective-permute-start(bf16[192,640]{1,0:T(8,128)(2,1)} %get-tuple-element.96), channel_id=1, source_target_pairs={{0,1},{1,0},{2,3},{3,2},{4,5},{5,4},{6,7},{7,6},{8,9},{9,8},{10,11... | collective-permute-start | bytes 737288 | tf_op jit(solution)/shard_map/ppermute | solution.py:66
  82.5 31.3 %collective-permute-start.5 = (bf16[192,640]{1,0:T(8,128)(2,1)}, bf16[192,640]{1,0:T(8,128)(2,1)S(1)}, u32[]{:S(2)}, u32[]{:S(2)}) collective-permute-start(bf16[192,640]{1,0:T(8,128)(2,1)} %get-tuple-element.97), channel_id=1, source_target_pairs={{0,3},{1,2},{2,1},{3,0},{4,7},{5,6},{6,5},{7,4},{8,11},{9,10},{10,... | collective-permute-start | bytes 737288 | tf_op jit(solution)/shard_map/ppermute | solution.py:66
  82.8 0.9 copy-start.3
  82.9 1.3 copy-start.4
  113.7 2.3 copy-start.9
  113.7 2.2 copy-start.10
  113.7 2.2 copy-start.11
  113.7 22.6 %collective-permute-start.7 = (bf16[192,640]{1,0:T(8,128)(2,1)}, bf16[192,640]{1,0:T(8,128)(2,1)S(1)}, u32[]{:S(2)}, u32[]{:S(2)}) collective-permute-start(bf16[192,640]{1,0:T(8,128)(2,1)} %get-tuple-element.108), channel_id=1, source_target_pairs={{0,2},{1,3},{2,0},{3,1},{4,6},{5,7},{6,4},{7,5},{8,10},{9,11},{10,... | collective-permute-start | bytes 737288 | tf_op jit(solution)/shard_map/ppermute | solution.py:66
  115.5 20.9 %collective-permute-start.8 = (bf16[192,640]{1,0:T(8,128)(2,1)}, bf16[192,640]{1,0:T(8,128)(2,1)S(1)}, u32[]{:S(2)}, u32[]{:S(2)}) collective-permute-start(bf16[192,640]{1,0:T(8,128)(2,1)} %get-tuple-element.109), channel_id=1, source_target_pairs={{0,1},{1,0},{2,3},{3,2},{4,5},{5,4},{6,7},{7,6},{8,9},{9,8},{10,11... | collective-permute-start | bytes 737288 | tf_op jit(solution)/shard_map/ppermute | solution.py:66
  115.5 20.9 %collective-permute-start.9 = (bf16[192,640]{1,0:T(8,128)(2,1)}, bf16[192,640]{1,0:T(8,128)(2,1)S(1)}, u32[]{:S(2)}, u32[]{:S(2)}) collective-permute-start(bf16[192,640]{1,0:T(8,128)(2,1)} %get-tuple-element.110), channel_id=1, source_target_pairs={{0,3},{1,2},{2,1},{3,0},{4,7},{5,6},{6,5},{7,4},{8,11},{9,10},{10,... | collective-permute-start | bytes 737288 | tf_op jit(solution)/shard_map/ppermute | solution.py:66
  134.5 217.7 %collective-permute-start.6 = (bf16[640,768]{1,0:T(8,128)(2,1)}, bf16[640,768]{1,0:T(8,128)(2,1)S(1)}, u32[]{:S(2)}, u32[]{:S(2)}) collective-permute-start(bf16[640,768]{1,0:T(8,128)(2,1)} %get-tuple-element.106), channel_id=1, source_target_pairs={{0,0},{1,4},{2,2},{3,6},{4,1},{5,5},{6,3},{7,7},{8,8},{9,12},{10,1... | collective-permute-start | bytes 2949128 | tf_op jit(solution)/shard_map/ppermute | solution.py:66
  136.4 0.7 copy-start.15
  136.4 0.8 copy-start.16
  136.4 0.9 copy-start.17
  171.6 19.3 %collective-permute-start.10 = (bf16[192,640]{1,0:T(8,128)(2,1)}, bf16[192,640]{1,0:T(8,128)(2,1)S(1)}, u32[]{:S(2)}, u32[]{:S(2)}) collective-permute-start(bf16[192,640]{1,0:T(8,128)(2,1)} %get-tuple-element.136), channel_id=1, source_target_pairs={{0,2},{1,3},{2,0},{3,1},{4,6},{5,7},{6,4},{7,5},{8,10},{9,11},{10,... | collective-permute-start | bytes 737288 | tf_op jit(solution)/shard_map/ppermute | solution.py:66
  173.4 17.6 %collective-permute-start.11 = (bf16[192,640]{1,0:T(8,128)(2,1)}, bf16[192,640]{1,0:T(8,128)(2,1)S(1)}, u32[]{:S(2)}, u32[]{:S(2)}) collective-permute-start(bf16[192,640]{1,0:T(8,128)(2,1)} %get-tuple-element.137), channel_id=1, source_target_pairs={{0,1},{1,0},{2,3},{3,2},{4,5},{5,4},{6,7},{7,6},{8,9},{9,8},{10,11... | collective-permute-start | bytes 737288 | tf_op jit(solution)/shard_map/ppermute | solution.py:66
  174.4 16.6 %collective-permute-start.12 = (bf16[192,640]{1,0:T(8,128)(2,1)}, bf16[192,640]{1,0:T(8,128)(2,1)S(1)}, u32[]{:S(2)}, u32[]{:S(2)}) collective-permute-start(bf16[192,640]{1,0:T(8,128)(2,1)} %get-tuple-element.138), channel_id=1, source_target_pairs={{0,3},{1,2},{2,1},{3,0},{4,7},{5,6},{6,5},{7,4},{8,11},{9,10},{10,... | collective-permute-start | bytes 737288 | tf_op jit(solution)/shard_map/ppermute | solution.py:66
  190.9 0.7 copy-start.12
  190.9 0.8 copy-start.13
  190.9 0.8 copy-start.14
  339.8 4.4 %copy-start.7 = (f32[16,768]{1,0:T(8,128)S(1)}, f32[16,768]{1,0:T(8,128)}, u32[]{:S(2)}) copy-start(f32[16,768]{1,0:T(8,128)} %get-tuple-element.151) | copy-start | bytes 147460
  339.8 4.4 %copy-start = (bf16[384,3072]{1,0:T(8,128)(2,1)S(1)}, bf16[384,3072]{1,0:T(8,128)(2,1)}, u32[]{:S(2)}) copy-start(bf16[384,3072]{1,0:T(8,128)(2,1)} %get-tuple-element.150) | copy-start | bytes 7077892
  344.2 2.8 copy-start.6
  344.2 5.8 %copy-start.1 = (bf16[6,192,768]{2,1,0:T(8,128)(2,1)S(1)}, bf16[6,192,768]{2,1,0:T(8,128)(2,1)}, u32[]{:S(2)}) copy-start(bf16[6,192,768]{2,1,0:T(8,128)(2,1)} %get-tuple-element.147) | copy-start | bytes 5308420
  350.0 3.1 copy-start.5

commit v7 on v6

--- a/solution.py
+++ b/solution.py
@@ -618,14 +618,15 @@
 
 
 def weight_grad_kernel(
-    pref, grad_ffn, gelu, grad_hidden, act_one, grad_attn, ctx, grad_down, grad_up, grad_out
+    pref, grad_ffn, gelu, grad_hidden, act_one, grad_attn, ctx, grad_down, grad_up, grad_out, turned
 ):
     @pl.when(pl.program_id(0) == 0)
     def _():
+        turned[...] = grad_ffn[...].T
         value = dot(grad_attn[...], ctx[...], 0, 1).astype(BF)
         grad_out[...] = value.reshape(grad_out.shape)
 
-    value = dot(grad_ffn[...], gelu[...], 0, 0).astype(BF)
+    value = dot(turned[...], gelu[...], 1, 0).astype(BF)
     grad_down[...] = value.reshape(grad_down.shape)
     value = dot(grad_hidden[...], act_one[...], 0, 0).astype(BF)
     grad_up[...] = value.reshape(grad_up.shape)
@@ -653,7 +654,7 @@
             whole((2, half, width)),
         ],
         (count,),
-        [],
+        [pltpu.VMEM((width, tok), BF)],
         2 * tok * width * (2 * hidden + width),
     )
 
@@ -993,6 +994,15 @@
     rows = width // 4
     own = along + 2 * side_of
 
+    row = lax.broadcasted_iota(jnp.int32, (AUG, tok), 0)
+    ones = jnp.where(row < 3, 1.0, 0.0).astype(BF)
+    shifts = []
+    for part in range(2):
+        line = bias[part : part + 1, 0:rows]
+        for j in range(1, 4):
+            line = jnp.where(own == j, bias[part : part + 1, j * rows : (j + 1) * rows], line)
+        shifts.append(dot(thirds(line), ones, 0, 0))
+
     def project(slot):
         act = jnp.clip(xs[slot], -CLIP, CLIP)
         first = (1 - along if slot % 2 else along) + 2 * (1 - side_of if slot // 2 else side_of)
@@ -1001,7 +1011,7 @@
             at = pl.multiple_of(part * width + own * rows, 16)
             value = dot(w_qkv[pl.ds(at, rows), :], act, 1, 1)
             if part != 1:
-                value = value + bias[part // 2, pl.ds(pl.multiple_of(own * rows, 8), rows), :]
+                value = value + shifts[part // 2]
             proj[part * rows : (part + 1) * rows, there] = value.astype(BF)
         stores.append(copies.local(proj.at[:, there], o_qkv.at[:, there]))
         stores.append(copies.local(xs.at[slot], (x0, x1, x2, x3)[slot]))
@@ -1420,6 +1430,27 @@
     )
 
 
+def widen_kernel(*refs):
+    half = len(refs) // 2
+    for source, target in zip(refs[:half], refs[half:]):
+        target[...] = source[...].astype(F32)
+
+
+def widen(values, steps):
+    specs = [pl.BlockSpec((v.shape[0] // steps, v.shape[1]), lambda i: (i, 0)) for v in values]
+    return pl.pallas_call(
+        widen_kernel,
+        grid=(steps,),
+        in_specs=specs,
+        out_specs=specs,
+        out_shape=[shape_of(v.shape, F32) for v in values],
+        compiler_params=pltpu.CompilerParams(vmem_limit_bytes=VMEM_LIMIT),
+        cost_estimate=pl.CostEstimate(
+            flops=0, bytes_accessed=6 * sum(v.size for v in values), transcendentals=0
+        ),
+    )(*values)
+
+
 def binarize(latent):
     row_scale = jnp.mean(jnp.abs(latent), axis=1, keepdims=True)
     return (row_scale * jnp.sign(latent)).astype(BF)
@@ -1452,13 +1483,12 @@
     own = (seq_at % 2 + 2 * core).astype(jnp.int32)
     width = hidden.shape[2]
 
-    bias_cols = biases[:2].reshape(2, width, 1)
     latents = (latent_qkv, latent_out, latent_up, latent_down)
     teachers = (teacher_qkv, teacher_out, teacher_up, teacher_down)
     if fsdp == 2:
         pref, qkv, x_slots, teach, bins, t_weights = entry(
             bit_list("seq"), bit_list("fsdp")[0], hidden[0], teacher_hidden[0], segments,
-            latents, teachers, bias_cols,
+            latents, teachers, biases,
         )
         x = x_slots[0]
     else:
@@ -1470,7 +1500,7 @@
         bins = [gather_rows(binarize(w)) for w in latents]
         teach = swap_groups(teacher_hidden[0])
         t_weights = [gather_rows(w) for w in teachers]
-        qkv = qkv_project(pref, x_slots, bins[0], bias_cols)
+        qkv = qkv_project(pref, x_slots, bins[0], biases[:2].reshape(2, width, 1))
     bin_qkv, bin_out, bin_up, bin_down = bins
     t_qkv, t_out, t_up, t_down = t_weights
     t_along, t_beside = to_slot(teach, 1), to_slot(teach, 2)
@@ -1513,6 +1543,9 @@
         )
         total_up = total_up.reshape(-1, width)
         total_qkv = total_qkv.reshape(-1, width)
+        total_qkv, total_out, total_up, total_down = widen(
+            (total_qkv, total_out, total_up, total_down), 6
+        )
     else:
         dqkv_slots = attention_back(pref, qkv, gctx_pieces, ctx_full, lse)
         dqkv_pieces = exchange(dqkv_slots)

time: 359 us -> 357 us (level)
  other arithmetic: 10.4 us -> 0 us
  Pallas kernels: 319 us -> 328 us
    convert_element_type x4 -> x0, other arithmetic: 10.4 us -> none  [the longest x1 4.36 us: on_device(): total_up.astype(F32)]
    pallas_call x0 -> x1, Pallas kernels: none -> 8.87 us  [widen(): pl.pallas_call(widen_kernel, grid=(steps,), in_specs=specs, out_specs=spe...]
  transfers between devices with their start and end apart: 13 -> 13, of which waited for: 0 -> 0; matrix products, arithmetic and copies ran while one was open for 4% -> 1% of each run, Pallas kernels for 76% -> 79%
where the time goes in v7:
time: 357 us; the launch traced here: 352 us
  Pallas kernels  328 us (92%)
  starting transfers between devices  14 us (4%)
  local copies, waits for them, and re-layouts  8.95 us (3%)
    pallas_call x2, Pallas kernels, remote_call(): pl.pallas_call(kernel, in_specs=in_specs, out_specs=out_specs, out_shape=...  199 us
    pallas_call x7, Pallas kernels, call(): pl.pallas_call(kernel, grid_spec=pltpu.PrefetchScalarGridSpec(num_scalar_...  120 us
    ppermute x13, starting transfers between devices, permute(): return lax.ppermute(values, AXES, pairs)  14 us
    pallas_call x1, Pallas kernels, widen(): pl.pallas_call(widen_kernel, grid=(steps,), in_specs=specs, out_specs=spe...  8.87 us
  transfers between devices with their start and end apart: 13, of which 0 were waited for; matrix products, arithmetic and copies ran while one was open for 1% of the time, Pallas kernels for 79%

profile of v7, /device:TPU:0, one launch (start us, length us, event | category | flops | bytes accessed | tf_op | source)
XLA Modules:
  0.0 351.9 jit_solution(5664237035456246403)
XLA Ops:
  0.6 51.0 %shard_map.222 = (s32[3]{0:T(128)}, bf16[576,2560]{1,0:T(8,128)(2,1)}, bf16[640,768]{1,0:T(8,128)(2,1)}, bf16[640,768]{1,0:T(8,128)(2,1)}, bf16[640,768]{1,0:T(8...) custom-call(bf16[640,768]{1,0:T(8,128)(2,1)} %bitcast.22, ...), custom_call_target="tpu_custom_call" | custom-call | flops 49999998976 | bytes 100000000 | tf_op jit(solution)/shard_map/pallas_call | solution.py:861
  51.7 0.1 collective-permute-start
  51.8 3.7 %collective-permute-start.1 = (bf16[640,768]{1,0:T(8,128)(2,1)}, bf16[640,768]{1,0:T(8,128)(2,1)S(1)}, u32[]{:S(2)}, u32[]{:S(2)}) collective-permute-start(bf16[640,768]{1,0:T(8,128)(2,1)} %get-tuple-element.86.refs_1_.x), channel_id=1, source_target_pairs={{0,1},{1,0},{2,3},{3,2},{4,5},{5,4},{6,7},{7,6},{8,9},{9,8},{10,11... | collective-permute-start | bytes 2949128 | tf_op jit(solution)/shard_map/ppermute | solution.py:66
  55.5 22.2 %shard_map.223 = (bf16[192,640]{1,0:T(8,128)(2,1)}, bf16[192,640]{1,0:T(8,128)(2,1)}, bf16[192,640]{1,0:T(8,128)(2,1)}, bf16[192,640]{1,0:T(8,128)(2,1)}, f32[19...) custom-call(s32[3]{0:T(128)} %get-tuple-element.85.refs_0_.pref, ...), custom_call_target="tpu_custom_call" | custom-call | flops 16000000000 | bytes 14776320 | tf_op jit(solution)/shard_map/pallas_call | solution.py:145
  77.6 0.0 collective-permute-done.refs_2_
  77.6 0.0 copy-start
  77.6 0.1 collective-permute-start.2
  77.7 0.7 fusion.1
  78.4 1.7 collective-permute-start.3
  80.1 0.1 collective-permute-start.4
  80.2 0.4 collective-permute-start.5
  80.6 0.0 collective-permute-done.1.refs_3_
  80.6 0.0 collective-permute-done.2.refs_4_
  80.6 0.0 copy-start.3
  80.6 0.9 copy-done.1
  81.5 0.3 copy-done.3
  81.8 8.4 %shard_map.224.refs_1_.refs_2_.refs_3_ = bf16[576,2560]{1,0:T(8,128)(2,1)} custom-call(s32[3]{0:T(128)} %get-tuple-element.85.refs_0_.pref, bf16[640,768]{1,0:T(8,128)(2,1)} %get-tuple-element.86.refs_1_.x, bf16[640,768]{1,0:T(8,128)(2,1)} %copy-done, bf16[640,768]{1,0:T(8,128)(2,1)} %copy-done.1, bf16[640,768]{1,0:T(8,128)(2,1)} %copy-done.3, ...), custom_call_target="tpu_custom_call" | custom-call | flops 2264924160 | bytes 17498112 | tf_op jit(solution)/shard_map/pallas_call | solution.py:145
  90.2 21.2 %shard_map.225 = (bf16[192,640]{1,0:T(8,128)(2,1)}, bf16[192,640]{1,0:T(8,128)(2,1)}, bf16[192,640]{1,0:T(8,128)(2,1)}, bf16[192,640]{1,0:T(8,128)(2,1)}, f32[192,2560]{1,0:T(8,128)}, /*index=5*/f32[3,1,2560]{2,1,0:T(1,128)}) custom-call(s32[3]{0:T(128)} %get-tuple-element.85.refs_0_.pref, bf16[576,2560]{1,0:T(8,128)(2,1)} %shard_map.224.refs_1_.refs_2_.refs_3_, ...), custom_call_target="tpu_custom_call" | custom-call | flops 16000000000 | bytes 11827200 | tf_op jit(solution)/shard_map/pallas_call | solution.py:145
  111.4 0.0 collective-permute-done.3.c1
  111.4 0.0 collective-permute-done.4.c2
  111.5 1.7 collective-permute-start.7
  113.2 0.5 collective-permute-start.9
  113.7 18.6 %shard_map.226 = (bf16[768,640]{1,0:T(8,128)(2,1)}, bf16[640,768]{1,0:T(8,128)(2,1)}, f32[640,768]{1,0:T(8,128)}, f32[640,1]{1,0:T(8,128)}, bf16[640,3072]{1,0:T...) custom-call(s32[3]{0:T(128)} %get-tuple-element.85.refs_0_.pref, ...), custom_call_target="tpu_custom_call" | custom-call | flops 6794772480 | bytes 27364352 | tf_op jit(solution)/shard_map/pallas_call | solution.py:145
  132.3 1.9 collective-permute-start.6
  134.1 0.0 collective-permute-done.9.c3
  134.2 0.7 copy-done.11
  134.8 0.1 copy-done.12
  134.9 0.1 copy-done.13
  135.0 16.7 %shard_map.227 = (f32[640,768]{1,0:T(8,128)}, bf16[640,768]{1,0:T(8,128)(2,1)}, f32[3,768]{1,0:T(4,128)}) custom-call(s32[3]{0:T(128)} %get-tuple-element.85.refs_0_.pref, bf16[192,640]{1,0:T(8,128)(2,1)} %get-tuple-element.111.c0, bf16[192,640]{1,0:T(8,128)(2,1)} %copy-done.11, bf16[192,640]{1,0:T(8,128)(2,1)} %copy-done.12, bf16[192,640]{1,0:T(8,128)(2,1)} %copy-done.13, ...), custom_call_target="tpu_custom_call" | custom-call | flops 6794772480 | bytes 17522176 | tf_op jit(solution)/shard_map/pallas_call | solution.py:145
  151.7 17.6 %shard_map.228 = (bf16[640,3072]{1,0:T(8,128)(2,1)}, f32[1,3072]{1,0:T(1,128)}, f32[640,768]{1,0:T(8,128)}, bf16[640,768]{1,0:T(8,128)(2,1)}, bf16[192,640]{1,0:...) custom-call(s32[3]{0:T(128)} %get-tuple-element.85.refs_0_.pref, ...), custom_call_target="tpu_custom_call" | custom-call | flops 6794772480 | bytes 27364864 | tf_op jit(solution)/shard_map/pallas_call | solution.py:145
  169.4 1.7 collective-permute-start.10
  171.1 1.0 collective-permute-start.11
  172.1 1.3 collective-permute-start.12
  173.4 15.2 %shard_map.229 = (bf16[2,4,384,768]{3,2,1,0:T(8,128)(2,1)}, bf16[8,384,768]{2,1,0:T(8,128)(2,1)}, bf16[2,384,768]{2,1,0:T(8,128)(2,1)}) custom-call(s32[3]{0:T(128)} %get-tuple-element.85.refs_0_.pref, bf16[640,768]{1,0:T(8,128)(2,1)} %get-tuple-element.120.grad_ffn, bf16[640,3072]{1,0:T(8,128)(2,1)} %get-tuple-element.121.gelu, ...), custom_call_target="tpu_custom_call" | custom-call | flops 6794772480 | bytes 22413312 | tf_op jit(solution)/shard_map/pallas_call | solution.py:145
  188.6 0.0 copy-start.8
  188.6 0.0 collective-permute-done.11.refs_12_
  188.6 0.6 copy-done.8
  189.3 0.1 copy-done.9
  189.4 0.1 copy-done.10
  189.4 148.0 %shard_map.230 = (bf16[384,3072]{1,0:T(8,128)(2,1)}, bf16[4,384,768]{2,1,0:T(8,128)(2,1)}, bf16[384,768]{1,0:T(8,128)(2,1)}, f32[16,768]{1,0:T(8,128)}, bf16[6,1...) custom-call(s32[3]{0:T(128)} %get-tuple-element.85.refs_0_.pref, bf16[2,4,384,768]{3,2,1,0:T(8,128)(2,1)} %get-tuple-element.130.refs_1_, ...), custom_call_target="tpu_custom_call" | custom-call | flops 49999998976 | bytes 100000000 | tf_op jit(solution)/shard_map/pallas_call | solution.py:861
  337.4 0.7 slice.25
  338.2 0.7 slice.23
  338.9 0.7 dynamic_slice.7
  339.6 8.9 %shard_map.231 = (f32[1152,768]{1,0:T(8,128)}, f32[384,768]{1,0:T(8,128)}, f32[1536,768]{1,0:T(8,128)}, f32[384,3072]{1,0:T(8,128)}) custom-call(bf16[1152,768]{1,0:T(8,128)(2,1)} %bitcast.19, bf16[384,768]{1,0:T(8,128)(2,1)} %get-tuple-element.152.refs_1_, bf16[1536,768]{1,0:T(8,128)(2,1)} %bitcast.18, bf16[384,3072]{1,0:T(8,128)(2,1)} %get-tuple-element.154.refs_3_), custom_call_target="tpu_custom_call" | custom-call | bytes 21233664 | tf_op jit(solution)/shard_map/pallas_call | solution.py:1441
  348.5 0.6 constant_dynamic-slice_fusion
  349.1 0.7 fusion
  349.8 0.9 copy.27
  350.7 0.9 copy.28
  (25 shorter events, 0.1 us)
Async XLA Ops:
  51.7 25.9 %collective-permute-start = (bf16[640,768]{1,0:T(8,128)(2,1)}, bf16[640,768]{1,0:T(8,128)(2,1)S(1)}, u32[]{:S(2)}, u32[]{:S(2)}) collective-permute-start(bf16[640,768]{1,0:T(8,128)(2,1)} %get-tuple-element.86.refs_1_.x), channel_id=1, source_target_pairs={{0,2},{1,3},{2,0},{3,1},{4,6},{5,7},{6,4},{7,5},{8,10},{9,11},{10,... | collective-permute-start | bytes 2949128 | tf_op jit(solution)/shard_map/ppermute | solution.py:66
  51.8 28.8 %collective-permute-start.1 = (bf16[640,768]{1,0:T(8,128)(2,1)}, bf16[640,768]{1,0:T(8,128)(2,1)S(1)}, u32[]{:S(2)}, u32[]{:S(2)}) collective-permute-start(bf16[640,768]{1,0:T(8,128)(2,1)} %get-tuple-element.86.refs_1_.x), channel_id=1, source_target_pairs={{0,1},{1,0},{2,3},{3,2},{4,5},{5,4},{6,7},{7,6},{8,9},{9,8},{10,11... | collective-permute-start | bytes 2949128 | tf_op jit(solution)/shard_map/ppermute | solution.py:66
  55.4 22.3 %copy-start.4 = (f32[4,768]{1,0:T(4,128)S(1)}, f32[4,768]{1,0:T(4,128)}, u32[]{:S(2)}) copy-start(f32[4,768]{1,0:T(4,128)} %refs_11_.1) | copy-start | bytes 36868
  77.6 3.0 copy-start
  77.6 2.9 collective-permute-start.2
  78.4 33.0 %collective-permute-start.3 = (bf16[192,640]{1,0:T(8,128)(2,1)}, bf16[192,640]{1,0:T(8,128)(2,1)S(1)}, u32[]{:S(2)}, u32[]{:S(2)}) collective-permute-start(bf16[192,640]{1,0:T(8,128)(2,1)} %get-tuple-element.99), channel_id=1, source_target_pairs={{0,2},{1,3},{2,0},{3,1},{4,6},{5,7},{6,4},{7,5},{8,10},{9,11},{10,... | collective-permute-start | bytes 737288 | tf_op jit(solution)/shard_map/ppermute | solution.py:66
  80.1 31.3 %collective-permute-start.4 = (bf16[192,640]{1,0:T(8,128)(2,1)}, bf16[192,640]{1,0:T(8,128)(2,1)S(1)}, u32[]{:S(2)}, u32[]{:S(2)}) collective-permute-start(bf16[192,640]{1,0:T(8,128)(2,1)} %get-tuple-element.100), channel_id=1, source_target_pairs={{0,1},{1,0},{2,3},{3,2},{4,5},{5,4},{6,7},{7,6},{8,9},{9,8},{10,11... | collective-permute-start | bytes 737288 | tf_op jit(solution)/shard_map/ppermute | solution.py:66
  80.2 31.3 %collective-permute-start.5 = (bf16[192,640]{1,0:T(8,128)(2,1)}, bf16[192,640]{1,0:T(8,128)(2,1)S(1)}, u32[]{:S(2)}, u32[]{:S(2)}) collective-permute-start(bf16[192,640]{1,0:T(8,128)(2,1)} %get-tuple-element.101), channel_id=1, source_target_pairs={{0,3},{1,2},{2,1},{3,0},{4,7},{5,6},{6,5},{7,4},{8,11},{9,10},{10,... | collective-permute-start | bytes 737288 | tf_op jit(solution)/shard_map/ppermute | solution.py:66
  80.6 0.9 copy-start.1
  80.6 1.3 copy-start.3
  111.4 2.3 copy-start.5
  111.4 2.2 copy-start.6
  111.5 2.2 copy-start.7
  111.5 22.7 %collective-permute-start.7 = (bf16[192,640]{1,0:T(8,128)(2,1)}, bf16[192,640]{1,0:T(8,128)(2,1)S(1)}, u32[]{:S(2)}, u32[]{:S(2)}) collective-permute-start(bf16[192,640]{1,0:T(8,128)(2,1)} %get-tuple-element.112), channel_id=1, source_target_pairs={{0,2},{1,3},{2,0},{3,1},{4,6},{5,7},{6,4},{7,5},{8,10},{9,11},{10,... | collective-permute-start | bytes 737288 | tf_op jit(solution)/shard_map/ppermute | solution.py:66
  113.2 20.9 %collective-permute-start.8 = (bf16[192,640]{1,0:T(8,128)(2,1)}, bf16[192,640]{1,0:T(8,128)(2,1)S(1)}, u32[]{:S(2)}, u32[]{:S(2)}) collective-permute-start(bf16[192,640]{1,0:T(8,128)(2,1)} %get-tuple-element.113), channel_id=1, source_target_pairs={{0,1},{1,0},{2,3},{3,2},{4,5},{5,4},{6,7},{7,6},{8,9},{9,8},{10,11... | collective-permute-start | bytes 737288 | tf_op jit(solution)/shard_map/ppermute | solution.py:66
  113.2 20.9 %collective-permute-start.9 = (bf16[192,640]{1,0:T(8,128)(2,1)}, bf16[192,640]{1,0:T(8,128)(2,1)S(1)}, u32[]{:S(2)}, u32[]{:S(2)}) collective-permute-start(bf16[192,640]{1,0:T(8,128)(2,1)} %get-tuple-element.114), channel_id=1, source_target_pairs={{0,3},{1,2},{2,1},{3,0},{4,7},{5,6},{6,5},{7,4},{8,11},{9,10},{10,... | collective-permute-start | bytes 737288 | tf_op jit(solution)/shard_map/ppermute | solution.py:66
  132.3 217.5 %collective-permute-start.6 = (bf16[640,768]{1,0:T(8,128)(2,1)}, bf16[640,768]{1,0:T(8,128)(2,1)S(1)}, u32[]{:S(2)}, u32[]{:S(2)}) collective-permute-start(bf16[640,768]{1,0:T(8,128)(2,1)} %get-tuple-element.110), channel_id=1, source_target_pairs={{0,0},{1,4},{2,2},{3,6},{4,1},{5,5},{6,3},{7,7},{8,8},{9,12},{10,1... | collective-permute-start | bytes 2949128 | tf_op jit(solution)/shard_map/ppermute | solution.py:66
  134.1 0.7 copy-start.11
  134.1 0.8 copy-start.12
  134.1 0.9 copy-start.13
  169.4 19.2 %collective-permute-start.10 = (bf16[192,640]{1,0:T(8,128)(2,1)}, bf16[192,640]{1,0:T(8,128)(2,1)S(1)}, u32[]{:S(2)}, u32[]{:S(2)}) collective-permute-start(bf16[192,640]{1,0:T(8,128)(2,1)} %get-tuple-element.140), channel_id=1, source_target_pairs={{0,2},{1,3},{2,0},{3,1},{4,6},{5,7},{6,4},{7,5},{8,10},{9,11},{10,... | collective-permute-start | bytes 737288 | tf_op jit(solution)/shard_map/ppermute | solution.py:66
  171.1 17.5 %collective-permute-start.11 = (bf16[192,640]{1,0:T(8,128)(2,1)}, bf16[192,640]{1,0:T(8,128)(2,1)S(1)}, u32[]{:S(2)}, u32[]{:S(2)}) collective-permute-start(bf16[192,640]{1,0:T(8,128)(2,1)} %get-tuple-element.141), channel_id=1, source_target_pairs={{0,1},{1,0},{2,3},{3,2},{4,5},{5,4},{6,7},{7,6},{8,9},{9,8},{10,11... | collective-permute-start | bytes 737288 | tf_op jit(solution)/shard_map/ppermute | solution.py:66
  172.1 16.5 %collective-permute-start.12 = (bf16[192,640]{1,0:T(8,128)(2,1)}, bf16[192,640]{1,0:T(8,128)(2,1)S(1)}, u32[]{:S(2)}, u32[]{:S(2)}) collective-permute-start(bf16[192,640]{1,0:T(8,128)(2,1)} %get-tuple-element.142), channel_id=1, source_target_pairs={{0,3},{1,2},{2,1},{3,0},{4,7},{5,6},{6,5},{7,4},{8,11},{9,10},{10,... | collective-permute-start | bytes 737288 | tf_op jit(solution)/shard_map/ppermute | solution.py:66
  188.6 0.7 copy-start.8
  188.6 0.8 copy-start.9
  188.6 0.8 copy-start.10
  339.6 11.1 %copy-start.2 = (bf16[640,768]{1,0:T(8,128)(2,1)S(1)}, bf16[640,768]{1,0:T(8,128)(2,1)}, u32[]{:S(2)}) copy-start(bf16[640,768]{1,0:T(8,128)(2,1)} %get-tuple-element.150) | copy-start | bytes 2949124

commit v8 on v7

--- a/solution.py
+++ b/solution.py
@@ -20,25 +20,26 @@
 FC = 1024
 AUG = 16
 VMEM_LIMIT = 56 * 2**20
+TAIL_LIMIT = 60 * 2**20
 ORDERS = ((0, 1, 2), (1, 0, 2), (0, 2, 1), (1, 2, 0), (2, 0, 1), (2, 1, 0))
 PIECE_PLAN = (
-    (2, 20.0, 95.4, 86.9),
-    (0, 170.2, 97.1, 111.4),
-    (1, 20.8, 80.9, 96.5),
-    (3, 19.5, 100.8, 153.8),
-    (1, 294.8, 80.8, 122.2),
-    (0, 19.9, 101.0, 166.8),
-    (4, 10.7, 73.5, 199.5),
-    (1, 169.6, 90.3, 133.2),
-    (3, 33.7, 57.9, 88.5),
+    (0, 6.2, 33.2, 64.8),
+    (2, 13.6, 75.8, 115.6),
+    (1, 87.9, 109.7, 109.9),
+    (1, 18.5, 61.3, 92.2),
+    (4, 8.4, 94.5, 125.6),
+    (0, 9.7, 53.1, 89.3),
+    (0, 30.0, 114.5, 110.0),
+    (1, 23.6, 99.1, 76.0),
+    (1, 15.8, 49.7, 87.1),
 )
 HEAD_PLAN = (
-    (0, 1, 24.6, 50.5, 104.3),
-    (1, 1, 29.3, 52.8, 136.5),
-    (0, 3, 312.0, 93.4, 93.4),
+    (1, 1, 238.2, 90.7, 81.4),
+    (0, 3, 170.9, 119.6, 73.4),
+    (1, 1, 16.1, 96.9, 77.0),
 )
-HIDDEN_PLAN = (0.0, (203.8, 62.6, 390.1, 383.5))
-VECTOR_PLAN = (7.8, 182.0)
+HIDDEN_PLAN = (0.0, (416.8, 50.8, 134.5, 451.6))
+VECTOR_PLAN = (75.4, 88.5)
 
 
 def dot(left, right, left_dim, right_dim):
@@ -856,7 +857,7 @@
         sums[n + 1] = sums[n] + far[n]
 
 
-def remote_call(kernel, args, in_specs, outs, out_specs, scratch, copies, local, number):
+def remote_call(kernel, args, in_specs, outs, out_specs, scratch, copies, local, number, limit=VMEM_LIMIT):
     sems = pltpu.SemaphoreType.DMA
     return pl.pallas_call(
         kernel,
@@ -865,7 +866,7 @@
         out_shape=outs,
         scratch_shapes=scratch + [sems((copies,)), sems((copies,)), sems((local,))],
         compiler_params=pltpu.CompilerParams(
-            vmem_limit_bytes=VMEM_LIMIT, collective_id=number, has_side_effects=True
+            vmem_limit_bytes=limit, collective_id=number, has_side_effects=True
         ),
         cost_estimate=pl.CostEstimate(flops=5 * 10**10, bytes_accessed=10**8, transcendentals=0),
     )(*args)
@@ -1427,6 +1428,7 @@
         pieces * (1 + 2 * steps) + steps + 1 + 3 * heads + 1 + 3 * (2 * steps - 1) + 1,
         2 * pieces + 14 + 1 + 5,
         4,
+        TAIL_LIMIT,
     )
 
 

time: 357 us -> 348 us (0.975)
  the two profiles are of different devices: /device:TPU:0 before, /device:TPU:24 now
where the time goes in v8:
time: 348 us; the launch traced here: 343 us
  Pallas kernels  322 us (93%)
  starting transfers between devices  10.3 us (3%)
  local copies, waits for them, and re-layouts  8.93 us (3%)
    pallas_call x2, Pallas kernels, remote_call(): pl.pallas_call(kernel, in_specs=in_specs, out_specs=out_specs, out_shape=...  194 us
    pallas_call x7, Pallas kernels, call(): pl.pallas_call(kernel, grid_spec=pltpu.PrefetchScalarGridSpec(num_scalar_...  120 us
    ppermute x13, starting transfers between devices, permute(): return lax.ppermute(values, AXES, pairs)  10.3 us
    pallas_call x1, Pallas kernels, widen(): pl.pallas_call(widen_kernel, grid=(steps,), in_specs=specs, out_specs=spe...  8.87 us
  transfers between devices with their start and end apart: 13, of which 1 were waited for; matrix products, arithmetic and copies ran while one was open for 1% of the time, Pallas kernels for 79%

profile of v8, /device:TPU:24, one launch (start us, length us, event | category | flops | bytes accessed | tf_op | source)
XLA Modules:
  0.0 343.3 jit_solution(10679314372139887325)
XLA Ops:
  0.6 51.1 %shard_map.222 = (s32[3]{0:T(128)}, bf16[576,2560]{1,0:T(8,128)(2,1)}, bf16[640,768]{1,0:T(8,128)(2,1)}, bf16[640,768]{1,0:T(8,128)(2,1)}, bf16[640,768]{1,0:T(8...) custom-call(bf16[640,768]{1,0:T(8,128)(2,1)} %bitcast.22, ...), custom_call_target="tpu_custom_call" | custom-call | flops 49999998976 | bytes 100000000 | tf_op jit(solution)/shard_map/pallas_call | solution.py:862
  51.8 0.1 collective-permute-start
  51.8 0.1 collective-permute-start.1
  51.9 0.0 copy-start.4
  51.9 22.0 %shard_map.223 = (bf16[192,640]{1,0:T(8,128)(2,1)}, bf16[192,640]{1,0:T(8,128)(2,1)}, bf16[192,640]{1,0:T(8,128)(2,1)}, bf16[192,640]{1,0:T(8,128)(2,1)}, f32[19...) custom-call(s32[3]{0:T(128)} %get-tuple-element.85.refs_0_.pref, ...), custom_call_target="tpu_custom_call" | custom-call | flops 16000000000 | bytes 14776320 | tf_op jit(solution)/shard_map/pallas_call | solution.py:146
  74.0 0.6 collective-permute-done.refs_2_
  74.6 0.1 collective-permute-start.2
  74.7 0.7 fusion.1
  75.4 1.8 collective-permute-start.3
  77.2 0.0 collective-permute-start.4
  77.2 0.3 collective-permute-start.5
  77.5 0.0 copy-start.3
  77.5 0.9 copy-done.1
  78.4 0.3 copy-done.3
  78.8 8.4 %shard_map.224.refs_1_.refs_2_.refs_3_ = bf16[576,2560]{1,0:T(8,128)(2,1)} custom-call(s32[3]{0:T(128)} %get-tuple-element.85.refs_0_.pref, bf16[640,768]{1,0:T(8,128)(2,1)} %get-tuple-element.86.refs_1_.x, bf16[640,768]{1,0:T(8,128)(2,1)} %copy-done, bf16[640,768]{1,0:T(8,128)(2,1)} %copy-done.1, bf16[640,768]{1,0:T(8,128)(2,1)} %copy-done.3, ...), custom_call_target="tpu_custom_call" | custom-call | flops 2264924160 | bytes 17498112 | tf_op jit(solution)/shard_map/pallas_call | solution.py:146
  87.2 21.2 %shard_map.225 = (bf16[192,640]{1,0:T(8,128)(2,1)}, bf16[192,640]{1,0:T(8,128)(2,1)}, bf16[192,640]{1,0:T(8,128)(2,1)}, bf16[192,640]{1,0:T(8,128)(2,1)}, f32[192,2560]{1,0:T(8,128)}, /*index=5*/f32[3,1,2560]{2,1,0:T(1,128)}) custom-call(s32[3]{0:T(128)} %get-tuple-element.85.refs_0_.pref, bf16[576,2560]{1,0:T(8,128)(2,1)} %shard_map.224.refs_1_.refs_2_.refs_3_, ...), custom_call_target="tpu_custom_call" | custom-call | flops 16000000000 | bytes 11827200 | tf_op jit(solution)/shard_map/pallas_call | solution.py:146
  108.3 0.0 collective-permute-done.3.c1
  108.4 0.0 collective-permute-done.4.c2
  108.4 1.9 collective-permute-start.7
  110.3 0.0 collective-permute-start.8
  110.3 0.3 collective-permute-start.9
  110.6 18.6 %shard_map.226 = (bf16[768,640]{1,0:T(8,128)(2,1)}, bf16[640,768]{1,0:T(8,128)(2,1)}, f32[640,768]{1,0:T(8,128)}, f32[640,1]{1,0:T(8,128)}, bf16[640,3072]{1,0:T...) custom-call(s32[3]{0:T(128)} %get-tuple-element.85.refs_0_.pref, ...), custom_call_target="tpu_custom_call" | custom-call | flops 6794772480 | bytes 27364352 | tf_op jit(solution)/shard_map/pallas_call | solution.py:146
  129.2 3.5 %collective-permute-start.6 = (bf16[640,768]{1,0:T(8,128)(2,1)}, bf16[640,768]{1,0:T(8,128)(2,1)S(1)}, u32[]{:S(2)}, u32[]{:S(2)}) collective-permute-start(bf16[640,768]{1,0:T(8,128)(2,1)} %get-tuple-element.110), channel_id=1, source_target_pairs={{0,0},{1,4},{2,2},{3,6},{4,1},{5,5},{6,3},{7,7},{8,8},{9,12},{10,1... | collective-permute-start | bytes 2949128 | tf_op jit(solution)/shard_map/ppermute | solution.py:67
  132.7 0.0 collective-permute-done.7.c1
  132.7 0.0 collective-permute-done.8.c2
  132.8 0.7 copy-done.11
  133.4 0.1 copy-done.12
  133.5 0.1 copy-done.13
  133.6 16.7 %shard_map.227 = (f32[640,768]{1,0:T(8,128)}, bf16[640,768]{1,0:T(8,128)(2,1)}, f32[3,768]{1,0:T(4,128)}) custom-call(s32[3]{0:T(128)} %get-tuple-element.85.refs_0_.pref, bf16[192,640]{1,0:T(8,128)(2,1)} %get-tuple-element.111.c0, bf16[192,640]{1,0:T(8,128)(2,1)} %copy-done.11, bf16[192,640]{1,0:T(8,128)(2,1)} %copy-done.12, bf16[192,640]{1,0:T(8,128)(2,1)} %copy-done.13, ...), custom_call_target="tpu_custom_call" | custom-call | flops 6794772480 | bytes 17522176 | tf_op jit(solution)/shard_map/pallas_call | solution.py:146
  150.3 17.6 %shard_map.228 = (bf16[640,3072]{1,0:T(8,128)(2,1)}, f32[1,3072]{1,0:T(1,128)}, f32[640,768]{1,0:T(8,128)}, bf16[640,768]{1,0:T(8,128)(2,1)}, bf16[192,640]{1,0:...) custom-call(s32[3]{0:T(128)} %get-tuple-element.85.refs_0_.pref, ...), custom_call_target="tpu_custom_call" | custom-call | flops 6794772480 | bytes 27364864 | tf_op jit(solution)/shard_map/pallas_call | solution.py:146
  168.0 0.5 collective-permute-start.10
  168.5 0.0 collective-permute-start.11
  168.5 1.7 collective-permute-start.12
  170.2 15.2 %shard_map.229 = (bf16[2,4,384,768]{3,2,1,0:T(8,128)(2,1)}, bf16[8,384,768]{2,1,0:T(8,128)(2,1)}, bf16[2,384,768]{2,1,0:T(8,128)(2,1)}) custom-call(s32[3]{0:T(128)} %get-tuple-element.85.refs_0_.pref, bf16[640,768]{1,0:T(8,128)(2,1)} %get-tuple-element.120.grad_ffn, bf16[640,3072]{1,0:T(8,128)(2,1)} %get-tuple-element.121.gelu, ...), custom_call_target="tpu_custom_call" | custom-call | flops 6794772480 | bytes 22413312 | tf_op jit(solution)/shard_map/pallas_call | solution.py:146
  185.4 0.0 collective-permute-done.10.refs_11_
  185.4 0.0 copy-start.8
  185.4 0.6 copy-done.8
  186.1 0.1 copy-done.9
  186.2 0.1 copy-done.10
  186.2 142.5 %shard_map.230 = (bf16[384,3072]{1,0:T(8,128)(2,1)}, bf16[4,384,768]{2,1,0:T(8,128)(2,1)}, bf16[384,768]{1,0:T(8,128)(2,1)}, f32[16,768]{1,0:T(8,128)}, bf16[6,1...) custom-call(s32[3]{0:T(128)} %get-tuple-element.85.refs_0_.pref, bf16[2,4,384,768]{3,2,1,0:T(8,128)(2,1)} %get-tuple-element.130.refs_1_, ...), custom_call_target="tpu_custom_call" | custom-call | flops 49999998976 | bytes 100000000 | tf_op jit(solution)/shard_map/pallas_call | solution.py:862
  328.8 0.7 slice.25
  329.5 0.7 slice.23
  330.2 0.7 dynamic_slice.7
  330.9 8.9 %shard_map.231 = (f32[1152,768]{1,0:T(8,128)}, f32[384,768]{1,0:T(8,128)}, f32[1536,768]{1,0:T(8,128)}, f32[384,3072]{1,0:T(8,128)}) custom-call(bf16[1152,768]{1,0:T(8,128)(2,1)} %bitcast.19, bf16[384,768]{1,0:T(8,128)(2,1)} %get-tuple-element.152.refs_1_, bf16[1536,768]{1,0:T(8,128)(2,1)} %bitcast.18, bf16[384,3072]{1,0:T(8,128)(2,1)} %get-tuple-element.154.refs_3_), custom_call_target="tpu_custom_call" | custom-call | bytes 21233664 | tf_op jit(solution)/shard_map/pallas_call | solution.py:1443
  339.8 0.6 constant_dynamic-slice_fusion
  340.4 0.7 fusion
  341.1 0.9 copy.27
  342.0 0.9 copy.28
  (25 shorter events, 0.1 us)
Async XLA Ops:
  51.8 22.8 %collective-permute-start = (bf16[640,768]{1,0:T(8,128)(2,1)}, bf16[640,768]{1,0:T(8,128)(2,1)S(1)}, u32[]{:S(2)}, u32[]{:S(2)}) collective-permute-start(bf16[640,768]{1,0:T(8,128)(2,1)} %get-tuple-element.86.refs_1_.x), channel_id=1, source_target_pairs={{0,2},{1,3},{2,0},{3,1},{4,6},{5,7},{6,4},{7,5},{8,10},{9,11},{10,... | collective-permute-start | bytes 2949128 | tf_op jit(solution)/shard_map/ppermute | solution.py:67
  51.8 25.7 %collective-permute-start.1 = (bf16[640,768]{1,0:T(8,128)(2,1)}, bf16[640,768]{1,0:T(8,128)(2,1)S(1)}, u32[]{:S(2)}, u32[]{:S(2)}) collective-permute-start(bf16[640,768]{1,0:T(8,128)(2,1)} %get-tuple-element.86.refs_1_.x), channel_id=1, source_target_pairs={{0,1},{1,0},{2,3},{3,2},{4,5},{5,4},{6,7},{7,6},{8,9},{9,8},{10,11... | collective-permute-start | bytes 2949128 | tf_op jit(solution)/shard_map/ppermute | solution.py:67
  51.9 22.7 %copy-start.4 = (f32[4,768]{1,0:T(4,128)S(1)}, f32[4,768]{1,0:T(4,128)}, u32[]{:S(2)}) copy-start(f32[4,768]{1,0:T(4,128)} %refs_11_.1) | copy-start | bytes 36868
  74.6 2.9 copy-start
  74.6 2.9 collective-permute-start.2
  75.4 33.0 %collective-permute-start.3 = (bf16[192,640]{1,0:T(8,128)(2,1)}, bf16[192,640]{1,0:T(8,128)(2,1)S(1)}, u32[]{:S(2)}, u32[]{:S(2)}) collective-permute-start(bf16[192,640]{1,0:T(8,128)(2,1)} %get-tuple-element.99), channel_id=1, source_target_pairs={{0,2},{1,3},{2,0},{3,1},{4,6},{5,7},{6,4},{7,5},{8,10},{9,11},{10,... | collective-permute-start | bytes 737288 | tf_op jit(solution)/shard_map/ppermute | solution.py:67
  77.2 31.2 %collective-permute-start.4 = (bf16[192,640]{1,0:T(8,128)(2,1)}, bf16[192,640]{1,0:T(8,128)(2,1)S(1)}, u32[]{:S(2)}, u32[]{:S(2)}) collective-permute-start(bf16[192,640]{1,0:T(8,128)(2,1)} %get-tuple-element.100), channel_id=1, source_target_pairs={{0,1},{1,0},{2,3},{3,2},{4,5},{5,4},{6,7},{7,6},{8,9},{9,8},{10,11... | collective-permute-start | bytes 737288 | tf_op jit(solution)/shard_map/ppermute | solution.py:67
  77.2 31.2 %collective-permute-start.5 = (bf16[192,640]{1,0:T(8,128)(2,1)}, bf16[192,640]{1,0:T(8,128)(2,1)S(1)}, u32[]{:S(2)}, u32[]{:S(2)}) collective-permute-start(bf16[192,640]{1,0:T(8,128)(2,1)} %get-tuple-element.101), channel_id=1, source_target_pairs={{0,3},{1,2},{2,1},{3,0},{4,7},{5,6},{6,5},{7,4},{8,11},{9,10},{10,... | collective-permute-start | bytes 737288 | tf_op jit(solution)/shard_map/ppermute | solution.py:67
  77.5 0.9 copy-start.1
  77.5 1.3 copy-start.3
  108.3 2.3 copy-start.5
  108.4 2.2 copy-start.6
  108.4 2.2 copy-start.7
  108.4 24.3 %collective-permute-start.7 = (bf16[192,640]{1,0:T(8,128)(2,1)}, bf16[192,640]{1,0:T(8,128)(2,1)S(1)}, u32[]{:S(2)}, u32[]{:S(2)}) collective-permute-start(bf16[192,640]{1,0:T(8,128)(2,1)} %get-tuple-element.112), channel_id=1, source_target_pairs={{0,2},{1,3},{2,0},{3,1},{4,6},{5,7},{6,4},{7,5},{8,10},{9,11},{10,... | collective-permute-start | bytes 737288 | tf_op jit(solution)/shard_map/ppermute | solution.py:67
  110.3 22.4 %collective-permute-start.8 = (bf16[192,640]{1,0:T(8,128)(2,1)}, bf16[192,640]{1,0:T(8,128)(2,1)S(1)}, u32[]{:S(2)}, u32[]{:S(2)}) collective-permute-start(bf16[192,640]{1,0:T(8,128)(2,1)} %get-tuple-element.113), channel_id=1, source_target_pairs={{0,1},{1,0},{2,3},{3,2},{4,5},{5,4},{6,7},{7,6},{8,9},{9,8},{10,11... | collective-permute-start | bytes 737288 | tf_op jit(solution)/shard_map/ppermute | solution.py:67
  110.3 22.5 %collective-permute-start.9 = (bf16[192,640]{1,0:T(8,128)(2,1)}, bf16[192,640]{1,0:T(8,128)(2,1)S(1)}, u32[]{:S(2)}, u32[]{:S(2)}) collective-permute-start(bf16[192,640]{1,0:T(8,128)(2,1)} %get-tuple-element.114), channel_id=1, source_target_pairs={{0,3},{1,2},{2,1},{3,0},{4,7},{5,6},{6,5},{7,4},{8,11},{9,10},{10,... | collective-permute-start | bytes 737288 | tf_op jit(solution)/shard_map/ppermute | solution.py:67
  129.2 211.9 %collective-permute-start.6 = (bf16[640,768]{1,0:T(8,128)(2,1)}, bf16[640,768]{1,0:T(8,128)(2,1)S(1)}, u32[]{:S(2)}, u32[]{:S(2)}) collective-permute-start(bf16[640,768]{1,0:T(8,128)(2,1)} %get-tuple-element.110), channel_id=1, source_target_pairs={{0,0},{1,4},{2,2},{3,6},{4,1},{5,5},{6,3},{7,7},{8,8},{9,12},{10,1... | collective-permute-start | bytes 2949128 | tf_op jit(solution)/shard_map/ppermute | solution.py:67
  132.7 0.7 copy-start.11
  132.8 0.8 copy-start.12
  132.8 0.8 copy-start.13
  168.0 17.4 %collective-permute-start.10 = (bf16[192,640]{1,0:T(8,128)(2,1)}, bf16[192,640]{1,0:T(8,128)(2,1)S(1)}, u32[]{:S(2)}, u32[]{:S(2)}) collective-permute-start(bf16[192,640]{1,0:T(8,128)(2,1)} %get-tuple-element.140), channel_id=1, source_target_pairs={{0,2},{1,3},{2,0},{3,1},{4,6},{5,7},{6,4},{7,5},{8,10},{9,11},{10,... | collective-permute-start | bytes 737288 | tf_op jit(solution)/shard_map/ppermute | solution.py:67
  168.5 16.9 %collective-permute-start.11 = (bf16[192,640]{1,0:T(8,128)(2,1)}, bf16[192,640]{1,0:T(8,128)(2,1)S(1)}, u32[]{:S(2)}, u32[]{:S(2)}) collective-permute-start(bf16[192,640]{1,0:T(8,128)(2,1)} %get-tuple-element.141), channel_id=1, source_target_pairs={{0,1},{1,0},{2,3},{3,2},{4,5},{5,4},{6,7},{7,6},{8,9},{9,8},{10,11... | collective-permute-start | bytes 737288 | tf_op jit(solution)/shard_map/ppermute | solution.py:67
  168.5 16.9 %collective-permute-start.12 = (bf16[192,640]{1,0:T(8,128)(2,1)}, bf16[192,640]{1,0:T(8,128)(2,1)S(1)}, u32[]{:S(2)}, u32[]{:S(2)}) collective-permute-start(bf16[192,640]{1,0:T(8,128)(2,1)} %get-tuple-element.142), channel_id=1, source_target_pairs={{0,3},{1,2},{2,1},{3,0},{4,7},{5,6},{6,5},{7,4},{8,11},{9,10},{10,... | collective-permute-start | bytes 737288 | tf_op jit(solution)/shard_map/ppermute | solution.py:67
  185.4 0.7 copy-start.8
  185.4 0.8 copy-start.9
  185.4 0.8 copy-start.10
  330.9 11.1 %copy-start.2 = (bf16[640,768]{1,0:T(8,128)(2,1)S(1)}, bf16[640,768]{1,0:T(8,128)(2,1)}, u32[]{:S(2)}) copy-start(bf16[640,768]{1,0:T(8,128)(2,1)} %get-tuple-element.150) | copy-start | bytes 2949124

commit v9 on v8

--- a/solution.py
+++ b/solution.py
@@ -927,7 +927,7 @@
     over = [copies.plan(xs.at[0, cut], xs.at[1, cut], next_chip) for cut in cuts]
     beside = [copies.plan(xs.at[0, cut], xs.at[2, cut], sibling) for cut in cuts]
     relay = [copies.plan(xs.at[1, cut], xs.at[3, cut], sibling) for cut in cuts]
-    t_swap = copies.plan(teach, held, partner)
+    t_swap = [copies.plan(teach.at[cut], held.at[cut], partner) for cut in cuts]
     t_load = copies.plan_local(teach, held)
     seg_copy = copies.remote(segments, others, sibling)
 
@@ -988,7 +988,7 @@
             swap[c].wait_recv()
             over[c].start()
             beside[c].start()
-        t_swap.start()
+            t_swap[c].start()
 
     qkv_copy.wait_recv()
     stores.append(copies.local(w_qkv, b_qkv))
@@ -1041,7 +1041,8 @@
 
     @pl.when(moves)
     def _():
-        t_swap.wait_recv()
+        for copy in t_swap:
+            copy.wait_recv()
 
     @pl.when(stays)
     def _():
@@ -1055,7 +1056,7 @@
 
     @pl.when(moves)
     def _():
-        for copy in swap + [t_swap]:
+        for copy in swap + t_swap:
             copy.wait_send()
 
     for copy in over + beside + relay:
@@ -1085,7 +1086,7 @@
         + [pltpu.VMEM(shape, F32) for shape in halves]
         + own
         + [pltpu.VMEM((3 * width // 4, 4 * tok), BF), pltpu.VMEM(segments.shape, jnp.int32)],
-        26,
+        29,
         30,
         3,
     )

time: 348 us -> 348 us (level)
  no operation moved by 1% of the time
where the time goes in v9:
time: 348 us; the launch traced here: 343 us
  Pallas kernels  322 us (93%)
  local copies, waits for them, and re-layouts  8.88 us (3%)
  starting transfers between devices  8.87 us (3%)
    pallas_call x2, Pallas kernels, remote_call(): pl.pallas_call(kernel, in_specs=in_specs, out_specs=out_specs, out_shape=...  193 us
    pallas_call x7, Pallas kernels, call(): pl.pallas_call(kernel, grid_spec=pltpu.PrefetchScalarGridSpec(num_scalar_...  120 us
    pallas_call x1, Pallas kernels, widen(): pl.pallas_call(widen_kernel, grid=(steps,), in_specs=specs, out_specs=spe...  8.87 us
    ppermute x13, starting transfers between devices, permute(): return lax.ppermute(values, AXES, pairs)  8.87 us
  transfers between devices with their start and end apart: 13, of which 1 were waited for; matrix products, arithmetic and copies ran while one was open for 1% of the time, Pallas kernels for 79%

profile of v9, /device:TPU:24, one launch (start us, length us, event | category | flops | bytes accessed | tf_op | source)
XLA Modules:
  0.0 342.7 jit_solution(550545094954353606)
XLA Ops:
  0.6 51.6 %shard_map.222 = (s32[3]{0:T(128)}, bf16[576,2560]{1,0:T(8,128)(2,1)}, bf16[640,768]{1,0:T(8,128)(2,1)}, bf16[640,768]{1,0:T(8,128)(2,1)}, bf16[640,768]{1,0:T(8...) custom-call(bf16[640,768]{1,0:T(8,128)(2,1)} %bitcast.22, ...), custom_call_target="tpu_custom_call" | custom-call | flops 49999998976 | bytes 100000000 | tf_op jit(solution)/shard_map/pallas_call | solution.py:862
  52.3 0.1 collective-permute-start
  52.4 0.3 collective-permute-start.1
  52.7 22.2 %shard_map.223 = (bf16[192,640]{1,0:T(8,128)(2,1)}, bf16[192,640]{1,0:T(8,128)(2,1)}, bf16[192,640]{1,0:T(8,128)(2,1)}, bf16[192,640]{1,0:T(8,128)(2,1)}, f32[19...) custom-call(s32[3]{0:T(128)} %get-tuple-element.85.refs_0_.pref, ...), custom_call_target="tpu_custom_call" | custom-call | flops 16000000000 | bytes 14776320 | tf_op jit(solution)/shard_map/pallas_call | solution.py:146
  74.8 1.6 collective-permute-done.refs_2_
  76.5 0.0 collective-permute-start.2
  76.5 0.6 fusion.1
  77.1 0.6 collective-permute-start.3
  77.7 0.0 collective-permute-start.4
  77.7 1.5 collective-permute-start.5
  79.3 0.0 copy-start.3
  79.3 0.9 copy-done.1
  80.2 0.3 copy-done.3
  80.5 8.4 %shard_map.224.refs_1_.refs_2_.refs_3_ = bf16[576,2560]{1,0:T(8,128)(2,1)} custom-call(s32[3]{0:T(128)} %get-tuple-element.85.refs_0_.pref, bf16[640,768]{1,0:T(8,128)(2,1)} %get-tuple-element.86.refs_1_.x, bf16[640,768]{1,0:T(8,128)(2,1)} %copy-done, bf16[640,768]{1,0:T(8,128)(2,1)} %copy-done.1, bf16[640,768]{1,0:T(8,128)(2,1)} %copy-done.3, ...), custom_call_target="tpu_custom_call" | custom-call | flops 2264924160 | bytes 17498112 | tf_op jit(solution)/shard_map/pallas_call | solution.py:146
  88.9 21.2 %shard_map.225 = (bf16[192,640]{1,0:T(8,128)(2,1)}, bf16[192,640]{1,0:T(8,128)(2,1)}, bf16[192,640]{1,0:T(8,128)(2,1)}, bf16[192,640]{1,0:T(8,128)(2,1)}, f32[192,2560]{1,0:T(8,128)}, /*index=5*/f32[3,1,2560]{2,1,0:T(1,128)}) custom-call(s32[3]{0:T(128)} %get-tuple-element.85.refs_0_.pref, bf16[576,2560]{1,0:T(8,128)(2,1)} %shard_map.224.refs_1_.refs_2_.refs_3_, ...), custom_call_target="tpu_custom_call" | custom-call | flops 16000000000 | bytes 11827200 | tf_op jit(solution)/shard_map/pallas_call | solution.py:146
  110.1 0.0 collective-permute-done.4.c2
  110.2 0.0 collective-permute-done.5.c3
  110.2 0.7 collective-permute-start.7
  110.8 0.0 collective-permute-start.8
  110.8 1.5 collective-permute-start.9
  112.4 18.6 %shard_map.226 = (bf16[768,640]{1,0:T(8,128)(2,1)}, bf16[640,768]{1,0:T(8,128)(2,1)}, f32[640,768]{1,0:T(8,128)}, f32[640,1]{1,0:T(8,128)}, bf16[640,3072]{1,0:T...) custom-call(s32[3]{0:T(128)} %get-tuple-element.85.refs_0_.pref, ...), custom_call_target="tpu_custom_call" | custom-call | flops 6794772480 | bytes 27364352 | tf_op jit(solution)/shard_map/pallas_call | solution.py:146
  131.0 1.9 collective-permute-start.6
  132.9 0.0 collective-permute-done.8.c2
  132.9 0.0 collective-permute-done.9.c3
  133.0 0.7 copy-done.11
  133.6 0.1 copy-done.12
  133.7 0.1 copy-done.13
  133.8 16.7 %shard_map.227 = (f32[640,768]{1,0:T(8,128)}, bf16[640,768]{1,0:T(8,128)(2,1)}, f32[3,768]{1,0:T(4,128)}) custom-call(s32[3]{0:T(128)} %get-tuple-element.85.refs_0_.pref, bf16[192,640]{1,0:T(8,128)(2,1)} %get-tuple-element.111.c0, bf16[192,640]{1,0:T(8,128)(2,1)} %copy-done.11, bf16[192,640]{1,0:T(8,128)(2,1)} %copy-done.12, bf16[192,640]{1,0:T(8,128)(2,1)} %copy-done.13, ...), custom_call_target="tpu_custom_call" | custom-call | flops 6794772480 | bytes 17522176 | tf_op jit(solution)/shard_map/pallas_call | solution.py:146
  150.5 17.6 %shard_map.228 = (bf16[640,3072]{1,0:T(8,128)(2,1)}, f32[1,3072]{1,0:T(1,128)}, f32[640,768]{1,0:T(8,128)}, bf16[640,768]{1,0:T(8,128)(2,1)}, bf16[192,640]{1,0:...) custom-call(s32[3]{0:T(128)} %get-tuple-element.85.refs_0_.pref, ...), custom_call_target="tpu_custom_call" | custom-call | flops 6794772480 | bytes 27364864 | tf_op jit(solution)/shard_map/pallas_call | solution.py:146
  168.2 0.7 collective-permute-start.10
  168.8 1.5 collective-permute-start.12
  170.4 15.2 %shard_map.229 = (bf16[2,4,384,768]{3,2,1,0:T(8,128)(2,1)}, bf16[8,384,768]{2,1,0:T(8,128)(2,1)}, bf16[2,384,768]{2,1,0:T(8,128)(2,1)}) custom-call(s32[3]{0:T(128)} %get-tuple-element.85.refs_0_.pref, bf16[640,768]{1,0:T(8,128)(2,1)} %get-tuple-element.120.grad_ffn, bf16[640,3072]{1,0:T(8,128)(2,1)} %get-tuple-element.121.gelu, ...), custom_call_target="tpu_custom_call" | custom-call | flops 6794772480 | bytes 22413312 | tf_op jit(solution)/shard_map/pallas_call | solution.py:146
  185.6 0.0 collective-permute-done.10.refs_11_
  185.6 0.0 copy-start.8
  185.6 0.0 collective-permute-done.11.refs_12_
  185.6 0.0 collective-permute-done.12.refs_13_
  185.6 0.6 copy-done.8
  186.3 0.1 copy-done.9
  186.4 0.1 copy-done.10
  186.4 141.8 %shard_map.230 = (bf16[384,3072]{1,0:T(8,128)(2,1)}, bf16[4,384,768]{2,1,0:T(8,128)(2,1)}, bf16[384,768]{1,0:T(8,128)(2,1)}, f32[16,768]{1,0:T(8,128)}, bf16[6,1...) custom-call(s32[3]{0:T(128)} %get-tuple-element.85.refs_0_.pref, bf16[2,4,384,768]{3,2,1,0:T(8,128)(2,1)} %get-tuple-element.130.refs_1_, ...), custom_call_target="tpu_custom_call" | custom-call | flops 49999998976 | bytes 100000000 | tf_op jit(solution)/shard_map/pallas_call | solution.py:862
  328.2 0.7 slice.25
  328.9 0.7 slice.23
  329.7 0.7 dynamic_slice.7
  330.4 8.9 %shard_map.231 = (f32[1152,768]{1,0:T(8,128)}, f32[384,768]{1,0:T(8,128)}, f32[1536,768]{1,0:T(8,128)}, f32[384,3072]{1,0:T(8,128)}) custom-call(bf16[1152,768]{1,0:T(8,128)(2,1)} %bitcast.19, bf16[384,768]{1,0:T(8,128)(2,1)} %get-tuple-element.152.refs_1_, bf16[1536,768]{1,0:T(8,128)(2,1)} %bitcast.18, bf16[384,3072]{1,0:T(8,128)(2,1)} %get-tuple-element.154.refs_3_), custom_call_target="tpu_custom_call" | custom-call | bytes 21233664 | tf_op jit(solution)/shard_map/pallas_call | solution.py:1444
  339.3 0.6 constant_dynamic-slice_fusion
  339.8 0.7 fusion
  340.5 0.9 copy.27
  341.5 0.9 copy.28
  (25 shorter events, 0.1 us)
Async XLA Ops:
  52.3 24.2 %collective-permute-start = (bf16[640,768]{1,0:T(8,128)(2,1)}, bf16[640,768]{1,0:T(8,128)(2,1)S(1)}, u32[]{:S(2)}, u32[]{:S(2)}) collective-permute-start(bf16[640,768]{1,0:T(8,128)(2,1)} %get-tuple-element.86.refs_1_.x), channel_id=1, source_target_pairs={{0,2},{1,3},{2,0},{3,1},{4,6},{5,7},{6,4},{7,5},{8,10},{9,11},{10,... | collective-permute-start | bytes 2949128 | tf_op jit(solution)/shard_map/ppermute | solution.py:67
  52.4 26.9 %collective-permute-start.1 = (bf16[640,768]{1,0:T(8,128)(2,1)}, bf16[640,768]{1,0:T(8,128)(2,1)S(1)}, u32[]{:S(2)}, u32[]{:S(2)}) collective-permute-start(bf16[640,768]{1,0:T(8,128)(2,1)} %get-tuple-element.86.refs_1_.x), channel_id=1, source_target_pairs={{0,1},{1,0},{2,3},{3,2},{4,5},{5,4},{6,7},{7,6},{8,9},{9,8},{10,11... | collective-permute-start | bytes 2949128 | tf_op jit(solution)/shard_map/ppermute | solution.py:67
  52.7 23.8 %copy-start.4 = (f32[4,768]{1,0:T(4,128)S(1)}, f32[4,768]{1,0:T(4,128)}, u32[]{:S(2)}) copy-start(f32[4,768]{1,0:T(4,128)} %refs_11_.1) | copy-start | bytes 36868
  76.5 2.8 copy-start
  76.5 2.8 collective-permute-start.2
  77.1 33.0 %collective-permute-start.3 = (bf16[192,640]{1,0:T(8,128)(2,1)}, bf16[192,640]{1,0:T(8,128)(2,1)S(1)}, u32[]{:S(2)}, u32[]{:S(2)}) collective-permute-start(bf16[192,640]{1,0:T(8,128)(2,1)} %get-tuple-element.99), channel_id=1, source_target_pairs={{0,2},{1,3},{2,0},{3,1},{4,6},{5,7},{6,4},{7,5},{8,10},{9,11},{10,... | collective-permute-start | bytes 737288 | tf_op jit(solution)/shard_map/ppermute | solution.py:67
  77.7 32.4 %collective-permute-start.4 = (bf16[192,640]{1,0:T(8,128)(2,1)}, bf16[192,640]{1,0:T(8,128)(2,1)S(1)}, u32[]{:S(2)}, u32[]{:S(2)}) collective-permute-start(bf16[192,640]{1,0:T(8,128)(2,1)} %get-tuple-element.100), channel_id=1, source_target_pairs={{0,1},{1,0},{2,3},{3,2},{4,5},{5,4},{6,7},{7,6},{8,9},{9,8},{10,11... | collective-permute-start | bytes 737288 | tf_op jit(solution)/shard_map/ppermute | solution.py:67
  77.7 32.4 %collective-permute-start.5 = (bf16[192,640]{1,0:T(8,128)(2,1)}, bf16[192,640]{1,0:T(8,128)(2,1)S(1)}, u32[]{:S(2)}, u32[]{:S(2)}) collective-permute-start(bf16[192,640]{1,0:T(8,128)(2,1)} %get-tuple-element.101), channel_id=1, source_target_pairs={{0,3},{1,2},{2,1},{3,0},{4,7},{5,6},{6,5},{7,4},{8,11},{9,10},{10,... | collective-permute-start | bytes 737288 | tf_op jit(solution)/shard_map/ppermute | solution.py:67
  79.3 0.9 copy-start.1
  79.3 1.3 copy-start.3
  110.1 2.3 copy-start.5
  110.1 2.2 copy-start.6
  110.2 2.2 copy-start.7
  110.2 22.7 %collective-permute-start.7 = (bf16[192,640]{1,0:T(8,128)(2,1)}, bf16[192,640]{1,0:T(8,128)(2,1)S(1)}, u32[]{:S(2)}, u32[]{:S(2)}) collective-permute-start(bf16[192,640]{1,0:T(8,128)(2,1)} %get-tuple-element.112), channel_id=1, source_target_pairs={{0,2},{1,3},{2,0},{3,1},{4,6},{5,7},{6,4},{7,5},{8,10},{9,11},{10,... | collective-permute-start | bytes 737288 | tf_op jit(solution)/shard_map/ppermute | solution.py:67
  110.8 22.1 %collective-permute-start.8 = (bf16[192,640]{1,0:T(8,128)(2,1)}, bf16[192,640]{1,0:T(8,128)(2,1)S(1)}, u32[]{:S(2)}, u32[]{:S(2)}) collective-permute-start(bf16[192,640]{1,0:T(8,128)(2,1)} %get-tuple-element.113), channel_id=1, source_target_pairs={{0,1},{1,0},{2,3},{3,2},{4,5},{5,4},{6,7},{7,6},{8,9},{9,8},{10,11... | collective-permute-start | bytes 737288 | tf_op jit(solution)/shard_map/ppermute | solution.py:67
  110.8 22.1 %collective-permute-start.9 = (bf16[192,640]{1,0:T(8,128)(2,1)}, bf16[192,640]{1,0:T(8,128)(2,1)S(1)}, u32[]{:S(2)}, u32[]{:S(2)}) collective-permute-start(bf16[192,640]{1,0:T(8,128)(2,1)} %get-tuple-element.114), channel_id=1, source_target_pairs={{0,3},{1,2},{2,1},{3,0},{4,7},{5,6},{6,5},{7,4},{8,11},{9,10},{10,... | collective-permute-start | bytes 737288 | tf_op jit(solution)/shard_map/ppermute | solution.py:67
  131.0 209.5 %collective-permute-start.6 = (bf16[640,768]{1,0:T(8,128)(2,1)}, bf16[640,768]{1,0:T(8,128)(2,1)S(1)}, u32[]{:S(2)}, u32[]{:S(2)}) collective-permute-start(bf16[640,768]{1,0:T(8,128)(2,1)} %get-tuple-element.110), channel_id=1, source_target_pairs={{0,0},{1,4},{2,2},{3,6},{4,1},{5,5},{6,3},{7,7},{8,8},{9,12},{10,1... | collective-permute-start | bytes 2949128 | tf_op jit(solution)/shard_map/ppermute | solution.py:67
  132.9 0.7 copy-start.11
  132.9 0.8 copy-start.12
  132.9 0.8 copy-start.13
  168.2 17.4 %collective-permute-start.10 = (bf16[192,640]{1,0:T(8,128)(2,1)}, bf16[192,640]{1,0:T(8,128)(2,1)S(1)}, u32[]{:S(2)}, u32[]{:S(2)}) collective-permute-start(bf16[192,640]{1,0:T(8,128)(2,1)} %get-tuple-element.140), channel_id=1, source_target_pairs={{0,2},{1,3},{2,0},{3,1},{4,6},{5,7},{6,4},{7,5},{8,10},{9,11},{10,... | collective-permute-start | bytes 737288 | tf_op jit(solution)/shard_map/ppermute | solution.py:67
  168.8 16.8 %collective-permute-start.11 = (bf16[192,640]{1,0:T(8,128)(2,1)}, bf16[192,640]{1,0:T(8,128)(2,1)S(1)}, u32[]{:S(2)}, u32[]{:S(2)}) collective-permute-start(bf16[192,640]{1,0:T(8,128)(2,1)} %get-tuple-element.141), channel_id=1, source_target_pairs={{0,1},{1,0},{2,3},{3,2},{4,5},{5,4},{6,7},{7,6},{8,9},{9,8},{10,11... | collective-permute-start | bytes 737288 | tf_op jit(solution)/shard_map/ppermute | solution.py:67
  168.8 16.8 %collective-permute-start.12 = (bf16[192,640]{1,0:T(8,128)(2,1)}, bf16[192,640]{1,0:T(8,128)(2,1)S(1)}, u32[]{:S(2)}, u32[]{:S(2)}) collective-permute-start(bf16[192,640]{1,0:T(8,128)(2,1)} %get-tuple-element.142), channel_id=1, source_target_pairs={{0,3},{1,2},{2,1},{3,0},{4,7},{5,6},{6,5},{7,4},{8,11},{9,10},{10,... | collective-permute-start | bytes 737288 | tf_op jit(solution)/shard_map/ppermute | solution.py:67
  185.6 0.7 copy-start.8
  185.6 0.8 copy-start.9
  185.6 0.8 copy-start.10
  330.4 11.1 %copy-start.2 = (bf16[640,768]{1,0:T(8,128)(2,1)S(1)}, bf16[640,768]{1,0:T(8,128)(2,1)}, u32[]{:S(2)}) copy-start(bf16[640,768]{1,0:T(8,128)(2,1)} %get-tuple-element.150) | copy-start | bytes 2949124
